TPU v7x, 512 devices: a whole 4x8x8 slice. The times are simulated.
512 devices in a mesh: dp: 32 (over z, y_lo), expert: 16 (over x, y_hi, core).
Axes of the slice: x: 4, y: 8 (y_hi: 2, y_lo: 4; y = y_hi * 4 + y_lo), z: 8, core: 2. Of those that a mesh axis runs over, the one named last changes fastest.
Arguments:
- grad_out: bfloat16 [65536, 2880], P(('dp', 'expert')), may hold values from -256 to 256
- hidden_act: bfloat16 [65536, 4, 360], P(('dp', 'expert')), may hold values from -6 to 6
- gate_weights: bfloat16 [65536, 4], P(('dp', 'expert')), may hold values from 0.099609375 to 0.69921875
- routing: int32 [65536, 4], P(('dp', 'expert')), may hold values from 0 to 15, all different within a row; in each aligned block of 128 rows (0 to 127, 128 to 255, ...) at most 40 rows name the same one
- resp_lengths: int32 [512, 4], P(('dp', 'expert')), may hold values from 1 to 64, 128 in all within a row
- advantage: float32 [512, 4], P(('dp', 'expert')), may hold values from -4 to 4
- w_down: bfloat16 [16, 360, 2880], P('expert', None, 'dp'), may hold values from -0.3125 to 0.3125
Outputs:
- grad_down: float32 [16, 360, 2880], P('expert', None, 'dp')
- grad_hidden: float32 [65536, 4, 360], P(('dp', 'expert'))
- grad_gates: float32 [65536, 4], P(('dp', 'expert'))
Inputs may be any that keep to these rules, and one draw needn't show every extreme that they name: `routing`: each token names 4 different experts; within the 128 tokens of one device no expert is named more than 40 times, a bound that some block reaches. `resp_lengths`: the 4 lengths of one device add up to 128; the largest is 64.
All inputs are finite; a program needn't handle non-finite values.
Results may differ from a plain program's by a relative error of at most 0.0041.
Values may be sent and summed in bfloat16 or wider, within the bound.
No kernel may reach another device: no remote copies, remote signals or barrier semaphores. Data moves between devices by JAX's collectives and lax.ppermute only.
A program may use at most 64 MiB of HBM per device.

v0:
```python
import jax
import jax.numpy as jnp
from jax import lax
from jax.sharding import PartitionSpec as P


def weight_terms(hid_recv, gated):
    partial_term = lax.dot_general(
        hid_recv, gated, (((0,), (0,)), ((), ())), preferred_element_type=jnp.float32
    )
    return lax.psum_scatter(partial_term, "dp", scatter_dimension=1, tiled=True)[None]


def local(grad_out, hidden_act, gate_weights, routing, resp_lengths, advantage, w_down):
    rows = grad_out.shape[0]
    width = grad_out.shape[1]
    topk = routing.shape[1]
    ffw = hidden_act.shape[2]
    nexp = lax.axis_size("expert")
    cap = min(rows, 5 * rows * topk // (4 * nexp))
    items = rows * topk
    slots = nexp * cap
    ends = jnp.cumsum(resp_lengths[0])
    starts = ends - resp_lengths[0]
    position = jnp.arange(rows, dtype=jnp.int32)
    inside = (position[:, None] >= starts[None, :]) & (position[:, None] < ends[None, :])
    ratio = advantage[0] / resp_lengths[0].astype(jnp.float32)
    scale = jnp.sum(jnp.where(inside, ratio[None, :], 0.0), axis=1)
    cotan = (scale[:, None] * grad_out.astype(jnp.float32)).astype(jnp.bfloat16)
    dest = routing.reshape(-1)
    onehot = (dest[:, None] == jnp.arange(nexp, dtype=jnp.int32)[None, :]).astype(jnp.int32)
    rank = jnp.cumsum(onehot, axis=0) - onehot
    place = jnp.sum(rank * onehot, axis=1)
    flat = dest * cap + place
    slot_item = (
        jnp.full((slots,), items, jnp.int32).at[flat].set(jnp.arange(items, dtype=jnp.int32))
    )
    valid = slot_item < items
    safe = jnp.minimum(slot_item, items - 1)
    send_cot = jnp.where(valid[:, None], cotan[safe // topk], jnp.zeros((), jnp.bfloat16))
    send_hid = jnp.where(
        valid[:, None], hidden_act.reshape(items, ffw)[safe], jnp.zeros((), jnp.bfloat16)
    )
    send_gate = jnp.where(valid, gate_weights.reshape(items)[safe], jnp.zeros((), jnp.bfloat16))
    recv_cot, recv_hid, recv_gate = (
        lax.all_to_all(
            send_cot.reshape(nexp, cap, width), "expert", split_axis=0, concat_axis=0, tiled=True
        ),
        lax.all_to_all(
            send_hid.reshape(nexp, cap, ffw), "expert", split_axis=0, concat_axis=0, tiled=True
        ),
        lax.all_to_all(
            send_gate.reshape(nexp, cap), "expert", split_axis=0, concat_axis=0, tiled=True
        ),
    )
    recv_cot = recv_cot.reshape(slots, width)
    recv_hid = recv_hid.reshape(slots, ffw)
    recv_gate = recv_gate.reshape(slots).astype(jnp.float32)
    gated = (recv_gate[:, None] * recv_cot.astype(jnp.float32)).astype(jnp.bfloat16)
    local_weight = w_down[0]
    piece = lax.all_gather(local_weight, "dp", axis=1, tiled=True)
    back_sum = lax.dot_general(
        recv_cot, piece, (((1,), (1,)), ((), ())), preferred_element_type=jnp.float32
    )
    output = jnp.dot(recv_hid, piece, preferred_element_type=jnp.float32)
    gate_sum = jnp.sum(recv_cot.astype(jnp.float32) * output, axis=1)
    dhid = recv_gate[:, None] * back_sum
    result_hid, result_gate = (
        lax.all_to_all(
            dhid.reshape(nexp, cap, ffw), "expert", split_axis=0, concat_axis=0, tiled=True
        ),
        lax.all_to_all(
            gate_sum.reshape(nexp, cap), "expert", split_axis=0, concat_axis=0, tiled=True
        ),
    )
    grad_down = weight_terms(recv_hid, gated)
    grad_hidden = result_hid.reshape(slots, ffw)[flat].reshape(rows, topk, ffw)
    grad_gates = result_gate.reshape(slots)[flat].reshape(rows, topk)
    return (grad_down, grad_hidden, grad_gates)


def solution(mesh):
    placed = (
        P(("dp", "expert"), None),
        P(("dp", "expert"), None, None),
        P(("dp", "expert"), None),
        P(("dp", "expert"), None),
        P(("dp", "expert"), None),
        P(("dp", "expert"), None),
        P("expert", None, "dp"),
    )
    return jax.shard_map(
        local,
        mesh=mesh,
        in_specs=placed,
        out_specs=(
            P("expert", None, "dp"),
            P(("dp", "expert"), None, None),
            P(("dp", "expert"), None),
        ),
        check_vma=False,
    )
```

profile of v0, /device:TPU:2, one launch (start us, length us, event | category | flops | bytes accessed | tf_op | source)
XLA Modules:
  0.0 483.2 jit_solution(13386527901734005974)
XLA Ops:
  7.2 0.7 broadcast_multiply_fusion
  7.8 0.8 copy.72
  8.6 0.1 eq.29
  8.7 0.1 eq.25
  8.9 0.8 copy.76
  9.7 0.1 reshape.133
  9.8 0.1 copy.71
  9.9 0.1 mul.49
  10.0 1.2 reduce-window.10
  11.2 0.2 slice_reduce_fusion
  11.4 0.1 fusion.10
  11.6 2.4 scatter_custom_fusion
  14.0 4.3 gather_fusion.1
  18.4 0.7 all_to_all.28
  19.1 10.1 %all-to-all-start.1 = ((bf16[16,1,40]{2,1,0:T(2,128)(2,1)}), bf16[16,1,40]{2,1,0:T(2,128)(2,1)S(1)}, u32[]{:S(2)}, u32[]{:S(2)}) async-start(bf16[16,1,40]{2,1,0:T(2,128)(2,1)} %all_to_all.28), calls=%async_computation.1 | async-start | bytes 16384 | tf_op jit(solution)/shard_map/all_to_all | solution.py:52
  29.2 0.8 reduce-window.14
  30.0 0.7 fusion.17
  30.7 0.7 fusion.18
  31.3 0.1 broadcast_in_dim.68
  31.4 0.1 select_reduce_fusion
  31.5 1.3 multiply_convert_fusion.2
  32.8 0.3 copy.78
  33.1 4.6 gather_fusion.2
  37.7 4.4 broadcast_select_fusion
  42.1 0.0 all-to-all-done.1
  42.1 9.8 %all-to-all-start.2 = ((bf16[16,40,2880]{2,1,0:T(8,128)(2,1)}), bf16[16,40,2880]{2,1,0:T(8,128)(2,1)}, u32[]{:S(2)}, u32[]{:S(2)}) async-start(bf16[16,40,2880]{2,1,0:T(8,128)(2,1)} %broadcast_select_fusion), calls=%async_computation.2 | async-start | bytes 7536640 | tf_op jit(solution)/shard_map/all_to_all | solution.py:46
  51.9 0.0 all-gather.3.cloned.1.call-start
  52.0 0.8 copy.79
  52.7 0.0 all-gather.3.cloned.1.call-update
  52.8 0.2 copy.75
  53.0 0.2 reshape.132
  53.2 2.9 gather_fusion
  56.1 0.9 broadcast_select_fusion.1
  57.0 88.0 %all-to-all-done.2 = bf16[16,40,2880]{2,1,0:T(8,128)(2,1)} async-done(((bf16[16,40,2880]{2,1,0:T(8,128)(2,1)}), bf16[16,40,2880]{2,1,0:T(8,128)(2,1)}, u32[]{:S(2)}, u32[]{:S(2)}) %all-to-all-start.2) | async-done | bytes 3686432 | tf_op jit(solution)/shard_map/all_to_all | solution.py:46
  145.0 9.9 %all-to-all-start = ((bf16[16,40,360]{2,1,0:T(8,128)(2,1)}), bf16[16,40,360]{2,1,0:T(8,128)(2,1)S(1)}, u32[]{:S(2)}, u32[]{:S(2)}) async-start(bf16[16,40,360]{2,1,0:T(8,128)(2,1)} %broadcast_select_fusion.1), calls=%async_computation | async-start | bytes 983040 | tf_op jit(solution)/shard_map/all_to_all | solution.py:49
  154.9 0.1 reshape.144
  155.0 124.1 %all-gather.3.cloned.1.call-done = bf16[1,360,2880]{1,0,2:T(2,128)(2,1)} async-done(((bf16[1,360,90]{1,0,2:T(2,128)(2,1)}), bf16[1,360,2880]{1,0,2:T(2,128)(2,1)}) %all-gather.3.cloned.1.call-update) | async-done | bytes 2073616 | tf_op jit(solution)/shard_map/all_gather | solution.py:61
  279.1 11.0 %copy.80 = bf16[1,360,2880]{2,1,0:T(8,128)(2,1)S(1)} copy(bf16[1,360,2880]{1,0,2:T(2,128)(2,1)} %all-gather.3.cloned.1.call-done) | data formatting | bytes 4147200 | tf_op jit(solution)/shard_map/all_gather | solution.py:61
  290.2 6.0 %copy.82 = bf16[640,2880]{0,1:T(8,128)(2,1)} copy(bf16[640,2880]{1,0:T(8,128)(2,1)} %bitcast.13) | data formatting | bytes 7372800 | tf_op jit(solution)/shard_map/reshape | solution.py:56
  296.2 4.0 fusion.5
  300.2 0.0 all-to-all-done
  300.2 4.4 multiply_reduce_fusion
  304.6 0.7 all_to_all.26
  305.3 11.3 %all-to-all-start.4 = ((f32[16,1,40]{2,1,0:T(1,128)}), f32[16,1,40]{2,1,0:T(1,128)S(1)}, u32[]{:S(2)}, u32[]{:S(2)}) async-start(f32[16,1,40]{2,1,0:T(1,128)} %all_to_all.26), calls=%async_computation.4 | async-start | bytes 16384 | tf_op jit(solution)/shard_map/all_to_all | solution.py:72
  316.6 6.5 %convolution_bitcast_fusion = f32[360,2880]{0,1:T(8,128)} fusion(bf16[16,40,360]{2,1,0:T(8,128)(2,1)S(1)} %all-to-all-done, bf16[16,40,2880]{2,1,0:T(8,128)(2,1)} %all-to-all-done.2, f32[16,40]{1,0:T(8,128)S(1)} %bitcast.60), kind=kOutput, calls=%fused_computation.8 | convolution fusion | flops 1332633600 | bytes 8296960 | tf_op jit(solution)/shard_map/dot_general | solution.py:8
  323.1 1.3 copy.81
  324.4 0.7 all-to-all-done.4
  325.1 8.9 %all-to-all-start.3 = ((f32[16,40,360]{2,1,0:T(8,128)}), f32[16,40,360]{2,1,0:T(8,128)S(1)}, u32[]{:S(2)}, u32[]{:S(2)}) async-start(f32[16,40,360]{2,1,0:T(8,128)} %bitcast.15), calls=%async_computation.3 | async-start | bytes 1966080 | tf_op jit(solution)/shard_map/all_to_all | solution.py:69
  334.0 129.1 %fusion = f32[360,96]{0,1:T(8,128)S(1)} fusion(f32[360,2880]{0,1:T(8,128)} %convolution_bitcast_fusion), kind=kCustom, calls=%all-reduce-scatter | all-reduce-scatter fusion | flops 1105921 | bytes 4287488
  463.1 1.3 collective-permute-start
  464.4 1.3 collective-permute-start.1
  465.7 1.3 dynamic-slice.4
  467.6 0.5 broadcast.102
  468.2 0.7 reduce.9
  468.8 0.1 reshape.141
  468.9 2.3 gather_fusion.4
  471.2 0.1 reshape.142
  471.3 0.7 copy.85
  472.0 0.0 collective-permute-done
  472.0 0.5 concatenate
  472.5 0.8 copy.83
  473.3 1.6 gather_fusion.3
  474.9 0.2 reshape.139
  475.1 1.2 copy.84
  (19 shorter events, 0.2 us)
Async XLA Ops:
  19.1 23.1 %all-to-all-start.1 = ((bf16[16,1,40]{2,1,0:T(2,128)(2,1)}), bf16[16,1,40]{2,1,0:T(2,128)(2,1)S(1)}, u32[]{:S(2)}, u32[]{:S(2)}) async-start(bf16[16,1,40]{2,1,0:T(2,128)(2,1)} %all_to_all.28), calls=%async_computation.1 | async-start | bytes 16384 | tf_op jit(solution)/shard_map/all_to_all | solution.py:52
  42.1 9.8 %copy-start.1 = (bf16[1,360,90]{1,2,0:T(8,128)(2,1)S(1)}, bf16[1,360,90]{1,2,0:T(8,128)(2,1)}, u32[]{:S(2)}) copy-start(bf16[1,360,90]{1,2,0:T(8,128)(2,1)} %param.13) | copy-start | bytes 194404
  42.1 10.6 %copy-start = (bf16[128,4,360]{0,2,1:T(8,128)(2,1)S(1)}, bf16[128,4,360]{0,2,1:T(8,128)(2,1)}, u32[]{:S(2)}) copy-start(bf16[128,4,360]{0,2,1:T(8,128)(2,1)} %param.8) | copy-start | bytes 1105924
  42.1 102.9 %all-to-all-start.2 = ((bf16[16,40,2880]{2,1,0:T(8,128)(2,1)}), bf16[16,40,2880]{2,1,0:T(8,128)(2,1)}, u32[]{:S(2)}, u32[]{:S(2)}) async-start(bf16[16,40,2880]{2,1,0:T(8,128)(2,1)} %broadcast_select_fusion), calls=%async_computation.2 | async-start | bytes 7536640 | tf_op jit(solution)/shard_map/all_to_all | solution.py:46
  51.9 227.2 %all-gather.3.cloned.1.call-start = ((), (), s32[]{:S(2)}) async-start(), calls=%async_computation.5 | async-start | bytes 4561920 | tf_op jit(solution)/shard_map/all_gather | solution.py:61
  145.0 155.1 %all-to-all-start = ((bf16[16,40,360]{2,1,0:T(8,128)(2,1)}), bf16[16,40,360]{2,1,0:T(8,128)(2,1)S(1)}, u32[]{:S(2)}, u32[]{:S(2)}) async-start(bf16[16,40,360]{2,1,0:T(8,128)(2,1)} %broadcast_select_fusion.1), calls=%async_computation | async-start | bytes 983040 | tf_op jit(solution)/shard_map/all_to_all | solution.py:49
  305.3 19.8 %all-to-all-start.4 = ((f32[16,1,40]{2,1,0:T(1,128)}), f32[16,1,40]{2,1,0:T(1,128)S(1)}, u32[]{:S(2)}, u32[]{:S(2)}) async-start(f32[16,1,40]{2,1,0:T(1,128)} %all_to_all.26), calls=%async_computation.4 | async-start | bytes 16384 | tf_op jit(solution)/shard_map/all_to_all | solution.py:72
  325.1 148.2 %all-to-all-start.3 = ((f32[16,40,360]{2,1,0:T(8,128)}), f32[16,40,360]{2,1,0:T(8,128)S(1)}, u32[]{:S(2)}, u32[]{:S(2)}) async-start(f32[16,40,360]{2,1,0:T(8,128)} %bitcast.15), calls=%async_computation.3 | async-start | bytes 1966080 | tf_op jit(solution)/shard_map/all_to_all | solution.py:69
  463.1 8.9 %collective-permute-start = (f32[360,96]{0,1:T(8,128)S(1)}, f32[360,96]{0,1:T(8,128)S(1)}, u32[]{:S(2)}, u32[]{:S(2)}) collective-permute-start(f32[360,96]{0,1:T(8,128)S(1)} %fusion), channel_id=1, source_target_pairs={{0,16},{16,32},{32,48},{48,64},{64,80},{80,96},{96,112},{112,128},... | collective-permute-start | bytes 414728
  464.4 7.6 %collective-permute-start.1 = (f32[360,90]{0,1:T(8,128)S(1)}, f32[360,90]{0,1:T(8,128)S(1)}, u32[]{:S(2)}, u32[]{:S(2)}) collective-permute-start(f32[360,90]{0,1:T(8,128)S(1)} %slice.19), channel_id=1, source_target_pairs={{0,32},{16,48},{32,64},{48,80},{64,96},{80,112},{96,128},{112,144}... | collective-permute-start | bytes 388808
Sparse Core Ops, SparseCore 0:
  55.4 223.6 all-gather.2
where the time goes:
time: 484 us; the launch traced here: 483 us
  waiting for transfers between devices  213 us (44%)
  blocking collectives  129 us (27%)
  starting transfers between devices  52.6 us (11%)
  local copies, waits for them, and re-layouts  47.2 us (10%)
  between operations  15 us (3%)
  matrix products  14.9 us (3%)
  other arithmetic  11.6 us (2%)
    unnamed x1, blocking collectives  129 us
    all_gather x1, waiting for transfers between devices, local(): piece = lax.all_gather(local_weight, 'dp', axis=1, tiled=True)  124 us
    all_to_all x1, waiting for transfers between devices, local(): lax.all_to_all(send_cot.reshape(nexp, cap, width), 'expert', split_axis=0...  88 us
    all_to_all x1, starting transfers between devices, local(): lax.all_to_all(gate_sum.reshape(nexp, cap), 'expert', split_axis=0, conca...  11.3 us
    all_gather x1, local copies, waits for them, and re-layouts, local(): piece = lax.all_gather(local_weight, 'dp', axis=1, tiled=True)  11 us
    all_to_all x1, starting transfers between devices, local(): lax.all_to_all(send_gate.reshape(nexp, cap), 'expert', split_axis=0, conc...  10.1 us
    all_to_all x1, starting transfers between devices, local(): lax.all_to_all(send_hid.reshape(nexp, cap, ffw), 'expert', split_axis=0,...  9.86 us
    all_to_all x1, starting transfers between devices, local(): lax.all_to_all(send_cot.reshape(nexp, cap, width), 'expert', split_axis=0...  9.77 us
  transfers between devices with their start and end apart: 8, of which 3 were waited for; matrix products, arithmetic and copies ran while one was open for 38% of the time, Pallas kernels for 0%

commit v1 on v0

v1 whole, which is shorter than its diff:
```python
import functools

import jax
import jax.numpy as jnp
from jax import lax
from jax.experimental import pallas as pl
from jax.experimental.pallas import tpu as pltpu
from jax.sharding import Mesh, PartitionSpec as P

BF = jnp.bfloat16
F32 = jnp.float32
NT = (((1,), (1,)), ((), ()))
TN = (((0,), (0,)), ((), ()))
NN = (((1,), (0,)), ((), ()))
ROWS, D, TOPK, FFW, NEXP, CAP, NDP = 128, 2880, 4, 360, 16, 40, 32
OWN = D // NDP
PAD = 96
WIDE = NDP * PAD
HALF = NEXP // 2
HSLOT = HALF * CAP
VMEM = pl.BlockSpec(memory_space=pltpu.VMEM)
SMEM = pl.BlockSpec(memory_space=pltpu.SMEM)


def params(mib=40):
    return pltpu.CompilerParams(vmem_limit_bytes=mib << 20)


def prep_kernel(yh_ref, len_ref, adv_ref, g_ref, r_ref, cot_ref, pm_ref, scr):
    pos = lax.broadcasted_iota(jnp.int32, (8, ROWS), 1)
    start = jnp.int32(0)
    scale = jnp.zeros((8, ROWS), F32)
    for s in range(4):
        n = len_ref[0, s]
        ratio = jnp.full((8, ROWS), adv_ref[0, s], F32) / jnp.full((8, ROWS), n, jnp.int32).astype(F32)
        scale = jnp.where((pos >= start) & (pos < start + n), ratio, scale)
        start = start + n
    scr[0:D] = g_ref[...].astype(F32) * scale[0:1]
    scr[D:] = jnp.zeros((8, ROWS), F32)
    keep = lax.broadcasted_iota(jnp.int32, (PAD, ROWS), 0) < OWN
    for d in range(NDP):
        block = scr[d * OWN : d * OWN + PAD]
        cot_ref[d * PAD : (d + 1) * PAD] = jnp.where(keep, block, 0.0).astype(BF)
    row = lax.broadcasted_iota(jnp.int32, (NEXP, ROWS), 0)
    eid = ((row >> 1) & 3) * 4 + (row >> 3) * 2 + (row & 1)
    hit = r_ref[0:1] == eid
    for k in range(1, TOPK):
        hit = hit | (r_ref[k : k + 1] == eid)
    a = lax.broadcasted_iota(jnp.int32, (ROWS, ROWS), 0)
    b = lax.broadcasted_iota(jnp.int32, (ROWS, ROWS), 1)
    before = (a < b).astype(F32).astype(BF)
    rank = lax.dot_general(hit.astype(F32).astype(BF), before, NN, preferred_element_type=F32)
    place = jnp.where(hit, rank, -1.0)
    pm_ref[...] = place
    other = jnp.where(yh_ref[0] == 0, place[HALF:], place[:HALF])
    cot_ref[WIDE:] = jnp.concatenate([other, jnp.zeros((HALF, ROWS), F32)], axis=0).astype(BF)


def prep(yh, lens, adv, gt, rt):
    return pl.pallas_call(
        prep_kernel,
        in_specs=[SMEM, SMEM, SMEM, VMEM, VMEM],
        out_specs=[VMEM, VMEM],
        out_shape=[jax.ShapeDtypeStruct((WIDE + 16, ROWS), BF), jax.ShapeDtypeStruct((NEXP, ROWS), F32)],
        scratch_shapes=[pltpu.VMEM((D + 8, ROWS), F32)],
        compiler_params=params(),
        name="prep",
    )(yh, lens, adv, gt, rt)


def slot_onehot(place, n):
    c = lax.broadcasted_iota(jnp.int32, (n, CAP, ROWS), 1).astype(F32)
    return (place[:, None, :] == c).astype(F32).reshape(n * CAP, ROWS)


def select_kernel(yh_ref, cot_ref, pm_ref, out_ref):
    place = jnp.where(yh_ref[0] == 0, pm_ref[:HALF], pm_ref[HALF:])
    s = slot_onehot(place, HALF).astype(BF)
    step = 768
    for i in range(0, WIDE, step):
        out_ref[:, i : i + step] = lax.dot_general(
            s, cot_ref[i : i + step], NT, preferred_element_type=F32
        ).astype(BF)


def select_own(yh, cot, pm):
    return pl.pallas_call(
        select_kernel,
        in_specs=[SMEM, VMEM, VMEM],
        out_specs=VMEM,
        out_shape=jax.ShapeDtypeStruct((HSLOT, WIDE), BF),
        compiler_params=params(),
        name="select_own",
    )(yh, cot, pm)


def forward_kernel(cot_ref, out_ref):
    place = cot_ref[WIDE:].astype(F32)[:HALF]
    s = slot_onehot(place, HALF).astype(BF)
    step = 768
    for i in range(0, WIDE, step):
        out_ref[:, i : i + step] = lax.dot_general(
            s, cot_ref[i : i + step], NT, preferred_element_type=F32
        ).astype(BF)


def select_partner(cot):
    return pl.pallas_call(
        forward_kernel,
        in_specs=[VMEM],
        out_specs=VMEM,
        out_shape=jax.ShapeDtypeStruct((HSLOT, WIDE), BF),
        compiler_params=params(),
        name="select_partner",
    )(cot)


def picks(pm_ref, r_ref):
    row = lax.broadcasted_iota(jnp.int32, (NEXP, ROWS), 0)
    eid = ((row >> 1) & 3) * 4 + (row >> 3) * 2 + (row & 1)
    place = pm_ref[...]
    return [
        slot_onehot(jnp.where(r_ref[k : k + 1] == eid, place, -1.0), NEXP).astype(BF)
        for k in range(TOPK)
    ]


def hid_kernel(h_ref, gate_ref, pm_ref, r_ref, out_ref):
    acc = jnp.zeros((NEXP * CAP, FFW), F32)
    gate = gate_ref[...].astype(F32)
    for k, s in enumerate(picks(pm_ref, r_ref)):
        hs = (h_ref[k].astype(F32) * gate[k : k + 1]).astype(BF)
        acc = acc + lax.dot_general(s, hs, NT, preferred_element_type=F32)
    out_ref[...] = acc.astype(BF)


def send_hidden(ht, gt, pm, rt):
    return pl.pallas_call(
        hid_kernel,
        in_specs=[VMEM] * 4,
        out_specs=VMEM,
        out_shape=jax.ShapeDtypeStruct((NEXP * CAP, FFW), BF),
        compiler_params=params(),
        name="send_hidden",
    )(ht, gt, pm, rt)


def term_kernel(yh_ref, own_ref, par_ref, h_ref, out_ref):
    yh = yh_ref[0]
    acc = lax.dot_general(own_ref[...], h_ref[yh], TN, preferred_element_type=F32)
    acc = acc + lax.dot_general(par_ref[...], h_ref[1 - yh], TN, preferred_element_type=F32)
    out_ref[...] = acc.astype(BF)


def grad_term(yh, own, par, hid):
    step = 768
    return pl.pallas_call(
        term_kernel,
        grid=(WIDE // step,),
        in_specs=[
            SMEM,
            pl.BlockSpec((HSLOT, step), lambda i: (0, i)),
            pl.BlockSpec((HSLOT, step), lambda i: (0, i)),
            pl.BlockSpec((2, HSLOT, FFW), lambda i: (0, 0, 0)),
        ],
        out_specs=pl.BlockSpec((step, FFW), lambda i: (i, 0)),
        out_shape=jax.ShapeDtypeStruct((WIDE, FFW), BF),
        compiler_params=params(),
        name="grad_term",
    )(yh, own, par, hid)


def back_kernel(yh_ref, own_ref, par_ref, w_ref, out_ref):
    yh = yh_ref[0]
    w = w_ref[...]
    out_ref[yh] = lax.dot_general(own_ref[...], w, NN, preferred_element_type=F32).astype(BF)
    out_ref[1 - yh] = lax.dot_general(par_ref[...], w, NN, preferred_element_type=F32).astype(BF)


def back_product(yh, own, par, w):
    return pl.pallas_call(
        back_kernel,
        in_specs=[SMEM, VMEM, VMEM, VMEM],
        out_specs=VMEM,
        out_shape=jax.ShapeDtypeStruct((2, HSLOT, FFW), BF),
        compiler_params=params(),
        name="back_product",
    )(yh, own, par, w)


def sum_kernel(x_ref, out_ref):
    acc = x_ref[0].astype(F32)
    for d in range(1, NDP):
        acc = acc + x_ref[d].astype(F32)
    out_ref[...] = acc[:OWN]


def sum_terms(x):
    return pl.pallas_call(
        sum_kernel,
        in_specs=[VMEM],
        out_specs=VMEM,
        out_shape=jax.ShapeDtypeStruct((OWN, FFW), F32),
        compiler_params=params(),
        name="sum_terms",
    )(x)


def home_kernel(x_ref, h_ref, gate_ref, pm_ref, r_ref, gh_ref, gg_ref):
    x = x_ref[...]
    gate = gate_ref[...].astype(F32)
    for k, s in enumerate(picks(pm_ref, r_ref)):
        back = lax.dot_general(x, s, TN, preferred_element_type=F32)
        gh_ref[k] = back * gate[k : k + 1]
        gg_ref[k : k + 1] = jnp.sum(back * h_ref[k].astype(F32), axis=0, keepdims=True)


def bring_home(x, ht, gt, pm, rt):
    return pl.pallas_call(
        home_kernel,
        in_specs=[VMEM] * 5,
        out_specs=[VMEM, VMEM],
        out_shape=[
            jax.ShapeDtypeStruct((TOPK, FFW, ROWS), F32),
            jax.ShapeDtypeStruct((TOPK, ROWS), F32),
        ],
        compiler_params=params(),
        name="bring_home",
    )(x, ht, gt, pm, rt)


def local(grad_out, hidden_act, gate_weights, routing, resp_lengths, advantage, w_down):
    yh = lax.axis_index("yh").reshape(1).astype(jnp.int32)
    gt = grad_out.T
    ht = jnp.transpose(hidden_act, (1, 2, 0))
    gates = gate_weights.T
    rt = routing.T

    wt = jnp.pad(w_down[0].T, ((0, PAD - OWN), (0, 0)))
    w4 = lax.all_gather(wt, "yl", axis=0, tiled=True)
    weight = lax.all_gather(w4, "z", axis=0, tiled=True)

    cot, pm = prep(yh, resp_lengths, advantage, gt, rt)
    cot_par = lax.ppermute(cot, "yh", [(0, 1), (1, 0)])
    own = select_own(yh, cot, pm)
    own = lax.all_to_all(
        own.reshape(HALF, CAP, WIDE), ("x", "c"), split_axis=0, concat_axis=0, tiled=True
    ).reshape(HSLOT, WIDE)
    hid = send_hidden(ht, gates, pm, rt)
    hid = lax.all_to_all(
        hid.reshape(NEXP, CAP, FFW), ("yh", "x", "c"), split_axis=0, concat_axis=0, tiled=True
    ).reshape(2, HSLOT, FFW)
    par = select_partner(cot_par)
    par = lax.all_to_all(
        par.reshape(HALF, CAP, WIDE), ("x", "c"), split_axis=0, concat_axis=0, tiled=True
    ).reshape(HSLOT, WIDE)

    term = grad_term(yh, own, par, hid)
    terms = lax.all_to_all(
        term.reshape(NDP, PAD, FFW), ("z", "yl"), split_axis=0, concat_axis=0, tiled=True
    )
    back = back_product(yh, own, par, weight)
    back = lax.all_to_all(
        back.reshape(NEXP, CAP, FFW), ("yh", "x", "c"), split_axis=0, concat_axis=0, tiled=True
    ).reshape(NEXP * CAP, FFW)
    gh, gg = bring_home(back, ht, gates, pm, rt)
    gd = sum_terms(terms)
    return gd.T[None], jnp.transpose(gh, (2, 0, 1)), gg.T


def solution(mesh):
    fine = Mesh(mesh.devices.reshape(8, 4, 4, 2, 2), ("z", "yl", "x", "yh", "c"))
    every = ("z", "yl", "x", "yh", "c")
    rows2 = P(every, None)
    rows3 = P(every, None, None)
    cols = P(("x", "yh", "c"), None, ("z", "yl"))
    return jax.shard_map(
        local,
        mesh=fine,
        in_specs=(rows2, rows3, rows2, rows2, rows2, rows2, cols),
        out_specs=(cols, rows3, rows2),
        check_vma=False,
    )
```

time: 484 us -> 236 us (0.49)
  the two profiles are of different devices: /device:TPU:2 before, /device:TPU:96 now
where the time goes in v1:
time: 236 us
  waiting for transfers between devices  134 us (57%)
  starting transfers between devices  45.4 us (19%)
  Pallas kernels  16.9 us (7%)
  blocking collectives  14.9 us (6%)
  between operations  14.2 us (6%)
  local copies, waits for them, and re-layouts  9.61 us (4%)
    all_to_all x1, waiting for transfers between devices, local(): lax.all_to_all(term.reshape(NDP, PAD, FFW), ('z', 'yl'), split_axis=0, co...  66.4 us
    ppermute x1, waiting for transfers between devices, local(): cot_par = lax.ppermute(cot, 'yh', [(0, 1), (1, 0)])  36.8 us
    all_to_all x1, waiting for transfers between devices, local(): lax.all_to_all(par.reshape(HALF, CAP, WIDE), ('x', 'c'), split_axis=0, co...  24.4 us
    all_to_all x1, starting transfers between devices, local(): lax.all_to_all(term.reshape(NDP, PAD, FFW), ('z', 'yl'), split_axis=0, co...  17.2 us
    all_gather x1, blocking collectives, local(): w4 = lax.all_gather(wt, 'yl', axis=0, tiled=True)  14.9 us
    unnamed x25, local copies, waits for them, and re-layouts  9.6 us
    all_to_all x1, starting transfers between devices, local(): lax.all_to_all(back.reshape(NEXP, CAP, FFW), ('yh', 'x', 'c'), split_axis...  8.88 us
    all_to_all x1, starting transfers between devices, local(): lax.all_to_all(hid.reshape(NEXP, CAP, FFW), ('yh', 'x', 'c'), split_axis=...  7.83 us
  transfers between devices with their start and end apart: 7, of which 5 were waited for; matrix products, arithmetic and copies ran while one was open for 0% of the time, Pallas kernels for 6%

profile of v1, /device:TPU:96, one launch (start us, length us, event | category | flops | bytes accessed | tf_op | source)
XLA Modules:
  0.0 235.5 jit_solution(18052832174123906329)
XLA Ops:
  7.2 0.0 copy-start.5
  7.2 1.1 copy-done.5
  8.3 0.0 copy-start.6
  8.3 0.7 copy-done.6
  9.0 0.0 copy-start.9
  9.0 0.7 copy-done.9
  9.6 0.0 copy-start.10
  9.6 0.7 copy-done.10
  10.3 0.9 prep.1
  11.2 0.7 select_own.1
  11.8 0.0 copy-start.1
  11.9 1.3 copy-done.1
  13.1 0.0 copy-start.11
  13.1 4.4 %all-to-all-start = ((bf16[8,40,3072]{2,1,0:T(8,128)(2,1)}), bf16[8,40,3072]{2,1,0:T(8,128)(2,1)S(1)}, u32[]{:S(2)}, u32[]{:S(2)}) async-start(bf16[8,40,3072]{2,1,0:T(8,128)(2,1)} %bitcast.25), calls=%async_computation | async-start | bytes 3932160 | tf_op jit(solution)/shard_map/all_to_all | solution.py:246
  17.6 0.0 all-gather.2.cloned.1.call-start
  17.6 0.0 copy-done.11
  17.6 14.9 %all_gather.6 = bf16[384,360]{1,0:T(8,128)(2,1)} all-gather(bf16[96,360]{1,0:T(8,128)(2,1)S(1)} %pad.4), channel_id=1, replica_groups=mesh['z'=8,'yl'=4,'x'=4,'yh'=2,'c'=2] {'yl'}, dimensions={0}, use_global_device_ids=true | all-gather | bytes 345600 | tf_op jit(solution)/shard_map/all_gather | solution.py:240
  32.6 0.0 all-gather.2.cloned.1.call-update
  32.6 2.3 collective-permute-start
  34.9 36.8 %collective-permute-done.cot_ref = bf16[3088,128]{1,0:T(8,128)(2,1)S(1)} collective-permute-done((bf16[3088,128]{1,0:T(8,128)(2,1)S(1)}, bf16[3088,128]{1,0:T(8,128)(2,1)S(1)}, u32[]{:S(2)}, u32[]{:S(2)}) %collective-permute-start) | collective-permute-done | bytes 790560 | tf_op jit(solution)/shard_map/ppermute | solution.py:244
  71.7 0.7 select_partner.1
  72.4 0.0 copy-start.2
  72.4 1.3 copy-done.2
  73.7 0.0 all-to-all-done
  73.7 0.0 copy-start.4
  73.7 0.0 copy-start.7
  73.7 0.0 copy-start.8
  73.7 4.8 %all-to-all-start.1 = ((bf16[8,40,3072]{2,1,0:T(8,128)(2,1)}), bf16[8,40,3072]{2,1,0:T(8,128)(2,1)}, u32[]{:S(2)}, u32[]{:S(2)}) async-start(bf16[8,40,3072]{2,1,0:T(8,128)(2,1)} %bitcast.26), calls=%async_computation.1 | async-start | bytes 3932160 | tf_op jit(solution)/shard_map/all_to_all | solution.py:254
  78.5 0.0 copy-done.4
  78.5 0.0 copy-done.7
  78.5 0.0 copy-done.8
  78.5 1.5 send_hidden.1
  80.0 24.4 %all-to-all-done.1 = bf16[8,40,3072]{2,1,0:T(8,128)(2,1)} async-done(((bf16[8,40,3072]{2,1,0:T(8,128)(2,1)}), bf16[8,40,3072]{2,1,0:T(8,128)(2,1)}, u32[]{:S(2)}, u32[]{:S(2)}) %all-to-all-start.1) | async-done | bytes 1966112 | tf_op jit(solution)/shard_map/all_to_all | solution.py:254
  104.4 7.8 %all-to-all-start.2 = ((bf16[16,40,360]{2,1,0:T(8,128)(2,1)}), bf16[16,40,360]{2,1,0:T(8,128)(2,1)S(1)}, u32[]{:S(2)}, u32[]{:S(2)}) async-start(bf16[16,40,360]{2,1,0:T(8,128)(2,1)} %bitcast.9), calls=%async_computation.2 | async-start | bytes 983040 | tf_op jit(solution)/shard_map/all_to_all | solution.py:250
  112.2 0.0 all-gather.2.cloned.1.call-done.w_ref
  112.2 0.0 copy-start.3
  112.2 1.7 copy-done.3
  113.9 4.5 %back_product.1 = bf16[2,320,360]{2,1,0:T(8,128)(2,1)} custom-call(s32[1]{0:T(128)} %bitcast.yh_ref, bf16[320,3072]{1,0:T(8,128)(2,1)S(1)} %bitcast.22, bf16[320,3072]{1,0:T(8,128)(2,1)} %bitcast.6.par_ref, bf16[3072,360]{1,0:T(8,128)(2,1)S(1)} %copy-done.3), custom_call_target="tpu_custom_call" | custom-call | tf_op jit(solution)/shard_map/back_product/pallas_call | solution.py:181
  118.4 4.1 %all-to-all-done.2 = bf16[16,40,360]{2,1,0:T(8,128)(2,1)S(1)} async-done(((bf16[16,40,360]{2,1,0:T(8,128)(2,1)}), bf16[16,40,360]{2,1,0:T(8,128)(2,1)S(1)}, u32[]{:S(2)}, u32[]{:S(2)}) %all-to-all-start.2) | async-done | bytes 460832 | tf_op jit(solution)/shard_map/all_to_all | solution.py:250
  122.6 8.9 %all-to-all-start.4 = ((bf16[16,40,360]{2,1,0:T(8,128)(2,1)}), bf16[16,40,360]{2,1,0:T(8,128)(2,1)S(1)}, u32[]{:S(2)}, u32[]{:S(2)}) async-start(bf16[16,40,360]{2,1,0:T(8,128)(2,1)} %bitcast.16), calls=%async_computation.4 | async-start | bytes 983040 | tf_op jit(solution)/shard_map/all_to_all | solution.py:263
  131.4 5.0 %grad_term.1 = bf16[3072,360]{1,0:T(8,128)(2,1)S(1)} custom-call(s32[1]{0:T(128)} %bitcast.yh_ref, bf16[320,3072]{1,0:T(8,128)(2,1)S(1)} %bitcast.23, bf16[320,3072]{1,0:T(8,128)(2,1)} %bitcast.6.par_ref, bf16[2,320,360]{2,1,0:T(8,128)(2,1)S(1)} %bitcast.28), custom_call_target="tpu_custom_call" | custom-call | tf_op jit(solution)/shard_map/grad_term/pallas_call | solution.py:157
  136.5 0.0 copy-start
  136.5 1.4 copy-done
  137.9 2.7 %all-to-all-done.4 = bf16[16,40,360]{2,1,0:T(8,128)(2,1)S(1)} async-done(((bf16[16,40,360]{2,1,0:T(8,128)(2,1)}), bf16[16,40,360]{2,1,0:T(8,128)(2,1)S(1)}, u32[]{:S(2)}, u32[]{:S(2)}) %all-to-all-start.4) | async-done | bytes 460832 | tf_op jit(solution)/shard_map/all_to_all | solution.py:263
  140.7 17.2 %all-to-all-start.3 = ((bf16[32,96,360]{2,1,0:T(8,128)(2,1)}), bf16[32,96,360]{2,1,0:T(8,128)(2,1)}, u32[]{:S(2)}, u32[]{:S(2)}) async-start(bf16[32,96,360]{2,1,0:T(8,128)(2,1)} %bitcast.24), calls=%async_computation.3 | async-start | bytes 4718592 | tf_op jit(solution)/shard_map/all_to_all | solution.py:259
  157.9 1.6 bring_home.1
  159.5 66.4 %all-to-all-done.3.x_ref = bf16[32,96,360]{2,1,0:T(8,128)(2,1)} async-done(((bf16[32,96,360]{2,1,0:T(8,128)(2,1)}), bf16[32,96,360]{2,1,0:T(8,128)(2,1)}, u32[]{:S(2)}, u32[]{:S(2)}) %all-to-all-start.3) | async-done | bytes 2211872 | tf_op jit(solution)/shard_map/all_to_all | solution.py:259
  225.9 2.0 sum_terms.1
  227.9 0.8 copy.10
  (1 shorter events, 0.0 us)
Async XLA Ops:
  7.2 1.1 copy-start.5
  8.3 0.7 copy-start.6
  9.0 0.7 copy-start.9
  9.6 0.7 copy-start.10
  11.8 1.3 copy-start.1
  13.1 4.5 %copy-start.11 = (bf16[1,360,90]{1,2,0:T(8,128)(2,1)S(1)}, bf16[1,360,90]{1,2,0:T(8,128)(2,1)}, u32[]{:S(2)}) copy-start(bf16[1,360,90]{1,2,0:T(8,128)(2,1)} %param.13) | copy-start | bytes 194404
  13.1 60.5 %all-to-all-start = ((bf16[8,40,3072]{2,1,0:T(8,128)(2,1)}), bf16[8,40,3072]{2,1,0:T(8,128)(2,1)S(1)}, u32[]{:S(2)}, u32[]{:S(2)}) async-start(bf16[8,40,3072]{2,1,0:T(8,128)(2,1)} %bitcast.25), calls=%async_computation | async-start | bytes 3932160 | tf_op jit(solution)/shard_map/all_to_all | solution.py:246
  17.6 94.7 %all-gather.2.cloned.1.call-start = ((), (), s32[]{:S(2)}) async-start(), calls=%async_computation.5 | async-start | bytes 2654208 | tf_op jit(solution)/shard_map/all_gather | solution.py:241
  32.6 39.1 %collective-permute-start = (bf16[3088,128]{1,0:T(8,128)(2,1)S(1)}, bf16[3088,128]{1,0:T(8,128)(2,1)S(1)}, u32[]{:S(2)}, u32[]{:S(2)}) collective-permute-start(bf16[3088,128]{1,0:T(8,128)(2,1)S(1)} %get-tuple-element.7.cot_ref), channel_id=1, source_target_pairs={{0,2},{2,0},{1,3},{3,1},{4,6},{6,4},{5,7},{7,5},{8,10},{10,8},{9,1... | collective-permute-start | bytes 2371592 | tf_op jit(solution)/shard_map/ppermute | solution.py:244
  72.4 1.3 copy-start.2
  73.7 4.8 %copy-start.4 = (bf16[128,4,360]{0,2,1:T(8,128)(2,1)S(1)}, bf16[128,4,360]{0,2,1:T(8,128)(2,1)}, u32[]{:S(2)}) copy-start(bf16[128,4,360]{0,2,1:T(8,128)(2,1)} %param.8) | copy-start | bytes 1105924
  73.7 4.8 %copy-start.7 = (s32[128,4]{0,1:T(4,128)S(1)}, s32[128,4]{0,1:T(4,128)}, u32[]{:S(2)}) copy-start(s32[128,4]{0,1:T(4,128)} %param.10) | copy-start | bytes 6148
  73.7 4.8 %copy-start.8 = (bf16[128,4]{0,1:T(4,128)(2,1)S(1)}, bf16[128,4]{0,1:T(4,128)(2,1)}, u32[]{:S(2)}) copy-start(bf16[128,4]{0,1:T(4,128)(2,1)} %param.9) | copy-start | bytes 3076
  73.7 30.7 %all-to-all-start.1 = ((bf16[8,40,3072]{2,1,0:T(8,128)(2,1)}), bf16[8,40,3072]{2,1,0:T(8,128)(2,1)}, u32[]{:S(2)}, u32[]{:S(2)}) async-start(bf16[8,40,3072]{2,1,0:T(8,128)(2,1)} %bitcast.26), calls=%async_computation.1 | async-start | bytes 3932160 | tf_op jit(solution)/shard_map/all_to_all | solution.py:254
  104.4 18.2 %all-to-all-start.2 = ((bf16[16,40,360]{2,1,0:T(8,128)(2,1)}), bf16[16,40,360]{2,1,0:T(8,128)(2,1)S(1)}, u32[]{:S(2)}, u32[]{:S(2)}) async-start(bf16[16,40,360]{2,1,0:T(8,128)(2,1)} %bitcast.9), calls=%async_computation.2 | async-start | bytes 983040 | tf_op jit(solution)/shard_map/all_to_all | solution.py:250
  112.2 1.7 copy-start.3
  122.6 18.1 %all-to-all-start.4 = ((bf16[16,40,360]{2,1,0:T(8,128)(2,1)}), bf16[16,40,360]{2,1,0:T(8,128)(2,1)S(1)}, u32[]{:S(2)}, u32[]{:S(2)}) async-start(bf16[16,40,360]{2,1,0:T(8,128)(2,1)} %bitcast.16), calls=%async_computation.4 | async-start | bytes 983040 | tf_op jit(solution)/shard_map/all_to_all | solution.py:263
  136.5 1.4 copy-start
  140.7 85.2 %all-to-all-start.3 = ((bf16[32,96,360]{2,1,0:T(8,128)(2,1)}), bf16[32,96,360]{2,1,0:T(8,128)(2,1)}, u32[]{:S(2)}, u32[]{:S(2)}) async-start(bf16[32,96,360]{2,1,0:T(8,128)(2,1)} %bitcast.24), calls=%async_computation.3 | async-start | bytes 4718592 | tf_op jit(solution)/shard_map/all_to_all | solution.py:259
Sparse Core Ops, SparseCore 0:
  32.7 48.4 all-gather.1

commit v2 on v0

v2 whole, which is shorter than its diff:
```python
import jax
import jax.numpy as jnp
from jax import lax
from jax.experimental import pallas as pl
from jax.experimental.pallas import tpu as pltpu
from jax.sharding import Mesh, PartitionSpec as P

BF = jnp.bfloat16
F32 = jnp.float32
I32 = jnp.int32
NT = (((1,), (1,)), ((), ()))
TN = (((0,), (0,)), ((), ()))
NN = (((1,), (0,)), ((), ()))
ROWS, D, TOPK, FFW, NEXP, CAP = 128, 2880, 4, 360, 16, 40
NZ, NY, NX = 8, 4, 4
NDP = NZ * NY
OWN = D // NDP
PAD = 96
WIDE = NDP * PAD
HALF = NEXP // 2
HSLOT = HALF * CAP
HW = 384
COVER = 50_000_000_000
NC = 1
CY = NY // NC
CW = WIDE // NC
BLK = CY * PAD
VMEM = pl.BlockSpec(memory_space=pltpu.VMEM)
SMEM = pl.BlockSpec(memory_space=pltpu.SMEM)
ANY = pl.BlockSpec(memory_space=pltpu.HBM)


def call(body, name, ins, outs, scratch=(), mib=14, weight=None):
    outs = [jax.ShapeDtypeStruct(*o) for o in outs]
    return pl.pallas_call(
        body,
        in_specs=list(ins),
        out_specs=[VMEM] * len(outs),
        out_shape=outs,
        scratch_shapes=list(scratch),
        compiler_params=pltpu.CompilerParams(vmem_limit_bytes=mib << 20),
        name=name,
        cost_estimate=weight and pl.CostEstimate(flops=weight, transcendentals=0, bytes_accessed=0),
    )


def expert_ids():
    row = lax.broadcasted_iota(I32, (NEXP, ROWS), 0)
    return ((row >> 1) & 3) * 4 + (row >> 3) * 2 + (row & 1)


def slot_onehot(place, n):
    c = lax.broadcasted_iota(I32, (n, CAP, ROWS), 1).astype(F32)
    return (place[:, None, :] == c).astype(F32).reshape(n * CAP, ROWS)


def prep_kernel(pos_ref, len_hbm, adv_hbm, g_hbm, r_hbm, *refs):
    cots, (pm_ref, other_ref, g_ref, r_ref, len_ref, adv_ref, scr, sems) = refs[:NC], refs[NC:]
    pairs = [(g_hbm, g_ref), (r_hbm, r_ref), (len_hbm, len_ref), (adv_hbm, adv_ref)]
    copies = [pltpu.make_async_copy(a, b, sems.at[i]) for i, (a, b) in enumerate(pairs)]
    for c in copies:
        c.start()
    for c in copies[1:]:
        c.wait()
    eid = expert_ids()
    hit = r_ref[0:1] == eid
    for k in range(1, TOPK):
        hit = hit | (r_ref[k : k + 1] == eid)
    a = lax.broadcasted_iota(I32, (ROWS, ROWS), 0)
    b = lax.broadcasted_iota(I32, (ROWS, ROWS), 1)
    before = (a < b).astype(F32).astype(BF)
    rank = lax.dot_general(hit.astype(F32).astype(BF), before, NN, preferred_element_type=F32)
    place = jnp.where(hit, rank, -1.0)
    pm_ref[...] = place
    other_ref[...] = jnp.where(pos_ref[2] == 0, place[HALF:], place[:HALF])
    pos = lax.broadcasted_iota(I32, (8, ROWS), 1)
    start = jnp.int32(0)
    scale = jnp.zeros((8, ROWS), F32)
    for s in range(4):
        n = len_ref[0, s]
        ratio = jnp.full((8, ROWS), adv_ref[0, s], F32) / jnp.full((8, ROWS), n, I32).astype(F32)
        scale = jnp.where((pos >= start) & (pos < start + n), ratio, scale)
        start = start + n
    copies[0].wait()
    scr[0:D] = g_ref[...].astype(F32) * scale[0:1]
    scr[D:] = jnp.zeros((8, ROWS), F32)
    keep = lax.broadcasted_iota(I32, (PAD, ROWS), 0) < OWN
    for d in range(NDP):
        z, y = d // NY, d % NY
        block = scr[d * OWN : d * OWN + PAD]
        at = (z * CY + y % CY) * PAD
        cots[y // CY][at : at + PAD] = jnp.where(keep, block, 0.0).astype(BF)


def prep(pos, lens, adv, gt, rt):
    outs = [((CW, ROWS), BF)] * NC + [((NEXP, ROWS), F32), ((HALF, ROWS), F32)]
    scratch = [
        pltpu.VMEM((D, ROWS), BF),
        pltpu.VMEM((TOPK, ROWS), I32),
        pltpu.SMEM((1, 4), I32),
        pltpu.SMEM((1, 4), F32),
        pltpu.VMEM((D + 8, ROWS), F32),
        pltpu.SemaphoreType.DMA((4,)),
    ]
    res = call(prep_kernel, "prep", [SMEM] + [ANY] * 4, outs, scratch)(pos, lens, adv, gt, rt)
    return res[:NC], res[NC], res[NC + 1]


def spread(s, cot_ref, out_ref, at):
    step = 768
    for i in range(0, CW, step):
        out_ref[:, at + i : at + i + step] = lax.dot_general(
            s, cot_ref[i : i + step], NT, preferred_element_type=F32
        ).astype(BF)


def hidden_rows(h_ref, gate_ref, r_ref, place, eid):
    n = place.shape[0]
    acc = jnp.zeros((n * CAP, HW), F32)
    for k in range(TOPK):
        s = slot_onehot(jnp.where(r_ref[k : k + 1] == eid, place, -1.0), n).astype(BF)
        rows = jnp.concatenate(
            [h_ref[k], gate_ref[k : k + 1], jnp.zeros((HW - FFW - 1, ROWS), BF)], axis=0
        )
        acc = acc + lax.dot_general(s, rows, NT, preferred_element_type=F32)
    return acc.astype(BF)


def other_kernel(pos_ref, h_ref, gate_ref, r_ref, pm_ref, out_ref):
    first = pos_ref[2] == 0
    eid = expert_ids()
    place = jnp.where(first, pm_ref[HALF:], pm_ref[:HALF])
    out_ref[...] = hidden_rows(h_ref, gate_ref, r_ref, place, jnp.where(first, eid[HALF:], eid[:HALF]))


def own_kernel(pos_ref, h_ref, gate_ref, r_ref, pm_ref, *refs):
    cots, out_ref = refs[:NC], refs[NC]
    first = pos_ref[2] == 0
    eid = expert_ids()
    place = jnp.where(first, pm_ref[:HALF], pm_ref[HALF:])
    s = slot_onehot(place, HALF).astype(BF)
    for i, cot_ref in enumerate(cots):
        spread(s, cot_ref, out_ref, i * CW)
    out_ref[:, WIDE:] = hidden_rows(
        h_ref, gate_ref, r_ref, place, jnp.where(first, eid[:HALF], eid[HALF:])
    )


def partner_kernel(cot_ref, place_ref, h_ref, _, out_ref):
    spread(slot_onehot(place_ref[...], HALF).astype(BF), cot_ref, out_ref, 0)
    out_ref[:, CW:] = h_ref[...]


def term_kernel(js, rounded, n_after=0):
    def body(pos_ref, own_ref, par_ref, *outs):
        outs = outs[len(outs) - len(js) :]
        hid = [own_ref[:, WIDE:], par_ref[:, CW:]]
        gate = [h[:, FFW : FFW + 1].astype(F32) for h in hid]
        hid = [h[:, :FFW] for h in hid]
        for j, out_ref in zip(js, outs):
            at = pl.multiple_of(((pos_ref[0] + j) % NZ) * BLK, BLK)
            acc = jnp.zeros((BLK, FFW), F32)
            for ref, h, g in zip((own_ref, par_ref), hid, gate):
                gated = (ref[:, pl.ds(at, BLK)].astype(F32) * g).astype(BF)
                acc = acc + lax.dot_general(gated, h, TN, preferred_element_type=F32)
            out_ref[...] = acc.astype(out_ref.dtype)

    dtype = BF if rounded else F32
    return call(
        body, "grad_term", [SMEM, VMEM, VMEM] + [ANY] * n_after, [((BLK, FFW), dtype)] * len(js)
    )


def step_kernel(*refs):
    n = len(refs) // 3
    for x_ref, t_ref, out_ref in zip(refs[:n], refs[n : 2 * n], refs[-n:]):
        out_ref[...] = (x_ref[...].astype(F32) + t_ref[...]).astype(BF)


def ring_step(xs, ts, after=()):
    n, m = len(xs), len(after)

    def body(*refs):
        step_kernel(*refs[: 2 * n], *refs[2 * n + m :])

    ins = [VMEM] * (2 * n) + [ANY] * m
    return call(body, "ring_step", ins, [((BLK, FFW), BF)] * n)(*xs, *ts, *after)


def z_kernel(pos_ref, t_ref, a_ref, b_ref, keep_ref, *outs):
    for j in range(NY):
        at = pl.multiple_of(((pos_ref[1] + j) % NY) * PAD, PAD)
        rows = pl.ds(at, PAD)
        v = t_ref[rows] + (a_ref[rows].astype(F32) + b_ref[rows].astype(F32))
        if j == 0:
            keep_ref[...] = v
        else:
            outs[j - 1][...] = v.astype(BF)


def y_kernel(t_ref, a_ref, b_ref, c_ref, out_ref):
    v = (t_ref[...] + a_ref[...].astype(F32)) + (b_ref[...].astype(F32) + c_ref[...].astype(F32))
    out_ref[...] = v[:OWN]


def pad_kernel(w_ref, out_ref):
    out_ref[...] = jnp.zeros((PAD, HW), BF)
    out_ref[:OWN, :FFW] = w_ref[...]


def weight_kernel(pos_ref, *refs):
    out_ref = refs[NY]
    for j in range(NY):
        y = (pos_ref[1] + NY - j) % NY
        for z in range(NZ):
            out_ref[z, y] = refs[j][z * PAD : (z + 1) * PAD]


def back_kernel(pos_ref, own_ref, par_ref, w_ref, _, out_ref):
    yh = pos_ref[2]
    w = w_ref[:, :FFW]
    out_ref[yh] = lax.dot_general(
        own_ref[:, :WIDE], w, NN, preferred_element_type=F32
    ).astype(BF)
    out_ref[1 - yh] = lax.dot_general(
        par_ref[:, :WIDE], w, NN, preferred_element_type=F32
    ).astype(BF)


def home_kernel(x_ref, h_ref, gate_ref, pm_ref, r_ref, gh_ref, gg_ref):
    x = x_ref[...]
    gate = gate_ref[...].astype(F32)
    eid = expert_ids()
    place = pm_ref[...]
    for k in range(TOPK):
        s = slot_onehot(jnp.where(r_ref[k : k + 1] == eid, place, -1.0), NEXP).astype(BF)
        back = lax.dot_general(x, s, TN, preferred_element_type=F32)
        gh_ref[k] = back * gate[k : k + 1]
        gg_ref[k : k + 1] = jnp.sum(back * h_ref[k].astype(F32), axis=0, keepdims=True)


def shift(x, axis, n, by):
    return lax.ppermute(x, axis, [(i, (i + by) % n) for i in range(n)])


def exchange(x, axes):
    return lax.all_to_all(x, axes, split_axis=0, concat_axis=0, tiled=True)


def local(grad_out, hidden_act, gate_weights, routing, resp_lengths, advantage, w_down):
    pos = jnp.stack([lax.axis_index(a).astype(I32) for a in ("z", "yl", "yh")])
    gt = grad_out.T
    ht = jnp.transpose(hidden_act, (1, 2, 0))
    gates = gate_weights.T
    rt = routing.T

    wt = call(pad_kernel, "weight_pad", [VMEM], [((PAD, HW), BF)])(w_down[0].T)[0]
    wz = lax.all_gather(wt, "z", axis=0, tiled=True)
    cots, pm, other = prep(pos, resp_lengths, advantage, gt, rt)
    cot_par = shift(cots[0], "yh", 2, 1)
    place_par = shift(other, "yh", 2, 1)
    hid_par = call(
        other_kernel, "send_other", [SMEM] + [VMEM] * 4, [((HSLOT, HW), BF)], weight=COVER
    )(
        pos, ht, gates, rt, pm
    )[0]
    hid_par = shift(hid_par, "yh", 2, 1)
    own = call(
        own_kernel, "send_own", [SMEM] + [VMEM] * (4 + NC), [((HSLOT, WIDE + HW), BF)], weight=COVER
    )(pos, ht, gates, rt, pm, *cots)[0]
    own = exchange(own.reshape(HALF, CAP, WIDE + HW), ("x", "c")).reshape(HSLOT, WIDE + HW)

    par = call(partner_kernel, "send_partner", [VMEM] * 3 + [ANY], [((HSLOT, CW + HW), BF)])(
        cot_par, place_par, hid_par, wz
    )[0]
    parts = [wz] + [shift(wz, "yl", NY, j) for j in range(1, NY)]
    weight = call(weight_kernel, "weight_part", [SMEM] + [VMEM] * NY, [((NZ, NY, PAD, HW), BF)])(
        pos, *parts
    )[0].reshape(WIDE, HW)
    par = exchange(par.reshape(HALF, CAP, CW + HW), ("x", "c")).reshape(HSLOT, CW + HW)

    up, down = term_kernel((4, 5), True, NY - 1)(pos, own, par, *parts[1:])
    t3, t6, t2, t7, t1, t0 = term_kernel((3, 6, 2, 7, 1, 0), False)(pos, own, par)
    up, down = shift(up, "z", NZ, 1), shift(down, "z", NZ, -1)
    up, down = ring_step((up, down), (t3, t6))
    back = call(back_kernel, "back_product", [SMEM] + [VMEM] * 3 + [ANY], [((2, HSLOT, FFW), BF)])(
        pos, own, par, weight, up
    )[0]
    up, down = shift(up, "z", NZ, 1), shift(down, "z", NZ, -1)
    up, down = ring_step((up, down), (t2, t7), (back,))
    up, down = shift(up, "z", NZ, 1), shift(down, "z", NZ, -1)
    up = shift(ring_step((up,), (t1,))[0], "z", NZ, 1)
    kept, s1, s2, s3 = call(
        z_kernel, "z_sum", [SMEM] + [VMEM] * 3, [((PAD, FFW), F32)] + [((PAD, FFW), BF)] * 3
    )(pos, t0, up, down)
    got = [shift(s, "yl", NY, j + 1) for j, s in enumerate((s1, s2, s3))]
    gd = call(y_kernel, "y_sum", [VMEM] * 4, [((OWN, FFW), F32)])(kept, *got)[0]

    back = exchange(back.reshape(NEXP, CAP, FFW), ("yh", "x", "c")).reshape(NEXP * CAP, FFW)
    gh, gg = call(
        home_kernel,
        "bring_home",
        [VMEM] * 5,
        [((TOPK, FFW, ROWS), F32), ((TOPK, ROWS), F32)],
    )(back, ht, gates, pm, rt)
    return gd.T[None], jnp.transpose(gh, (2, 0, 1)), gg.T


def solution(mesh):
    every = ("z", "yl", "x", "yh", "c")
    fine = Mesh(mesh.devices.reshape(NZ, NY, NX, 2, 2), every)
    rows2 = P(every, None)
    rows3 = P(every, None, None)
    cols = P(("x", "yh", "c"), None, ("z", "yl"))
    return jax.shard_map(
        local,
        mesh=fine,
        in_specs=(rows2, rows3, rows2, rows2, rows2, rows2, cols),
        out_specs=(cols, rows3, rows2),
        check_vma=False,
    )
```

time: 484 us -> 217 us (0.45)
  the two profiles are of different devices: /device:TPU:2 before, /device:TPU:56 now
where the time goes in v2:
time: 217 us; the launch traced here: 216 us
  starting transfers between devices  89.5 us (41%)
  waiting for transfers between devices  56.4 us (26%)
  blocking collectives  31.7 us (15%)
  Pallas kernels  24.4 us (11%)
  local copies, waits for them, and re-layouts  12.9 us (6%)
    ppermute x16, starting transfers between devices, shift(): return lax.ppermute(x, axis, [(i, (i + by) % n) for i in range(n)])  69.7 us
    ppermute x16, waiting for transfers between devices, shift(): return lax.ppermute(x, axis, [(i, (i + by) % n) for i in range(n)])  56.3 us
    all_gather x1, blocking collectives, local(): wz = lax.all_gather(wt, 'z', axis=0, tiled=True)  31.7 us
    all_to_all x3, starting transfers between devices, exchange(): return lax.all_to_all(x, axes, split_axis=0, concat_axis=0, tiled=True)  19.8 us
    unnamed x57, local copies, waits for them, and re-layouts  12.9 us
    pallas_call x1, Pallas kernels, local(): call(back_kernel, 'back_product', [SMEM] + [VMEM] * 3 + [ANY], [((2, HSLO...  4.69 us
  transfers between devices with their start and end apart: 19, of which 8 were waited for; matrix products, arithmetic and copies ran while one was open for 0% of the time, Pallas kernels for 8%

profile of v2, /device:TPU:56, one launch (start us, length us, event | category | flops | bytes accessed | tf_op | source)
XLA Modules:
  0.0 216.0 jit_solution(14351030914118833858)
XLA Ops:
  0.6 0.1 pad_add_fusion.pos_ref
  0.7 1.1 copy-done.8
  1.8 0.7 copy-done.21
  2.5 0.7 copy-done.26
  3.2 0.7 copy-done.27
  3.8 2.7 %prep.1 = (bf16[3072,128]{1,0:T(8,128)(2,1)}, f32[16,128]{1,0:T(8,128)S(1)}, f32[8,128]{1,0:T(8,128)S(1)}) custom-call(s32[3]{0:T(128)S(1)} %pad_add_fusion.pos_ref, s32[1,4]{1,0:T(1,128)S(1)} %copy-done.26, f32[1,4]{1,0:T(1,128)S(1)} %copy-done.27, bf16[2880,128]{1,0:T(8,128)(2,1)S(1)} %bitcast.29, s32[4,128]{1,0:T(4,128)S(1)} %bitcast.35), custom_call_target="tpu_custom_call" | custom-call | tf_op jit(solution)/shard_map/prep/pallas_call | solution.py:105
  6.5 4.7 %collective-permute-start.1 = (f32[8,128]{1,0:T(8,128)S(1)}, f32[8,128]{1,0:T(8,128)S(1)}, u32[]{:S(2)}, u32[]{:S(2)}) collective-permute-start(f32[8,128]{1,0:T(8,128)S(1)} %get-tuple-element.26), channel_id=1, source_target_pairs={{0,2},{2,0},{1,3},{3,1},{4,6},{6,4},{5,7},{7,5},{8,10},{10,8},{9,1... | collective-permute-start | bytes 12296 | tf_op jit(solution)/shard_map/ppermute | solution.py:243
  11.3 5.0 %collective-permute-start = (bf16[3072,128]{1,0:T(8,128)(2,1)}, bf16[3072,128]{1,0:T(8,128)(2,1)}, u32[]{:S(2)}, u32[]{:S(2)}) collective-permute-start(bf16[3072,128]{1,0:T(8,128)(2,1)} %get-tuple-element.25.refs_0_), channel_id=1, source_target_pairs={{0,2},{2,0},{1,3},{3,1},{4,6},{6,4},{5,7},{7,5},{8,10},{10,8},{9,1... | collective-permute-start | bytes 2359304 | tf_op jit(solution)/shard_map/ppermute | solution.py:243
  16.3 0.0 copy-start.17
  16.3 1.0 copy-done.17
  17.3 0.7 copy-done.22
  18.0 0.7 copy-done.24
  18.7 2.1 send_own.1
  20.7 1.4 copy-done.7
  22.1 4.4 %all-to-all-start = ((bf16[8,40,3456]{2,1,0:T(8,128)(2,1)}), bf16[8,40,3456]{2,1,0:T(8,128)(2,1)S(1)}, u32[]{:S(2)}, u32[]{:S(2)}) async-start(bf16[8,40,3456]{2,1,0:T(8,128)(2,1)} %bitcast.27), calls=%async_computation | async-start | bytes 4423680 | tf_op jit(solution)/shard_map/all_to_all | solution.py:247
  26.6 0.0 copy-start.20
  26.6 1.0 send_other.1
  27.5 4.7 %collective-permute-start.2 = (bf16[320,384]{1,0:T(8,128)(2,1)S(1)}, bf16[320,384]{1,0:T(8,128)(2,1)S(1)}, u32[]{:S(2)}, u32[]{:S(2)}) collective-permute-start(bf16[320,384]{1,0:T(8,128)(2,1)S(1)} %send_other.1), channel_id=1, source_target_pairs={{0,2},{2,0},{1,3},{3,1},{4,6},{6,4},{5,7},{7,5},{8,10},{10,8},{9,1... | collective-permute-start | bytes 737288 | tf_op jit(solution)/shard_map/ppermute | solution.py:243
  32.3 31.7 %all_gather.3._.refs_0_ = bf16[768,384]{1,0:T(8,128)(2,1)S(1)} all-gather(bf16[96,384]{1,0:T(8,128)(2,1)S(1)} %weight_pad.1), channel_id=1, replica_groups=mesh['z'=8,'yl'=4,'x'=4,'yh'=2,'c'=2] {'z'}, dimensions={0}, use_global_device_ids=true | all-gather | bytes 663552 | tf_op jit(solution)/shard_map/all_gather | solution.py:258
  64.0 1.8 send_partner.1
  65.9 1.4 copy-done
  67.2 4.9 %all-to-all-start.1 = ((bf16[8,40,3456]{2,1,0:T(8,128)(2,1)}), bf16[8,40,3456]{2,1,0:T(8,128)(2,1)}, u32[]{:S(2)}, u32[]{:S(2)}) async-start(bf16[8,40,3456]{2,1,0:T(8,128)(2,1)} %bitcast.26), calls=%async_computation.1 | async-start | bytes 4423680 | tf_op jit(solution)/shard_map/all_to_all | solution.py:247
  72.1 2.3 %collective-permute-start.5 = (bf16[768,384]{1,0:T(8,128)(2,1)S(1)}, bf16[768,384]{1,0:T(8,128)(2,1)S(1)}, u32[]{:S(2)}, u32[]{:S(2)}) collective-permute-start(bf16[768,384]{1,0:T(8,128)(2,1)S(1)} %all_gather.3._.refs_0_), channel_id=1, source_target_pairs={{0,48},{16,0},{32,16},{48,32},{1,49},{17,1},{33,17},{49,33},{2,50}... | collective-permute-start | bytes 1769480 | tf_op jit(solution)/shard_map/ppermute | solution.py:243
  74.5 2.4 %collective-permute-start.4 = (bf16[768,384]{1,0:T(8,128)(2,1)S(1)}, bf16[768,384]{1,0:T(8,128)(2,1)S(1)}, u32[]{:S(2)}, u32[]{:S(2)}) collective-permute-start(bf16[768,384]{1,0:T(8,128)(2,1)S(1)} %all_gather.3._.refs_0_), channel_id=1, source_target_pairs={{0,32},{16,48},{32,0},{48,16},{1,33},{17,49},{33,1},{49,17},{2,34}... | collective-permute-start | bytes 1769480 | tf_op jit(solution)/shard_map/ppermute | solution.py:243
  76.9 4.8 %collective-permute-start.3 = (bf16[768,384]{1,0:T(8,128)(2,1)S(1)}, bf16[768,384]{1,0:T(8,128)(2,1)S(1)}, u32[]{:S(2)}, u32[]{:S(2)}) collective-permute-start(bf16[768,384]{1,0:T(8,128)(2,1)S(1)} %all_gather.3._.refs_0_), channel_id=1, source_target_pairs={{0,16},{16,32},{32,48},{48,0},{1,17},{17,33},{33,49},{49,1},{2,18}... | collective-permute-start | bytes 1769480 | tf_op jit(solution)/shard_map/ppermute | solution.py:243
  81.7 10.4 %collective-permute-done.5.outs_2_.refs_3_ = bf16[768,384]{1,0:T(8,128)(2,1)S(1)} collective-permute-done((bf16[768,384]{1,0:T(8,128)(2,1)S(1)}, bf16[768,384]{1,0:T(8,128)(2,1)S(1)}, u32[]{:S(2)}, u32[]{:S(2)}) %collective-permute-start.5) | collective-permute-done | bytes 589856 | tf_op jit(solution)/shard_map/ppermute | solution.py:243
  92.1 24.9 %collective-permute-done.4.outs_1_.refs_2_ = bf16[768,384]{1,0:T(8,128)(2,1)S(1)} collective-permute-done((bf16[768,384]{1,0:T(8,128)(2,1)S(1)}, bf16[768,384]{1,0:T(8,128)(2,1)S(1)}, u32[]{:S(2)}, u32[]{:S(2)}) %collective-permute-start.4) | collective-permute-done | bytes 589856 | tf_op jit(solution)/shard_map/ppermute | solution.py:243
  116.9 0.8 copy-done.1
  117.8 0.0 collective-permute-done.3.outs_0_.refs_1_
  117.8 0.9 copy-done.4
  118.6 0.0 all-to-all-done.1
  118.6 1.1 copy-done.2
  119.7 1.1 copy-done.5
  120.7 2.7 %grad_term.3 = (bf16[384,360]{1,0:T(8,128)(2,1)S(1)}, bf16[384,360]{1,0:T(8,128)(2,1)S(1)}) custom-call(s32[3]{0:T(128)S(1)} %pad_add_fusion.pos_ref, bf16[320,3456]{1,0:T(8,128)(2,1)S(1)} %bitcast.22, bf16[320,3456]{1,0:T(8,128)(2,1)} %bitcast.12.par_ref, bf16[768,384]{1,0:T(8,128)(2,1)S(1)} %copy-done.5, bf16[768,384]{1,0:T(8,128)(2,1)S(1)} %copy-done.2, ...), custom_call_target="tpu_custom_call" | custom-call | tf_op jit(solution)/shard_map/grad_term/pallas_call | solution.py:282
  123.5 3.6 %collective-permute-start.6 = (bf16[384,360]{1,0:T(8,128)(2,1)S(1)}, bf16[384,360]{1,0:T(8,128)(2,1)S(1)}, u32[]{:S(2)}, u32[]{:S(2)}) collective-permute-start(bf16[384,360]{1,0:T(8,128)(2,1)S(1)} %get-tuple-element.28), channel_id=1, source_target_pairs={{0,64},{64,128},{128,192},{192,256},{256,320},{320,384},{384,448},... | collective-permute-start | bytes 829448 | tf_op jit(solution)/shard_map/ppermute | solution.py:243
  127.1 5.3 %collective-permute-start.7 = (bf16[384,360]{1,0:T(8,128)(2,1)S(1)}, bf16[384,360]{1,0:T(8,128)(2,1)S(1)}, u32[]{:S(2)}, u32[]{:S(2)}) collective-permute-start(bf16[384,360]{1,0:T(8,128)(2,1)S(1)} %get-tuple-element.29), channel_id=1, source_target_pairs={{0,448},{64,0},{128,64},{192,128},{256,192},{320,256},{384,320},{4... | collective-permute-start | bytes 829448 | tf_op jit(solution)/shard_map/ppermute | solution.py:243
  132.4 4.2 %grad_term.2 = (f32[384,360]{1,0:T(8,128)S(1)}, f32[384,360]{1,0:T(8,128)S(1)}, f32[384,360]{1,0:T(8,128)S(1)}, f32[384,360]{1,0:T(8,128)S(1)}, f32[384,360]{1,0:T(8,128)S(1)}, /*index=5*/f32[384,360]{1,0:T(8,128)S(1)}) custom-call(s32[3]{0:T(128)S(1)} %pad_add_fusion.pos_ref, bf16[320,3456]{1,0:T(8,128)(2,1)S(1)} %bitcast.23, bf16[320,3456]{1,0:T(8,128)(2,1)} %bitcast.12.par_ref), custom_call_target="tpu_custom_call" | custom-call | tf_op jit(solution)/shard_map/grad_term/pallas_call | solution.py:283
  136.6 0.0 copy-start.9
  136.7 0.8 collective-permute-done.6.refs_0_
  137.4 1.3 collective-permute-done.7.refs_1_
  138.8 0.9 ring_step.3
  139.7 5.6 %collective-permute-start.9 = (bf16[384,360]{1,0:T(8,128)(2,1)}, bf16[384,360]{1,0:T(8,128)(2,1)}, u32[]{:S(2)}, u32[]{:S(2)}) collective-permute-start(bf16[384,360]{1,0:T(8,128)(2,1)} %get-tuple-element.33), channel_id=1, source_target_pairs={{0,448},{64,0},{128,64},{192,128},{256,192},{320,256},{384,320},{4... | collective-permute-start | bytes 829448 | tf_op jit(solution)/shard_map/ppermute | solution.py:243
  145.3 1.9 collective-permute-start.8
  147.2 0.8 weight_part.1
  148.1 4.7 %back_product.1.refs_4_ = bf16[2,320,360]{2,1,0:T(8,128)(2,1)} custom-call(s32[3]{0:T(128)S(1)} %pad_add_fusion.pos_ref, bf16[320,3456]{1,0:T(8,128)(2,1)S(1)} %bitcast.24, bf16[320,3456]{1,0:T(8,128)(2,1)} %bitcast.12.par_ref, bf16[3072,384]{1,0:T(8,128)(2,1)S(1)} %bitcast.25, bf16[384,360]{1,0:T(8,128)(2,1)} %get-tuple-element.32._), custom_call_target="tpu_custom_call" | custom-call | tf_op jit(solution)/shard_map/back_product/pallas_call | solution.py:286
  152.8 10.5 %all-to-all-start.2 = ((bf16[16,40,360]{2,1,0:T(8,128)(2,1)}), bf16[16,40,360]{2,1,0:T(8,128)(2,1)S(1)}, u32[]{:S(2)}, u32[]{:S(2)}) async-start(bf16[16,40,360]{2,1,0:T(8,128)(2,1)} %bitcast.16), calls=%async_computation.2 | async-start | bytes 983040 | tf_op jit(solution)/shard_map/all_to_all | solution.py:247
  163.3 0.0 collective-permute-done.9.refs_1_
  163.3 0.0 copy-start.19
  163.3 0.0 copy-start.25
  163.3 1.2 ring_step.4
  164.5 1.9 collective-permute-start.10
  166.5 5.1 %collective-permute-start.12 = (bf16[384,360]{1,0:T(8,128)(2,1)S(1)}, bf16[384,360]{1,0:T(8,128)(2,1)S(1)}, u32[]{:S(2)}, u32[]{:S(2)}) collective-permute-start(bf16[384,360]{1,0:T(8,128)(2,1)S(1)} %get-tuple-element.38), channel_id=1, source_target_pairs={{0,448},{64,0},{128,64},{192,128},{256,192},{320,256},{384,320},{4... | collective-permute-start | bytes 829448 | tf_op jit(solution)/shard_map/ppermute | solution.py:243
  171.6 5.4 %collective-permute-done.10.refs_0_ = bf16[384,360]{1,0:T(8,128)(2,1)S(1)} collective-permute-done((bf16[384,360]{1,0:T(8,128)(2,1)S(1)}, bf16[384,360]{1,0:T(8,128)(2,1)S(1)}, u32[]{:S(2)}, u32[]{:S(2)}) %collective-permute-start.10) | collective-permute-done | bytes 276512 | tf_op jit(solution)/shard_map/ppermute | solution.py:243
  177.0 0.1 ring_step.5
  177.0 1.9 collective-permute-start.11
  179.0 9.7 %collective-permute-done.11.a_ref = bf16[384,360]{1,0:T(8,128)(2,1)S(1)} collective-permute-done((bf16[384,360]{1,0:T(8,128)(2,1)S(1)}, bf16[384,360]{1,0:T(8,128)(2,1)S(1)}, u32[]{:S(2)}, u32[]{:S(2)}) %collective-permute-start.11) | collective-permute-done | bytes 276512 | tf_op jit(solution)/shard_map/ppermute | solution.py:243
  188.7 0.7 z_sum.1
  189.4 15.9 %collective-permute-start.13 = (bf16[96,360]{1,0:T(8,128)(2,1)S(1)}, bf16[96,360]{1,0:T(8,128)(2,1)S(1)}, u32[]{:S(2)}, u32[]{:S(2)}) collective-permute-start(bf16[96,360]{1,0:T(8,128)(2,1)S(1)} %get-tuple-element.40), channel_id=1, source_target_pairs={{0,16},{16,32},{32,48},{48,0},{1,17},{17,33},{33,49},{49,1},{2,18}... | collective-permute-start | bytes 207368 | tf_op jit(solution)/shard_map/ppermute | solution.py:243
  205.2 1.9 collective-permute-start.14
  207.2 2.5 %collective-permute-start.15 = (bf16[96,360]{1,0:T(8,128)(2,1)S(1)}, bf16[96,360]{1,0:T(8,128)(2,1)S(1)}, u32[]{:S(2)}, u32[]{:S(2)}) collective-permute-start(bf16[96,360]{1,0:T(8,128)(2,1)S(1)} %get-tuple-element.42), channel_id=1, source_target_pairs={{0,48},{16,0},{32,16},{48,32},{1,49},{17,1},{33,17},{49,33},{2,50}... | collective-permute-start | bytes 207368 | tf_op jit(solution)/shard_map/ppermute | solution.py:243
  209.7 1.6 bring_home.1
  211.3 1.8 collective-permute-done.14.b_ref
  213.2 2.0 collective-permute-done.15.c_ref
  215.2 0.8 copy.10
  (48 shorter events, 0.1 us)
Async XLA Ops:
  0.7 1.1 copy-start.8
  1.8 0.7 copy-start.21
  2.5 0.7 copy-start.26
  3.2 0.7 copy-start.27
  6.5 57.5 %collective-permute-start.1 = (f32[8,128]{1,0:T(8,128)S(1)}, f32[8,128]{1,0:T(8,128)S(1)}, u32[]{:S(2)}, u32[]{:S(2)}) collective-permute-start(f32[8,128]{1,0:T(8,128)S(1)} %get-tuple-element.26), channel_id=1, source_target_pairs={{0,2},{2,0},{1,3},{3,1},{4,6},{6,4},{5,7},{7,5},{8,10},{10,8},{9,1... | collective-permute-start | bytes 12296 | tf_op jit(solution)/shard_map/ppermute | solution.py:243
  11.3 52.7 %collective-permute-start = (bf16[3072,128]{1,0:T(8,128)(2,1)}, bf16[3072,128]{1,0:T(8,128)(2,1)}, u32[]{:S(2)}, u32[]{:S(2)}) collective-permute-start(bf16[3072,128]{1,0:T(8,128)(2,1)} %get-tuple-element.25.refs_0_), channel_id=1, source_target_pairs={{0,2},{2,0},{1,3},{3,1},{4,6},{6,4},{5,7},{7,5},{8,10},{10,8},{9,1... | collective-permute-start | bytes 2359304 | tf_op jit(solution)/shard_map/ppermute | solution.py:243
  16.3 1.0 copy-start.17
  17.3 0.7 copy-start.22
  18.0 0.7 copy-start.24
  20.7 1.4 copy-start.7
  22.1 4.4 %copy-start.18 = (bf16[128,4,360]{0,2,1:T(8,128)(2,1)S(1)}, bf16[128,4,360]{0,2,1:T(8,128)(2,1)}, u32[]{:S(2)}) copy-start(bf16[128,4,360]{0,2,1:T(8,128)(2,1)} %param.8) | copy-start | bytes 1105924
  22.1 4.4 %copy-start.23 = (s32[128,4]{0,1:T(4,128)S(1)}, s32[128,4]{0,1:T(4,128)}, u32[]{:S(2)}) copy-start(s32[128,4]{0,1:T(4,128)} %param.10) | copy-start | bytes 6148
  22.1 45.1 %all-to-all-start = ((bf16[8,40,3456]{2,1,0:T(8,128)(2,1)}), bf16[8,40,3456]{2,1,0:T(8,128)(2,1)S(1)}, u32[]{:S(2)}, u32[]{:S(2)}) async-start(bf16[8,40,3456]{2,1,0:T(8,128)(2,1)} %bitcast.27), calls=%async_computation | async-start | bytes 4423680 | tf_op jit(solution)/shard_map/all_to_all | solution.py:247
  26.6 5.7 %copy-start.20 = (bf16[1,360,90]{1,2,0:T(8,128)(2,1)S(1)}, bf16[1,360,90]{1,2,0:T(8,128)(2,1)}, u32[]{:S(2)}) copy-start(bf16[1,360,90]{1,2,0:T(8,128)(2,1)} %param.13) | copy-start | bytes 194404
  27.5 36.5 %collective-permute-start.2 = (bf16[320,384]{1,0:T(8,128)(2,1)S(1)}, bf16[320,384]{1,0:T(8,128)(2,1)S(1)}, u32[]{:S(2)}, u32[]{:S(2)}) collective-permute-start(bf16[320,384]{1,0:T(8,128)(2,1)S(1)} %send_other.1), channel_id=1, source_target_pairs={{0,2},{2,0},{1,3},{3,1},{4,6},{6,4},{5,7},{7,5},{8,10},{10,8},{9,1... | collective-permute-start | bytes 737288 | tf_op jit(solution)/shard_map/ppermute | solution.py:243
  65.8 1.4 copy-start
  67.2 51.4 %all-to-all-start.1 = ((bf16[8,40,3456]{2,1,0:T(8,128)(2,1)}), bf16[8,40,3456]{2,1,0:T(8,128)(2,1)}, u32[]{:S(2)}, u32[]{:S(2)}) async-start(bf16[8,40,3456]{2,1,0:T(8,128)(2,1)} %bitcast.26), calls=%async_computation.1 | async-start | bytes 4423680 | tf_op jit(solution)/shard_map/all_to_all | solution.py:247
  72.1 19.9 %collective-permute-start.5 = (bf16[768,384]{1,0:T(8,128)(2,1)S(1)}, bf16[768,384]{1,0:T(8,128)(2,1)S(1)}, u32[]{:S(2)}, u32[]{:S(2)}) collective-permute-start(bf16[768,384]{1,0:T(8,128)(2,1)S(1)} %all_gather.3._.refs_0_), channel_id=1, source_target_pairs={{0,48},{16,0},{32,16},{48,32},{1,49},{17,1},{33,17},{49,33},{2,50}... | collective-permute-start | bytes 1769480 | tf_op jit(solution)/shard_map/ppermute | solution.py:243
  74.5 42.5 %collective-permute-start.4 = (bf16[768,384]{1,0:T(8,128)(2,1)S(1)}, bf16[768,384]{1,0:T(8,128)(2,1)S(1)}, u32[]{:S(2)}, u32[]{:S(2)}) collective-permute-start(bf16[768,384]{1,0:T(8,128)(2,1)S(1)} %all_gather.3._.refs_0_), channel_id=1, source_target_pairs={{0,32},{16,48},{32,0},{48,16},{1,33},{17,49},{33,1},{49,17},{2,34}... | collective-permute-start | bytes 1769480 | tf_op jit(solution)/shard_map/ppermute | solution.py:243
  76.9 40.9 %collective-permute-start.3 = (bf16[768,384]{1,0:T(8,128)(2,1)S(1)}, bf16[768,384]{1,0:T(8,128)(2,1)S(1)}, u32[]{:S(2)}, u32[]{:S(2)}) collective-permute-start(bf16[768,384]{1,0:T(8,128)(2,1)S(1)} %all_gather.3._.refs_0_), channel_id=1, source_target_pairs={{0,16},{16,32},{32,48},{48,0},{1,17},{17,33},{33,49},{49,1},{2,18}... | collective-permute-start | bytes 1769480 | tf_op jit(solution)/shard_map/ppermute | solution.py:243
  116.9 0.8 copy-start.1
  117.8 0.9 copy-start.4
  118.6 1.1 copy-start.2
  119.7 1.1 copy-start.5
  123.5 14.0 %collective-permute-start.6 = (bf16[384,360]{1,0:T(8,128)(2,1)S(1)}, bf16[384,360]{1,0:T(8,128)(2,1)S(1)}, u32[]{:S(2)}, u32[]{:S(2)}) collective-permute-start(bf16[384,360]{1,0:T(8,128)(2,1)S(1)} %get-tuple-element.28), channel_id=1, source_target_pairs={{0,64},{64,128},{128,192},{192,256},{256,320},{320,384},{384,448},... | collective-permute-start | bytes 829448 | tf_op jit(solution)/shard_map/ppermute | solution.py:243
  127.0 20.2 %copy-start.3 = (bf16[768,384]{1,0:T(8,128)(2,1)S(1)}, bf16[768,384]{1,0:T(8,128)(2,1)}, u32[]{:S(2)}) copy-start(bf16[768,384]{1,0:T(8,128)(2,1)} %copy-done.1) | copy-start | bytes 1769476
  127.1 20.2 %copy-start.6 = (bf16[768,384]{1,0:T(8,128)(2,1)S(1)}, bf16[768,384]{1,0:T(8,128)(2,1)}, u32[]{:S(2)}) copy-start(bf16[768,384]{1,0:T(8,128)(2,1)} %copy-done.4) | copy-start | bytes 1769476
  127.1 11.7 %collective-permute-start.7 = (bf16[384,360]{1,0:T(8,128)(2,1)S(1)}, bf16[384,360]{1,0:T(8,128)(2,1)S(1)}, u32[]{:S(2)}, u32[]{:S(2)}) collective-permute-start(bf16[384,360]{1,0:T(8,128)(2,1)S(1)} %get-tuple-element.29), channel_id=1, source_target_pairs={{0,448},{64,0},{128,64},{192,128},{256,192},{320,256},{384,320},{4... | collective-permute-start | bytes 829448 | tf_op jit(solution)/shard_map/ppermute | solution.py:243
  136.6 11.4 %copy-start.9 = (f32[384,360]{1,0:T(8,128)}, f32[384,360]{1,0:T(8,128)S(1)}, u32[]{:S(2)}) copy-start(f32[384,360]{1,0:T(8,128)S(1)} %get-tuple-element.27.t_ref) | copy-start | bytes 1658884
  136.6 11.4 %copy-start.11 = (f32[384,360]{1,0:T(8,128)}, f32[384,360]{1,0:T(8,128)S(1)}, u32[]{:S(2)}) copy-start(f32[384,360]{1,0:T(8,128)S(1)} %get-tuple-element.37.refs_1_) | copy-start | bytes 1658884
  136.6 11.4 %copy-start.13 = (f32[384,360]{1,0:T(8,128)}, f32[384,360]{1,0:T(8,128)S(1)}, u32[]{:S(2)}) copy-start(f32[384,360]{1,0:T(8,128)S(1)} %get-tuple-element.34.refs_2_) | copy-start | bytes 1658884
  136.7 11.4 %copy-start.15 = (f32[384,360]{1,0:T(8,128)}, f32[384,360]{1,0:T(8,128)S(1)}, u32[]{:S(2)}) copy-start(f32[384,360]{1,0:T(8,128)S(1)} %get-tuple-element.35.refs_3_) | copy-start | bytes 1658884
  139.7 23.6 %collective-permute-start.9 = (bf16[384,360]{1,0:T(8,128)(2,1)}, bf16[384,360]{1,0:T(8,128)(2,1)}, u32[]{:S(2)}, u32[]{:S(2)}) collective-permute-start(bf16[384,360]{1,0:T(8,128)(2,1)} %get-tuple-element.33), channel_id=1, source_target_pairs={{0,448},{64,0},{128,64},{192,128},{256,192},{320,256},{384,320},{4... | collective-permute-start | bytes 829448 | tf_op jit(solution)/shard_map/ppermute | solution.py:243
  145.3 18.0 %collective-permute-start.8 = (bf16[384,360]{1,0:T(8,128)(2,1)}, bf16[384,360]{1,0:T(8,128)(2,1)}, u32[]{:S(2)}, u32[]{:S(2)}) collective-permute-start(bf16[384,360]{1,0:T(8,128)(2,1)} %get-tuple-element.32._), channel_id=1, source_target_pairs={{0,64},{64,128},{128,192},{192,256},{256,320},{320,384},{384,448},... | collective-permute-start | bytes 829448 | tf_op jit(solution)/shard_map/ppermute | solution.py:243
  148.0 15.2 %copy-start.14 = (f32[384,360]{1,0:T(8,128)S(1)}, f32[384,360]{1,0:T(8,128)}, u32[]{:S(2)}) copy-start(f32[384,360]{1,0:T(8,128)} %copy-done.13) | copy-start | bytes 1658884
  148.1 15.2 %copy-start.16 = (f32[384,360]{1,0:T(8,128)S(1)}, f32[384,360]{1,0:T(8,128)}, u32[]{:S(2)}) copy-start(f32[384,360]{1,0:T(8,128)} %copy-done.15) | copy-start | bytes 1658884
  152.8 24.2 %copy-start.12 = (f32[384,360]{1,0:T(8,128)S(1)}, f32[384,360]{1,0:T(8,128)}, u32[]{:S(2)}) copy-start(f32[384,360]{1,0:T(8,128)} %copy-done.11) | copy-start | bytes 1658884
  152.8 35.9 %copy-start.10 = (f32[384,360]{1,0:T(8,128)S(1)}, f32[384,360]{1,0:T(8,128)}, u32[]{:S(2)}) copy-start(f32[384,360]{1,0:T(8,128)} %copy-done.9) | copy-start | bytes 1658884
  152.8 56.9 %all-to-all-start.2 = ((bf16[16,40,360]{2,1,0:T(8,128)(2,1)}), bf16[16,40,360]{2,1,0:T(8,128)(2,1)S(1)}, u32[]{:S(2)}, u32[]{:S(2)}) async-start(bf16[16,40,360]{2,1,0:T(8,128)(2,1)} %bitcast.16), calls=%async_computation.2 | async-start | bytes 983040 | tf_op jit(solution)/shard_map/all_to_all | solution.py:247
  163.3 46.3 %copy-start.19 = (bf16[128,4,360]{0,2,1:T(8,128)(2,1)S(1)}, bf16[128,4,360]{0,2,1:T(8,128)(2,1)}, u32[]{:S(2)}) copy-start(bf16[128,4,360]{0,2,1:T(8,128)(2,1)} %param.8) | copy-start | bytes 1105924
  163.3 46.3 %copy-start.25 = (bf16[128,4]{0,1:T(4,128)(2,1)S(1)}, bf16[128,4]{0,1:T(4,128)(2,1)}, u32[]{:S(2)}) copy-start(bf16[128,4]{0,1:T(4,128)(2,1)} %param.9) | copy-start | bytes 3076
  164.5 12.4 %collective-permute-start.10 = (bf16[384,360]{1,0:T(8,128)(2,1)S(1)}, bf16[384,360]{1,0:T(8,128)(2,1)S(1)}, u32[]{:S(2)}, u32[]{:S(2)}) collective-permute-start(bf16[384,360]{1,0:T(8,128)(2,1)S(1)} %get-tuple-element.36), channel_id=1, source_target_pairs={{0,64},{64,128},{128,192},{192,256},{256,320},{320,384},{384,448},... | collective-permute-start | bytes 829448 | tf_op jit(solution)/shard_map/ppermute | solution.py:243
  166.5 12.5 %collective-permute-start.12 = (bf16[384,360]{1,0:T(8,128)(2,1)S(1)}, bf16[384,360]{1,0:T(8,128)(2,1)S(1)}, u32[]{:S(2)}, u32[]{:S(2)}) collective-permute-start(bf16[384,360]{1,0:T(8,128)(2,1)S(1)} %get-tuple-element.38), channel_id=1, source_target_pairs={{0,448},{64,0},{128,64},{192,128},{256,192},{320,256},{384,320},{4... | collective-permute-start | bytes 829448 | tf_op jit(solution)/shard_map/ppermute | solution.py:243
  177.0 11.7 %collective-permute-start.11 = (bf16[384,360]{1,0:T(8,128)(2,1)S(1)}, bf16[384,360]{1,0:T(8,128)(2,1)S(1)}, u32[]{:S(2)}, u32[]{:S(2)}) collective-permute-start(bf16[384,360]{1,0:T(8,128)(2,1)S(1)} %ring_step.5), channel_id=1, source_target_pairs={{0,64},{64,128},{128,192},{192,256},{256,320},{320,384},{384,448},... | collective-permute-start | bytes 829448 | tf_op jit(solution)/shard_map/ppermute | solution.py:243
  189.4 22.0 %collective-permute-start.13 = (bf16[96,360]{1,0:T(8,128)(2,1)S(1)}, bf16[96,360]{1,0:T(8,128)(2,1)S(1)}, u32[]{:S(2)}, u32[]{:S(2)}) collective-permute-start(bf16[96,360]{1,0:T(8,128)(2,1)S(1)} %get-tuple-element.40), channel_id=1, source_target_pairs={{0,16},{16,32},{32,48},{48,0},{1,17},{17,33},{33,49},{49,1},{2,18}... | collective-permute-start | bytes 207368 | tf_op jit(solution)/shard_map/ppermute | solution.py:243
  205.2 7.9 %collective-permute-start.14 = (bf16[96,360]{1,0:T(8,128)(2,1)S(1)}, bf16[96,360]{1,0:T(8,128)(2,1)S(1)}, u32[]{:S(2)}, u32[]{:S(2)}) collective-permute-start(bf16[96,360]{1,0:T(8,128)(2,1)S(1)} %get-tuple-element.41), channel_id=1, source_target_pairs={{0,32},{16,48},{32,0},{48,16},{1,33},{17,49},{33,1},{49,17},{2,34}... | collective-permute-start | bytes 207368 | tf_op jit(solution)/shard_map/ppermute | solution.py:243
  207.2 8.0 %collective-permute-start.15 = (bf16[96,360]{1,0:T(8,128)(2,1)S(1)}, bf16[96,360]{1,0:T(8,128)(2,1)S(1)}, u32[]{:S(2)}, u32[]{:S(2)}) collective-permute-start(bf16[96,360]{1,0:T(8,128)(2,1)S(1)} %get-tuple-element.42), channel_id=1, source_target_pairs={{0,48},{16,0},{32,16},{48,32},{1,49},{17,1},{33,17},{49,33},{2,50}... | collective-permute-start | bytes 207368 | tf_op jit(solution)/shard_map/ppermute | solution.py:243

commit v3 on v2

v3 whole, which is shorter than its diff:
```python
import jax
import jax.numpy as jnp
from jax import lax
from jax.experimental import pallas as pl
from jax.experimental.pallas import tpu as pltpu
from jax.sharding import Mesh, PartitionSpec as P

BF = jnp.bfloat16
F32 = jnp.float32
I32 = jnp.int32
NT = (((1,), (1,)), ((), ()))
TN = (((0,), (0,)), ((), ()))
NN = (((1,), (0,)), ((), ()))
ROWS, D, TOPK, FFW, NEXP, CAP = 128, 2880, 4, 360, 16, 40
NZ, NY, NX = 8, 4, 4
NDP = NZ * NY
OWN = D // NDP
PAD = 96
WIDE = NDP * PAD
HALF = NEXP // 2
HSLOT = HALF * CAP
HW = 384
COVER = 50_000_000_000
BLK = NY * PAD
PART = PAD // 2
VMEM = pl.BlockSpec(memory_space=pltpu.VMEM)
SMEM = pl.BlockSpec(memory_space=pltpu.SMEM)
ANY = pl.BlockSpec(memory_space=pltpu.HBM)


def call(body, name, ins, outs, scratch=(), mib=14, weight=None):
    outs = [jax.ShapeDtypeStruct(*o) for o in outs]
    return pl.pallas_call(
        body,
        in_specs=list(ins),
        out_specs=[VMEM] * len(outs),
        out_shape=outs,
        scratch_shapes=list(scratch),
        compiler_params=pltpu.CompilerParams(vmem_limit_bytes=mib << 20),
        name=name,
        cost_estimate=weight and pl.CostEstimate(flops=weight, transcendentals=0, bytes_accessed=0),
    )


def expert_ids():
    row = lax.broadcasted_iota(I32, (NEXP, ROWS), 0)
    return ((row >> 1) & 3) * 4 + (row >> 3) * 2 + (row & 1)


def slot_onehot(place, n):
    c = lax.broadcasted_iota(I32, (n, CAP, ROWS), 1).astype(F32)
    return (place[:, None, :] == c).astype(F32).reshape(n * CAP, ROWS)


def prep_kernel(pos_ref, len_hbm, adv_hbm, g_hbm, r_hbm, cot_ref, pm_ref, *refs):
    g_ref, r_ref, len_ref, adv_ref, scr, sems = refs
    pairs = [(g_hbm, g_ref), (r_hbm, r_ref), (len_hbm, len_ref), (adv_hbm, adv_ref)]
    copies = [pltpu.make_async_copy(a, b, sems.at[i]) for i, (a, b) in enumerate(pairs)]
    for c in copies:
        c.start()
    for c in copies[1:]:
        c.wait()
    eid = expert_ids()
    hit = r_ref[0:1] == eid
    for k in range(1, TOPK):
        hit = hit | (r_ref[k : k + 1] == eid)
    a = lax.broadcasted_iota(I32, (ROWS, ROWS), 0)
    b = lax.broadcasted_iota(I32, (ROWS, ROWS), 1)
    before = (a < b).astype(F32).astype(BF)
    rank = lax.dot_general(hit.astype(F32).astype(BF), before, NN, preferred_element_type=F32)
    place = jnp.where(hit, rank, -1.0)
    pm_ref[...] = place
    other = jnp.where(pos_ref[2] == 0, place[HALF:], place[:HALF])
    cot_ref[WIDE:] = jnp.concatenate([other, jnp.zeros((HALF, ROWS), F32)], axis=0).astype(BF)
    pos = lax.broadcasted_iota(I32, (8, ROWS), 1)
    start = jnp.int32(0)
    scale = jnp.zeros((8, ROWS), F32)
    for s in range(4):
        n = len_ref[0, s]
        ratio = jnp.full((8, ROWS), adv_ref[0, s], F32) / jnp.full((8, ROWS), n, I32).astype(F32)
        scale = jnp.where((pos >= start) & (pos < start + n), ratio, scale)
        start = start + n
    copies[0].wait()
    scr[0:D] = g_ref[...].astype(F32) * scale[0:1]
    scr[D:] = jnp.zeros((8, ROWS), F32)
    keep = lax.broadcasted_iota(I32, (PAD, ROWS), 0) < OWN
    for d in range(NDP):
        block = scr[d * OWN : d * OWN + PAD]
        cot_ref[d * PAD : (d + 1) * PAD] = jnp.where(keep, block, 0.0).astype(BF)


def prep(pos, lens, adv, gt, rt):
    outs = [((WIDE + 16, ROWS), BF), ((NEXP, ROWS), F32)]
    scratch = [
        pltpu.VMEM((D, ROWS), BF),
        pltpu.VMEM((TOPK, ROWS), I32),
        pltpu.SMEM((1, 4), I32),
        pltpu.SMEM((1, 4), F32),
        pltpu.VMEM((D + 8, ROWS), F32),
        pltpu.SemaphoreType.DMA((4,)),
    ]
    args = [pltpu.with_memory_space_constraint(v, pltpu.HBM) for v in (lens, adv, gt, rt)]
    return call(prep_kernel, "prep", [SMEM] + [ANY] * 4, outs, scratch)(pos, *args)


def spread(s, cot_ref, out_ref):
    step = 768
    for i in range(0, WIDE, step):
        out_ref[:, i : i + step] = lax.dot_general(
            s, cot_ref[i : i + step], NT, preferred_element_type=F32
        ).astype(BF)


def hidden_rows(h_ref, gate_ref, r_ref, place, eid):
    n = place.shape[0]
    acc = jnp.zeros((n * CAP, HW), F32)
    for k in range(TOPK):
        s = slot_onehot(jnp.where(r_ref[k : k + 1] == eid, place, -1.0), n).astype(BF)
        rows = jnp.concatenate(
            [h_ref[k], gate_ref[k : k + 1], jnp.zeros((HW - FFW - 1, ROWS), BF)], axis=0
        )
        acc = acc + lax.dot_general(s, rows, NT, preferred_element_type=F32)
    return acc.astype(BF)


def other_kernel(pos_ref, h_ref, gate_ref, r_ref, pm_ref, out_ref):
    first = pos_ref[2] == 0
    eid = expert_ids()
    place = jnp.where(first, pm_ref[HALF:], pm_ref[:HALF])
    out_ref[...] = hidden_rows(h_ref, gate_ref, r_ref, place, jnp.where(first, eid[HALF:], eid[:HALF]))


def own_kernel(pos_ref, h_ref, gate_ref, r_ref, pm_ref, cot_ref, out_ref):
    first = pos_ref[2] == 0
    eid = expert_ids()
    place = jnp.where(first, pm_ref[:HALF], pm_ref[HALF:])
    spread(slot_onehot(place, HALF).astype(BF), cot_ref, out_ref)
    out_ref[:, WIDE:] = hidden_rows(
        h_ref, gate_ref, r_ref, place, jnp.where(first, eid[:HALF], eid[HALF:])
    )


def partner_kernel(cot_ref, h_ref, out_ref):
    place = cot_ref[WIDE:].astype(F32)[:HALF]
    spread(slot_onehot(place, HALF).astype(BF), cot_ref, out_ref)
    out_ref[:, WIDE:] = h_ref[...]


def term_kernel(pos_ref, own_ref, par_ref, hown_ref, hpar_ref, z_ref, keep_ref, a_ref, b_ref, c_ref, scr):
    acc = jnp.zeros((BLK, FFW), F32)
    for ref, h in ((own_ref, hown_ref), (par_ref, hpar_ref)):
        gate = h[:, FFW : FFW + 1].astype(F32)
        gated = (ref[...].astype(F32) * gate).astype(BF)
        acc = acc + lax.dot_general(gated, h[:, :FFW], TN, preferred_element_type=F32)
    scr[...] = acc
    for y in range(NY):
        z_ref[0, y] = acc[y * PAD : y * PAD + PART].astype(BF)
    for j, out_ref in enumerate((keep_ref, a_ref, b_ref, c_ref)):
        at = pl.multiple_of(((pos_ref[1] + j) % NY) * PAD + PART, 16)
        out_ref[0] = scr[pl.ds(at, PART)].astype(out_ref.dtype)


def grad_term(pos, own, par):
    cols = pl.BlockSpec((HSLOT, BLK), lambda z: (0, z))
    hid = pl.BlockSpec((HSLOT, HW), lambda z: (0, WIDE // HW))
    row = pl.BlockSpec((1, PART, FFW), lambda z: (z, 0, 0))
    return pl.pallas_call(
        term_kernel,
        grid=(NZ,),
        in_specs=[SMEM, cols, cols, hid, hid],
        out_specs=[pl.BlockSpec((1, NY, PART, FFW), lambda z: (z, 0, 0, 0))] + [row] * NY,
        out_shape=[jax.ShapeDtypeStruct((NZ, NY, PART, FFW), BF)]
        + [jax.ShapeDtypeStruct((NZ, PART, FFW), F32)]
        + [jax.ShapeDtypeStruct((NZ, PART, FFW), BF)] * (NY - 1),
        scratch_shapes=[pltpu.VMEM((BLK, FFW), F32)],
        compiler_params=pltpu.CompilerParams(vmem_limit_bytes=14 << 20),
        name="grad_term",
    )(pos, own, par, own, par)


def y_sum_kernel(keep_ref, a_ref, b_ref, c_ref, *refs):
    out_ref = refs[-1]
    for z in range(NZ):
        v = keep_ref[z] + a_ref[z].astype(F32)
        out_ref[z] = (v + (b_ref[z].astype(F32) + c_ref[z].astype(F32))).astype(BF)


def z_sum_kernel(pos_ref, x_ref, keep_ref, *outs):
    for j in range(NY):
        y = (pos_ref[1] + j) % NY
        v = x_ref[0, y].astype(F32)
        for z in range(1, NZ):
            v = v + x_ref[z, y].astype(F32)
        if j == 0:
            keep_ref[...] = v
        else:
            outs[j - 1][...] = v.astype(BF)


def last_kernel(keep_ref, a_ref, b_ref, c_ref, x_ref, out_ref):
    v = keep_ref[...] + a_ref[...].astype(F32)
    out_ref[:PART] = v + (b_ref[...].astype(F32) + c_ref[...].astype(F32))
    v = x_ref[0].astype(F32)
    for z in range(1, NZ):
        v = v + x_ref[z].astype(F32)
    out_ref[PART:] = v[: OWN - PART]


def pad_kernel(w_ref, _, out_ref):
    out_ref[...] = jnp.zeros((PAD, HW), BF)
    out_ref[:OWN, :FFW] = w_ref[...]


def weight_kernel(pos_ref, *refs):
    out_ref = refs[NY]
    for j in range(NY):
        out_ref[(pos_ref[1] + NY - j) % NY] = refs[j][...]


def peer(pos_ref, r, sign):
    dx, dc = r // 2, r % 2
    return ((pos_ref[3] + NX + sign * dx) % NX) * 2 + (pos_ref[4] + dc) % 2


def back_kernel(pos_ref, own_ref, par_ref, w_ref, *refs):
    outs, scr = refs[:HALF], refs[HALF]
    w = w_ref[:, :FFW]
    for i, ref in enumerate((own_ref, par_ref)):
        scr[...] = lax.dot_general(ref[:, :WIDE], w, NN, preferred_element_type=F32)
        for r, out_ref in enumerate(outs):
            at = pl.multiple_of(peer(pos_ref, r, 1) * CAP, 8)
            out_ref[i] = scr[pl.ds(at, CAP)].astype(BF)


def stack_kernel(*refs):
    for r in range(HALF):
        refs[HALF][r] = refs[r][1]


def home_kernel(pos_ref, h_ref, gate_ref, pm_ref, r_ref, other_ref, *refs):
    owns, gh_ref, gg_ref = refs[:HALF], refs[HALF], refs[HALF + 1]
    gate = gate_ref[...].astype(F32)
    c = lax.broadcasted_iota(I32, (CAP, ROWS), 0).astype(F32)
    yh = pos_ref[2]
    pieces, places, ids = [], [], []
    for half in range(2):
        side = yh if half == 0 else 1 - yh
        for r in range(HALF):
            i = peer(pos_ref, r, -1)
            pieces.append((owns[r][0] if half == 0 else other_ref[r]).astype(F32))
            places.append(pm_ref[pl.ds(side * HALF + i, 1)])
            ids.append((i // 2) * 4 + side * 2 + i % 2)
    x = jnp.concatenate(pieces, axis=0).astype(BF)
    for k in range(TOPK):
        rk = r_ref[k : k + 1]
        rows = [
            (jnp.where(rk == e, p, -1.0) == c).astype(F32) for p, e in zip(places, ids)
        ]
        s = jnp.concatenate(rows, axis=0).astype(BF)
        back = lax.dot_general(x, s, TN, preferred_element_type=F32)
        gh_ref[k] = back * gate[k : k + 1]
        gg_ref[k : k + 1] = jnp.sum(back * h_ref[k].astype(F32), axis=0, keepdims=True)


def shift(x, axis, n, by):
    return lax.ppermute(x, axis, [(i, (i + by) % n) for i in range(n)])


def to_peer(x, r):
    dx, dc = r // 2, r % 2
    if r == 0:
        return x
    pairs = [(i, ((i // 2 + dx) % NX) * 2 + (i + dc) % 2) for i in range(HALF)]
    return lax.ppermute(x, ("x", "c"), pairs)


def exchange(x, axes):
    return lax.all_to_all(x, axes, split_axis=0, concat_axis=0, tiled=True)


def local(grad_out, hidden_act, gate_weights, routing, resp_lengths, advantage, w_down):
    pos = jnp.stack([lax.axis_index(a).astype(I32) for a in ("z", "yl", "yh", "x", "c")])
    gt = grad_out.T
    ht = jnp.transpose(hidden_act, (1, 2, 0))
    gates = gate_weights.T
    rt = routing.T

    cot, pm = prep(pos, resp_lengths, advantage, gt, rt)
    cot_par = shift(cot, "yh", 2, 1)
    hid_par = call(
        other_kernel, "send_other", [SMEM] + [VMEM] * 4, [((HSLOT, HW), BF)], weight=COVER
    )(pos, ht, gates, rt, pm)[0]
    hid_par = shift(hid_par, "yh", 2, 1)
    own = call(
        own_kernel, "send_own", [SMEM] + [VMEM] * 5, [((HSLOT, WIDE + HW), BF)], weight=COVER
    )(pos, ht, gates, rt, pm, cot)[0]
    wt = call(pad_kernel, "weight_pad", [VMEM, ANY], [((PAD, HW), BF)])(w_down[0].T, pm)[0]
    own = exchange(own.reshape(HALF, CAP, WIDE + HW), ("x", "c")).reshape(HSLOT, WIDE + HW)

    parts = [wt] + [shift(wt, "yl", NY, j) for j in range(1, NY)]
    weight = call(weight_kernel, "weight_part", [SMEM] + [VMEM] * NY, [((NY, PAD, HW), BF)])(
        pos, *parts
    )[0].reshape(NY * PAD, HW)
    weight = lax.all_gather(weight, "z", axis=0, tiled=True)

    par = call(partner_kernel, "send_partner", [VMEM] * 2, [((HSLOT, WIDE + HW), BF)])(
        cot_par, hid_par
    )[0]
    par = exchange(par.reshape(HALF, CAP, WIDE + HW), ("x", "c")).reshape(HSLOT, WIDE + HW)

    zs, keep, *ys = grad_term(pos, own, par)
    zs = exchange(zs, "z")
    ys = [shift(y, "yl", NY, j + 1) for j, y in enumerate(ys)]
    backs = call(
        back_kernel,
        "back_product",
        [SMEM] + [VMEM] * 3,
        [((2, CAP, FFW), BF)] * HALF,
        [pltpu.VMEM((HSLOT, FFW), F32)],
    )(pos, own, par, weight)
    backs = [to_peer(b, r) for r, b in enumerate(backs)]
    ys = call(
        y_sum_kernel, "y_sum", [VMEM] * NY + [ANY] * 5, [((NZ, PART, FFW), BF)]
    )(keep, *ys, *backs[1:6])[0]
    ys = exchange(ys, "z")
    keep, *zs = call(
        z_sum_kernel,
        "z_sum",
        [SMEM, VMEM],
        [((PART, FFW), F32)] + [((PART, FFW), BF)] * (NY - 1),
    )(pos, zs)
    zs = [shift(z, "yl", NY, j + 1) for j, z in enumerate(zs)]
    gd = call(last_kernel, "last_sum", [VMEM] * (NY + 1), [((OWN, FFW), F32)])(keep, *zs, ys)[0]

    other = call(stack_kernel, "stack_other", [VMEM] * HALF, [((HALF, CAP, FFW), BF)])(*backs)[0]
    other = shift(other, "yh", 2, 1)
    gh, gg = call(
        home_kernel,
        "bring_home",
        [SMEM] + [VMEM] * (5 + HALF),
        [((TOPK, FFW, ROWS), F32), ((TOPK, ROWS), F32)],
    )(pos, ht, gates, pm, rt, other, *backs)
    return gd.T[None], jnp.transpose(gh, (2, 0, 1)), gg.T


def solution(mesh):
    every = ("z", "yl", "x", "yh", "c")
    fine = Mesh(mesh.devices.reshape(NZ, NY, NX, 2, 2), every)
    rows2 = P(every, None)
    rows3 = P(every, None, None)
    cols = P(("x", "yh", "c"), None, ("z", "yl"))
    return jax.shard_map(
        local,
        mesh=fine,
        in_specs=(rows2, rows3, rows2, rows2, rows2, rows2, cols),
        out_specs=(cols, rows3, rows2),
        check_vma=False,
    )
```

time: 217 us -> 220 us (1.014)
  the two profiles are of different devices: /device:TPU:56 before, /device:TPU:1 now
where the time goes in v3:
time: 220 us; the launch traced here: 219 us
  starting transfers between devices  103 us (47%)
  blocking collectives  32.3 us (15%)
  waiting for transfers between devices  30.9 us (14%)
  Pallas kernels  22.5 us (10%)
  local copies, waits for them, and re-layouts  14.9 us (7%)
  between operations  14.5 us (7%)
    ppermute x12, starting transfers between devices, shift(): return lax.ppermute(x, axis, [(i, (i + by) % n) for i in range(n)])  60.7 us
    all_to_all x1, blocking collectives, exchange(): return lax.all_to_all(x, axes, split_axis=0, concat_axis=0, tiled=True)  32.3 us
    all_to_all x3, starting transfers between devices, exchange(): return lax.all_to_all(x, axes, split_axis=0, concat_axis=0, tiled=True)  22.9 us
    ppermute x7, starting transfers between devices, to_peer(): return lax.ppermute(x, ('x', 'c'), pairs)  19.9 us
    unnamed x45, local copies, waits for them, and re-layouts  14.9 us
    ppermute x12, waiting for transfers between devices, shift(): return lax.ppermute(x, axis, [(i, (i + by) % n) for i in range(n)])  13.9 us
    ppermute x7, waiting for transfers between devices, to_peer(): return lax.ppermute(x, ('x', 'c'), pairs)  9.81 us
    all_to_all x3, waiting for transfers between devices, exchange(): return lax.all_to_all(x, axes, split_axis=0, concat_axis=0, tiled=True)  7.16 us
  transfers between devices with their start and end apart: 23, of which 8 were waited for; matrix products, arithmetic and copies ran while one was open for 0% of the time, Pallas kernels for 9%

profile of v3, /device:TPU:1, one launch (start us, length us, event | category | flops | bytes accessed | tf_op | source)
XLA Modules:
  0.0 218.5 jit_solution(6987498936022054778)
XLA Ops:
  7.2 0.1 stack.23.pos_ref
  7.3 2.9 %prep.1 = (bf16[3088,128]{1,0:T(8,128)(2,1)}, f32[16,128]{1,0:T(8,128)S(1)}) custom-call(s32[5]{0:T(128)S(1)} %stack.23.pos_ref, s32[1,4]{1,0:T(1,128)} %len_hbm.1, f32[1,4]{1,0:T(1,128)} %adv_hbm.1, bf16[2880,128]{1,0:T(8,128)(2,1)} %bitcast.42, s32[4,128]{1,0:T(4,128)} %bitcast.35), custom_call_target="tpu_custom_call" | custom-call | tf_op jit(solution)/shard_map/prep/pallas_call | solution.py:103
  10.1 0.0 copy-start.11
  10.2 0.9 copy-done.11
  11.0 4.0 %collective-permute-start.8 = (bf16[96,384]{1,0:T(8,128)(2,1)S(1)}, bf16[96,384]{1,0:T(8,128)(2,1)S(1)}, u32[]{:S(2)}, u32[]{:S(2)}) collective-permute-start(bf16[96,384]{1,0:T(8,128)(2,1)S(1)} %weight_pad.1.refs_0_), channel_id=1, source_target_pairs={{0,16},{16,32},{32,48},{48,0},{1,17},{17,33},{33,49},{49,1},{2,18}... | collective-permute-start | bytes 221192 | tf_op jit(solution)/shard_map/ppermute | solution.py:266
  15.1 4.2 %collective-permute-start.9 = (bf16[96,384]{1,0:T(8,128)(2,1)S(1)}, bf16[96,384]{1,0:T(8,128)(2,1)}, u32[]{:S(2)}, u32[]{:S(2)}) collective-permute-start(bf16[96,384]{1,0:T(8,128)(2,1)S(1)} %weight_pad.1.refs_0_), channel_id=1, source_target_pairs={{0,32},{16,48},{32,0},{48,16},{1,33},{17,49},{33,1},{49,17},{2,34}... | collective-permute-start | bytes 221192 | tf_op jit(solution)/shard_map/ppermute | solution.py:266
  19.3 3.0 %collective-permute-start.10 = (bf16[96,384]{1,0:T(8,128)(2,1)S(1)}, bf16[96,384]{1,0:T(8,128)(2,1)}, u32[]{:S(2)}, u32[]{:S(2)}) collective-permute-start(bf16[96,384]{1,0:T(8,128)(2,1)S(1)} %weight_pad.1.refs_0_), channel_id=1, source_target_pairs={{0,48},{16,0},{32,16},{48,32},{1,49},{17,1},{33,17},{49,33},{2,50}... | collective-permute-start | bytes 221192 | tf_op jit(solution)/shard_map/ppermute | solution.py:266
  22.3 6.1 %collective-permute-start = (bf16[3088,128]{1,0:T(8,128)(2,1)}, bf16[3088,128]{1,0:T(8,128)(2,1)S(1)}, u32[]{:S(2)}, u32[]{:S(2)}) collective-permute-start(bf16[3088,128]{1,0:T(8,128)(2,1)} %get-tuple-element.25.cot_ref), channel_id=1, source_target_pairs={{0,2},{2,0},{1,3},{3,1},{4,6},{6,4},{5,7},{7,5},{8,10},{10,8},{9,1... | collective-permute-start | bytes 2371592 | tf_op jit(solution)/shard_map/ppermute | solution.py:266
  28.4 0.0 copy-start.8
  28.4 1.0 copy-done.8
  29.4 0.7 copy-done.12
  30.0 0.7 copy-done.14
  30.7 2.1 send_own.1
  32.8 1.4 copy-done.4
  34.2 5.9 %all-to-all-start = ((bf16[8,40,3456]{2,1,0:T(8,128)(2,1)}), bf16[8,40,3456]{2,1,0:T(8,128)(2,1)S(1)}, u32[]{:S(2)}, u32[]{:S(2)}) async-start(bf16[8,40,3456]{2,1,0:T(8,128)(2,1)} %bitcast.29), calls=%async_computation | async-start | bytes 4423680 | tf_op jit(solution)/shard_map/all_to_all | solution.py:278
  40.1 0.0 collective-permute-done.8.refs_1_
  40.2 1.7 weight_part.1
  41.8 0.0 all-gather.2.cloned.1.call-update
  41.9 1.0 send_other.1
  42.9 6.3 %collective-permute-start.1 = (bf16[320,384]{1,0:T(8,128)(2,1)S(1)}, bf16[320,384]{1,0:T(8,128)(2,1)S(1)}, u32[]{:S(2)}, u32[]{:S(2)}) collective-permute-start(bf16[320,384]{1,0:T(8,128)(2,1)S(1)} %send_other.1), channel_id=1, source_target_pairs={{0,2},{2,0},{1,3},{3,1},{4,6},{6,4},{5,7},{7,5},{8,10},{10,8},{9,1... | collective-permute-start | bytes 737288 | tf_op jit(solution)/shard_map/ppermute | solution.py:266
  49.2 9.3 %collective-permute-done.1.h_ref = bf16[320,384]{1,0:T(8,128)(2,1)S(1)} collective-permute-done((bf16[320,384]{1,0:T(8,128)(2,1)S(1)}, bf16[320,384]{1,0:T(8,128)(2,1)S(1)}, u32[]{:S(2)}, u32[]{:S(2)}) %collective-permute-start.1) | collective-permute-done | bytes 245792 | tf_op jit(solution)/shard_map/ppermute | solution.py:266
  58.5 0.7 send_partner.1
  59.2 1.4 copy-done.2
  60.5 7.2 %all-to-all-done = bf16[8,40,3456]{2,1,0:T(8,128)(2,1)S(1)} async-done(((bf16[8,40,3456]{2,1,0:T(8,128)(2,1)}), bf16[8,40,3456]{2,1,0:T(8,128)(2,1)S(1)}, u32[]{:S(2)}, u32[]{:S(2)}) %all-to-all-start) | async-done | bytes 2211872 | tf_op jit(solution)/shard_map/all_to_all | solution.py:278
  67.7 32.3 %all_to_all.20 = bf16[8,40,3456]{2,1,0:T(8,128)(2,1)S(1)} all-to-all(bf16[8,40,3456]{2,1,0:T(8,128)(2,1)} %bitcast.28), channel_id=1, replica_groups=mesh['z'=8,'yl'=4,'x'=4,'yh'=2,'c'=2] {'x','c'}, dimensions={0} | all-to-all | bytes 4423680 | tf_op jit(solution)/shard_map/all_to_all | solution.py:278
  100.0 6.4 %grad_term.1 = (bf16[8,4,48,360]{3,2,1,0:T(8,128)(2,1)S(1)}, f32[8,48,360]{2,1,0:T(8,128)S(1)}, bf16[8,48,360]{2,1,0:T(8,128)(2,1)S(1)}, bf16[8,48,360]{2,1,0:T(8,128)(2,1)S(1)}, bf16[8,48,360]{2,1,0:T(8,128)(2,1)S(1)}) custom-call(s32[5]{0:T(128)S(1)} %stack.23.pos_ref, bf16[320,3456]{1,0:T(8,128)(2,1)S(1)} %bitcast.22, bf16[320,3456]{1,0:T(8,128)(2,1)S(1)} %bitcast.25, ...), custom_call_target="tpu_custom_call" | custom-call | tf_op jit(solution)/shard_map/grad_term/pallas_call | solution.py:167
  106.4 1.0 copy-done.5
  107.5 0.8 copy-done.6
  108.3 0.7 copy-done.17
  109.0 0.8 copy-done.18
  109.8 0.8 copy-done.19
  110.6 10.1 %all-to-all-start.2 = ((bf16[8,4,48,360]{3,2,1,0:T(8,128)(2,1)}), bf16[8,4,48,360]{3,2,1,0:T(8,128)(2,1)S(1)}, u32[]{:S(2)}, u32[]{:S(2)}) async-start(bf16[8,4,48,360]{3,2,1,0:T(8,128)(2,1)} %copy-done.5), calls=%async_computation.2 | async-start | bytes 2359296 | tf_op jit(solution)/shard_map/all_to_all | solution.py:278
  120.6 17.5 %collective-permute-start.5 = (bf16[8,48,360]{2,1,0:T(8,128)(2,1)}, bf16[8,48,360]{2,1,0:T(8,128)(2,1)}, u32[]{:S(2)}, u32[]{:S(2)}) collective-permute-start(bf16[8,48,360]{2,1,0:T(8,128)(2,1)} %copy-done.19), channel_id=1, source_target_pairs={{0,16},{16,32},{32,48},{48,0},{1,17},{17,33},{33,49},{49,1},{2,18}... | collective-permute-start | bytes 829448 | tf_op jit(solution)/shard_map/ppermute | solution.py:266
  138.1 1.9 collective-permute-start.6
  140.0 4.0 %collective-permute-start.7 = (bf16[8,48,360]{2,1,0:T(8,128)(2,1)}, bf16[8,48,360]{2,1,0:T(8,128)(2,1)}, u32[]{:S(2)}, u32[]{:S(2)}) collective-permute-start(bf16[8,48,360]{2,1,0:T(8,128)(2,1)} %copy-done.17), channel_id=1, source_target_pairs={{0,48},{16,0},{32,16},{48,32},{1,49},{17,1},{33,17},{49,33},{2,50}... | collective-permute-start | bytes 829448 | tf_op jit(solution)/shard_map/ppermute | solution.py:266
  144.0 0.0 all-gather.2.cloned.1.call-done.w_ref
  144.1 1.6 copy-done.1
  145.7 1.7 copy-done.3
  147.4 2.8 %back_product.1 = (bf16[2,40,360]{2,1,0:T(8,128)(2,1)S(1)}, bf16[2,40,360]{2,1,0:T(8,128)(2,1)S(1)}, bf16[2,40,360]{2,1,0:T(8,128)(2,1)S(1)}, bf16[2,40,360]{2,1...) custom-call(s32[5]{0:T(128)S(1)} %stack.23.pos_ref, ...), custom_call_target="tpu_custom_call" | custom-call | tf_op jit(solution)/shard_map/back_product/pallas_call | solution.py:314
  150.1 0.0 copy-start.20
  150.1 0.6 copy-done.20
  150.8 3.4 %collective-permute-start.11 = (bf16[2,40,360]{2,1,0:T(8,128)(2,1)S(1)}, bf16[2,40,360]{2,1,0:T(8,128)(2,1)S(1)}, u32[]{:S(2)}, u32[]{:S(2)}) collective-permute-start(bf16[2,40,360]{2,1,0:T(8,128)(2,1)S(1)} %get-tuple-element.35), channel_id=1, source_target_pairs={{0,1},{1,0},{4,5},{5,4},{8,9},{9,8},{12,13},{13,12},{2,3},{3,2},{6... | collective-permute-start | bytes 172808 | tf_op jit(solution)/shard_map/ppermute | solution.py:274
  154.2 2.2 %collective-permute-start.12 = (bf16[2,40,360]{2,1,0:T(8,128)(2,1)S(1)}, bf16[2,40,360]{2,1,0:T(8,128)(2,1)S(1)}, u32[]{:S(2)}, u32[]{:S(2)}) collective-permute-start(bf16[2,40,360]{2,1,0:T(8,128)(2,1)S(1)} %get-tuple-element.36), channel_id=1, source_target_pairs={{0,4},{1,5},{4,8},{5,9},{8,12},{9,13},{12,0},{13,1},{2,6},{3,7},{6... | collective-permute-start | bytes 172808 | tf_op jit(solution)/shard_map/ppermute | solution.py:274
  156.4 2.1 collective-permute-start.13
  158.5 5.5 %collective-permute-start.14 = (bf16[2,40,360]{2,1,0:T(8,128)(2,1)S(1)}, bf16[2,40,360]{2,1,0:T(8,128)(2,1)S(1)}, u32[]{:S(2)}, u32[]{:S(2)}) collective-permute-start(bf16[2,40,360]{2,1,0:T(8,128)(2,1)S(1)} %get-tuple-element.38), channel_id=1, source_target_pairs={{0,8},{1,9},{4,12},{5,13},{8,0},{9,1},{12,4},{13,5},{2,10},{3,11},... | collective-permute-start | bytes 172808 | tf_op jit(solution)/shard_map/ppermute | solution.py:274
  164.0 2.0 collective-permute-start.15
  166.1 0.2 collective-permute-done.14.refs_3_.refs_4_
  166.2 5.4 %collective-permute-done.15.refs_4_.refs_5_ = bf16[2,40,360]{2,1,0:T(8,128)(2,1)S(1)} collective-permute-done((bf16[2,40,360]{2,1,0:T(8,128)(2,1)S(1)}, bf16[2,40,360]{2,1,0:T(8,128)(2,1)S(1)}, u32[]{:S(2)}, u32[]{:S(2)}) %collective-permute-start.15) | collective-permute-done | bytes 57632 | tf_op jit(solution)/shard_map/ppermute | solution.py:274
  171.6 2.0 y_sum.1
  173.7 6.8 %all-to-all-start.3 = ((bf16[8,48,360]{2,1,0:T(8,128)(2,1)}), bf16[8,48,360]{2,1,0:T(8,128)(2,1)S(1)}, u32[]{:S(2)}, u32[]{:S(2)}) async-start(bf16[8,48,360]{2,1,0:T(8,128)(2,1)} %y_sum.1), calls=%async_computation.3 | async-start | bytes 589824 | tf_op jit(solution)/shard_map/all_to_all | solution.py:278
  180.5 2.2 %collective-permute-start.16 = (bf16[2,40,360]{2,1,0:T(8,128)(2,1)S(1)}, bf16[2,40,360]{2,1,0:T(8,128)(2,1)S(1)}, u32[]{:S(2)}, u32[]{:S(2)}) collective-permute-start(bf16[2,40,360]{2,1,0:T(8,128)(2,1)S(1)} %copy-done.21), channel_id=1, source_target_pairs={{0,12},{1,13},{4,0},{5,1},{8,4},{9,5},{12,8},{13,9},{2,14},{3,15},... | collective-permute-start | bytes 172808 | tf_op jit(solution)/shard_map/ppermute | solution.py:274
  182.7 2.5 %collective-permute-start.17 = (bf16[2,40,360]{2,1,0:T(8,128)(2,1)S(1)}, bf16[2,40,360]{2,1,0:T(8,128)(2,1)S(1)}, u32[]{:S(2)}, u32[]{:S(2)}) collective-permute-start(bf16[2,40,360]{2,1,0:T(8,128)(2,1)S(1)} %get-tuple-element.42), channel_id=1, source_target_pairs={{0,13},{1,12},{4,1},{5,0},{8,5},{9,4},{12,9},{13,8},{2,15},{3,14},... | collective-permute-start | bytes 172808 | tf_op jit(solution)/shard_map/ppermute | solution.py:274
  185.2 0.5 collective-permute-done.16.refs_6_
  185.8 3.7 %collective-permute-done.17.refs_7_ = bf16[2,40,360]{2,1,0:T(8,128)(2,1)S(1)} collective-permute-done((bf16[2,40,360]{2,1,0:T(8,128)(2,1)S(1)}, bf16[2,40,360]{2,1,0:T(8,128)(2,1)S(1)}, u32[]{:S(2)}, u32[]{:S(2)}) %collective-permute-start.17) | collective-permute-done | bytes 57632 | tf_op jit(solution)/shard_map/ppermute | solution.py:274
  189.5 2.9 %collective-permute-start.18 = (bf16[8,40,360]{2,1,0:T(8,128)(2,1)S(1)}, bf16[8,40,360]{2,1,0:T(8,128)(2,1)S(1)}, u32[]{:S(2)}, u32[]{:S(2)}) collective-permute-start(bf16[8,40,360]{2,1,0:T(8,128)(2,1)S(1)} %stack_other.1), channel_id=1, source_target_pairs={{0,2},{2,0},{1,3},{3,1},{4,6},{6,4},{5,7},{7,5},{8,10},{10,8},{9,1... | collective-permute-start | bytes 691208 | tf_op jit(solution)/shard_map/ppermute | solution.py:266
  192.4 0.7 z_sum.1
  193.1 3.5 %collective-permute-start.2 = (bf16[48,360]{1,0:T(8,128)(2,1)S(1)}, bf16[48,360]{1,0:T(8,128)(2,1)S(1)}, u32[]{:S(2)}, u32[]{:S(2)}) collective-permute-start(bf16[48,360]{1,0:T(8,128)(2,1)S(1)} %get-tuple-element.28), channel_id=1, source_target_pairs={{0,16},{16,32},{32,48},{48,0},{1,17},{17,33},{33,49},{49,1},{2,18}... | collective-permute-start | bytes 103688 | tf_op jit(solution)/shard_map/ppermute | solution.py:266
  196.6 4.9 %collective-permute-start.3 = (bf16[48,360]{1,0:T(8,128)(2,1)S(1)}, bf16[48,360]{1,0:T(8,128)(2,1)S(1)}, u32[]{:S(2)}, u32[]{:S(2)}) collective-permute-start(bf16[48,360]{1,0:T(8,128)(2,1)S(1)} %get-tuple-element.29), channel_id=1, source_target_pairs={{0,32},{16,48},{32,0},{48,16},{1,33},{17,49},{33,1},{49,17},{2,34}... | collective-permute-start | bytes 103688 | tf_op jit(solution)/shard_map/ppermute | solution.py:266
  201.5 2.4 %collective-permute-start.4 = (bf16[48,360]{1,0:T(8,128)(2,1)S(1)}, bf16[48,360]{1,0:T(8,128)(2,1)S(1)}, u32[]{:S(2)}, u32[]{:S(2)}) collective-permute-start(bf16[48,360]{1,0:T(8,128)(2,1)S(1)} %get-tuple-element.30), channel_id=1, source_target_pairs={{0,48},{16,0},{32,16},{48,32},{1,49},{17,1},{33,17},{49,33},{2,50}... | collective-permute-start | bytes 103688 | tf_op jit(solution)/shard_map/ppermute | solution.py:266
  204.0 2.2 %bring_home.1 = (f32[4,360,128]{2,1,0:T(8,128)}, f32[4,128]{1,0:T(4,128)}) custom-call(s32[5]{0:T(128)S(1)} %stack.23.pos_ref, bf16[4,360,128]{2,1,0:T(8,128)(2,1)S(1)} %bitcast.33, bf16[4,128]{1,0:T(4,128)(2,1)S(1)} %bitcast.41, f32[16,128]{1,0:T(8,128)S(1)} %get-tuple-element.24.pm_ref._, s32[4,128]{1,0:T(4,128)S(1)} %bitcast.38, ...), custom_call_target="tpu_custom_call" | custom-call | tf_op jit(solution)/shard_map/bring_home/pallas_call | solution.py:337
  206.2 0.9 collective-permute-done.2.a_ref
  207.1 3.7 %collective-permute-done.3.b_ref = bf16[48,360]{1,0:T(8,128)(2,1)S(1)} collective-permute-done((bf16[48,360]{1,0:T(8,128)(2,1)S(1)}, bf16[48,360]{1,0:T(8,128)(2,1)S(1)}, u32[]{:S(2)}, u32[]{:S(2)}) %collective-permute-start.3) | collective-permute-done | bytes 34592 | tf_op jit(solution)/shard_map/ppermute | solution.py:266
  210.8 0.1 last_sum.1
  210.9 0.8 copy.10
  (43 shorter events, 0.1 us)
Async XLA Ops:
  10.1 0.9 copy-start.11
  11.0 29.1 %collective-permute-start.8 = (bf16[96,384]{1,0:T(8,128)(2,1)S(1)}, bf16[96,384]{1,0:T(8,128)(2,1)S(1)}, u32[]{:S(2)}, u32[]{:S(2)}) collective-permute-start(bf16[96,384]{1,0:T(8,128)(2,1)S(1)} %weight_pad.1.refs_0_), channel_id=1, source_target_pairs={{0,16},{16,32},{32,48},{48,0},{1,17},{17,33},{33,49},{49,1},{2,18}... | collective-permute-start | bytes 221192 | tf_op jit(solution)/shard_map/ppermute | solution.py:266
  15.1 25.1 %collective-permute-start.9 = (bf16[96,384]{1,0:T(8,128)(2,1)S(1)}, bf16[96,384]{1,0:T(8,128)(2,1)}, u32[]{:S(2)}, u32[]{:S(2)}) collective-permute-start(bf16[96,384]{1,0:T(8,128)(2,1)S(1)} %weight_pad.1.refs_0_), channel_id=1, source_target_pairs={{0,32},{16,48},{32,0},{48,16},{1,33},{17,49},{33,1},{49,17},{2,34}... | collective-permute-start | bytes 221192 | tf_op jit(solution)/shard_map/ppermute | solution.py:266
  19.3 20.8 %collective-permute-start.10 = (bf16[96,384]{1,0:T(8,128)(2,1)S(1)}, bf16[96,384]{1,0:T(8,128)(2,1)}, u32[]{:S(2)}, u32[]{:S(2)}) collective-permute-start(bf16[96,384]{1,0:T(8,128)(2,1)S(1)} %weight_pad.1.refs_0_), channel_id=1, source_target_pairs={{0,48},{16,0},{32,16},{48,32},{1,49},{17,1},{33,17},{49,33},{2,50}... | collective-permute-start | bytes 221192 | tf_op jit(solution)/shard_map/ppermute | solution.py:266
  22.3 36.2 %collective-permute-start = (bf16[3088,128]{1,0:T(8,128)(2,1)}, bf16[3088,128]{1,0:T(8,128)(2,1)S(1)}, u32[]{:S(2)}, u32[]{:S(2)}) collective-permute-start(bf16[3088,128]{1,0:T(8,128)(2,1)} %get-tuple-element.25.cot_ref), channel_id=1, source_target_pairs={{0,2},{2,0},{1,3},{3,1},{4,6},{6,4},{5,7},{7,5},{8,10},{10,8},{9,1... | collective-permute-start | bytes 2371592 | tf_op jit(solution)/shard_map/ppermute | solution.py:266
  28.4 1.0 copy-start.8
  29.4 0.7 copy-start.12
  30.0 0.7 copy-start.14
  32.8 1.4 copy-start.4
  34.2 7.7 %copy-start.9 = (bf16[128,4,360]{0,2,1:T(8,128)(2,1)S(1)}, bf16[128,4,360]{0,2,1:T(8,128)(2,1)}, u32[]{:S(2)}) copy-start(bf16[128,4,360]{0,2,1:T(8,128)(2,1)} %param.8) | copy-start | bytes 1105924
  34.2 7.7 %copy-start.13 = (s32[128,4]{0,1:T(4,128)S(1)}, s32[128,4]{0,1:T(4,128)}, u32[]{:S(2)}) copy-start(s32[128,4]{0,1:T(4,128)} %param.10) | copy-start | bytes 6148
  34.2 7.7 %copy-start.15 = (bf16[128,4]{0,1:T(4,128)(2,1)S(1)}, bf16[128,4]{0,1:T(4,128)(2,1)}, u32[]{:S(2)}) copy-start(bf16[128,4]{0,1:T(4,128)(2,1)} %param.9) | copy-start | bytes 3076
  34.2 33.5 %all-to-all-start = ((bf16[8,40,3456]{2,1,0:T(8,128)(2,1)}), bf16[8,40,3456]{2,1,0:T(8,128)(2,1)S(1)}, u32[]{:S(2)}, u32[]{:S(2)}) async-start(bf16[8,40,3456]{2,1,0:T(8,128)(2,1)} %bitcast.29), calls=%async_computation | async-start | bytes 4423680 | tf_op jit(solution)/shard_map/all_to_all | solution.py:278
  40.1 103.9 %all-gather.2.cloned.1.call-start = ((), (), s32[]{:S(2)}) async-start(), calls=%async_computation.4 | async-start | bytes 2654208 | tf_op jit(solution)/shard_map/all_gather | solution.py:304
  42.9 15.6 %collective-permute-start.1 = (bf16[320,384]{1,0:T(8,128)(2,1)S(1)}, bf16[320,384]{1,0:T(8,128)(2,1)S(1)}, u32[]{:S(2)}, u32[]{:S(2)}) collective-permute-start(bf16[320,384]{1,0:T(8,128)(2,1)S(1)} %send_other.1), channel_id=1, source_target_pairs={{0,2},{2,0},{1,3},{3,1},{4,6},{6,4},{5,7},{7,5},{8,10},{10,8},{9,1... | collective-permute-start | bytes 737288 | tf_op jit(solution)/shard_map/ppermute | solution.py:266
  59.2 1.4 copy-start.2
  100.0 6.4 %copy-start = (bf16[8,40,3456]{2,1,0:T(8,128)(2,1)}, bf16[8,40,3456]{2,1,0:T(8,128)(2,1)S(1)}, u32[]{:S(2)}) copy-start(bf16[8,40,3456]{2,1,0:T(8,128)(2,1)S(1)} %all_to_all.20) | copy-start | bytes 6635524
  106.4 1.1 copy-start.5
  107.5 0.8 copy-start.6
  108.3 0.7 copy-start.17
  109.0 0.8 copy-start.18
  109.8 0.8 copy-start.19
  110.6 63.1 %all-to-all-start.2 = ((bf16[8,4,48,360]{3,2,1,0:T(8,128)(2,1)}), bf16[8,4,48,360]{3,2,1,0:T(8,128)(2,1)S(1)}, u32[]{:S(2)}, u32[]{:S(2)}) async-start(bf16[8,4,48,360]{3,2,1,0:T(8,128)(2,1)} %copy-done.5), calls=%async_computation.2 | async-start | bytes 2359296 | tf_op jit(solution)/shard_map/all_to_all | solution.py:278
  120.6 35.8 %collective-permute-start.5 = (bf16[8,48,360]{2,1,0:T(8,128)(2,1)}, bf16[8,48,360]{2,1,0:T(8,128)(2,1)}, u32[]{:S(2)}, u32[]{:S(2)}) collective-permute-start(bf16[8,48,360]{2,1,0:T(8,128)(2,1)} %copy-done.19), channel_id=1, source_target_pairs={{0,16},{16,32},{32,48},{48,0},{1,17},{17,33},{33,49},{49,1},{2,18}... | collective-permute-start | bytes 829448 | tf_op jit(solution)/shard_map/ppermute | solution.py:266
  138.1 20.4 %collective-permute-start.6 = (bf16[8,48,360]{2,1,0:T(8,128)(2,1)}, bf16[8,48,360]{2,1,0:T(8,128)(2,1)}, u32[]{:S(2)}, u32[]{:S(2)}) collective-permute-start(bf16[8,48,360]{2,1,0:T(8,128)(2,1)} %copy-done.18), channel_id=1, source_target_pairs={{0,32},{16,48},{32,0},{48,16},{1,33},{17,49},{33,1},{49,17},{2,34}... | collective-permute-start | bytes 829448 | tf_op jit(solution)/shard_map/ppermute | solution.py:266
  140.0 23.9 %collective-permute-start.7 = (bf16[8,48,360]{2,1,0:T(8,128)(2,1)}, bf16[8,48,360]{2,1,0:T(8,128)(2,1)}, u32[]{:S(2)}, u32[]{:S(2)}) collective-permute-start(bf16[8,48,360]{2,1,0:T(8,128)(2,1)} %copy-done.17), channel_id=1, source_target_pairs={{0,48},{16,0},{32,16},{48,32},{1,49},{17,1},{33,17},{49,33},{2,50}... | collective-permute-start | bytes 829448 | tf_op jit(solution)/shard_map/ppermute | solution.py:266
  144.1 1.6 copy-start.1
  145.7 1.7 copy-start.3
  147.4 24.2 %copy-start.7 = (f32[8,48,360]{2,1,0:T(8,128)S(1)}, f32[8,48,360]{2,1,0:T(8,128)}, u32[]{:S(2)}) copy-start(f32[8,48,360]{2,1,0:T(8,128)} %copy-done.6) | copy-start | bytes 1658884
  150.1 0.6 copy-start.20
  150.8 29.7 %copy-start.21 = (bf16[2,40,360]{2,1,0:T(8,128)(2,1)S(1)}, bf16[2,40,360]{2,1,0:T(8,128)(2,1)}, u32[]{:S(2)}) copy-start(bf16[2,40,360]{2,1,0:T(8,128)(2,1)} %copy-done.20) | copy-start | bytes 172804
  150.8 15.3 %collective-permute-start.11 = (bf16[2,40,360]{2,1,0:T(8,128)(2,1)S(1)}, bf16[2,40,360]{2,1,0:T(8,128)(2,1)S(1)}, u32[]{:S(2)}, u32[]{:S(2)}) collective-permute-start(bf16[2,40,360]{2,1,0:T(8,128)(2,1)S(1)} %get-tuple-element.35), channel_id=1, source_target_pairs={{0,1},{1,0},{4,5},{5,4},{8,9},{9,8},{12,13},{13,12},{2,3},{3,2},{6... | collective-permute-start | bytes 172808 | tf_op jit(solution)/shard_map/ppermute | solution.py:274
  154.2 11.9 %collective-permute-start.12 = (bf16[2,40,360]{2,1,0:T(8,128)(2,1)S(1)}, bf16[2,40,360]{2,1,0:T(8,128)(2,1)S(1)}, u32[]{:S(2)}, u32[]{:S(2)}) collective-permute-start(bf16[2,40,360]{2,1,0:T(8,128)(2,1)S(1)} %get-tuple-element.36), channel_id=1, source_target_pairs={{0,4},{1,5},{4,8},{5,9},{8,12},{9,13},{12,0},{13,1},{2,6},{3,7},{6... | collective-permute-start | bytes 172808 | tf_op jit(solution)/shard_map/ppermute | solution.py:274
  156.4 9.6 %collective-permute-start.13 = (bf16[2,40,360]{2,1,0:T(8,128)(2,1)S(1)}, bf16[2,40,360]{2,1,0:T(8,128)(2,1)S(1)}, u32[]{:S(2)}, u32[]{:S(2)}) collective-permute-start(bf16[2,40,360]{2,1,0:T(8,128)(2,1)S(1)} %get-tuple-element.37), channel_id=1, source_target_pairs={{0,5},{1,4},{4,9},{5,8},{8,13},{9,12},{12,1},{13,0},{2,7},{3,6},{6... | collective-permute-start | bytes 172808 | tf_op jit(solution)/shard_map/ppermute | solution.py:274
  158.5 7.7 %collective-permute-start.14 = (bf16[2,40,360]{2,1,0:T(8,128)(2,1)S(1)}, bf16[2,40,360]{2,1,0:T(8,128)(2,1)S(1)}, u32[]{:S(2)}, u32[]{:S(2)}) collective-permute-start(bf16[2,40,360]{2,1,0:T(8,128)(2,1)S(1)} %get-tuple-element.38), channel_id=1, source_target_pairs={{0,8},{1,9},{4,12},{5,13},{8,0},{9,1},{12,4},{13,5},{2,10},{3,11},... | collective-permute-start | bytes 172808 | tf_op jit(solution)/shard_map/ppermute | solution.py:274
  164.0 7.6 %collective-permute-start.15 = (bf16[2,40,360]{2,1,0:T(8,128)(2,1)S(1)}, bf16[2,40,360]{2,1,0:T(8,128)(2,1)S(1)}, u32[]{:S(2)}, u32[]{:S(2)}) collective-permute-start(bf16[2,40,360]{2,1,0:T(8,128)(2,1)S(1)} %get-tuple-element.39), channel_id=1, source_target_pairs={{0,9},{1,8},{4,13},{5,12},{8,1},{9,0},{12,5},{13,4},{2,11},{3,10},... | collective-permute-start | bytes 172808 | tf_op jit(solution)/shard_map/ppermute | solution.py:274
  171.6 32.3 %copy-start.10 = (bf16[128,4,360]{0,2,1:T(8,128)(2,1)S(1)}, bf16[128,4,360]{0,2,1:T(8,128)(2,1)}, u32[]{:S(2)}) copy-start(bf16[128,4,360]{0,2,1:T(8,128)(2,1)} %param.8) | copy-start | bytes 1105924
  171.6 32.3 %copy-start.16 = (bf16[128,4]{0,1:T(4,128)(2,1)S(1)}, bf16[128,4]{0,1:T(4,128)(2,1)}, u32[]{:S(2)}) copy-start(bf16[128,4]{0,1:T(4,128)(2,1)} %param.9) | copy-start | bytes 3076
  173.7 37.1 %all-to-all-start.3 = ((bf16[8,48,360]{2,1,0:T(8,128)(2,1)}), bf16[8,48,360]{2,1,0:T(8,128)(2,1)S(1)}, u32[]{:S(2)}, u32[]{:S(2)}) async-start(bf16[8,48,360]{2,1,0:T(8,128)(2,1)} %y_sum.1), calls=%async_computation.3 | async-start | bytes 589824 | tf_op jit(solution)/shard_map/all_to_all | solution.py:278
  180.5 5.3 %collective-permute-start.16 = (bf16[2,40,360]{2,1,0:T(8,128)(2,1)S(1)}, bf16[2,40,360]{2,1,0:T(8,128)(2,1)S(1)}, u32[]{:S(2)}, u32[]{:S(2)}) collective-permute-start(bf16[2,40,360]{2,1,0:T(8,128)(2,1)S(1)} %copy-done.21), channel_id=1, source_target_pairs={{0,12},{1,13},{4,0},{5,1},{8,4},{9,5},{12,8},{13,9},{2,14},{3,15},... | collective-permute-start | bytes 172808 | tf_op jit(solution)/shard_map/ppermute | solution.py:274
  182.7 6.8 %collective-permute-start.17 = (bf16[2,40,360]{2,1,0:T(8,128)(2,1)S(1)}, bf16[2,40,360]{2,1,0:T(8,128)(2,1)S(1)}, u32[]{:S(2)}, u32[]{:S(2)}) collective-permute-start(bf16[2,40,360]{2,1,0:T(8,128)(2,1)S(1)} %get-tuple-element.42), channel_id=1, source_target_pairs={{0,13},{1,12},{4,1},{5,0},{8,5},{9,4},{12,9},{13,8},{2,15},{3,14},... | collective-permute-start | bytes 172808 | tf_op jit(solution)/shard_map/ppermute | solution.py:274
  189.5 14.4 %collective-permute-start.18 = (bf16[8,40,360]{2,1,0:T(8,128)(2,1)S(1)}, bf16[8,40,360]{2,1,0:T(8,128)(2,1)S(1)}, u32[]{:S(2)}, u32[]{:S(2)}) collective-permute-start(bf16[8,40,360]{2,1,0:T(8,128)(2,1)S(1)} %stack_other.1), channel_id=1, source_target_pairs={{0,2},{2,0},{1,3},{3,1},{4,6},{6,4},{5,7},{7,5},{8,10},{10,8},{9,1... | collective-permute-start | bytes 691208 | tf_op jit(solution)/shard_map/ppermute | solution.py:266
  193.1 14.0 %collective-permute-start.2 = (bf16[48,360]{1,0:T(8,128)(2,1)S(1)}, bf16[48,360]{1,0:T(8,128)(2,1)S(1)}, u32[]{:S(2)}, u32[]{:S(2)}) collective-permute-start(bf16[48,360]{1,0:T(8,128)(2,1)S(1)} %get-tuple-element.28), channel_id=1, source_target_pairs={{0,16},{16,32},{32,48},{48,0},{1,17},{17,33},{33,49},{49,1},{2,18}... | collective-permute-start | bytes 103688 | tf_op jit(solution)/shard_map/ppermute | solution.py:266
  196.6 14.2 %collective-permute-start.3 = (bf16[48,360]{1,0:T(8,128)(2,1)S(1)}, bf16[48,360]{1,0:T(8,128)(2,1)S(1)}, u32[]{:S(2)}, u32[]{:S(2)}) collective-permute-start(bf16[48,360]{1,0:T(8,128)(2,1)S(1)} %get-tuple-element.29), channel_id=1, source_target_pairs={{0,32},{16,48},{32,0},{48,16},{1,33},{17,49},{33,1},{49,17},{2,34}... | collective-permute-start | bytes 103688 | tf_op jit(solution)/shard_map/ppermute | solution.py:266
  201.5 9.2 %collective-permute-start.4 = (bf16[48,360]{1,0:T(8,128)(2,1)S(1)}, bf16[48,360]{1,0:T(8,128)(2,1)S(1)}, u32[]{:S(2)}, u32[]{:S(2)}) collective-permute-start(bf16[48,360]{1,0:T(8,128)(2,1)S(1)} %get-tuple-element.30), channel_id=1, source_target_pairs={{0,48},{16,0},{32,16},{48,32},{1,49},{17,1},{33,17},{49,33},{2,50}... | collective-permute-start | bytes 103688 | tf_op jit(solution)/shard_map/ppermute | solution.py:266
Sparse Core Ops, SparseCore 0:
  43.0 61.9 all-gather.1

commit v4 on v3

--- a/solution.py
+++ b/solution.py
@@ -19,21 +19,25 @@
 WIDE = NDP * PAD
 HALF = NEXP // 2
 HSLOT = HALF * CAP
+STEP = 768
+SPREAD = [
+    pltpu.VMEM((HALF * CAP, WIDE + 384), BF),
+    pltpu.SemaphoreType.DMA((WIDE // STEP + 1,)),
+]
 HW = 384
 COVER = 50_000_000_000
 BLK = NY * PAD
-PART = PAD // 2
 VMEM = pl.BlockSpec(memory_space=pltpu.VMEM)
 SMEM = pl.BlockSpec(memory_space=pltpu.SMEM)
 ANY = pl.BlockSpec(memory_space=pltpu.HBM)
 
 
-def call(body, name, ins, outs, scratch=(), mib=14, weight=None):
-    outs = [jax.ShapeDtypeStruct(*o) for o in outs]
+def call(body, name, ins, outs, scratch=(), mib=14, weight=None, where=None):
+    outs = [(pltpu.HBM if where else jax.ShapeDtypeStruct)(*o) for o in outs]
     return pl.pallas_call(
         body,
         in_specs=list(ins),
-        out_specs=[VMEM] * len(outs),
+        out_specs=[where or VMEM] * len(outs),
         out_shape=outs,
         scratch_shapes=list(scratch),
         compiler_params=pltpu.CompilerParams(vmem_limit_bytes=mib << 20),
@@ -103,12 +107,25 @@
     return call(prep_kernel, "prep", [SMEM] + [ANY] * 4, outs, scratch)(pos, *args)
 
 
-def spread(s, cot_ref, out_ref):
-    step = 768
-    for i in range(0, WIDE, step):
-        out_ref[:, i : i + step] = lax.dot_general(
-            s, cot_ref[i : i + step], NT, preferred_element_type=F32
+def spread(s, cot_ref, scr, out_hbm, sems):
+    copies = []
+    for n, i in enumerate(range(0, WIDE, STEP)):
+        cols = pl.ds(i, STEP)
+        scr[:, cols] = lax.dot_general(
+            s, cot_ref[i : i + STEP], NT, preferred_element_type=F32
         ).astype(BF)
+        copies.append(pltpu.make_async_copy(scr.at[:, cols], out_hbm.at[:, cols], sems.at[n]))
+        copies[-1].start()
+    return copies
+
+
+def finish(rows, copies, scr, out_hbm, sems):
+    cols = pl.ds(WIDE, HW)
+    scr[:, cols] = rows
+    copies.append(pltpu.make_async_copy(scr.at[:, cols], out_hbm.at[:, cols], sems.at[WIDE // STEP]))
+    copies[-1].start()
+    for c in copies:
+        c.wait()
 
 
 def hidden_rows(h_ref, gate_ref, r_ref, place, eid):
@@ -130,80 +147,50 @@
     out_ref[...] = hidden_rows(h_ref, gate_ref, r_ref, place, jnp.where(first, eid[HALF:], eid[:HALF]))
 
 
-def own_kernel(pos_ref, h_ref, gate_ref, r_ref, pm_ref, cot_ref, out_ref):
+def own_kernel(pos_ref, h_hbm, gate_hbm, r_hbm, pm_ref, cot_ref, out_hbm, *refs):
+    h_ref, gate_ref, r_ref, sem_in, scr, sems = refs
+    pairs = [(h_hbm, h_ref), (gate_hbm, gate_ref), (r_hbm, r_ref)]
+    loads = [pltpu.make_async_copy(a, b, sem_in.at[i]) for i, (a, b) in enumerate(pairs)]
+    for c in loads:
+        c.start()
     first = pos_ref[2] == 0
     eid = expert_ids()
     place = jnp.where(first, pm_ref[:HALF], pm_ref[HALF:])
-    spread(slot_onehot(place, HALF).astype(BF), cot_ref, out_ref)
-    out_ref[:, WIDE:] = hidden_rows(
-        h_ref, gate_ref, r_ref, place, jnp.where(first, eid[:HALF], eid[HALF:])
-    )
-
-
-def partner_kernel(cot_ref, h_ref, out_ref):
+    copies = spread(slot_onehot(place, HALF).astype(BF), cot_ref, scr, out_hbm, sems)
+    for c in loads:
+        c.wait()
+    rows = hidden_rows(h_ref, gate_ref, r_ref, place, jnp.where(first, eid[:HALF], eid[HALF:]))
+    finish(rows, copies, scr, out_hbm, sems)
+
+
+def partner_kernel(cot_ref, h_ref, _, out_hbm, scr, sems):
     place = cot_ref[WIDE:].astype(F32)[:HALF]
-    spread(slot_onehot(place, HALF).astype(BF), cot_ref, out_ref)
-    out_ref[:, WIDE:] = h_ref[...]
-
-
-def term_kernel(pos_ref, own_ref, par_ref, hown_ref, hpar_ref, z_ref, keep_ref, a_ref, b_ref, c_ref, scr):
-    acc = jnp.zeros((BLK, FFW), F32)
-    for ref, h in ((own_ref, hown_ref), (par_ref, hpar_ref)):
-        gate = h[:, FFW : FFW + 1].astype(F32)
-        gated = (ref[...].astype(F32) * gate).astype(BF)
-        acc = acc + lax.dot_general(gated, h[:, :FFW], TN, preferred_element_type=F32)
-    scr[...] = acc
-    for y in range(NY):
-        z_ref[0, y] = acc[y * PAD : y * PAD + PART].astype(BF)
-    for j, out_ref in enumerate((keep_ref, a_ref, b_ref, c_ref)):
-        at = pl.multiple_of(((pos_ref[1] + j) % NY) * PAD + PART, 16)
-        out_ref[0] = scr[pl.ds(at, PART)].astype(out_ref.dtype)
-
-
-def grad_term(pos, own, par):
-    cols = pl.BlockSpec((HSLOT, BLK), lambda z: (0, z))
-    hid = pl.BlockSpec((HSLOT, HW), lambda z: (0, WIDE // HW))
-    row = pl.BlockSpec((1, PART, FFW), lambda z: (z, 0, 0))
-    return pl.pallas_call(
-        term_kernel,
-        grid=(NZ,),
-        in_specs=[SMEM, cols, cols, hid, hid],
-        out_specs=[pl.BlockSpec((1, NY, PART, FFW), lambda z: (z, 0, 0, 0))] + [row] * NY,
-        out_shape=[jax.ShapeDtypeStruct((NZ, NY, PART, FFW), BF)]
-        + [jax.ShapeDtypeStruct((NZ, PART, FFW), F32)]
-        + [jax.ShapeDtypeStruct((NZ, PART, FFW), BF)] * (NY - 1),
-        scratch_shapes=[pltpu.VMEM((BLK, FFW), F32)],
-        compiler_params=pltpu.CompilerParams(vmem_limit_bytes=14 << 20),
-        name="grad_term",
-    )(pos, own, par, own, par)
-
-
-def y_sum_kernel(keep_ref, a_ref, b_ref, c_ref, *refs):
-    out_ref = refs[-1]
+    copies = spread(slot_onehot(place, HALF).astype(BF), cot_ref, scr, out_hbm, sems)
+    finish(h_ref[...], copies, scr, out_hbm, sems)
+
+
+def term_kernel(own_ref, par_ref, out_hbm, scr, sems):
+    hid = [ref[:, WIDE:] for ref in (own_ref, par_ref)]
+    gate = [h[:, FFW : FFW + 1].astype(F32) for h in hid]
+    copies = []
     for z in range(NZ):
-        v = keep_ref[z] + a_ref[z].astype(F32)
-        out_ref[z] = (v + (b_ref[z].astype(F32) + c_ref[z].astype(F32))).astype(BF)
-
-
-def z_sum_kernel(pos_ref, x_ref, keep_ref, *outs):
-    for j in range(NY):
-        y = (pos_ref[1] + j) % NY
-        v = x_ref[0, y].astype(F32)
-        for z in range(1, NZ):
-            v = v + x_ref[z, y].astype(F32)
-        if j == 0:
-            keep_ref[...] = v
-        else:
-            outs[j - 1][...] = v.astype(BF)
-
-
-def last_kernel(keep_ref, a_ref, b_ref, c_ref, x_ref, out_ref):
-    v = keep_ref[...] + a_ref[...].astype(F32)
-    out_ref[:PART] = v + (b_ref[...].astype(F32) + c_ref[...].astype(F32))
+        acc = jnp.zeros((BLK, FFW), F32)
+        for ref, h, g in zip((own_ref, par_ref), hid, gate):
+            gated = (ref[:, z * BLK : (z + 1) * BLK].astype(F32) * g).astype(BF)
+            acc = acc + lax.dot_general(gated, h[:, :FFW], TN, preferred_element_type=F32)
+        rows = pl.ds(z * BLK, BLK)
+        scr[rows] = acc.astype(BF)
+        copies.append(pltpu.make_async_copy(scr.at[rows], out_hbm.at[rows], sems.at[z]))
+        copies[-1].start()
+    for c in copies:
+        c.wait()
+
+
+def sum_kernel(x_ref, _, out_ref):
     v = x_ref[0].astype(F32)
-    for z in range(1, NZ):
-        v = v + x_ref[z].astype(F32)
-    out_ref[PART:] = v[: OWN - PART]
+    for d in range(1, NDP):
+        v = v + x_ref[d].astype(F32)
+    out_ref[...] = v[:OWN]
 
 
 def pad_kernel(w_ref, _, out_ref):
@@ -292,8 +279,19 @@
     )(pos, ht, gates, rt, pm)[0]
     hid_par = shift(hid_par, "yh", 2, 1)
     own = call(
-        own_kernel, "send_own", [SMEM] + [VMEM] * 5, [((HSLOT, WIDE + HW), BF)], weight=COVER
-    )(pos, ht, gates, rt, pm, cot)[0]
+        own_kernel,
+        "send_own",
+        [SMEM] + [ANY] * 3 + [VMEM] * 2,
+        [((HSLOT, WIDE + HW), BF)],
+        [
+            pltpu.VMEM((TOPK, FFW, ROWS), BF),
+            pltpu.VMEM((TOPK, ROWS), BF),
+            pltpu.VMEM((TOPK, ROWS), I32),
+            pltpu.SemaphoreType.DMA((3,)),
+        ]
+        + SPREAD,
+        where=ANY,
+    )(pos, *(pltpu.with_memory_space_constraint(v, pltpu.HBM) for v in (ht, gates, rt)), pm, cot)[0]
     wt = call(pad_kernel, "weight_pad", [VMEM, ANY], [((PAD, HW), BF)])(w_down[0].T, pm)[0]
     own = exchange(own.reshape(HALF, CAP, WIDE + HW), ("x", "c")).reshape(HSLOT, WIDE + HW)
 
@@ -301,16 +299,25 @@
     weight = call(weight_kernel, "weight_part", [SMEM] + [VMEM] * NY, [((NY, PAD, HW), BF)])(
         pos, *parts
     )[0].reshape(NY * PAD, HW)
-    weight = lax.all_gather(weight, "z", axis=0, tiled=True)
-
-    par = call(partner_kernel, "send_partner", [VMEM] * 2, [((HSLOT, WIDE + HW), BF)])(
-        cot_par, hid_par
+
+    par = call(partner_kernel, "send_partner", [VMEM] * 2 + [ANY], [((HSLOT, WIDE + HW), BF)], SPREAD, where=ANY)(
+        cot_par, hid_par, weight
     )[0]
     par = exchange(par.reshape(HALF, CAP, WIDE + HW), ("x", "c")).reshape(HSLOT, WIDE + HW)
 
-    zs, keep, *ys = grad_term(pos, own, par)
-    zs = exchange(zs, "z")
-    ys = [shift(y, "yl", NY, j + 1) for j, y in enumerate(ys)]
+    weight = lax.all_gather(weight, "z", axis=0, tiled=True)
+
+    terms = call(
+        term_kernel,
+        "grad_term",
+        [VMEM] * 2,
+        [((WIDE, FFW), BF)],
+        [pltpu.VMEM((WIDE, FFW), BF), pltpu.SemaphoreType.DMA((NZ,))],
+        mib=20,
+        where=ANY,
+    )(own, par)[0].reshape(NDP, PAD, FFW)
+    terms = exchange(terms, ("z", "yl"))
+
     backs = call(
         back_kernel,
         "back_product",
@@ -319,19 +326,6 @@
         [pltpu.VMEM((HSLOT, FFW), F32)],
     )(pos, own, par, weight)
     backs = [to_peer(b, r) for r, b in enumerate(backs)]
-    ys = call(
-        y_sum_kernel, "y_sum", [VMEM] * NY + [ANY] * 5, [((NZ, PART, FFW), BF)]
-    )(keep, *ys, *backs[1:6])[0]
-    ys = exchange(ys, "z")
-    keep, *zs = call(
-        z_sum_kernel,
-        "z_sum",
-        [SMEM, VMEM],
-        [((PART, FFW), F32)] + [((PART, FFW), BF)] * (NY - 1),
-    )(pos, zs)
-    zs = [shift(z, "yl", NY, j + 1) for j, z in enumerate(zs)]
-    gd = call(last_kernel, "last_sum", [VMEM] * (NY + 1), [((OWN, FFW), F32)])(keep, *zs, ys)[0]
-
     other = call(stack_kernel, "stack_other", [VMEM] * HALF, [((HALF, CAP, FFW), BF)])(*backs)[0]
     other = shift(other, "yh", 2, 1)
     gh, gg = call(
@@ -340,6 +334,7 @@
         [SMEM] + [VMEM] * (5 + HALF),
         [((TOPK, FFW, ROWS), F32), ((TOPK, ROWS), F32)],
     )(pos, ht, gates, pm, rt, other, *backs)
+    gd = call(sum_kernel, "sum_terms", [VMEM, ANY], [((OWN, FFW), F32)])(terms, gg)[0]
     return gd.T[None], jnp.transpose(gh, (2, 0, 1)), gg.T
 
 

time: 220 us -> 243 us (1.10)
  the two profiles are of different devices: /device:TPU:1 before, /device:TPU:65 now
where the time goes in v4:
time: 243 us; the launch traced here: 242 us
  starting transfers between devices  125 us (51%)
  waiting for transfers between devices  73.3 us (30%)
  Pallas kernels  24.2 us (10%)
  between operations  14.3 us (6%)
  local copies, waits for them, and re-layouts  4.89 us (2%)
    ppermute x7, starting transfers between devices, to_peer(): return lax.ppermute(x, ('x', 'c'), pairs)  71.7 us
    ppermute x6, waiting for transfers between devices, shift(): return lax.ppermute(x, axis, [(i, (i + by) % n) for i in range(n)])  42.2 us
    ppermute x6, starting transfers between devices, shift(): return lax.ppermute(x, axis, [(i, (i + by) % n) for i in range(n)])  32.1 us
    all_to_all x3, waiting for transfers between devices, exchange(): return lax.all_to_all(x, axes, split_axis=0, concat_axis=0, tiled=True)  27 us
    all_to_all x3, starting transfers between devices, exchange(): return lax.all_to_all(x, axes, split_axis=0, concat_axis=0, tiled=True)  21.4 us
    pallas_call x1, Pallas kernels, local(): call(term_kernel, 'grad_term', [VMEM] * 2, [((WIDE, FFW), BF)], [pltpu.VM...  5.76 us
  transfers between devices with their start and end apart: 17, of which 7 were waited for; matrix products, arithmetic and copies ran while one was open for 0% of the time, Pallas kernels for 8%

profile of v4, /device:TPU:65, one launch (start us, length us, event | category | flops | bytes accessed | tf_op | source)
XLA Modules:
  0.0 241.9 jit_solution(4329510125342349634)
XLA Ops:
  7.2 0.1 stack.23.pos_ref
  7.3 2.9 %prep.1 = (bf16[3088,128]{1,0:T(8,128)(2,1)}, f32[16,128]{1,0:T(8,128)S(1)}) custom-call(s32[5]{0:T(128)S(1)} %stack.23.pos_ref, s32[1,4]{1,0:T(1,128)} %len_hbm.1, f32[1,4]{1,0:T(1,128)} %adv_hbm.1, bf16[2880,128]{1,0:T(8,128)(2,1)} %bitcast.41, s32[4,128]{1,0:T(4,128)} %bitcast.30), custom_call_target="tpu_custom_call" | custom-call | tf_op jit(solution)/shard_map/prep/pallas_call | solution.py:107
  10.1 7.5 %collective-permute-start = (bf16[3088,128]{1,0:T(8,128)(2,1)}, bf16[3088,128]{1,0:T(8,128)(2,1)S(1)}, u32[]{:S(2)}, u32[]{:S(2)}) collective-permute-start(bf16[3088,128]{1,0:T(8,128)(2,1)} %get-tuple-element.16.cot_ref), channel_id=1, source_target_pairs={{0,2},{2,0},{1,3},{3,1},{4,6},{6,4},{5,7},{7,5},{8,10},{10,8},{9,1... | collective-permute-start | bytes 2371592 | tf_op jit(solution)/shard_map/ppermute | solution.py:253
  17.6 3.4 %send_own.1 = bf16[320,3456]{1,0:T(8,128)(2,1)} custom-call(s32[5]{0:T(128)S(1)} %stack.23.pos_ref, bf16[4,360,128]{2,1,0:T(8,128)(2,1)} %bitcast.25, bf16[4,128]{1,0:T(4,128)(2,1)} %bitcast.34, s32[4,128]{1,0:T(4,128)} %bitcast.31, f32[16,128]{1,0:T(8,128)S(1)} %get-tuple-element.15.pm_ref._, bf16[3088,128]{1,0:T(8,128)(2,1)} %get-tuple-element.16.cot_ref), custom_call_target="tpu_custom_call" | custom-call | tf_op jit(solution)/shard_map/send_own/pallas_call | solution.py:281
  21.0 0.0 copy-start.1
  21.0 0.0 copy-start.5
  21.1 0.0 copy-start.6
  21.1 5.4 %all-to-all-start = ((bf16[8,40,3456]{2,1,0:T(8,128)(2,1)}), bf16[8,40,3456]{2,1,0:T(8,128)(2,1)S(1)}, u32[]{:S(2)}, u32[]{:S(2)}) async-start(bf16[8,40,3456]{2,1,0:T(8,128)(2,1)} %bitcast.39), calls=%async_computation | async-start | bytes 4423680 | tf_op jit(solution)/shard_map/all_to_all | solution.py:265
  26.5 0.0 copy-done.1
  26.5 0.0 copy-done.5
  26.5 0.0 copy-done.6
  26.5 0.0 copy-start.4
  26.5 1.0 send_other.1
  27.5 1.9 collective-permute-start.1
  29.4 0.0 copy-done.4
  29.4 5.0 %collective-permute-start.4 = (bf16[96,384]{1,0:T(8,128)(2,1)S(1)}, bf16[96,384]{1,0:T(8,128)(2,1)S(1)}, u32[]{:S(2)}, u32[]{:S(2)}) collective-permute-start(bf16[96,384]{1,0:T(8,128)(2,1)S(1)} %weight_pad.1.refs_0_), channel_id=1, source_target_pairs={{0,48},{16,0},{32,16},{48,32},{1,49},{17,1},{33,17},{49,33},{2,50}... | collective-permute-start | bytes 221192 | tf_op jit(solution)/shard_map/ppermute | solution.py:253
  34.5 1.9 collective-permute-start.3
  36.4 2.4 collective-permute-start.2
  38.8 25.5 %collective-permute-done.4.refs_3_ = bf16[96,384]{1,0:T(8,128)(2,1)S(1)} collective-permute-done((bf16[96,384]{1,0:T(8,128)(2,1)S(1)}, bf16[96,384]{1,0:T(8,128)(2,1)S(1)}, u32[]{:S(2)}, u32[]{:S(2)}) %collective-permute-start.4) | collective-permute-done | bytes 73760 | tf_op jit(solution)/shard_map/ppermute | solution.py:253
  64.3 6.1 %collective-permute-done.3.refs_2_ = bf16[96,384]{1,0:T(8,128)(2,1)S(1)} collective-permute-done((bf16[96,384]{1,0:T(8,128)(2,1)S(1)}, bf16[96,384]{1,0:T(8,128)(2,1)S(1)}, u32[]{:S(2)}, u32[]{:S(2)}) %collective-permute-start.3) | collective-permute-done | bytes 73760 | tf_op jit(solution)/shard_map/ppermute | solution.py:253
  70.3 0.0 collective-permute-done.2.refs_1_
  70.4 1.3 weight_part.1
  71.6 0.0 collective-permute-done.1.h_ref
  71.6 0.0 copy-start.2
  71.6 0.7 copy-done.2
  72.3 0.0 collective-permute-done.cot_ref
  72.3 0.0 copy-start.3
  72.3 0.9 copy-done.3
  73.3 1.8 send_partner.1
  75.1 0.0 all-to-all-done
  75.1 4.8 %all-to-all-start.1 = ((bf16[8,40,3456]{2,1,0:T(8,128)(2,1)}), bf16[8,40,3456]{2,1,0:T(8,128)(2,1)}, u32[]{:S(2)}, u32[]{:S(2)}) async-start(bf16[8,40,3456]{2,1,0:T(8,128)(2,1)} %bitcast.40), calls=%async_computation.1 | async-start | bytes 4423680 | tf_op jit(solution)/shard_map/all_to_all | solution.py:265
  79.8 0.0 all-gather.2.cloned.1.call-start
  79.9 0.7 all-gather.2.cloned.1.call-update
  80.6 26.9 %all-to-all-done.1 = bf16[8,40,3456]{2,1,0:T(8,128)(2,1)} async-done(((bf16[8,40,3456]{2,1,0:T(8,128)(2,1)}), bf16[8,40,3456]{2,1,0:T(8,128)(2,1)}, u32[]{:S(2)}, u32[]{:S(2)}) %all-to-all-start.1) | async-done | bytes 2211872 | tf_op jit(solution)/shard_map/all_to_all | solution.py:265
  107.5 5.8 %grad_term.1 = bf16[3072,360]{1,0:T(8,128)(2,1)} custom-call(bf16[320,3456]{1,0:T(8,128)(2,1)S(1)} %bitcast.23, bf16[320,3456]{1,0:T(8,128)(2,1)} %bitcast.15.par_ref), custom_call_target="tpu_custom_call" | custom-call | tf_op jit(solution)/shard_map/grad_term/pallas_call | solution.py:310
  113.3 11.3 %all-to-all-start.2 = ((bf16[32,96,360]{2,1,0:T(8,128)(2,1)}), bf16[32,96,360]{2,1,0:T(8,128)(2,1)}, u32[]{:S(2)}, u32[]{:S(2)}) async-start(bf16[32,96,360]{2,1,0:T(8,128)(2,1)} %bitcast.38), calls=%async_computation.2 | async-start | bytes 4718592 | tf_op jit(solution)/shard_map/all_to_all | solution.py:265
  124.6 0.5 all-gather.2.cloned.1.call-done.w_ref
  125.0 0.0 copy-start
  125.0 1.7 copy-done
  126.7 3.9 %back_product.1 = (bf16[2,40,360]{2,1,0:T(8,128)(2,1)S(1)}, bf16[2,40,360]{2,1,0:T(8,128)(2,1)S(1)}, bf16[2,40,360]{2,1,0:T(8,128)(2,1)S(1)}, bf16[2,40,360]{2,1...) custom-call(s32[5]{0:T(128)S(1)} %stack.23.pos_ref, ...), custom_call_target="tpu_custom_call" | custom-call | tf_op jit(solution)/shard_map/back_product/pallas_call | solution.py:321
  130.6 29.8 %collective-permute-start.5 = (bf16[2,40,360]{2,1,0:T(8,128)(2,1)S(1)}, bf16[2,40,360]{2,1,0:T(8,128)(2,1)S(1)}, u32[]{:S(2)}, u32[]{:S(2)}) collective-permute-start(bf16[2,40,360]{2,1,0:T(8,128)(2,1)S(1)} %get-tuple-element.18), channel_id=1, source_target_pairs={{0,1},{1,0},{4,5},{5,4},{8,9},{9,8},{12,13},{13,12},{2,3},{3,2},{6... | collective-permute-start | bytes 172808 | tf_op jit(solution)/shard_map/ppermute | solution.py:261
  160.3 11.5 %collective-permute-start.6 = (bf16[2,40,360]{2,1,0:T(8,128)(2,1)S(1)}, bf16[2,40,360]{2,1,0:T(8,128)(2,1)S(1)}, u32[]{:S(2)}, u32[]{:S(2)}) collective-permute-start(bf16[2,40,360]{2,1,0:T(8,128)(2,1)S(1)} %get-tuple-element.19), channel_id=1, source_target_pairs={{0,4},{1,5},{4,8},{5,9},{8,12},{9,13},{12,0},{13,1},{2,6},{3,7},{6... | collective-permute-start | bytes 172808 | tf_op jit(solution)/shard_map/ppermute | solution.py:261
  171.8 18.9 %collective-permute-start.7 = (bf16[2,40,360]{2,1,0:T(8,128)(2,1)S(1)}, bf16[2,40,360]{2,1,0:T(8,128)(2,1)S(1)}, u32[]{:S(2)}, u32[]{:S(2)}) collective-permute-start(bf16[2,40,360]{2,1,0:T(8,128)(2,1)S(1)} %get-tuple-element.20), channel_id=1, source_target_pairs={{0,5},{1,4},{4,9},{5,8},{8,13},{9,12},{12,1},{13,0},{2,7},{3,6},{6... | collective-permute-start | bytes 172808 | tf_op jit(solution)/shard_map/ppermute | solution.py:261
  190.7 2.1 collective-permute-start.8
  192.8 5.1 %collective-permute-start.9 = (bf16[2,40,360]{2,1,0:T(8,128)(2,1)S(1)}, bf16[2,40,360]{2,1,0:T(8,128)(2,1)S(1)}, u32[]{:S(2)}, u32[]{:S(2)}) collective-permute-start(bf16[2,40,360]{2,1,0:T(8,128)(2,1)S(1)} %get-tuple-element.22), channel_id=1, source_target_pairs={{0,9},{1,8},{4,13},{5,12},{8,1},{9,0},{12,5},{13,4},{2,11},{3,10},... | collective-permute-start | bytes 172808 | tf_op jit(solution)/shard_map/ppermute | solution.py:261
  197.9 0.0 collective-permute-done.5.refs_1_
  197.9 1.9 collective-permute-start.10
  199.8 0.0 collective-permute-done.6.refs_2_
  199.8 2.5 %collective-permute-start.11 = (bf16[2,40,360]{2,1,0:T(8,128)(2,1)S(1)}, bf16[2,40,360]{2,1,0:T(8,128)(2,1)S(1)}, u32[]{:S(2)}, u32[]{:S(2)}) collective-permute-start(bf16[2,40,360]{2,1,0:T(8,128)(2,1)S(1)} %get-tuple-element.24), channel_id=1, source_target_pairs={{0,13},{1,12},{4,1},{5,0},{8,5},{9,4},{12,9},{13,8},{2,15},{3,14},... | collective-permute-start | bytes 172808 | tf_op jit(solution)/shard_map/ppermute | solution.py:261
  202.4 0.0 collective-permute-done.7.refs_3_
  202.4 0.0 collective-permute-done.8.refs_4_
  202.4 0.0 collective-permute-done.9.refs_5_
  202.4 1.0 collective-permute-done.10.refs_6_
  203.4 2.0 collective-permute-done.11.refs_7_
  205.5 13.4 %collective-permute-start.12 = (bf16[8,40,360]{2,1,0:T(8,128)(2,1)S(1)}, bf16[8,40,360]{2,1,0:T(8,128)(2,1)S(1)}, u32[]{:S(2)}, u32[]{:S(2)}) collective-permute-start(bf16[8,40,360]{2,1,0:T(8,128)(2,1)S(1)} %stack_other.1), channel_id=1, source_target_pairs={{0,2},{2,0},{1,3},{3,1},{4,6},{6,4},{5,7},{7,5},{8,10},{10,8},{9,1... | collective-permute-start | bytes 691208 | tf_op jit(solution)/shard_map/ppermute | solution.py:253
  218.9 10.6 %collective-permute-done.12.other_ref = bf16[8,40,360]{2,1,0:T(8,128)(2,1)S(1)} collective-permute-done((bf16[8,40,360]{2,1,0:T(8,128)(2,1)S(1)}, bf16[8,40,360]{2,1,0:T(8,128)(2,1)S(1)}, u32[]{:S(2)}, u32[]{:S(2)}) %collective-permute-start.12) | collective-permute-done | bytes 230432 | tf_op jit(solution)/shard_map/ppermute | solution.py:253
  229.4 2.2 bring_home.1
  231.6 0.0 all-to-all-done.2.x_ref
  231.6 0.0 copy-start.7
  231.6 0.7 copy-done.7
  232.3 2.0 sum_terms.1
  234.3 0.8 copy.10
  (2 shorter events, 0.0 us)
Async XLA Ops:
  10.1 62.2 %collective-permute-start = (bf16[3088,128]{1,0:T(8,128)(2,1)}, bf16[3088,128]{1,0:T(8,128)(2,1)S(1)}, u32[]{:S(2)}, u32[]{:S(2)}) collective-permute-start(bf16[3088,128]{1,0:T(8,128)(2,1)} %get-tuple-element.16.cot_ref), channel_id=1, source_target_pairs={{0,2},{2,0},{1,3},{3,1},{4,6},{6,4},{5,7},{7,5},{8,10},{10,8},{9,1... | collective-permute-start | bytes 2371592 | tf_op jit(solution)/shard_map/ppermute | solution.py:253
  21.0 5.4 %copy-start.1 = (bf16[128,4,360]{0,2,1:T(8,128)(2,1)S(1)}, bf16[128,4,360]{0,2,1:T(8,128)(2,1)}, u32[]{:S(2)}) copy-start(bf16[128,4,360]{0,2,1:T(8,128)(2,1)} %param.8) | copy-start | bytes 1105924
  21.0 5.4 %copy-start.5 = (s32[128,4]{0,1:T(4,128)S(1)}, s32[128,4]{0,1:T(4,128)}, u32[]{:S(2)}) copy-start(s32[128,4]{0,1:T(4,128)} %param.10) | copy-start | bytes 6148
  21.1 5.4 %copy-start.6 = (bf16[128,4]{0,1:T(4,128)(2,1)S(1)}, bf16[128,4]{0,1:T(4,128)(2,1)}, u32[]{:S(2)}) copy-start(bf16[128,4]{0,1:T(4,128)(2,1)} %param.9) | copy-start | bytes 3076
  21.1 54.0 %all-to-all-start = ((bf16[8,40,3456]{2,1,0:T(8,128)(2,1)}), bf16[8,40,3456]{2,1,0:T(8,128)(2,1)S(1)}, u32[]{:S(2)}, u32[]{:S(2)}) async-start(bf16[8,40,3456]{2,1,0:T(8,128)(2,1)} %bitcast.39), calls=%async_computation | async-start | bytes 4423680 | tf_op jit(solution)/shard_map/all_to_all | solution.py:265
  26.5 2.9 %copy-start.4 = (bf16[1,360,90]{1,2,0:T(8,128)(2,1)S(1)}, bf16[1,360,90]{1,2,0:T(8,128)(2,1)}, u32[]{:S(2)}) copy-start(bf16[1,360,90]{1,2,0:T(8,128)(2,1)} %param.13) | copy-start | bytes 194404
  27.5 44.2 %collective-permute-start.1 = (bf16[320,384]{1,0:T(8,128)(2,1)S(1)}, bf16[320,384]{1,0:T(8,128)(2,1)S(1)}, u32[]{:S(2)}, u32[]{:S(2)}) collective-permute-start(bf16[320,384]{1,0:T(8,128)(2,1)S(1)} %send_other.1), channel_id=1, source_target_pairs={{0,2},{2,0},{1,3},{3,1},{4,6},{6,4},{5,7},{7,5},{8,10},{10,8},{9,1... | collective-permute-start | bytes 737288 | tf_op jit(solution)/shard_map/ppermute | solution.py:253
  29.4 34.9 %collective-permute-start.4 = (bf16[96,384]{1,0:T(8,128)(2,1)S(1)}, bf16[96,384]{1,0:T(8,128)(2,1)S(1)}, u32[]{:S(2)}, u32[]{:S(2)}) collective-permute-start(bf16[96,384]{1,0:T(8,128)(2,1)S(1)} %weight_pad.1.refs_0_), channel_id=1, source_target_pairs={{0,48},{16,0},{32,16},{48,32},{1,49},{17,1},{33,17},{49,33},{2,50}... | collective-permute-start | bytes 221192 | tf_op jit(solution)/shard_map/ppermute | solution.py:253
  34.5 35.9 %collective-permute-start.3 = (bf16[96,384]{1,0:T(8,128)(2,1)S(1)}, bf16[96,384]{1,0:T(8,128)(2,1)S(1)}, u32[]{:S(2)}, u32[]{:S(2)}) collective-permute-start(bf16[96,384]{1,0:T(8,128)(2,1)S(1)} %weight_pad.1.refs_0_), channel_id=1, source_target_pairs={{0,32},{16,48},{32,0},{48,16},{1,33},{17,49},{33,1},{49,17},{2,34}... | collective-permute-start | bytes 221192 | tf_op jit(solution)/shard_map/ppermute | solution.py:253
  36.4 34.0 %collective-permute-start.2 = (bf16[96,384]{1,0:T(8,128)(2,1)S(1)}, bf16[96,384]{1,0:T(8,128)(2,1)S(1)}, u32[]{:S(2)}, u32[]{:S(2)}) collective-permute-start(bf16[96,384]{1,0:T(8,128)(2,1)S(1)} %weight_pad.1.refs_0_), channel_id=1, source_target_pairs={{0,16},{16,32},{32,48},{48,0},{1,17},{17,33},{33,49},{49,1},{2,18}... | collective-permute-start | bytes 221192 | tf_op jit(solution)/shard_map/ppermute | solution.py:253
  71.6 0.7 copy-start.2
  72.3 0.9 copy-start.3
  75.1 32.4 %all-to-all-start.1 = ((bf16[8,40,3456]{2,1,0:T(8,128)(2,1)}), bf16[8,40,3456]{2,1,0:T(8,128)(2,1)}, u32[]{:S(2)}, u32[]{:S(2)}) async-start(bf16[8,40,3456]{2,1,0:T(8,128)(2,1)} %bitcast.40), calls=%async_computation.1 | async-start | bytes 4423680 | tf_op jit(solution)/shard_map/all_to_all | solution.py:265
  79.8 45.2 %all-gather.2.cloned.1.call-start = ((), (), s32[]{:S(2)}) async-start(), calls=%async_computation.3 | async-start | bytes 2654208 | tf_op jit(solution)/shard_map/all_gather | solution.py:308
  113.3 118.3 %all-to-all-start.2 = ((bf16[32,96,360]{2,1,0:T(8,128)(2,1)}), bf16[32,96,360]{2,1,0:T(8,128)(2,1)}, u32[]{:S(2)}, u32[]{:S(2)}) async-start(bf16[32,96,360]{2,1,0:T(8,128)(2,1)} %bitcast.38), calls=%async_computation.2 | async-start | bytes 4718592 | tf_op jit(solution)/shard_map/all_to_all | solution.py:265
  125.0 1.7 copy-start
  130.6 67.3 %collective-permute-start.5 = (bf16[2,40,360]{2,1,0:T(8,128)(2,1)S(1)}, bf16[2,40,360]{2,1,0:T(8,128)(2,1)S(1)}, u32[]{:S(2)}, u32[]{:S(2)}) collective-permute-start(bf16[2,40,360]{2,1,0:T(8,128)(2,1)S(1)} %get-tuple-element.18), channel_id=1, source_target_pairs={{0,1},{1,0},{4,5},{5,4},{8,9},{9,8},{12,13},{13,12},{2,3},{3,2},{6... | collective-permute-start | bytes 172808 | tf_op jit(solution)/shard_map/ppermute | solution.py:261
  160.3 39.5 %collective-permute-start.6 = (bf16[2,40,360]{2,1,0:T(8,128)(2,1)S(1)}, bf16[2,40,360]{2,1,0:T(8,128)(2,1)S(1)}, u32[]{:S(2)}, u32[]{:S(2)}) collective-permute-start(bf16[2,40,360]{2,1,0:T(8,128)(2,1)S(1)} %get-tuple-element.19), channel_id=1, source_target_pairs={{0,4},{1,5},{4,8},{5,9},{8,12},{9,13},{12,0},{13,1},{2,6},{3,7},{6... | collective-permute-start | bytes 172808 | tf_op jit(solution)/shard_map/ppermute | solution.py:261
  171.8 30.6 %collective-permute-start.7 = (bf16[2,40,360]{2,1,0:T(8,128)(2,1)S(1)}, bf16[2,40,360]{2,1,0:T(8,128)(2,1)S(1)}, u32[]{:S(2)}, u32[]{:S(2)}) collective-permute-start(bf16[2,40,360]{2,1,0:T(8,128)(2,1)S(1)} %get-tuple-element.20), channel_id=1, source_target_pairs={{0,5},{1,4},{4,9},{5,8},{8,13},{9,12},{12,1},{13,0},{2,7},{3,6},{6... | collective-permute-start | bytes 172808 | tf_op jit(solution)/shard_map/ppermute | solution.py:261
  190.7 11.7 %collective-permute-start.8 = (bf16[2,40,360]{2,1,0:T(8,128)(2,1)S(1)}, bf16[2,40,360]{2,1,0:T(8,128)(2,1)S(1)}, u32[]{:S(2)}, u32[]{:S(2)}) collective-permute-start(bf16[2,40,360]{2,1,0:T(8,128)(2,1)S(1)} %get-tuple-element.21), channel_id=1, source_target_pairs={{0,8},{1,9},{4,12},{5,13},{8,0},{9,1},{12,4},{13,5},{2,10},{3,11},... | collective-permute-start | bytes 172808 | tf_op jit(solution)/shard_map/ppermute | solution.py:261
  192.8 9.6 %collective-permute-start.9 = (bf16[2,40,360]{2,1,0:T(8,128)(2,1)S(1)}, bf16[2,40,360]{2,1,0:T(8,128)(2,1)S(1)}, u32[]{:S(2)}, u32[]{:S(2)}) collective-permute-start(bf16[2,40,360]{2,1,0:T(8,128)(2,1)S(1)} %get-tuple-element.22), channel_id=1, source_target_pairs={{0,9},{1,8},{4,13},{5,12},{8,1},{9,0},{12,5},{13,4},{2,11},{3,10},... | collective-permute-start | bytes 172808 | tf_op jit(solution)/shard_map/ppermute | solution.py:261
  197.9 5.5 %collective-permute-start.10 = (bf16[2,40,360]{2,1,0:T(8,128)(2,1)S(1)}, bf16[2,40,360]{2,1,0:T(8,128)(2,1)S(1)}, u32[]{:S(2)}, u32[]{:S(2)}) collective-permute-start(bf16[2,40,360]{2,1,0:T(8,128)(2,1)S(1)} %get-tuple-element.23), channel_id=1, source_target_pairs={{0,12},{1,13},{4,0},{5,1},{8,4},{9,5},{12,8},{13,9},{2,14},{3,15},... | collective-permute-start | bytes 172808 | tf_op jit(solution)/shard_map/ppermute | solution.py:261
  199.8 5.6 %collective-permute-start.11 = (bf16[2,40,360]{2,1,0:T(8,128)(2,1)S(1)}, bf16[2,40,360]{2,1,0:T(8,128)(2,1)S(1)}, u32[]{:S(2)}, u32[]{:S(2)}) collective-permute-start(bf16[2,40,360]{2,1,0:T(8,128)(2,1)S(1)} %get-tuple-element.24), channel_id=1, source_target_pairs={{0,13},{1,12},{4,1},{5,0},{8,5},{9,4},{12,9},{13,8},{2,15},{3,14},... | collective-permute-start | bytes 172808 | tf_op jit(solution)/shard_map/ppermute | solution.py:261
  205.5 23.9 %collective-permute-start.12 = (bf16[8,40,360]{2,1,0:T(8,128)(2,1)S(1)}, bf16[8,40,360]{2,1,0:T(8,128)(2,1)S(1)}, u32[]{:S(2)}, u32[]{:S(2)}) collective-permute-start(bf16[8,40,360]{2,1,0:T(8,128)(2,1)S(1)} %stack_other.1), channel_id=1, source_target_pairs={{0,2},{2,0},{1,3},{3,1},{4,6},{6,4},{5,7},{7,5},{8,10},{10,8},{9,1... | collective-permute-start | bytes 691208 | tf_op jit(solution)/shard_map/ppermute | solution.py:253
  231.6 0.7 copy-start.7
Sparse Core Ops, SparseCore 0:
  83.3 41.6 all-gather.1

commit v5 on v4

--- a/solution.py
+++ b/solution.py
@@ -25,6 +25,7 @@
     pltpu.SemaphoreType.DMA((WIDE // STEP + 1,)),
 ]
 HW = 384
+NAG = 1
 COVER = 50_000_000_000
 BLK = NY * PAD
 VMEM = pl.BlockSpec(memory_space=pltpu.VMEM)
@@ -56,7 +57,7 @@
     return (place[:, None, :] == c).astype(F32).reshape(n * CAP, ROWS)
 
 
-def prep_kernel(pos_ref, len_hbm, adv_hbm, g_hbm, r_hbm, cot_ref, pm_ref, *refs):
+def prep_kernel(pos_ref, len_hbm, adv_hbm, g_hbm, r_hbm, _, cot_ref, pm_ref, *refs):
     g_ref, r_ref, len_ref, adv_ref, scr, sems = refs
     pairs = [(g_hbm, g_ref), (r_hbm, r_ref), (len_hbm, len_ref), (adv_hbm, adv_ref)]
     copies = [pltpu.make_async_copy(a, b, sems.at[i]) for i, (a, b) in enumerate(pairs)]
@@ -93,7 +94,7 @@
         cot_ref[d * PAD : (d + 1) * PAD] = jnp.where(keep, block, 0.0).astype(BF)
 
 
-def prep(pos, lens, adv, gt, rt):
+def prep(pos, lens, adv, gt, rt, first):
     outs = [((WIDE + 16, ROWS), BF), ((NEXP, ROWS), F32)]
     scratch = [
         pltpu.VMEM((D, ROWS), BF),
@@ -104,7 +105,7 @@
         pltpu.SemaphoreType.DMA((4,)),
     ]
     args = [pltpu.with_memory_space_constraint(v, pltpu.HBM) for v in (lens, adv, gt, rt)]
-    return call(prep_kernel, "prep", [SMEM] + [ANY] * 4, outs, scratch)(pos, *args)
+    return call(prep_kernel, "prep", [SMEM] + [ANY] * 5, outs, scratch)(pos, *args, first)
 
 
 def spread(s, cot_ref, scr, out_hbm, sems):
@@ -163,13 +164,14 @@
     finish(rows, copies, scr, out_hbm, sems)
 
 
-def partner_kernel(cot_ref, h_ref, _, out_hbm, scr, sems):
+def partner_kernel(cot_ref, h_ref, out_hbm, scr, sems):
     place = cot_ref[WIDE:].astype(F32)[:HALF]
     copies = spread(slot_onehot(place, HALF).astype(BF), cot_ref, scr, out_hbm, sems)
     finish(h_ref[...], copies, scr, out_hbm, sems)
 
 
-def term_kernel(own_ref, par_ref, out_hbm, scr, sems):
+def term_kernel(own_ref, par_ref, *refs):
+    out_hbm, scr, sems = refs[-3:]
     hid = [ref[:, WIDE:] for ref in (own_ref, par_ref)]
     gate = [h[:, FFW : FFW + 1].astype(F32) for h in hid]
     copies = []
@@ -193,7 +195,7 @@
     out_ref[...] = v[:OWN]
 
 
-def pad_kernel(w_ref, _, out_ref):
+def pad_kernel(w_ref, out_ref):
     out_ref[...] = jnp.zeros((PAD, HW), BF)
     out_ref[:OWN, :FFW] = w_ref[...]
 
@@ -209,9 +211,12 @@
     return ((pos_ref[3] + NX + sign * dx) % NX) * 2 + (pos_ref[4] + dc) % 2
 
 
-def back_kernel(pos_ref, own_ref, par_ref, w_ref, *refs):
-    outs, scr = refs[:HALF], refs[HALF]
-    w = w_ref[:, :FFW]
+def back_kernel(pos_ref, own_ref, par_ref, *refs):
+    ws, outs, scr = refs[:NAG], refs[NAG : NAG + HALF], refs[NAG + HALF]
+    n = BLK // NAG
+    w = jnp.concatenate(
+        [ref[z * n : (z + 1) * n, :FFW] for z in range(NZ) for ref in ws], axis=0
+    )
     for i, ref in enumerate((own_ref, par_ref)):
         scr[...] = lax.dot_general(ref[:, :WIDE], w, NN, preferred_element_type=F32)
         for r, out_ref in enumerate(outs):
@@ -272,7 +277,19 @@
     gates = gate_weights.T
     rt = routing.T
 
-    cot, pm = prep(pos, resp_lengths, advantage, gt, rt)
+    wt = call(pad_kernel, "weight_pad", [VMEM], [((PAD, HW), BF)])(w_down[0].T)[0]
+    parts = [wt] + [shift(wt, "yl", NY, j) for j in range(1, NY)]
+    w4 = call(weight_kernel, "weight_part", [SMEM] + [VMEM] * NY, [((NY, PAD, HW), BF)])(
+        pos, *parts
+    )[0].reshape(NY * PAD, HW)
+    weight = []
+    for i in range(NAG):
+        piece = w4[i * (BLK // NAG) : (i + 1) * (BLK // NAG)]
+        if weight:
+            piece, _ = lax.optimization_barrier((piece, weight[-1]))
+        weight.append(lax.all_gather(piece, "z", axis=0, tiled=True))
+
+    cot, pm = prep(pos, resp_lengths, advantage, gt, rt, w4)
     cot_par = shift(cot, "yh", 2, 1)
     hid_par = call(
         other_kernel, "send_other", [SMEM] + [VMEM] * 4, [((HSLOT, HW), BF)], weight=COVER
@@ -292,39 +309,32 @@
         + SPREAD,
         where=ANY,
     )(pos, *(pltpu.with_memory_space_constraint(v, pltpu.HBM) for v in (ht, gates, rt)), pm, cot)[0]
-    wt = call(pad_kernel, "weight_pad", [VMEM, ANY], [((PAD, HW), BF)])(w_down[0].T, pm)[0]
     own = exchange(own.reshape(HALF, CAP, WIDE + HW), ("x", "c")).reshape(HSLOT, WIDE + HW)
 
-    parts = [wt] + [shift(wt, "yl", NY, j) for j in range(1, NY)]
-    weight = call(weight_kernel, "weight_part", [SMEM] + [VMEM] * NY, [((NY, PAD, HW), BF)])(
-        pos, *parts
-    )[0].reshape(NY * PAD, HW)
-
-    par = call(partner_kernel, "send_partner", [VMEM] * 2 + [ANY], [((HSLOT, WIDE + HW), BF)], SPREAD, where=ANY)(
-        cot_par, hid_par, weight
+    par = call(partner_kernel, "send_partner", [VMEM] * 2, [((HSLOT, WIDE + HW), BF)], SPREAD, where=ANY)(
+        cot_par, hid_par
     )[0]
     par = exchange(par.reshape(HALF, CAP, WIDE + HW), ("x", "c")).reshape(HSLOT, WIDE + HW)
-
-    weight = lax.all_gather(weight, "z", axis=0, tiled=True)
 
     terms = call(
         term_kernel,
         "grad_term",
-        [VMEM] * 2,
+        [VMEM] * 2 + [ANY] * NAG,
         [((WIDE, FFW), BF)],
         [pltpu.VMEM((WIDE, FFW), BF), pltpu.SemaphoreType.DMA((NZ,))],
         mib=20,
         where=ANY,
-    )(own, par)[0].reshape(NDP, PAD, FFW)
+    )(own, par, *weight)[0].reshape(NDP, PAD, FFW)
     terms = exchange(terms, ("z", "yl"))
 
     backs = call(
         back_kernel,
         "back_product",
-        [SMEM] + [VMEM] * 3,
+        [SMEM] + [VMEM] * (2 + NAG),
         [((2, CAP, FFW), BF)] * HALF,
         [pltpu.VMEM((HSLOT, FFW), F32)],
-    )(pos, own, par, weight)
+        mib=20,
+    )(pos, own, par, *weight)
     backs = [to_peer(b, r) for r, b in enumerate(backs)]
     other = call(stack_kernel, "stack_other", [VMEM] * HALF, [((HALF, CAP, FFW), BF)])(*backs)[0]
     other = shift(other, "yh", 2, 1)

time: 243 us -> 219 us (0.901)
  the two profiles are of different devices: /device:TPU:65 before, /device:TPU:96 now
where the time goes in v5:
time: 219 us; the launch traced here: 218 us
  waiting for transfers between devices  80.1 us (37%)
  starting transfers between devices  59.9 us (27%)
  blocking collectives  33.2 us (15%)
  Pallas kernels  21 us (10%)
  between operations  14.3 us (7%)
  local copies, waits for them, and re-layouts  9.03 us (4%)
    ppermute x6, waiting for transfers between devices, shift(): return lax.ppermute(x, axis, [(i, (i + by) % n) for i in range(n)])  55 us
    all_to_all x1, blocking collectives, exchange(): return lax.all_to_all(x, axes, split_axis=0, concat_axis=0, tiled=True)  33.2 us
    ppermute x6, starting transfers between devices, shift(): return lax.ppermute(x, axis, [(i, (i + by) % n) for i in range(n)])  23.6 us
    all_to_all x2, waiting for transfers between devices, exchange(): return lax.all_to_all(x, axes, split_axis=0, concat_axis=0, tiled=True)  22.5 us
    ppermute x7, starting transfers between devices, to_peer(): return lax.ppermute(x, ('x', 'c'), pairs)  21.4 us
    all_to_all x2, starting transfers between devices, exchange(): return lax.all_to_all(x, axes, split_axis=0, concat_axis=0, tiled=True)  14.8 us
    unnamed x19, local copies, waits for them, and re-layouts  8.95 us
  transfers between devices with their start and end apart: 16, of which 6 were waited for; matrix products, arithmetic and copies ran while one was open for 0% of the time, Pallas kernels for 6%

profile of v5, /device:TPU:96, one launch (start us, length us, event | category | flops | bytes accessed | tf_op | source)
XLA Modules:
  0.0 217.5 jit_solution(18112285225988032857)
XLA Ops:
  7.2 0.0 all-gather.2.cloned.1.call-start
  7.2 0.0 copy-start.5
  7.2 0.9 copy-done.5
  8.1 2.8 %collective-permute-start.2 = (bf16[96,384]{1,0:T(8,128)(2,1)S(1)}, bf16[96,384]{1,0:T(8,128)(2,1)S(1)}, u32[]{:S(2)}, u32[]{:S(2)}) collective-permute-start(bf16[96,384]{1,0:T(8,128)(2,1)S(1)} %weight_pad.1.refs_0_), channel_id=1, source_target_pairs={{0,48},{16,0},{32,16},{48,32},{1,49},{17,1},{33,17},{49,33},{2,50}... | collective-permute-start | bytes 221192 | tf_op jit(solution)/shard_map/ppermute | solution.py:258
  10.9 3.1 %collective-permute-start.1 = (bf16[96,384]{1,0:T(8,128)(2,1)S(1)}, bf16[96,384]{1,0:T(8,128)(2,1)S(1)}, u32[]{:S(2)}, u32[]{:S(2)}) collective-permute-start(bf16[96,384]{1,0:T(8,128)(2,1)S(1)} %weight_pad.1.refs_0_), channel_id=1, source_target_pairs={{0,32},{16,48},{32,0},{48,16},{1,33},{17,49},{33,1},{49,17},{2,34}... | collective-permute-start | bytes 221192 | tf_op jit(solution)/shard_map/ppermute | solution.py:258
  14.1 2.6 %collective-permute-start = (bf16[96,384]{1,0:T(8,128)(2,1)S(1)}, bf16[96,384]{1,0:T(8,128)(2,1)S(1)}, u32[]{:S(2)}, u32[]{:S(2)}) collective-permute-start(bf16[96,384]{1,0:T(8,128)(2,1)S(1)} %weight_pad.1.refs_0_), channel_id=1, source_target_pairs={{0,16},{16,32},{32,48},{48,0},{1,17},{17,33},{33,49},{49,1},{2,18}... | collective-permute-start | bytes 221192 | tf_op jit(solution)/shard_map/ppermute | solution.py:258
  16.7 0.1 stack.23.pos_ref
  16.8 0.0 collective-permute-done.2.refs_3_
  16.8 2.3 %collective-permute-done.1.refs_2_ = bf16[96,384]{1,0:T(8,128)(2,1)S(1)} collective-permute-done((bf16[96,384]{1,0:T(8,128)(2,1)S(1)}, bf16[96,384]{1,0:T(8,128)(2,1)S(1)}, u32[]{:S(2)}, u32[]{:S(2)}) %collective-permute-start.1) | collective-permute-done | bytes 73760 | tf_op jit(solution)/shard_map/ppermute | solution.py:258
  19.0 3.1 %collective-permute-done.refs_1_ = bf16[96,384]{1,0:T(8,128)(2,1)S(1)} collective-permute-done((bf16[96,384]{1,0:T(8,128)(2,1)S(1)}, bf16[96,384]{1,0:T(8,128)(2,1)S(1)}, u32[]{:S(2)}, u32[]{:S(2)}) %collective-permute-start) | collective-permute-done | bytes 73760 | tf_op jit(solution)/shard_map/ppermute | solution.py:258
  22.1 1.3 weight_part.1
  23.4 0.0 all-gather.2.cloned.1.call-update
  23.4 1.9 prep.1
  25.4 3.5 %collective-permute-start.3 = (bf16[3088,128]{1,0:T(8,128)(2,1)S(1)}, bf16[3088,128]{1,0:T(8,128)(2,1)}, u32[]{:S(2)}, u32[]{:S(2)}) collective-permute-start(bf16[3088,128]{1,0:T(8,128)(2,1)S(1)} %get-tuple-element.16.cot_ref), channel_id=1, source_target_pairs={{0,2},{2,0},{1,3},{3,1},{4,6},{6,4},{5,7},{7,5},{8,10},{10,8},{9,1... | collective-permute-start | bytes 2371592 | tf_op jit(solution)/shard_map/ppermute | solution.py:258
  28.9 2.8 %send_own.1 = bf16[320,3456]{1,0:T(8,128)(2,1)} custom-call(s32[5]{0:T(128)S(1)} %stack.23.pos_ref, bf16[4,360,128]{2,1,0:T(8,128)(2,1)} %bitcast.27, bf16[4,128]{1,0:T(4,128)(2,1)} %bitcast.36, s32[4,128]{1,0:T(4,128)} %bitcast.33, f32[16,128]{1,0:T(8,128)S(1)} %get-tuple-element.15.pm_ref, bf16[3088,128]{1,0:T(8,128)(2,1)S(1)} %get-tuple-element.16.cot_ref), custom_call_target="tpu_custom_call" | custom-call | tf_op jit(solution)/shard_map/send_own/pallas_call | solution.py:298
  31.7 0.0 copy-start.4
  31.7 0.0 copy-start.6
  31.7 0.0 copy-start.7
  31.8 4.4 %all-to-all-start = ((bf16[8,40,3456]{2,1,0:T(8,128)(2,1)}), bf16[8,40,3456]{2,1,0:T(8,128)(2,1)S(1)}, u32[]{:S(2)}, u32[]{:S(2)}) async-start(bf16[8,40,3456]{2,1,0:T(8,128)(2,1)} %bitcast.42), calls=%async_computation | async-start | bytes 4423680 | tf_op jit(solution)/shard_map/all_to_all | solution.py:270
  36.2 0.0 copy-done.4
  36.2 0.0 copy-done.6
  36.2 0.0 copy-done.7
  36.2 1.0 send_other.1
  37.2 6.3 %collective-permute-start.4 = (bf16[320,384]{1,0:T(8,128)(2,1)S(1)}, bf16[320,384]{1,0:T(8,128)(2,1)S(1)}, u32[]{:S(2)}, u32[]{:S(2)}) collective-permute-start(bf16[320,384]{1,0:T(8,128)(2,1)S(1)} %send_other.1), channel_id=1, source_target_pairs={{0,2},{2,0},{1,3},{3,1},{4,6},{6,4},{5,7},{7,5},{8,10},{10,8},{9,1... | collective-permute-start | bytes 737288 | tf_op jit(solution)/shard_map/ppermute | solution.py:258
  43.5 32.7 %collective-permute-done.4.h_ref = bf16[320,384]{1,0:T(8,128)(2,1)S(1)} collective-permute-done((bf16[320,384]{1,0:T(8,128)(2,1)S(1)}, bf16[320,384]{1,0:T(8,128)(2,1)S(1)}, u32[]{:S(2)}, u32[]{:S(2)}) %collective-permute-start.4) | collective-permute-done | bytes 245792 | tf_op jit(solution)/shard_map/ppermute | solution.py:258
  76.2 0.0 collective-permute-done.3.cot_ref
  76.2 2.9 %send_partner.1 = bf16[320,3456]{1,0:T(8,128)(2,1)} custom-call(bf16[3088,128]{1,0:T(8,128)(2,1)} %collective-permute-done.3.cot_ref, bf16[320,384]{1,0:T(8,128)(2,1)S(1)} %collective-permute-done.4.h_ref), custom_call_target="tpu_custom_call" | custom-call | tf_op jit(solution)/shard_map/send_partner/pallas_call | solution.py:314
  79.0 0.0 all-to-all-done
  79.0 33.2 %all_to_all.15 = bf16[8,40,3456]{2,1,0:T(8,128)(2,1)} all-to-all(bf16[8,40,3456]{2,1,0:T(8,128)(2,1)} %bitcast.41), channel_id=1, replica_groups=mesh['z'=8,'yl'=4,'x'=4,'yh'=2,'c'=2] {'x','c'}, dimensions={0} | all-to-all | bytes 4423680 | tf_op jit(solution)/shard_map/all_to_all | solution.py:270
  112.2 0.0 all-gather.2.cloned.1.call-done.refs_0_
  112.2 0.0 copy-start
  112.2 1.6 copy-done
  113.8 0.0 copy-start.2
  113.8 1.7 copy-done.2
  115.5 4.1 %grad_term.1 = bf16[3072,360]{1,0:T(8,128)(2,1)} custom-call(bf16[320,3456]{1,0:T(8,128)(2,1)S(1)} %bitcast.23, bf16[320,3456]{1,0:T(8,128)(2,1)S(1)} %bitcast.25, bf16[3072,384]{1,0:T(8,128)(2,1)S(1)} %copy-done.2), custom_call_target="tpu_custom_call" | custom-call | tf_op jit(solution)/shard_map/grad_term/pallas_call | solution.py:319
  119.6 10.3 %all-to-all-start.2 = ((bf16[32,96,360]{2,1,0:T(8,128)(2,1)}), bf16[32,96,360]{2,1,0:T(8,128)(2,1)}, u32[]{:S(2)}, u32[]{:S(2)}) async-start(bf16[32,96,360]{2,1,0:T(8,128)(2,1)} %bitcast.40), calls=%async_computation.2 | async-start | bytes 4718592 | tf_op jit(solution)/shard_map/all_to_all | solution.py:270
  130.0 0.0 copy-start.1
  130.0 1.6 copy-done.1
  131.6 0.0 copy-start.3
  131.6 1.7 copy-done.3
  133.3 2.8 %back_product.1 = (bf16[2,40,360]{2,1,0:T(8,128)(2,1)S(1)}, bf16[2,40,360]{2,1,0:T(8,128)(2,1)S(1)}, bf16[2,40,360]{2,1,0:T(8,128)(2,1)S(1)}, bf16[2,40,360]{2,1...) custom-call(s32[5]{0:T(128)S(1)} %stack.23.pos_ref, ...), custom_call_target="tpu_custom_call" | custom-call | tf_op jit(solution)/shard_map/back_product/pallas_call | solution.py:330
  136.0 1.9 collective-permute-start.5
  138.0 2.5 %collective-permute-start.6 = (bf16[2,40,360]{2,1,0:T(8,128)(2,1)S(1)}, bf16[2,40,360]{2,1,0:T(8,128)(2,1)S(1)}, u32[]{:S(2)}, u32[]{:S(2)}) collective-permute-start(bf16[2,40,360]{2,1,0:T(8,128)(2,1)S(1)} %get-tuple-element.19), channel_id=1, source_target_pairs={{0,4},{1,5},{4,8},{5,9},{8,12},{9,13},{12,0},{13,1},{2,6},{3,7},{6... | collective-permute-start | bytes 172808 | tf_op jit(solution)/shard_map/ppermute | solution.py:266
  140.4 2.0 collective-permute-start.7
  142.5 5.7 %collective-permute-start.8 = (bf16[2,40,360]{2,1,0:T(8,128)(2,1)S(1)}, bf16[2,40,360]{2,1,0:T(8,128)(2,1)S(1)}, u32[]{:S(2)}, u32[]{:S(2)}) collective-permute-start(bf16[2,40,360]{2,1,0:T(8,128)(2,1)S(1)} %get-tuple-element.21), channel_id=1, source_target_pairs={{0,8},{1,9},{4,12},{5,13},{8,0},{9,1},{12,4},{13,5},{2,10},{3,11},... | collective-permute-start | bytes 172808 | tf_op jit(solution)/shard_map/ppermute | solution.py:266
  148.2 1.9 collective-permute-start.9
  150.2 0.0 collective-permute-done.5.refs_1_
  150.2 4.2 %collective-permute-start.10 = (bf16[2,40,360]{2,1,0:T(8,128)(2,1)S(1)}, bf16[2,40,360]{2,1,0:T(8,128)(2,1)S(1)}, u32[]{:S(2)}, u32[]{:S(2)}) collective-permute-start(bf16[2,40,360]{2,1,0:T(8,128)(2,1)S(1)} %get-tuple-element.23), channel_id=1, source_target_pairs={{0,12},{1,13},{4,0},{5,1},{8,4},{9,5},{12,8},{13,9},{2,14},{3,15},... | collective-permute-start | bytes 172808 | tf_op jit(solution)/shard_map/ppermute | solution.py:266
  154.3 0.0 collective-permute-done.6.refs_2_
  154.3 3.2 %collective-permute-start.11 = (bf16[2,40,360]{2,1,0:T(8,128)(2,1)S(1)}, bf16[2,40,360]{2,1,0:T(8,128)(2,1)S(1)}, u32[]{:S(2)}, u32[]{:S(2)}) collective-permute-start(bf16[2,40,360]{2,1,0:T(8,128)(2,1)S(1)} %get-tuple-element.24), channel_id=1, source_target_pairs={{0,13},{1,12},{4,1},{5,0},{8,5},{9,4},{12,9},{13,8},{2,15},{3,14},... | collective-permute-start | bytes 172808 | tf_op jit(solution)/shard_map/ppermute | solution.py:266
  157.5 0.0 collective-permute-done.7.refs_3_
  157.5 0.0 collective-permute-done.8.refs_4_
  157.5 0.0 collective-permute-done.9.refs_5_
  157.6 0.0 collective-permute-done.10.refs_6_
  157.6 2.6 %collective-permute-done.11.refs_7_ = bf16[2,40,360]{2,1,0:T(8,128)(2,1)S(1)} collective-permute-done((bf16[2,40,360]{2,1,0:T(8,128)(2,1)S(1)}, bf16[2,40,360]{2,1,0:T(8,128)(2,1)S(1)}, u32[]{:S(2)}, u32[]{:S(2)}) %collective-permute-start.11) | collective-permute-done | bytes 57632 | tf_op jit(solution)/shard_map/ppermute | solution.py:266
  160.2 5.3 %collective-permute-start.12 = (bf16[8,40,360]{2,1,0:T(8,128)(2,1)S(1)}, bf16[8,40,360]{2,1,0:T(8,128)(2,1)S(1)}, u32[]{:S(2)}, u32[]{:S(2)}) collective-permute-start(bf16[8,40,360]{2,1,0:T(8,128)(2,1)S(1)} %stack_other.1), channel_id=1, source_target_pairs={{0,2},{2,0},{1,3},{3,1},{4,6},{6,4},{5,7},{7,5},{8,10},{10,8},{9,1... | collective-permute-start | bytes 691208 | tf_op jit(solution)/shard_map/ppermute | solution.py:258
  165.6 16.9 %collective-permute-done.12.other_ref = bf16[8,40,360]{2,1,0:T(8,128)(2,1)S(1)} collective-permute-done((bf16[8,40,360]{2,1,0:T(8,128)(2,1)S(1)}, bf16[8,40,360]{2,1,0:T(8,128)(2,1)S(1)}, u32[]{:S(2)}, u32[]{:S(2)}) %collective-permute-start.12) | collective-permute-done | bytes 230432 | tf_op jit(solution)/shard_map/ppermute | solution.py:258
  182.5 2.2 %bring_home.1 = (f32[4,360,128]{2,1,0:T(8,128)}, f32[4,128]{1,0:T(4,128)}) custom-call(s32[5]{0:T(128)S(1)} %stack.23.pos_ref, bf16[4,360,128]{2,1,0:T(8,128)(2,1)S(1)} %bitcast.29, bf16[4,128]{1,0:T(4,128)(2,1)S(1)} %bitcast.38, f32[16,128]{1,0:T(8,128)S(1)} %get-tuple-element.15.pm_ref, s32[4,128]{1,0:T(4,128)S(1)} %bitcast.35, ...), custom_call_target="tpu_custom_call" | custom-call | tf_op jit(solution)/shard_map/bring_home/pallas_call | solution.py:341
  184.8 22.5 %all-to-all-done.2.x_ref = bf16[32,96,360]{2,1,0:T(8,128)(2,1)} async-done(((bf16[32,96,360]{2,1,0:T(8,128)(2,1)}), bf16[32,96,360]{2,1,0:T(8,128)(2,1)}, u32[]{:S(2)}, u32[]{:S(2)}) %all-to-all-start.2) | async-done | bytes 2211872 | tf_op jit(solution)/shard_map/all_to_all | solution.py:270
  207.2 0.0 copy-start.8
  207.2 0.7 copy-done.8
  207.9 2.0 sum_terms.1
  209.9 0.8 copy.10
  (2 shorter events, 0.0 us)
Async XLA Ops:
  7.2 105.0 %all-gather.2.cloned.1.call-start = ((), (), s32[]{:S(2)}) async-start(), calls=%async_computation.3 | async-start | bytes 2654208 | tf_op jit(solution)/shard_map/all_gather | solution.py:290
  7.2 0.9 copy-start.5
  8.1 8.7 %collective-permute-start.2 = (bf16[96,384]{1,0:T(8,128)(2,1)S(1)}, bf16[96,384]{1,0:T(8,128)(2,1)S(1)}, u32[]{:S(2)}, u32[]{:S(2)}) collective-permute-start(bf16[96,384]{1,0:T(8,128)(2,1)S(1)} %weight_pad.1.refs_0_), channel_id=1, source_target_pairs={{0,48},{16,0},{32,16},{48,32},{1,49},{17,1},{33,17},{49,33},{2,50}... | collective-permute-start | bytes 221192 | tf_op jit(solution)/shard_map/ppermute | solution.py:258
  10.9 8.1 %collective-permute-start.1 = (bf16[96,384]{1,0:T(8,128)(2,1)S(1)}, bf16[96,384]{1,0:T(8,128)(2,1)S(1)}, u32[]{:S(2)}, u32[]{:S(2)}) collective-permute-start(bf16[96,384]{1,0:T(8,128)(2,1)S(1)} %weight_pad.1.refs_0_), channel_id=1, source_target_pairs={{0,32},{16,48},{32,0},{48,16},{1,33},{17,49},{33,1},{49,17},{2,34}... | collective-permute-start | bytes 221192 | tf_op jit(solution)/shard_map/ppermute | solution.py:258
  14.1 8.0 %collective-permute-start = (bf16[96,384]{1,0:T(8,128)(2,1)S(1)}, bf16[96,384]{1,0:T(8,128)(2,1)S(1)}, u32[]{:S(2)}, u32[]{:S(2)}) collective-permute-start(bf16[96,384]{1,0:T(8,128)(2,1)S(1)} %weight_pad.1.refs_0_), channel_id=1, source_target_pairs={{0,16},{16,32},{32,48},{48,0},{1,17},{17,33},{33,49},{49,1},{2,18}... | collective-permute-start | bytes 221192 | tf_op jit(solution)/shard_map/ppermute | solution.py:258
  25.4 50.8 %collective-permute-start.3 = (bf16[3088,128]{1,0:T(8,128)(2,1)S(1)}, bf16[3088,128]{1,0:T(8,128)(2,1)}, u32[]{:S(2)}, u32[]{:S(2)}) collective-permute-start(bf16[3088,128]{1,0:T(8,128)(2,1)S(1)} %get-tuple-element.16.cot_ref), channel_id=1, source_target_pairs={{0,2},{2,0},{1,3},{3,1},{4,6},{6,4},{5,7},{7,5},{8,10},{10,8},{9,1... | collective-permute-start | bytes 2371592 | tf_op jit(solution)/shard_map/ppermute | solution.py:258
  31.7 4.5 %copy-start.4 = (bf16[128,4,360]{0,2,1:T(8,128)(2,1)S(1)}, bf16[128,4,360]{0,2,1:T(8,128)(2,1)}, u32[]{:S(2)}) copy-start(bf16[128,4,360]{0,2,1:T(8,128)(2,1)} %param.8) | copy-start | bytes 1105924
  31.7 4.5 %copy-start.6 = (s32[128,4]{0,1:T(4,128)S(1)}, s32[128,4]{0,1:T(4,128)}, u32[]{:S(2)}) copy-start(s32[128,4]{0,1:T(4,128)} %param.10) | copy-start | bytes 6148
  31.7 4.5 %copy-start.7 = (bf16[128,4]{0,1:T(4,128)(2,1)S(1)}, bf16[128,4]{0,1:T(4,128)(2,1)}, u32[]{:S(2)}) copy-start(bf16[128,4]{0,1:T(4,128)(2,1)} %param.9) | copy-start | bytes 3076
  31.8 47.3 %all-to-all-start = ((bf16[8,40,3456]{2,1,0:T(8,128)(2,1)}), bf16[8,40,3456]{2,1,0:T(8,128)(2,1)S(1)}, u32[]{:S(2)}, u32[]{:S(2)}) async-start(bf16[8,40,3456]{2,1,0:T(8,128)(2,1)} %bitcast.42), calls=%async_computation | async-start | bytes 4423680 | tf_op jit(solution)/shard_map/all_to_all | solution.py:270
  37.2 39.0 %collective-permute-start.4 = (bf16[320,384]{1,0:T(8,128)(2,1)S(1)}, bf16[320,384]{1,0:T(8,128)(2,1)S(1)}, u32[]{:S(2)}, u32[]{:S(2)}) collective-permute-start(bf16[320,384]{1,0:T(8,128)(2,1)S(1)} %send_other.1), channel_id=1, source_target_pairs={{0,2},{2,0},{1,3},{3,1},{4,6},{6,4},{5,7},{7,5},{8,10},{10,8},{9,1... | collective-permute-start | bytes 737288 | tf_op jit(solution)/shard_map/ppermute | solution.py:258
  112.2 1.6 copy-start
  113.8 1.7 copy-start.2
  119.6 87.6 %all-to-all-start.2 = ((bf16[32,96,360]{2,1,0:T(8,128)(2,1)}), bf16[32,96,360]{2,1,0:T(8,128)(2,1)}, u32[]{:S(2)}, u32[]{:S(2)}) async-start(bf16[32,96,360]{2,1,0:T(8,128)(2,1)} %bitcast.40), calls=%async_computation.2 | async-start | bytes 4718592 | tf_op jit(solution)/shard_map/all_to_all | solution.py:270
  130.0 1.6 copy-start.1
  131.6 1.7 copy-start.3
  136.0 14.1 %collective-permute-start.5 = (bf16[2,40,360]{2,1,0:T(8,128)(2,1)S(1)}, bf16[2,40,360]{2,1,0:T(8,128)(2,1)S(1)}, u32[]{:S(2)}, u32[]{:S(2)}) collective-permute-start(bf16[2,40,360]{2,1,0:T(8,128)(2,1)S(1)} %get-tuple-element.18), channel_id=1, source_target_pairs={{0,1},{1,0},{4,5},{5,4},{8,9},{9,8},{12,13},{13,12},{2,3},{3,2},{6... | collective-permute-start | bytes 172808 | tf_op jit(solution)/shard_map/ppermute | solution.py:266
  138.0 16.4 %collective-permute-start.6 = (bf16[2,40,360]{2,1,0:T(8,128)(2,1)S(1)}, bf16[2,40,360]{2,1,0:T(8,128)(2,1)S(1)}, u32[]{:S(2)}, u32[]{:S(2)}) collective-permute-start(bf16[2,40,360]{2,1,0:T(8,128)(2,1)S(1)} %get-tuple-element.19), channel_id=1, source_target_pairs={{0,4},{1,5},{4,8},{5,9},{8,12},{9,13},{12,0},{13,1},{2,6},{3,7},{6... | collective-permute-start | bytes 172808 | tf_op jit(solution)/shard_map/ppermute | solution.py:266
  140.4 17.1 %collective-permute-start.7 = (bf16[2,40,360]{2,1,0:T(8,128)(2,1)S(1)}, bf16[2,40,360]{2,1,0:T(8,128)(2,1)S(1)}, u32[]{:S(2)}, u32[]{:S(2)}) collective-permute-start(bf16[2,40,360]{2,1,0:T(8,128)(2,1)S(1)} %get-tuple-element.20), channel_id=1, source_target_pairs={{0,5},{1,4},{4,9},{5,8},{8,13},{9,12},{12,1},{13,0},{2,7},{3,6},{6... | collective-permute-start | bytes 172808 | tf_op jit(solution)/shard_map/ppermute | solution.py:266
  142.5 15.1 %collective-permute-start.8 = (bf16[2,40,360]{2,1,0:T(8,128)(2,1)S(1)}, bf16[2,40,360]{2,1,0:T(8,128)(2,1)S(1)}, u32[]{:S(2)}, u32[]{:S(2)}) collective-permute-start(bf16[2,40,360]{2,1,0:T(8,128)(2,1)S(1)} %get-tuple-element.21), channel_id=1, source_target_pairs={{0,8},{1,9},{4,12},{5,13},{8,0},{9,1},{12,4},{13,5},{2,10},{3,11},... | collective-permute-start | bytes 172808 | tf_op jit(solution)/shard_map/ppermute | solution.py:266
  148.2 9.3 %collective-permute-start.9 = (bf16[2,40,360]{2,1,0:T(8,128)(2,1)S(1)}, bf16[2,40,360]{2,1,0:T(8,128)(2,1)S(1)}, u32[]{:S(2)}, u32[]{:S(2)}) collective-permute-start(bf16[2,40,360]{2,1,0:T(8,128)(2,1)S(1)} %get-tuple-element.22), channel_id=1, source_target_pairs={{0,9},{1,8},{4,13},{5,12},{8,1},{9,0},{12,5},{13,4},{2,11},{3,10},... | collective-permute-start | bytes 172808 | tf_op jit(solution)/shard_map/ppermute | solution.py:266
  150.2 7.4 %collective-permute-start.10 = (bf16[2,40,360]{2,1,0:T(8,128)(2,1)S(1)}, bf16[2,40,360]{2,1,0:T(8,128)(2,1)S(1)}, u32[]{:S(2)}, u32[]{:S(2)}) collective-permute-start(bf16[2,40,360]{2,1,0:T(8,128)(2,1)S(1)} %get-tuple-element.23), channel_id=1, source_target_pairs={{0,12},{1,13},{4,0},{5,1},{8,4},{9,5},{12,8},{13,9},{2,14},{3,15},... | collective-permute-start | bytes 172808 | tf_op jit(solution)/shard_map/ppermute | solution.py:266
  154.3 5.9 %collective-permute-start.11 = (bf16[2,40,360]{2,1,0:T(8,128)(2,1)S(1)}, bf16[2,40,360]{2,1,0:T(8,128)(2,1)S(1)}, u32[]{:S(2)}, u32[]{:S(2)}) collective-permute-start(bf16[2,40,360]{2,1,0:T(8,128)(2,1)S(1)} %get-tuple-element.24), channel_id=1, source_target_pairs={{0,13},{1,12},{4,1},{5,0},{8,5},{9,4},{12,9},{13,8},{2,15},{3,14},... | collective-permute-start | bytes 172808 | tf_op jit(solution)/shard_map/ppermute | solution.py:266
  160.2 22.3 %collective-permute-start.12 = (bf16[8,40,360]{2,1,0:T(8,128)(2,1)S(1)}, bf16[8,40,360]{2,1,0:T(8,128)(2,1)S(1)}, u32[]{:S(2)}, u32[]{:S(2)}) collective-permute-start(bf16[8,40,360]{2,1,0:T(8,128)(2,1)S(1)} %stack_other.1), channel_id=1, source_target_pairs={{0,2},{2,0},{1,3},{3,1},{4,6},{6,4},{5,7},{7,5},{8,10},{10,8},{9,1... | collective-permute-start | bytes 691208 | tf_op jit(solution)/shard_map/ppermute | solution.py:258
  207.2 0.7 copy-start.8
Sparse Core Ops, SparseCore 0:
  23.6 47.7 all-gather.1

commit v6 on v4

--- a/solution.py
+++ b/solution.py
@@ -20,13 +20,14 @@
 HALF = NEXP // 2
 HSLOT = HALF * CAP
 STEP = 768
-SPREAD = [
-    pltpu.VMEM((HALF * CAP, WIDE + 384), BF),
-    pltpu.SemaphoreType.DMA((WIDE // STEP + 1,)),
-]
 HW = 384
 COVER = 50_000_000_000
 BLK = NY * PAD
+CW = WIDE // 2
+def spread_scratch(width):
+    return [pltpu.VMEM((HSLOT, width), BF), pltpu.SemaphoreType.DMA((WIDE // STEP + 1,))]
+
+
 VMEM = pl.BlockSpec(memory_space=pltpu.VMEM)
 SMEM = pl.BlockSpec(memory_space=pltpu.SMEM)
 ANY = pl.BlockSpec(memory_space=pltpu.HBM)
@@ -56,7 +57,7 @@
     return (place[:, None, :] == c).astype(F32).reshape(n * CAP, ROWS)
 
 
-def prep_kernel(pos_ref, len_hbm, adv_hbm, g_hbm, r_hbm, cot_ref, pm_ref, *refs):
+def prep_kernel(pos_ref, len_hbm, adv_hbm, g_hbm, r_hbm, low_ref, high_ref, pm_ref, *refs):
     g_ref, r_ref, len_ref, adv_ref, scr, sems = refs
     pairs = [(g_hbm, g_ref), (r_hbm, r_ref), (len_hbm, len_ref), (adv_hbm, adv_ref)]
     copies = [pltpu.make_async_copy(a, b, sems.at[i]) for i, (a, b) in enumerate(pairs)]
@@ -75,7 +76,7 @@
     place = jnp.where(hit, rank, -1.0)
     pm_ref[...] = place
     other = jnp.where(pos_ref[2] == 0, place[HALF:], place[:HALF])
-    cot_ref[WIDE:] = jnp.concatenate([other, jnp.zeros((HALF, ROWS), F32)], axis=0).astype(BF)
+    low_ref[CW:] = jnp.concatenate([other, jnp.zeros((HALF, ROWS), F32)], axis=0).astype(BF)
     pos = lax.broadcasted_iota(I32, (8, ROWS), 1)
     start = jnp.int32(0)
     scale = jnp.zeros((8, ROWS), F32)
@@ -90,11 +91,12 @@
     keep = lax.broadcasted_iota(I32, (PAD, ROWS), 0) < OWN
     for d in range(NDP):
         block = scr[d * OWN : d * OWN + PAD]
-        cot_ref[d * PAD : (d + 1) * PAD] = jnp.where(keep, block, 0.0).astype(BF)
+        cot_ref, at = (low_ref, d * PAD) if d < NDP // 2 else (high_ref, d * PAD - CW)
+        cot_ref[at : at + PAD] = jnp.where(keep, block, 0.0).astype(BF)
 
 
 def prep(pos, lens, adv, gt, rt):
-    outs = [((WIDE + 16, ROWS), BF), ((NEXP, ROWS), F32)]
+    outs = [((CW + 16, ROWS), BF), ((CW, ROWS), BF), ((NEXP, ROWS), F32)]
     scratch = [
         pltpu.VMEM((D, ROWS), BF),
         pltpu.VMEM((TOPK, ROWS), I32),
@@ -107,25 +109,22 @@
     return call(prep_kernel, "prep", [SMEM] + [ANY] * 4, outs, scratch)(pos, *args)
 
 
-def spread(s, cot_ref, scr, out_hbm, sems):
+def send(copies, scr, out_hbm, at, n, sems):
+    cols = pl.ds(at, n)
+    copies.append(pltpu.make_async_copy(scr.at[:, cols], out_hbm.at[:, cols], sems.at[len(copies)]))
+    copies[-1].start()
+
+
+def spread(s, cots, scr, out_hbm, sems):
     copies = []
-    for n, i in enumerate(range(0, WIDE, STEP)):
-        cols = pl.ds(i, STEP)
-        scr[:, cols] = lax.dot_general(
-            s, cot_ref[i : i + STEP], NT, preferred_element_type=F32
-        ).astype(BF)
-        copies.append(pltpu.make_async_copy(scr.at[:, cols], out_hbm.at[:, cols], sems.at[n]))
-        copies[-1].start()
+    for n, cot_ref in enumerate(cots):
+        for i in range(0, CW, STEP):
+            at = n * CW + i
+            scr[:, at : at + STEP] = lax.dot_general(
+                s, cot_ref[i : i + STEP], NT, preferred_element_type=F32
+            ).astype(BF)
+            send(copies, scr, out_hbm, at, STEP, sems)
     return copies
-
-
-def finish(rows, copies, scr, out_hbm, sems):
-    cols = pl.ds(WIDE, HW)
-    scr[:, cols] = rows
-    copies.append(pltpu.make_async_copy(scr.at[:, cols], out_hbm.at[:, cols], sems.at[WIDE // STEP]))
-    copies[-1].start()
-    for c in copies:
-        c.wait()
 
 
 def hidden_rows(h_ref, gate_ref, r_ref, place, eid):
@@ -140,14 +139,14 @@
     return acc.astype(BF)
 
 
-def other_kernel(pos_ref, h_ref, gate_ref, r_ref, pm_ref, out_ref):
+def other_kernel(pos_ref, h_ref, gate_ref, r_ref, pm_ref, _, out_ref):
     first = pos_ref[2] == 0
     eid = expert_ids()
     place = jnp.where(first, pm_ref[HALF:], pm_ref[:HALF])
     out_ref[...] = hidden_rows(h_ref, gate_ref, r_ref, place, jnp.where(first, eid[HALF:], eid[:HALF]))
 
 
-def own_kernel(pos_ref, h_hbm, gate_hbm, r_hbm, pm_ref, cot_ref, out_hbm, *refs):
+def own_kernel(pos_ref, h_hbm, gate_hbm, r_hbm, pm_ref, low_ref, high_ref, out_hbm, *refs):
     h_ref, gate_ref, r_ref, sem_in, scr, sems = refs
     pairs = [(h_hbm, h_ref), (gate_hbm, gate_ref), (r_hbm, r_ref)]
     loads = [pltpu.make_async_copy(a, b, sem_in.at[i]) for i, (a, b) in enumerate(pairs)]
@@ -156,29 +155,45 @@
     first = pos_ref[2] == 0
     eid = expert_ids()
     place = jnp.where(first, pm_ref[:HALF], pm_ref[HALF:])
-    copies = spread(slot_onehot(place, HALF).astype(BF), cot_ref, scr, out_hbm, sems)
+    copies = spread(slot_onehot(place, HALF).astype(BF), (low_ref, high_ref), scr, out_hbm, sems)
     for c in loads:
         c.wait()
-    rows = hidden_rows(h_ref, gate_ref, r_ref, place, jnp.where(first, eid[:HALF], eid[HALF:]))
-    finish(rows, copies, scr, out_hbm, sems)
-
-
-def partner_kernel(cot_ref, h_ref, _, out_hbm, scr, sems):
-    place = cot_ref[WIDE:].astype(F32)[:HALF]
-    copies = spread(slot_onehot(place, HALF).astype(BF), cot_ref, scr, out_hbm, sems)
-    finish(h_ref[...], copies, scr, out_hbm, sems)
-
-
-def term_kernel(own_ref, par_ref, out_hbm, scr, sems):
-    hid = [ref[:, WIDE:] for ref in (own_ref, par_ref)]
+    scr[:, WIDE:] = hidden_rows(
+        h_ref, gate_ref, r_ref, place, jnp.where(first, eid[:HALF], eid[HALF:])
+    )
+    send(copies, scr, out_hbm, WIDE, HW, sems)
+    for c in copies:
+        c.wait()
+
+
+def low_kernel(cot_ref, h_ref, out_hbm, scr, sems):
+    place = cot_ref[CW:].astype(F32)[:HALF]
+    copies = spread(slot_onehot(place, HALF).astype(BF), (cot_ref,), scr, out_hbm, sems)
+    scr[:, CW:] = h_ref[...]
+    send(copies, scr, out_hbm, CW, HW, sems)
+    for c in copies:
+        c.wait()
+
+
+def high_kernel(cot_ref, pm_ref, out_hbm, scr, sems):
+    place = pm_ref[CW:].astype(F32)[:HALF]
+    for c in spread(slot_onehot(place, HALF).astype(BF), (cot_ref,), scr, out_hbm, sems):
+        c.wait()
+
+
+def term_kernel(own_ref, low_ref, high_ref, _, out_hbm, scr, sems):
+    hid = [own_ref[:, WIDE:], low_ref[:, CW:]]
     gate = [h[:, FFW : FFW + 1].astype(F32) for h in hid]
     copies = []
     for z in range(NZ):
         acc = jnp.zeros((BLK, FFW), F32)
-        for ref, h, g in zip((own_ref, par_ref), hid, gate):
-            gated = (ref[:, z * BLK : (z + 1) * BLK].astype(F32) * g).astype(BF)
+        at = z * BLK
+        cots = [own_ref[:, at : at + BLK]]
+        cots.append(low_ref[:, at : at + BLK] if at < CW else high_ref[:, at - CW : at - CW + BLK])
+        for cot, h, g in zip(cots, hid, gate):
+            gated = (cot.astype(F32) * g).astype(BF)
             acc = acc + lax.dot_general(gated, h[:, :FFW], TN, preferred_element_type=F32)
-        rows = pl.ds(z * BLK, BLK)
+        rows = pl.ds(at, BLK)
         scr[rows] = acc.astype(BF)
         copies.append(pltpu.make_async_copy(scr.at[rows], out_hbm.at[rows], sems.at[z]))
         copies[-1].start()
@@ -193,15 +208,19 @@
     out_ref[...] = v[:OWN]
 
 
-def pad_kernel(w_ref, _, out_ref):
+def pad_kernel(w_ref, out_ref):
     out_ref[...] = jnp.zeros((PAD, HW), BF)
     out_ref[:OWN, :FFW] = w_ref[...]
 
 
-def weight_kernel(pos_ref, *refs):
-    out_ref = refs[NY]
-    for j in range(NY):
-        out_ref[(pos_ref[1] + NY - j) % NY] = refs[j][...]
+def merge_kernel(bit):
+    def body(pos_ref, mine_ref, other_ref, out_ref):
+        i = (pos_ref[1] >> bit) & 1
+        n = mine_ref.shape[0]
+        out_ref[pl.ds(pl.multiple_of(i * n, n), n)] = mine_ref[...]
+        out_ref[pl.ds(pl.multiple_of((1 - i) * n, n), n)] = other_ref[...]
+
+    return body
 
 
 def peer(pos_ref, r, sign):
@@ -209,11 +228,14 @@
     return ((pos_ref[3] + NX + sign * dx) % NX) * 2 + (pos_ref[4] + dc) % 2
 
 
-def back_kernel(pos_ref, own_ref, par_ref, w_ref, *refs):
+def back_kernel(pos_ref, own_ref, low_ref, high_ref, w_ref, *refs):
     outs, scr = refs[:HALF], refs[HALF]
-    w = w_ref[:, :FFW]
-    for i, ref in enumerate((own_ref, par_ref)):
-        scr[...] = lax.dot_general(ref[:, :WIDE], w, NN, preferred_element_type=F32)
+    for i in range(2):
+        parts = (own_ref[:, :CW], own_ref[:, CW:WIDE]) if i == 0 else (low_ref[:, :CW], high_ref[...])
+        acc = lax.dot_general(parts[0], w_ref[:CW, :FFW], NN, preferred_element_type=F32)
+        scr[...] = acc + lax.dot_general(
+            parts[1], w_ref[CW:, :FFW], NN, preferred_element_type=F32
+        )
         for r, out_ref in enumerate(outs):
             at = pl.multiple_of(peer(pos_ref, r, 1) * CAP, 8)
             out_ref[i] = scr[pl.ds(at, CAP)].astype(BF)
@@ -272,16 +294,23 @@
     gates = gate_weights.T
     rt = routing.T
 
-    cot, pm = prep(pos, resp_lengths, advantage, gt, rt)
-    cot_par = shift(cot, "yh", 2, 1)
-    hid_par = call(
-        other_kernel, "send_other", [SMEM] + [VMEM] * 4, [((HSLOT, HW), BF)], weight=COVER
-    )(pos, ht, gates, rt, pm)[0]
-    hid_par = shift(hid_par, "yh", 2, 1)
+    weight = call(pad_kernel, "weight_pad", [VMEM], [((PAD, HW), BF)])(w_down[0].T)[0]
+    for bit in range(2):
+        other = lax.ppermute(weight, "yl", [(i, i ^ (1 << bit)) for i in range(NY)])
+        weight = call(
+            merge_kernel(bit), "weight_pair", [SMEM] + [VMEM] * 2, [((2 * weight.shape[0], HW), BF)]
+        )(pos, weight, other)[0]
+    pair = weight
+    weight = lax.all_gather(weight, "z", axis=0, tiled=True)
+
+    low, high, pm = prep(pos, resp_lengths, advantage, gt, rt)
+    low_out, high_out, _ = lax.optimization_barrier((low, high, pair))
+    low_par = shift(low_out, "yh", 2, 1)
+    high_par = shift(high_out, "yh", 2, 1)
     own = call(
         own_kernel,
         "send_own",
-        [SMEM] + [ANY] * 3 + [VMEM] * 2,
+        [SMEM] + [ANY] * 3 + [VMEM] * 3,
         [((HSLOT, WIDE + HW), BF)],
         [
             pltpu.VMEM((TOPK, FFW, ROWS), BF),
@@ -289,42 +318,60 @@
             pltpu.VMEM((TOPK, ROWS), I32),
             pltpu.SemaphoreType.DMA((3,)),
         ]
-        + SPREAD,
+        + spread_scratch(WIDE + HW),
         where=ANY,
-    )(pos, *(pltpu.with_memory_space_constraint(v, pltpu.HBM) for v in (ht, gates, rt)), pm, cot)[0]
-    wt = call(pad_kernel, "weight_pad", [VMEM, ANY], [((PAD, HW), BF)])(w_down[0].T, pm)[0]
+    )(pos, *(pltpu.with_memory_space_constraint(v, pltpu.HBM) for v in (ht, gates, rt)), pm, low, high)[0]
+    hid_par = call(
+        other_kernel, "send_other", [SMEM] + [VMEM] * 4 + [ANY], [((HSLOT, HW), BF)]
+    )(pos, ht, gates, rt, pm, pltpu.with_memory_space_constraint(own, pltpu.HBM))[0]
+    hid_par = shift(hid_par, "yh", 2, 1)
     own = exchange(own.reshape(HALF, CAP, WIDE + HW), ("x", "c")).reshape(HSLOT, WIDE + HW)
 
-    parts = [wt] + [shift(wt, "yl", NY, j) for j in range(1, NY)]
-    weight = call(weight_kernel, "weight_part", [SMEM] + [VMEM] * NY, [((NY, PAD, HW), BF)])(
-        pos, *parts
-    )[0].reshape(NY * PAD, HW)
-
-    par = call(partner_kernel, "send_partner", [VMEM] * 2 + [ANY], [((HSLOT, WIDE + HW), BF)], SPREAD, where=ANY)(
-        cot_par, hid_par, weight
-    )[0]
-    par = exchange(par.reshape(HALF, CAP, WIDE + HW), ("x", "c")).reshape(HSLOT, WIDE + HW)
-
-    weight = lax.all_gather(weight, "z", axis=0, tiled=True)
+    def forward(x, after):
+        width = x.shape[1]
+        x, _ = lax.optimization_barrier((x, after))
+        return exchange(x.reshape(HALF, CAP, width), ("x", "c")).reshape(HSLOT, width)
+
+    par_low = call(
+        low_kernel,
+        "send_low",
+        [VMEM] * 2,
+        [((HSLOT, CW + HW), BF)],
+        spread_scratch(CW + HW),
+        where=ANY,
+        weight=COVER,
+    )(low_par, hid_par)[0]
+    par_low = forward(par_low, own)
+    par_high = call(
+        high_kernel,
+        "send_high",
+        [VMEM] * 2,
+        [((HSLOT, CW), BF)],
+        spread_scratch(CW),
+        where=ANY,
+        weight=COVER,
+    )(high_par, low_par)[0]
+    par_high = forward(par_high, par_low)
 
     terms = call(
         term_kernel,
         "grad_term",
-        [VMEM] * 2,
+        [VMEM] * 3 + [ANY],
         [((WIDE, FFW), BF)],
         [pltpu.VMEM((WIDE, FFW), BF), pltpu.SemaphoreType.DMA((NZ,))],
         mib=20,
         where=ANY,
-    )(own, par)[0].reshape(NDP, PAD, FFW)
-    terms = exchange(terms, ("z", "yl"))
+    )(own, par_low, par_high, pltpu.with_memory_space_constraint(weight, pltpu.HBM))[0]
+    terms = exchange(terms.reshape(NDP, PAD, FFW), ("z", "yl"))
 
     backs = call(
         back_kernel,
         "back_product",
-        [SMEM] + [VMEM] * 3,
+        [SMEM] + [VMEM] * 4,
         [((2, CAP, FFW), BF)] * HALF,
         [pltpu.VMEM((HSLOT, FFW), F32)],
-    )(pos, own, par, weight)
+        mib=20,
+    )(pos, own, par_low, par_high, weight)
     backs = [to_peer(b, r) for r, b in enumerate(backs)]
     other = call(stack_kernel, "stack_other", [VMEM] * HALF, [((HALF, CAP, FFW), BF)])(*backs)[0]
     other = shift(other, "yh", 2, 1)

time: 243 us -> 216 us (0.89)
  the two profiles are of different devices: /device:TPU:65 before, /device:TPU:96 now
where the time goes in v6:
time: 216 us; the launch traced here: 214 us
  waiting for transfers between devices  86.6 us (40%)
  starting transfers between devices  61.5 us (28%)
  Pallas kernels  24.9 us (12%)
  blocking collectives  19.6 us (9%)
  between operations  14.4 us (7%)
  local copies, waits for them, and re-layouts  7.53 us (3%)
    all_to_all x3, waiting for transfers between devices, exchange(): return lax.all_to_all(x, axes, split_axis=0, concat_axis=0, tiled=True)  37.5 us
    ppermute x4, waiting for transfers between devices, shift(): return lax.ppermute(x, axis, [(i, (i + by) % n) for i in range(n)])  37.2 us
    ppermute x7, starting transfers between devices, to_peer(): return lax.ppermute(x, ('x', 'c'), pairs)  21.4 us
    all_to_all x1, blocking collectives, exchange(): return lax.all_to_all(x, axes, split_axis=0, concat_axis=0, tiled=True)  19.6 us
    all_to_all x3, starting transfers between devices, exchange(): return lax.all_to_all(x, axes, split_axis=0, concat_axis=0, tiled=True)  18.4 us
    ppermute x4, starting transfers between devices, shift(): return lax.ppermute(x, axis, [(i, (i + by) % n) for i in range(n)])  16.4 us
    ppermute x2, waiting for transfers between devices, local(): other = lax.ppermute(weight, 'yl', [(i, i ^ 1 << bit) for i in range(NY)])  8.51 us
    unnamed x23, local copies, waits for them, and re-layouts  7.45 us
  transfers between devices with their start and end apart: 17, of which 8 were waited for; matrix products, arithmetic and copies ran while one was open for 0% of the time, Pallas kernels for 8%

profile of v6, /device:TPU:96, one launch (start us, length us, event | category | flops | bytes accessed | tf_op | source)
XLA Modules:
  0.0 214.4 jit_solution(11547538771466668179)
XLA Ops:
  7.2 0.0 copy-start.5
  7.2 0.9 copy-done.5
  8.1 2.6 %collective-permute-start = (bf16[96,384]{1,0:T(8,128)(2,1)S(1)}, bf16[96,384]{1,0:T(8,128)(2,1)S(1)}, u32[]{:S(2)}, u32[]{:S(2)}) collective-permute-start(bf16[96,384]{1,0:T(8,128)(2,1)S(1)} %weight_pad.1.mine_ref), channel_id=1, source_target_pairs={{0,16},{16,0},{32,48},{48,32},{1,17},{17,1},{33,49},{49,33},{2,18}... | collective-permute-start | bytes 221192 | tf_op jit(solution)/shard_map/ppermute | solution.py:299
  10.7 0.1 stack.23.pos_ref
  10.8 3.6 %collective-permute-done.other_ref = bf16[96,384]{1,0:T(8,128)(2,1)S(1)} collective-permute-done((bf16[96,384]{1,0:T(8,128)(2,1)S(1)}, bf16[96,384]{1,0:T(8,128)(2,1)S(1)}, u32[]{:S(2)}, u32[]{:S(2)}) %collective-permute-start) | collective-permute-done | bytes 73760 | tf_op jit(solution)/shard_map/ppermute | solution.py:299
  14.3 0.6 weight_pair.2.mine_ref
  14.9 2.7 %collective-permute-start.1 = (bf16[192,384]{1,0:T(8,128)(2,1)S(1)}, bf16[192,384]{1,0:T(8,128)(2,1)S(1)}, u32[]{:S(2)}, u32[]{:S(2)}) collective-permute-start(bf16[192,384]{1,0:T(8,128)(2,1)S(1)} %weight_pair.2.mine_ref), channel_id=1, source_target_pairs={{0,32},{16,48},{32,0},{48,16},{1,33},{17,49},{33,1},{49,17},{2,34}... | collective-permute-start | bytes 442376 | tf_op jit(solution)/shard_map/ppermute | solution.py:299
  17.6 0.0 copy-start.3
  17.6 0.0 copy-start.6
  17.6 0.0 copy-start.7
  17.6 2.7 %prep.1 = (bf16[1552,128]{1,0:T(8,128)(2,1)S(1)}, bf16[1536,128]{1,0:T(8,128)(2,1)}, f32[16,128]{1,0:T(8,128)S(1)}) custom-call(s32[5]{0:T(128)S(1)} %stack.23.pos_ref, s32[1,4]{1,0:T(1,128)} %len_hbm.1, f32[1,4]{1,0:T(1,128)} %adv_hbm.1, bf16[2880,128]{1,0:T(8,128)(2,1)} %bitcast.47, s32[4,128]{1,0:T(4,128)} %bitcast.35), custom_call_target="tpu_custom_call" | custom-call | tf_op jit(solution)/shard_map/prep/pallas_call | solution.py:109
  20.3 5.0 %collective-permute-done.1.other_ref = bf16[192,384]{1,0:T(8,128)(2,1)S(1)} collective-permute-done((bf16[192,384]{1,0:T(8,128)(2,1)S(1)}, bf16[192,384]{1,0:T(8,128)(2,1)S(1)}, u32[]{:S(2)}, u32[]{:S(2)}) %collective-permute-start.1) | collective-permute-done | bytes 147488 | tf_op jit(solution)/shard_map/ppermute | solution.py:299
  25.3 1.3 weight_pair.3
  26.6 2.0 collective-permute-start.2
  28.6 3.3 %send_own.1._ = bf16[320,3456]{1,0:T(8,128)(2,1)} custom-call(s32[5]{0:T(128)S(1)} %stack.23.pos_ref, bf16[4,360,128]{2,1,0:T(8,128)(2,1)} %bitcast.30, bf16[4,128]{1,0:T(4,128)(2,1)} %bitcast.39, s32[4,128]{1,0:T(4,128)} %bitcast.36, f32[16,128]{1,0:T(8,128)S(1)} %get-tuple-element.20.pm_ref, bf16[1552,128]{1,0:T(8,128)(2,1)S(1)} %get-tuple-element.23.low_ref, ...), custom_call_target="tpu_custom_call" | custom-call | tf_op jit(solution)/shard_map/send_own/pallas_call | solution.py:310
  31.9 0.0 copy-done.3
  31.9 0.0 copy-done.6
  31.9 0.0 copy-done.7
  31.9 1.0 send_other.1
  32.9 7.7 %collective-permute-start.3 = (bf16[320,384]{1,0:T(8,128)(2,1)S(1)}, bf16[320,384]{1,0:T(8,128)(2,1)}, u32[]{:S(2)}, u32[]{:S(2)}) collective-permute-start(bf16[320,384]{1,0:T(8,128)(2,1)S(1)} %send_other.1), channel_id=1, source_target_pairs={{0,2},{2,0},{1,3},{3,1},{4,6},{6,4},{5,7},{7,5},{8,10},{10,8},{9,1... | collective-permute-start | bytes 737288 | tf_op jit(solution)/shard_map/ppermute | solution.py:275
  40.7 4.3 %all-to-all-start = ((bf16[8,40,3456]{2,1,0:T(8,128)(2,1)}), bf16[8,40,3456]{2,1,0:T(8,128)(2,1)S(1)}, u32[]{:S(2)}, u32[]{:S(2)}) async-start(bf16[8,40,3456]{2,1,0:T(8,128)(2,1)} %bitcast.43), calls=%async_computation | async-start | bytes 4423680 | tf_op jit(solution)/shard_map/all_to_all | solution.py:287
  45.0 0.0 all-gather.2.cloned.1.call-start
  45.0 0.7 all-gather.2.cloned.1.call-update
  45.7 2.0 collective-permute-start.4
  47.7 21.9 %collective-permute-done.3.h_ref = bf16[320,384]{1,0:T(8,128)(2,1)} collective-permute-done((bf16[320,384]{1,0:T(8,128)(2,1)S(1)}, bf16[320,384]{1,0:T(8,128)(2,1)}, u32[]{:S(2)}, u32[]{:S(2)}) %collective-permute-start.3) | collective-permute-done | bytes 245792 | tf_op jit(solution)/shard_map/ppermute | solution.py:275
  69.6 0.0 collective-permute-done.2.cot_ref.pm_ref
  69.6 2.5 %send_low.1 = bf16[320,1920]{1,0:T(8,128)(2,1)} custom-call(bf16[1552,128]{1,0:T(8,128)(2,1)S(1)} %collective-permute-done.2.cot_ref.pm_ref, bf16[320,384]{1,0:T(8,128)(2,1)} %collective-permute-done.3.h_ref), custom_call_target="tpu_custom_call" | custom-call | flops 49999998976 | tf_op jit(solution)/shard_map/send_low/pallas_call | solution.py:335
  72.1 0.0 copy-done.9
  72.1 1.3 all-to-all-done
  73.4 3.6 %all-to-all-start.1 = ((bf16[8,40,1920]{2,1,0:T(8,128)(2,1)}), bf16[8,40,1920]{2,1,0:T(8,128)(2,1)S(1)}, u32[]{:S(2)}, u32[]{:S(2)}) async-start(bf16[8,40,1920]{2,1,0:T(8,128)(2,1)} %bitcast.45), calls=%async_computation.1 | async-start | bytes 2457600 | tf_op jit(solution)/shard_map/all_to_all | solution.py:287
  77.0 0.0 collective-permute-done.4.cot_ref
  77.0 0.0 copy-start.10
  77.0 1.0 copy-done.10
  78.0 2.4 %send_high.1 = bf16[320,1536]{1,0:T(8,128)(2,1)} custom-call(bf16[1536,128]{1,0:T(8,128)(2,1)} %collective-permute-done.4.cot_ref, bf16[1552,128]{1,0:T(8,128)(2,1)S(1)} %copy-done.10), custom_call_target="tpu_custom_call" | custom-call | flops 49999998976 | tf_op jit(solution)/shard_map/send_high/pallas_call | solution.py:345
  80.4 14.4 %all-to-all-done.1 = bf16[8,40,1920]{2,1,0:T(8,128)(2,1)S(1)} async-done(((bf16[8,40,1920]{2,1,0:T(8,128)(2,1)}), bf16[8,40,1920]{2,1,0:T(8,128)(2,1)S(1)}, u32[]{:S(2)}, u32[]{:S(2)}) %all-to-all-start.1) | async-done | bytes 1228832 | tf_op jit(solution)/shard_map/all_to_all | solution.py:287
  94.8 19.6 %all_to_all.20 = bf16[8,40,1536]{2,1,0:T(8,128)(2,1)} all-to-all(bf16[8,40,1536]{2,1,0:T(8,128)(2,1)} %bitcast.46), channel_id=1, replica_groups=mesh['z'=8,'yl'=4,'x'=4,'yh'=2,'c'=2] {'x','c'}, dimensions={0} | all-to-all | bytes 1966080 | tf_op jit(solution)/shard_map/all_to_all | solution.py:287
  114.4 1.2 copy-done.1
  115.6 4.2 %grad_term.1 = bf16[3072,360]{1,0:T(8,128)(2,1)} custom-call(bf16[320,3456]{1,0:T(8,128)(2,1)S(1)} %bitcast.24, bf16[320,1920]{1,0:T(8,128)(2,1)S(1)} %bitcast.26, bf16[320,1536]{1,0:T(8,128)(2,1)S(1)} %bitcast.28, bf16[3072,384]{1,0:T(8,128)(2,1)} %all-gather.2.cloned.1.call-done._.w_ref), custom_call_target="tpu_custom_call" | custom-call | tf_op jit(solution)/shard_map/grad_term/pallas_call | solution.py:356
  119.8 10.5 %all-to-all-start.3 = ((bf16[32,96,360]{2,1,0:T(8,128)(2,1)}), bf16[32,96,360]{2,1,0:T(8,128)(2,1)}, u32[]{:S(2)}, u32[]{:S(2)}) async-start(bf16[32,96,360]{2,1,0:T(8,128)(2,1)} %bitcast.44), calls=%async_computation.3 | async-start | bytes 4718592 | tf_op jit(solution)/shard_map/all_to_all | solution.py:287
  130.3 0.0 copy-start
  130.3 1.7 copy-done
  132.0 1.2 copy-done.2
  133.2 2.8 %back_product.1 = (bf16[2,40,360]{2,1,0:T(8,128)(2,1)S(1)}, bf16[2,40,360]{2,1,0:T(8,128)(2,1)S(1)}, bf16[2,40,360]{2,1,0:T(8,128)(2,1)S(1)}, bf16[2,40,360]{2,1...) custom-call(s32[5]{0:T(128)S(1)} %stack.23.pos_ref, ...), custom_call_target="tpu_custom_call" | custom-call | tf_op jit(solution)/shard_map/back_product/pallas_call | solution.py:367
  135.9 1.9 collective-permute-start.5
  137.9 2.5 %collective-permute-start.6 = (bf16[2,40,360]{2,1,0:T(8,128)(2,1)S(1)}, bf16[2,40,360]{2,1,0:T(8,128)(2,1)S(1)}, u32[]{:S(2)}, u32[]{:S(2)}) collective-permute-start(bf16[2,40,360]{2,1,0:T(8,128)(2,1)S(1)} %get-tuple-element.29), channel_id=1, source_target_pairs={{0,4},{1,5},{4,8},{5,9},{8,12},{9,13},{12,0},{13,1},{2,6},{3,7},{6... | collective-permute-start | bytes 172808 | tf_op jit(solution)/shard_map/ppermute | solution.py:283
  140.4 2.0 collective-permute-start.7
  142.4 5.8 %collective-permute-start.8 = (bf16[2,40,360]{2,1,0:T(8,128)(2,1)S(1)}, bf16[2,40,360]{2,1,0:T(8,128)(2,1)S(1)}, u32[]{:S(2)}, u32[]{:S(2)}) collective-permute-start(bf16[2,40,360]{2,1,0:T(8,128)(2,1)S(1)} %get-tuple-element.31), channel_id=1, source_target_pairs={{0,8},{1,9},{4,12},{5,13},{8,0},{9,1},{12,4},{13,5},{2,10},{3,11},... | collective-permute-start | bytes 172808 | tf_op jit(solution)/shard_map/ppermute | solution.py:283
  148.1 1.9 collective-permute-start.9
  150.1 0.0 collective-permute-done.5.refs_1_
  150.1 4.1 %collective-permute-start.10 = (bf16[2,40,360]{2,1,0:T(8,128)(2,1)S(1)}, bf16[2,40,360]{2,1,0:T(8,128)(2,1)S(1)}, u32[]{:S(2)}, u32[]{:S(2)}) collective-permute-start(bf16[2,40,360]{2,1,0:T(8,128)(2,1)S(1)} %get-tuple-element.33), channel_id=1, source_target_pairs={{0,12},{1,13},{4,0},{5,1},{8,4},{9,5},{12,8},{13,9},{2,14},{3,15},... | collective-permute-start | bytes 172808 | tf_op jit(solution)/shard_map/ppermute | solution.py:283
  154.2 0.0 collective-permute-done.6.refs_2_
  154.2 3.2 %collective-permute-start.11 = (bf16[2,40,360]{2,1,0:T(8,128)(2,1)S(1)}, bf16[2,40,360]{2,1,0:T(8,128)(2,1)S(1)}, u32[]{:S(2)}, u32[]{:S(2)}) collective-permute-start(bf16[2,40,360]{2,1,0:T(8,128)(2,1)S(1)} %get-tuple-element.34), channel_id=1, source_target_pairs={{0,13},{1,12},{4,1},{5,0},{8,5},{9,4},{12,9},{13,8},{2,15},{3,14},... | collective-permute-start | bytes 172808 | tf_op jit(solution)/shard_map/ppermute | solution.py:283
  157.4 0.0 collective-permute-done.7.refs_3_
  157.5 0.0 collective-permute-done.8.refs_4_
  157.5 0.0 collective-permute-done.9.refs_5_
  157.5 0.0 collective-permute-done.10.refs_6_
  157.5 2.6 %collective-permute-done.11.refs_7_ = bf16[2,40,360]{2,1,0:T(8,128)(2,1)S(1)} collective-permute-done((bf16[2,40,360]{2,1,0:T(8,128)(2,1)S(1)}, bf16[2,40,360]{2,1,0:T(8,128)(2,1)S(1)}, u32[]{:S(2)}, u32[]{:S(2)}) %collective-permute-start.11) | collective-permute-done | bytes 57632 | tf_op jit(solution)/shard_map/ppermute | solution.py:283
  160.2 4.6 %collective-permute-start.12 = (bf16[8,40,360]{2,1,0:T(8,128)(2,1)S(1)}, bf16[8,40,360]{2,1,0:T(8,128)(2,1)S(1)}, u32[]{:S(2)}, u32[]{:S(2)}) collective-permute-start(bf16[8,40,360]{2,1,0:T(8,128)(2,1)S(1)} %stack_other.1), channel_id=1, source_target_pairs={{0,2},{2,0},{1,3},{3,1},{4,6},{6,4},{5,7},{7,5},{8,10},{10,8},{9,1... | collective-permute-start | bytes 691208 | tf_op jit(solution)/shard_map/ppermute | solution.py:275
  164.8 15.3 %collective-permute-done.12.other_ref = bf16[8,40,360]{2,1,0:T(8,128)(2,1)S(1)} collective-permute-done((bf16[8,40,360]{2,1,0:T(8,128)(2,1)S(1)}, bf16[8,40,360]{2,1,0:T(8,128)(2,1)S(1)}, u32[]{:S(2)}, u32[]{:S(2)}) %collective-permute-start.12) | collective-permute-done | bytes 230432 | tf_op jit(solution)/shard_map/ppermute | solution.py:275
  180.1 2.2 %bring_home.1 = (f32[4,360,128]{2,1,0:T(8,128)}, f32[4,128]{1,0:T(4,128)}) custom-call(s32[5]{0:T(128)S(1)} %stack.23.pos_ref, bf16[4,360,128]{2,1,0:T(8,128)(2,1)S(1)} %bitcast.32, bf16[4,128]{1,0:T(4,128)(2,1)S(1)} %bitcast.41, f32[16,128]{1,0:T(8,128)S(1)} %get-tuple-element.20.pm_ref, s32[4,128]{1,0:T(4,128)S(1)} %bitcast.38, ...), custom_call_target="tpu_custom_call" | custom-call | tf_op jit(solution)/shard_map/bring_home/pallas_call | solution.py:378
  182.3 21.8 %all-to-all-done.3.x_ref = bf16[32,96,360]{2,1,0:T(8,128)(2,1)} async-done(((bf16[32,96,360]{2,1,0:T(8,128)(2,1)}), bf16[32,96,360]{2,1,0:T(8,128)(2,1)}, u32[]{:S(2)}, u32[]{:S(2)}) %all-to-all-start.3) | async-done | bytes 2211872 | tf_op jit(solution)/shard_map/all_to_all | solution.py:287
  204.1 0.7 copy-done.8
  204.8 2.0 sum_terms.1
  206.8 0.8 copy.10
  (9 shorter events, 0.0 us)
Async XLA Ops:
  7.2 0.9 copy-start.5
  8.1 6.2 %collective-permute-start = (bf16[96,384]{1,0:T(8,128)(2,1)S(1)}, bf16[96,384]{1,0:T(8,128)(2,1)S(1)}, u32[]{:S(2)}, u32[]{:S(2)}) collective-permute-start(bf16[96,384]{1,0:T(8,128)(2,1)S(1)} %weight_pad.1.mine_ref), channel_id=1, source_target_pairs={{0,16},{16,0},{32,48},{48,32},{1,17},{17,1},{33,49},{49,33},{2,18}... | collective-permute-start | bytes 221192 | tf_op jit(solution)/shard_map/ppermute | solution.py:299
  14.9 10.4 %collective-permute-start.1 = (bf16[192,384]{1,0:T(8,128)(2,1)S(1)}, bf16[192,384]{1,0:T(8,128)(2,1)S(1)}, u32[]{:S(2)}, u32[]{:S(2)}) collective-permute-start(bf16[192,384]{1,0:T(8,128)(2,1)S(1)} %weight_pair.2.mine_ref), channel_id=1, source_target_pairs={{0,32},{16,48},{32,0},{48,16},{1,33},{17,49},{33,1},{49,17},{2,34}... | collective-permute-start | bytes 442376 | tf_op jit(solution)/shard_map/ppermute | solution.py:299
  17.6 14.3 %copy-start.3 = (bf16[128,4,360]{0,2,1:T(8,128)(2,1)S(1)}, bf16[128,4,360]{0,2,1:T(8,128)(2,1)}, u32[]{:S(2)}) copy-start(bf16[128,4,360]{0,2,1:T(8,128)(2,1)} %param.8) | copy-start | bytes 1105924
  17.6 14.3 %copy-start.6 = (s32[128,4]{0,1:T(4,128)S(1)}, s32[128,4]{0,1:T(4,128)}, u32[]{:S(2)}) copy-start(s32[128,4]{0,1:T(4,128)} %param.10) | copy-start | bytes 6148
  17.6 14.3 %copy-start.7 = (bf16[128,4]{0,1:T(4,128)(2,1)S(1)}, bf16[128,4]{0,1:T(4,128)(2,1)}, u32[]{:S(2)}) copy-start(bf16[128,4]{0,1:T(4,128)(2,1)} %param.9) | copy-start | bytes 3076
  26.6 43.0 %collective-permute-start.2 = (bf16[1552,128]{1,0:T(8,128)(2,1)S(1)}, bf16[1552,128]{1,0:T(8,128)(2,1)S(1)}, u32[]{:S(2)}, u32[]{:S(2)}) collective-permute-start(bf16[1552,128]{1,0:T(8,128)(2,1)S(1)} %get-tuple-element.23.low_ref), channel_id=1, source_target_pairs={{0,2},{2,0},{1,3},{3,1},{4,6},{6,4},{5,7},{7,5},{8,10},{10,8},{9,1... | collective-permute-start | bytes 1191944 | tf_op jit(solution)/shard_map/ppermute | solution.py:275
  32.9 36.7 %collective-permute-start.3 = (bf16[320,384]{1,0:T(8,128)(2,1)S(1)}, bf16[320,384]{1,0:T(8,128)(2,1)}, u32[]{:S(2)}, u32[]{:S(2)}) collective-permute-start(bf16[320,384]{1,0:T(8,128)(2,1)S(1)} %send_other.1), channel_id=1, source_target_pairs={{0,2},{2,0},{1,3},{3,1},{4,6},{6,4},{5,7},{7,5},{8,10},{10,8},{9,1... | collective-permute-start | bytes 737288 | tf_op jit(solution)/shard_map/ppermute | solution.py:275
  40.7 32.7 %all-to-all-start = ((bf16[8,40,3456]{2,1,0:T(8,128)(2,1)}), bf16[8,40,3456]{2,1,0:T(8,128)(2,1)S(1)}, u32[]{:S(2)}, u32[]{:S(2)}) async-start(bf16[8,40,3456]{2,1,0:T(8,128)(2,1)} %bitcast.43), calls=%async_computation | async-start | bytes 4423680 | tf_op jit(solution)/shard_map/all_to_all | solution.py:287
  45.0 69.4 %all-gather.2.cloned.1.call-start = ((), (), s32[]{:S(2)}) async-start(), calls=%async_computation.4 | async-start | bytes 2654208 | tf_op jit(solution)/shard_map/all_gather | solution.py:304
  45.7 31.3 %collective-permute-start.4 = (bf16[1536,128]{1,0:T(8,128)(2,1)}, bf16[1536,128]{1,0:T(8,128)(2,1)}, u32[]{:S(2)}, u32[]{:S(2)}) collective-permute-start(bf16[1536,128]{1,0:T(8,128)(2,1)} %get-tuple-element.25.high_ref), channel_id=1, source_target_pairs={{0,2},{2,0},{1,3},{3,1},{4,6},{6,4},{5,7},{7,5},{8,10},{10,8},{9,1... | collective-permute-start | bytes 1179656 | tf_op jit(solution)/shard_map/ppermute | solution.py:275
  69.6 2.5 %copy-start.9 = (bf16[1552,128]{1,0:T(8,128)(2,1)}, bf16[1552,128]{1,0:T(8,128)(2,1)S(1)}, u32[]{:S(2)}) copy-start(bf16[1552,128]{1,0:T(8,128)(2,1)S(1)} %collective-permute-done.2.cot_ref.pm_ref) | copy-start | bytes 1191940
  73.4 21.4 %all-to-all-start.1 = ((bf16[8,40,1920]{2,1,0:T(8,128)(2,1)}), bf16[8,40,1920]{2,1,0:T(8,128)(2,1)S(1)}, u32[]{:S(2)}, u32[]{:S(2)}) async-start(bf16[8,40,1920]{2,1,0:T(8,128)(2,1)} %bitcast.45), calls=%async_computation.1 | async-start | bytes 2457600 | tf_op jit(solution)/shard_map/all_to_all | solution.py:287
  77.0 1.0 copy-start.10
  114.4 1.2 copy-start.1
  119.8 84.4 %all-to-all-start.3 = ((bf16[32,96,360]{2,1,0:T(8,128)(2,1)}), bf16[32,96,360]{2,1,0:T(8,128)(2,1)}, u32[]{:S(2)}, u32[]{:S(2)}) async-start(bf16[32,96,360]{2,1,0:T(8,128)(2,1)} %bitcast.44), calls=%async_computation.3 | async-start | bytes 4718592 | tf_op jit(solution)/shard_map/all_to_all | solution.py:287
  130.3 1.7 copy-start
  132.0 1.2 copy-start.2
  133.2 46.9 %copy-start.4 = (bf16[128,4,360]{0,2,1:T(8,128)(2,1)S(1)}, bf16[128,4,360]{0,2,1:T(8,128)(2,1)}, u32[]{:S(2)}) copy-start(bf16[128,4,360]{0,2,1:T(8,128)(2,1)} %param.8) | copy-start | bytes 1105924
  135.9 14.1 %collective-permute-start.5 = (bf16[2,40,360]{2,1,0:T(8,128)(2,1)S(1)}, bf16[2,40,360]{2,1,0:T(8,128)(2,1)S(1)}, u32[]{:S(2)}, u32[]{:S(2)}) collective-permute-start(bf16[2,40,360]{2,1,0:T(8,128)(2,1)S(1)} %get-tuple-element.28), channel_id=1, source_target_pairs={{0,1},{1,0},{4,5},{5,4},{8,9},{9,8},{12,13},{13,12},{2,3},{3,2},{6... | collective-permute-start | bytes 172808 | tf_op jit(solution)/shard_map/ppermute | solution.py:283
  137.9 16.4 %collective-permute-start.6 = (bf16[2,40,360]{2,1,0:T(8,128)(2,1)S(1)}, bf16[2,40,360]{2,1,0:T(8,128)(2,1)S(1)}, u32[]{:S(2)}, u32[]{:S(2)}) collective-permute-start(bf16[2,40,360]{2,1,0:T(8,128)(2,1)S(1)} %get-tuple-element.29), channel_id=1, source_target_pairs={{0,4},{1,5},{4,8},{5,9},{8,12},{9,13},{12,0},{13,1},{2,6},{3,7},{6... | collective-permute-start | bytes 172808 | tf_op jit(solution)/shard_map/ppermute | solution.py:283
  140.4 17.1 %collective-permute-start.7 = (bf16[2,40,360]{2,1,0:T(8,128)(2,1)S(1)}, bf16[2,40,360]{2,1,0:T(8,128)(2,1)S(1)}, u32[]{:S(2)}, u32[]{:S(2)}) collective-permute-start(bf16[2,40,360]{2,1,0:T(8,128)(2,1)S(1)} %get-tuple-element.30), channel_id=1, source_target_pairs={{0,5},{1,4},{4,9},{5,8},{8,13},{9,12},{12,1},{13,0},{2,7},{3,6},{6... | collective-permute-start | bytes 172808 | tf_op jit(solution)/shard_map/ppermute | solution.py:283
  142.4 15.1 %collective-permute-start.8 = (bf16[2,40,360]{2,1,0:T(8,128)(2,1)S(1)}, bf16[2,40,360]{2,1,0:T(8,128)(2,1)S(1)}, u32[]{:S(2)}, u32[]{:S(2)}) collective-permute-start(bf16[2,40,360]{2,1,0:T(8,128)(2,1)S(1)} %get-tuple-element.31), channel_id=1, source_target_pairs={{0,8},{1,9},{4,12},{5,13},{8,0},{9,1},{12,4},{13,5},{2,10},{3,11},... | collective-permute-start | bytes 172808 | tf_op jit(solution)/shard_map/ppermute | solution.py:283
  148.1 9.3 %collective-permute-start.9 = (bf16[2,40,360]{2,1,0:T(8,128)(2,1)S(1)}, bf16[2,40,360]{2,1,0:T(8,128)(2,1)S(1)}, u32[]{:S(2)}, u32[]{:S(2)}) collective-permute-start(bf16[2,40,360]{2,1,0:T(8,128)(2,1)S(1)} %get-tuple-element.32), channel_id=1, source_target_pairs={{0,9},{1,8},{4,13},{5,12},{8,1},{9,0},{12,5},{13,4},{2,11},{3,10},... | collective-permute-start | bytes 172808 | tf_op jit(solution)/shard_map/ppermute | solution.py:283
  150.1 7.4 %collective-permute-start.10 = (bf16[2,40,360]{2,1,0:T(8,128)(2,1)S(1)}, bf16[2,40,360]{2,1,0:T(8,128)(2,1)S(1)}, u32[]{:S(2)}, u32[]{:S(2)}) collective-permute-start(bf16[2,40,360]{2,1,0:T(8,128)(2,1)S(1)} %get-tuple-element.33), channel_id=1, source_target_pairs={{0,12},{1,13},{4,0},{5,1},{8,4},{9,5},{12,8},{13,9},{2,14},{3,15},... | collective-permute-start | bytes 172808 | tf_op jit(solution)/shard_map/ppermute | solution.py:283
  154.2 5.9 %collective-permute-start.11 = (bf16[2,40,360]{2,1,0:T(8,128)(2,1)S(1)}, bf16[2,40,360]{2,1,0:T(8,128)(2,1)S(1)}, u32[]{:S(2)}, u32[]{:S(2)}) collective-permute-start(bf16[2,40,360]{2,1,0:T(8,128)(2,1)S(1)} %get-tuple-element.34), channel_id=1, source_target_pairs={{0,13},{1,12},{4,1},{5,0},{8,5},{9,4},{12,9},{13,8},{2,15},{3,14},... | collective-permute-start | bytes 172808 | tf_op jit(solution)/shard_map/ppermute | solution.py:283
  160.2 19.9 %collective-permute-start.12 = (bf16[8,40,360]{2,1,0:T(8,128)(2,1)S(1)}, bf16[8,40,360]{2,1,0:T(8,128)(2,1)S(1)}, u32[]{:S(2)}, u32[]{:S(2)}) collective-permute-start(bf16[8,40,360]{2,1,0:T(8,128)(2,1)S(1)} %stack_other.1), channel_id=1, source_target_pairs={{0,2},{2,0},{1,3},{3,1},{4,6},{6,4},{5,7},{7,5},{8,10},{10,8},{9,1... | collective-permute-start | bytes 691208 | tf_op jit(solution)/shard_map/ppermute | solution.py:275
  204.1 0.7 copy-start.8
Sparse Core Ops, SparseCore 0:
  47.9 48.3 all-gather.1

commit v7 on v6

--- a/solution.py
+++ b/solution.py
@@ -21,6 +21,7 @@
 HSLOT = HALF * CAP
 STEP = 768
 HW = 384
+COVER_LOW = 10_000_000_000
 COVER = 50_000_000_000
 BLK = NY * PAD
 CW = WIDE // 2
@@ -139,7 +140,7 @@
     return acc.astype(BF)
 
 
-def other_kernel(pos_ref, h_ref, gate_ref, r_ref, pm_ref, _, out_ref):
+def other_kernel(pos_ref, h_ref, gate_ref, r_ref, pm_ref, out_ref):
     first = pos_ref[2] == 0
     eid = expert_ids()
     place = jnp.where(first, pm_ref[HALF:], pm_ref[:HALF])
@@ -214,7 +215,8 @@
 
 
 def merge_kernel(bit):
-    def body(pos_ref, mine_ref, other_ref, out_ref):
+    def body(pos_ref, mine_ref, other_ref, *refs):
+        out_ref = refs[-1]
         i = (pos_ref[1] >> bit) & 1
         n = mine_ref.shape[0]
         out_ref[pl.ds(pl.multiple_of(i * n, n), n)] = mine_ref[...]
@@ -294,19 +296,7 @@
     gates = gate_weights.T
     rt = routing.T
 
-    weight = call(pad_kernel, "weight_pad", [VMEM], [((PAD, HW), BF)])(w_down[0].T)[0]
-    for bit in range(2):
-        other = lax.ppermute(weight, "yl", [(i, i ^ (1 << bit)) for i in range(NY)])
-        weight = call(
-            merge_kernel(bit), "weight_pair", [SMEM] + [VMEM] * 2, [((2 * weight.shape[0], HW), BF)]
-        )(pos, weight, other)[0]
-    pair = weight
-    weight = lax.all_gather(weight, "z", axis=0, tiled=True)
-
     low, high, pm = prep(pos, resp_lengths, advantage, gt, rt)
-    low_out, high_out, _ = lax.optimization_barrier((low, high, pair))
-    low_par = shift(low_out, "yh", 2, 1)
-    high_par = shift(high_out, "yh", 2, 1)
     own = call(
         own_kernel,
         "send_own",
@@ -321,9 +311,26 @@
         + spread_scratch(WIDE + HW),
         where=ANY,
     )(pos, *(pltpu.with_memory_space_constraint(v, pltpu.HBM) for v in (ht, gates, rt)), pm, low, high)[0]
-    hid_par = call(
-        other_kernel, "send_other", [SMEM] + [VMEM] * 4 + [ANY], [((HSLOT, HW), BF)]
-    )(pos, ht, gates, rt, pm, pltpu.with_memory_space_constraint(own, pltpu.HBM))[0]
+
+    weight = call(pad_kernel, "weight_pad", [VMEM], [((PAD, HW), BF)])(w_down[0].T)[0]
+    ready = pltpu.with_memory_space_constraint(own, pltpu.HBM)
+    for bit in range(2):
+        other = lax.ppermute(weight, "yl", [(i, i ^ (1 << bit)) for i in range(NY)])
+        weight = call(
+            merge_kernel(bit),
+            "weight_pair",
+            [SMEM] + [VMEM] * 2 + [ANY],
+            [((2 * weight.shape[0], HW), BF)],
+        )(pos, weight, other, ready)[0]
+    pair = weight
+    weight = lax.all_gather(weight, "z", axis=0, tiled=True)
+
+    low_out, high_out, pm_out, _ = lax.optimization_barrier((low, high, pm, pair))
+    low_par = shift(low_out, "yh", 2, 1)
+    high_par = shift(high_out, "yh", 2, 1)
+    hid_par = call(other_kernel, "send_other", [SMEM] + [VMEM] * 4, [((HSLOT, HW), BF)])(
+        pos, ht, gates, rt, pm_out
+    )[0]
     hid_par = shift(hid_par, "yh", 2, 1)
     own = exchange(own.reshape(HALF, CAP, WIDE + HW), ("x", "c")).reshape(HSLOT, WIDE + HW)
 
@@ -339,7 +346,7 @@
         [((HSLOT, CW + HW), BF)],
         spread_scratch(CW + HW),
         where=ANY,
-        weight=COVER,
+        weight=COVER_LOW,
     )(low_par, hid_par)[0]
     par_low = forward(par_low, own)
     par_high = call(

time: 216 us -> 227 us (1.051)
  waiting for transfers between devices: 86.6 us -> 97.8 us
    ppermute x4, waiting for transfers between devices: 37.2 us -> 46.1 us  [shift(): return lax.ppermute(x, axis, [(i, (i + by) % n) for i in range(n)])]
    ppermute x2, waiting for transfers between devices: 8.51 us -> 12.6 us  [local(): other = lax.ppermute(weight, 'yl', [(i, i ^ 1 << bit) for i in range(NY)])]
    unnamed x23 -> x19, local copies, waits for them, and re-layouts: 7.45 us -> 5.57 us
  transfers between devices with their start and end apart: 17 -> 17, of which waited for: 8 -> 8; matrix products, arithmetic and copies ran while one was open for 0% -> 0% of each run, Pallas kernels for 8% -> 6%
where the time goes in v7:
time: 227 us; the launch traced here: 226 us
  waiting for transfers between devices  97.8 us (43%)
  starting transfers between devices  63.2 us (28%)
  Pallas kernels  24.9 us (11%)
  blocking collectives  19.6 us (9%)
  between operations  14.4 us (6%)
  local copies, waits for them, and re-layouts  5.66 us (2%)
    ppermute x4, waiting for transfers between devices, shift(): return lax.ppermute(x, axis, [(i, (i + by) % n) for i in range(n)])  46.1 us
    all_to_all x3, waiting for transfers between devices, exchange(): return lax.all_to_all(x, axes, split_axis=0, concat_axis=0, tiled=True)  36.4 us
    ppermute x7, starting transfers between devices, to_peer(): return lax.ppermute(x, ('x', 'c'), pairs)  21.4 us
    all_to_all x3, starting transfers between devices, exchange(): return lax.all_to_all(x, axes, split_axis=0, concat_axis=0, tiled=True)  20.3 us
    all_to_all x1, blocking collectives, exchange(): return lax.all_to_all(x, axes, split_axis=0, concat_axis=0, tiled=True)  19.6 us
    ppermute x4, starting transfers between devices, shift(): return lax.ppermute(x, axis, [(i, (i + by) % n) for i in range(n)])  16.1 us
    ppermute x2, waiting for transfers between devices, local(): other = lax.ppermute(weight, 'yl', [(i, i ^ 1 << bit) for i in range(NY)])  12.6 us
    unnamed x19, local copies, waits for them, and re-layouts  5.57 us
  transfers between devices with their start and end apart: 17, of which 8 were waited for; matrix products, arithmetic and copies ran while one was open for 0% of the time, Pallas kernels for 6%

profile of v7, /device:TPU:96, one launch (start us, length us, event | category | flops | bytes accessed | tf_op | source)
XLA Modules:
  0.0 225.6 jit_solution(10856704283018709197)
XLA Ops:
  7.2 0.1 stack.23.pos_ref
  7.3 2.7 %prep.1 = (bf16[1552,128]{1,0:T(8,128)(2,1)S(1)}, bf16[1536,128]{1,0:T(8,128)(2,1)}, f32[16,128]{1,0:T(8,128)S(1)}) custom-call(s32[5]{0:T(128)S(1)} %stack.23.pos_ref, s32[1,4]{1,0:T(1,128)} %len_hbm.1, f32[1,4]{1,0:T(1,128)} %adv_hbm.1, bf16[2880,128]{1,0:T(8,128)(2,1)} %bitcast.47, s32[4,128]{1,0:T(4,128)} %bitcast.35), custom_call_target="tpu_custom_call" | custom-call | tf_op jit(solution)/shard_map/prep/pallas_call | solution.py:110
  10.0 3.3 %send_own.1.refs_0_ = bf16[320,3456]{1,0:T(8,128)(2,1)} custom-call(s32[5]{0:T(128)S(1)} %stack.23.pos_ref, bf16[4,360,128]{2,1,0:T(8,128)(2,1)} %bitcast.30, bf16[4,128]{1,0:T(4,128)(2,1)} %bitcast.39, s32[4,128]{1,0:T(4,128)} %bitcast.36, f32[16,128]{1,0:T(8,128)S(1)} %get-tuple-element.25.pm_ref, bf16[1552,128]{1,0:T(8,128)(2,1)S(1)} %get-tuple-element.24.low_ref, ...), custom_call_target="tpu_custom_call" | custom-call | tf_op jit(solution)/shard_map/send_own/pallas_call | solution.py:300
  13.3 0.0 copy-start.5
  13.3 4.4 %all-to-all-start = ((bf16[8,40,3456]{2,1,0:T(8,128)(2,1)}), bf16[8,40,3456]{2,1,0:T(8,128)(2,1)S(1)}, u32[]{:S(2)}, u32[]{:S(2)}) async-start(bf16[8,40,3456]{2,1,0:T(8,128)(2,1)} %bitcast.43), calls=%async_computation | async-start | bytes 4423680 | tf_op jit(solution)/shard_map/all_to_all | solution.py:289
  17.7 0.0 all-gather.2.cloned.1.call-start
  17.8 0.0 copy-done.5
  17.8 0.0 copy-start.3
  17.8 0.0 copy-start.6
  17.8 0.0 copy-start.7
  17.9 2.7 %collective-permute-start = (bf16[96,384]{1,0:T(8,128)(2,1)S(1)}, bf16[96,384]{1,0:T(8,128)(2,1)S(1)}, u32[]{:S(2)}, u32[]{:S(2)}) collective-permute-start(bf16[96,384]{1,0:T(8,128)(2,1)S(1)} %weight_pad.1.mine_ref), channel_id=1, source_target_pairs={{0,16},{16,0},{32,48},{48,32},{1,17},{17,1},{33,49},{49,33},{2,18}... | collective-permute-start | bytes 221192 | tf_op jit(solution)/shard_map/ppermute | solution.py:318
  20.6 3.9 %collective-permute-done.other_ref = bf16[96,384]{1,0:T(8,128)(2,1)S(1)} collective-permute-done((bf16[96,384]{1,0:T(8,128)(2,1)S(1)}, bf16[96,384]{1,0:T(8,128)(2,1)S(1)}, u32[]{:S(2)}, u32[]{:S(2)}) %collective-permute-start) | collective-permute-done | bytes 73760 | tf_op jit(solution)/shard_map/ppermute | solution.py:318
  24.5 0.6 weight_pair.2.mine_ref
  25.1 2.7 %collective-permute-start.1 = (bf16[192,384]{1,0:T(8,128)(2,1)S(1)}, bf16[192,384]{1,0:T(8,128)(2,1)S(1)}, u32[]{:S(2)}, u32[]{:S(2)}) collective-permute-start(bf16[192,384]{1,0:T(8,128)(2,1)S(1)} %weight_pair.2.mine_ref), channel_id=1, source_target_pairs={{0,32},{16,48},{32,0},{48,16},{1,33},{17,49},{33,1},{49,17},{2,34}... | collective-permute-start | bytes 442376 | tf_op jit(solution)/shard_map/ppermute | solution.py:318
  27.8 8.7 %collective-permute-done.1.other_ref = bf16[192,384]{1,0:T(8,128)(2,1)S(1)} collective-permute-done((bf16[192,384]{1,0:T(8,128)(2,1)S(1)}, bf16[192,384]{1,0:T(8,128)(2,1)S(1)}, u32[]{:S(2)}, u32[]{:S(2)}) %collective-permute-start.1) | collective-permute-done | bytes 147488 | tf_op jit(solution)/shard_map/ppermute | solution.py:318
  36.5 1.3 weight_pair.3
  37.8 2.0 collective-permute-start.2
  39.8 0.0 copy-done.3
  39.8 0.0 copy-done.6
  39.8 0.0 copy-done.7
  39.8 1.0 send_other.1
  40.8 7.7 %collective-permute-start.3 = (bf16[320,384]{1,0:T(8,128)(2,1)S(1)}, bf16[320,384]{1,0:T(8,128)(2,1)S(1)}, u32[]{:S(2)}, u32[]{:S(2)}) collective-permute-start(bf16[320,384]{1,0:T(8,128)(2,1)S(1)} %send_other.1), channel_id=1, source_target_pairs={{0,2},{2,0},{1,3},{3,1},{4,6},{6,4},{5,7},{7,5},{8,10},{10,8},{9,1... | collective-permute-start | bytes 737288 | tf_op jit(solution)/shard_map/ppermute | solution.py:277
  48.5 0.0 all-gather.2.cloned.1.call-update
  48.5 2.0 collective-permute-start.4
  50.6 29.8 %collective-permute-done.3.h_ref = bf16[320,384]{1,0:T(8,128)(2,1)S(1)} collective-permute-done((bf16[320,384]{1,0:T(8,128)(2,1)S(1)}, bf16[320,384]{1,0:T(8,128)(2,1)S(1)}, u32[]{:S(2)}, u32[]{:S(2)}) %collective-permute-start.3) | collective-permute-done | bytes 245792 | tf_op jit(solution)/shard_map/ppermute | solution.py:277
  80.4 0.0 collective-permute-done.2.cot_ref.pm_ref
  80.4 2.4 %send_low.1 = bf16[320,1920]{1,0:T(8,128)(2,1)} custom-call(bf16[1552,128]{1,0:T(8,128)(2,1)} %collective-permute-done.2.cot_ref.pm_ref, bf16[320,384]{1,0:T(8,128)(2,1)S(1)} %collective-permute-done.3.h_ref), custom_call_target="tpu_custom_call" | custom-call | flops 10000000000 | tf_op jit(solution)/shard_map/send_low/pallas_call | solution.py:342
  82.8 0.0 all-to-all-done
  82.8 4.1 %all-to-all-start.1 = ((bf16[8,40,1920]{2,1,0:T(8,128)(2,1)}), bf16[8,40,1920]{2,1,0:T(8,128)(2,1)S(1)}, u32[]{:S(2)}, u32[]{:S(2)}) async-start(bf16[8,40,1920]{2,1,0:T(8,128)(2,1)} %bitcast.45), calls=%async_computation.1 | async-start | bytes 2457600 | tf_op jit(solution)/shard_map/all_to_all | solution.py:289
  86.9 1.2 collective-permute-done.4.cot_ref
  88.1 2.5 %send_high.1 = bf16[320,1536]{1,0:T(8,128)(2,1)} custom-call(bf16[1536,128]{1,0:T(8,128)(2,1)} %collective-permute-done.4.cot_ref, bf16[1552,128]{1,0:T(8,128)(2,1)} %collective-permute-done.2.cot_ref.pm_ref), custom_call_target="tpu_custom_call" | custom-call | flops 49999998976 | tf_op jit(solution)/shard_map/send_high/pallas_call | solution.py:352
  90.6 14.2 %all-to-all-done.1 = bf16[8,40,1920]{2,1,0:T(8,128)(2,1)S(1)} async-done(((bf16[8,40,1920]{2,1,0:T(8,128)(2,1)}), bf16[8,40,1920]{2,1,0:T(8,128)(2,1)S(1)}, u32[]{:S(2)}, u32[]{:S(2)}) %all-to-all-start.1) | async-done | bytes 1228832 | tf_op jit(solution)/shard_map/all_to_all | solution.py:289
  104.8 19.6 %all_to_all.20 = bf16[8,40,1536]{2,1,0:T(8,128)(2,1)} all-to-all(bf16[8,40,1536]{2,1,0:T(8,128)(2,1)} %bitcast.46), channel_id=1, replica_groups=mesh['z'=8,'yl'=4,'x'=4,'yh'=2,'c'=2] {'x','c'}, dimensions={0} | all-to-all | bytes 1966080 | tf_op jit(solution)/shard_map/all_to_all | solution.py:289
  124.5 0.0 all-gather.2.cloned.1.call-done._.w_ref
  124.5 0.0 copy-start.1
  124.5 1.2 copy-done.1
  125.7 4.2 %grad_term.1 = bf16[3072,360]{1,0:T(8,128)(2,1)} custom-call(bf16[320,3456]{1,0:T(8,128)(2,1)S(1)} %bitcast.24, bf16[320,1920]{1,0:T(8,128)(2,1)S(1)} %bitcast.26, bf16[320,1536]{1,0:T(8,128)(2,1)S(1)} %bitcast.28, bf16[3072,384]{1,0:T(8,128)(2,1)} %all-gather.2.cloned.1.call-done._.w_ref), custom_call_target="tpu_custom_call" | custom-call | tf_op jit(solution)/shard_map/grad_term/pallas_call | solution.py:363
  129.8 11.7 %all-to-all-start.3 = ((bf16[32,96,360]{2,1,0:T(8,128)(2,1)}), bf16[32,96,360]{2,1,0:T(8,128)(2,1)}, u32[]{:S(2)}, u32[]{:S(2)}) async-start(bf16[32,96,360]{2,1,0:T(8,128)(2,1)} %bitcast.44), calls=%async_computation.3 | async-start | bytes 4718592 | tf_op jit(solution)/shard_map/all_to_all | solution.py:289
  141.5 0.0 copy-start
  141.6 1.7 copy-done
  143.2 1.2 copy-done.2
  144.4 2.8 %back_product.1 = (bf16[2,40,360]{2,1,0:T(8,128)(2,1)S(1)}, bf16[2,40,360]{2,1,0:T(8,128)(2,1)S(1)}, bf16[2,40,360]{2,1,0:T(8,128)(2,1)S(1)}, bf16[2,40,360]{2,1...) custom-call(s32[5]{0:T(128)S(1)} %stack.23.pos_ref, ...), custom_call_target="tpu_custom_call" | custom-call | tf_op jit(solution)/shard_map/back_product/pallas_call | solution.py:374
  147.2 1.9 collective-permute-start.5
  149.1 2.5 %collective-permute-start.6 = (bf16[2,40,360]{2,1,0:T(8,128)(2,1)S(1)}, bf16[2,40,360]{2,1,0:T(8,128)(2,1)S(1)}, u32[]{:S(2)}, u32[]{:S(2)}) collective-permute-start(bf16[2,40,360]{2,1,0:T(8,128)(2,1)S(1)} %get-tuple-element.31), channel_id=1, source_target_pairs={{0,4},{1,5},{4,8},{5,9},{8,12},{9,13},{12,0},{13,1},{2,6},{3,7},{6... | collective-permute-start | bytes 172808 | tf_op jit(solution)/shard_map/ppermute | solution.py:285
  151.6 2.0 collective-permute-start.7
  153.6 5.7 %collective-permute-start.8 = (bf16[2,40,360]{2,1,0:T(8,128)(2,1)S(1)}, bf16[2,40,360]{2,1,0:T(8,128)(2,1)S(1)}, u32[]{:S(2)}, u32[]{:S(2)}) collective-permute-start(bf16[2,40,360]{2,1,0:T(8,128)(2,1)S(1)} %get-tuple-element.33), channel_id=1, source_target_pairs={{0,8},{1,9},{4,12},{5,13},{8,0},{9,1},{12,4},{13,5},{2,10},{3,11},... | collective-permute-start | bytes 172808 | tf_op jit(solution)/shard_map/ppermute | solution.py:285
  159.4 1.9 collective-permute-start.9
  161.3 0.0 collective-permute-done.5.refs_1_
  161.3 4.2 %collective-permute-start.10 = (bf16[2,40,360]{2,1,0:T(8,128)(2,1)S(1)}, bf16[2,40,360]{2,1,0:T(8,128)(2,1)S(1)}, u32[]{:S(2)}, u32[]{:S(2)}) collective-permute-start(bf16[2,40,360]{2,1,0:T(8,128)(2,1)S(1)} %get-tuple-element.35), channel_id=1, source_target_pairs={{0,12},{1,13},{4,0},{5,1},{8,4},{9,5},{12,8},{13,9},{2,14},{3,15},... | collective-permute-start | bytes 172808 | tf_op jit(solution)/shard_map/ppermute | solution.py:285
  165.5 0.0 collective-permute-done.6.refs_2_
  165.5 3.2 %collective-permute-start.11 = (bf16[2,40,360]{2,1,0:T(8,128)(2,1)S(1)}, bf16[2,40,360]{2,1,0:T(8,128)(2,1)S(1)}, u32[]{:S(2)}, u32[]{:S(2)}) collective-permute-start(bf16[2,40,360]{2,1,0:T(8,128)(2,1)S(1)} %get-tuple-element.36), channel_id=1, source_target_pairs={{0,13},{1,12},{4,1},{5,0},{8,5},{9,4},{12,9},{13,8},{2,15},{3,14},... | collective-permute-start | bytes 172808 | tf_op jit(solution)/shard_map/ppermute | solution.py:285
  168.7 0.0 collective-permute-done.7.refs_3_
  168.7 0.0 collective-permute-done.8.refs_4_
  168.7 0.0 collective-permute-done.9.refs_5_
  168.7 0.0 collective-permute-done.10.refs_6_
  168.7 2.7 %collective-permute-done.11.refs_7_ = bf16[2,40,360]{2,1,0:T(8,128)(2,1)S(1)} collective-permute-done((bf16[2,40,360]{2,1,0:T(8,128)(2,1)S(1)}, bf16[2,40,360]{2,1,0:T(8,128)(2,1)S(1)}, u32[]{:S(2)}, u32[]{:S(2)}) %collective-permute-start.11) | collective-permute-done | bytes 57632 | tf_op jit(solution)/shard_map/ppermute | solution.py:285
  171.4 4.3 %collective-permute-start.12 = (bf16[8,40,360]{2,1,0:T(8,128)(2,1)S(1)}, bf16[8,40,360]{2,1,0:T(8,128)(2,1)S(1)}, u32[]{:S(2)}, u32[]{:S(2)}) collective-permute-start(bf16[8,40,360]{2,1,0:T(8,128)(2,1)S(1)} %stack_other.1), channel_id=1, source_target_pairs={{0,2},{2,0},{1,3},{3,1},{4,6},{6,4},{5,7},{7,5},{8,10},{10,8},{9,1... | collective-permute-start | bytes 691208 | tf_op jit(solution)/shard_map/ppermute | solution.py:277
  175.7 15.2 %collective-permute-done.12.other_ref = bf16[8,40,360]{2,1,0:T(8,128)(2,1)S(1)} collective-permute-done((bf16[8,40,360]{2,1,0:T(8,128)(2,1)S(1)}, bf16[8,40,360]{2,1,0:T(8,128)(2,1)S(1)}, u32[]{:S(2)}, u32[]{:S(2)}) %collective-permute-start.12) | collective-permute-done | bytes 230432 | tf_op jit(solution)/shard_map/ppermute | solution.py:277
  190.9 0.0 copy-done.4
  190.9 2.2 bring_home.1
  193.1 22.2 %all-to-all-done.3.x_ref = bf16[32,96,360]{2,1,0:T(8,128)(2,1)} async-done(((bf16[32,96,360]{2,1,0:T(8,128)(2,1)}), bf16[32,96,360]{2,1,0:T(8,128)(2,1)}, u32[]{:S(2)}, u32[]{:S(2)}) %all-to-all-start.3) | async-done | bytes 2211872 | tf_op jit(solution)/shard_map/all_to_all | solution.py:289
  215.3 0.7 copy-done.8
  215.9 2.0 sum_terms.1
  217.9 0.8 copy.10
  (5 shorter events, 0.0 us)
Async XLA Ops:
  13.3 4.5 %copy-start.5 = (bf16[1,360,90]{1,2,0:T(8,128)(2,1)S(1)}, bf16[1,360,90]{1,2,0:T(8,128)(2,1)}, u32[]{:S(2)}) copy-start(bf16[1,360,90]{1,2,0:T(8,128)(2,1)} %param.13) | copy-start | bytes 194404
  13.3 69.5 %all-to-all-start = ((bf16[8,40,3456]{2,1,0:T(8,128)(2,1)}), bf16[8,40,3456]{2,1,0:T(8,128)(2,1)S(1)}, u32[]{:S(2)}, u32[]{:S(2)}) async-start(bf16[8,40,3456]{2,1,0:T(8,128)(2,1)} %bitcast.43), calls=%async_computation | async-start | bytes 4423680 | tf_op jit(solution)/shard_map/all_to_all | solution.py:289
  17.7 106.7 %all-gather.2.cloned.1.call-start = ((), (), s32[]{:S(2)}) async-start(), calls=%async_computation.4 | async-start | bytes 2654208 | tf_op jit(solution)/shard_map/all_gather | solution.py:326
  17.8 22.0 %copy-start.3 = (bf16[128,4,360]{0,2,1:T(8,128)(2,1)S(1)}, bf16[128,4,360]{0,2,1:T(8,128)(2,1)}, u32[]{:S(2)}) copy-start(bf16[128,4,360]{0,2,1:T(8,128)(2,1)} %param.8) | copy-start | bytes 1105924
  17.8 21.9 %copy-start.6 = (s32[128,4]{0,1:T(4,128)S(1)}, s32[128,4]{0,1:T(4,128)}, u32[]{:S(2)}) copy-start(s32[128,4]{0,1:T(4,128)} %param.10) | copy-start | bytes 6148
  17.8 21.9 %copy-start.7 = (bf16[128,4]{0,1:T(4,128)(2,1)S(1)}, bf16[128,4]{0,1:T(4,128)(2,1)}, u32[]{:S(2)}) copy-start(bf16[128,4]{0,1:T(4,128)(2,1)} %param.9) | copy-start | bytes 3076
  17.9 6.7 %collective-permute-start = (bf16[96,384]{1,0:T(8,128)(2,1)S(1)}, bf16[96,384]{1,0:T(8,128)(2,1)S(1)}, u32[]{:S(2)}, u32[]{:S(2)}) collective-permute-start(bf16[96,384]{1,0:T(8,128)(2,1)S(1)} %weight_pad.1.mine_ref), channel_id=1, source_target_pairs={{0,16},{16,0},{32,48},{48,32},{1,17},{17,1},{33,49},{49,33},{2,18}... | collective-permute-start | bytes 221192 | tf_op jit(solution)/shard_map/ppermute | solution.py:318
  25.1 11.4 %collective-permute-start.1 = (bf16[192,384]{1,0:T(8,128)(2,1)S(1)}, bf16[192,384]{1,0:T(8,128)(2,1)S(1)}, u32[]{:S(2)}, u32[]{:S(2)}) collective-permute-start(bf16[192,384]{1,0:T(8,128)(2,1)S(1)} %weight_pair.2.mine_ref), channel_id=1, source_target_pairs={{0,32},{16,48},{32,0},{48,16},{1,33},{17,49},{33,1},{49,17},{2,34}... | collective-permute-start | bytes 442376 | tf_op jit(solution)/shard_map/ppermute | solution.py:318
  37.8 42.6 %collective-permute-start.2 = (bf16[1552,128]{1,0:T(8,128)(2,1)S(1)}, bf16[1552,128]{1,0:T(8,128)(2,1)}, u32[]{:S(2)}, u32[]{:S(2)}) collective-permute-start(bf16[1552,128]{1,0:T(8,128)(2,1)S(1)} %get-tuple-element.24.low_ref), channel_id=1, source_target_pairs={{0,2},{2,0},{1,3},{3,1},{4,6},{6,4},{5,7},{7,5},{8,10},{10,8},{9,1... | collective-permute-start | bytes 1191944 | tf_op jit(solution)/shard_map/ppermute | solution.py:277
  40.8 39.6 %collective-permute-start.3 = (bf16[320,384]{1,0:T(8,128)(2,1)S(1)}, bf16[320,384]{1,0:T(8,128)(2,1)S(1)}, u32[]{:S(2)}, u32[]{:S(2)}) collective-permute-start(bf16[320,384]{1,0:T(8,128)(2,1)S(1)} %send_other.1), channel_id=1, source_target_pairs={{0,2},{2,0},{1,3},{3,1},{4,6},{6,4},{5,7},{7,5},{8,10},{10,8},{9,1... | collective-permute-start | bytes 737288 | tf_op jit(solution)/shard_map/ppermute | solution.py:277
  48.5 39.6 %collective-permute-start.4 = (bf16[1536,128]{1,0:T(8,128)(2,1)}, bf16[1536,128]{1,0:T(8,128)(2,1)}, u32[]{:S(2)}, u32[]{:S(2)}) collective-permute-start(bf16[1536,128]{1,0:T(8,128)(2,1)} %get-tuple-element.27.high_ref), channel_id=1, source_target_pairs={{0,2},{2,0},{1,3},{3,1},{4,6},{6,4},{5,7},{7,5},{8,10},{10,8},{9,1... | collective-permute-start | bytes 1179656 | tf_op jit(solution)/shard_map/ppermute | solution.py:277
  82.8 22.0 %all-to-all-start.1 = ((bf16[8,40,1920]{2,1,0:T(8,128)(2,1)}), bf16[8,40,1920]{2,1,0:T(8,128)(2,1)S(1)}, u32[]{:S(2)}, u32[]{:S(2)}) async-start(bf16[8,40,1920]{2,1,0:T(8,128)(2,1)} %bitcast.45), calls=%async_computation.1 | async-start | bytes 2457600 | tf_op jit(solution)/shard_map/all_to_all | solution.py:289
  124.5 1.2 copy-start.1
  129.8 85.4 %all-to-all-start.3 = ((bf16[32,96,360]{2,1,0:T(8,128)(2,1)}), bf16[32,96,360]{2,1,0:T(8,128)(2,1)}, u32[]{:S(2)}, u32[]{:S(2)}) async-start(bf16[32,96,360]{2,1,0:T(8,128)(2,1)} %bitcast.44), calls=%async_computation.3 | async-start | bytes 4718592 | tf_op jit(solution)/shard_map/all_to_all | solution.py:289
  141.5 1.7 copy-start
  143.2 1.2 copy-start.2
  144.4 46.5 %copy-start.4 = (bf16[128,4,360]{0,2,1:T(8,128)(2,1)S(1)}, bf16[128,4,360]{0,2,1:T(8,128)(2,1)}, u32[]{:S(2)}) copy-start(bf16[128,4,360]{0,2,1:T(8,128)(2,1)} %param.8) | copy-start | bytes 1105924
  147.2 14.1 %collective-permute-start.5 = (bf16[2,40,360]{2,1,0:T(8,128)(2,1)S(1)}, bf16[2,40,360]{2,1,0:T(8,128)(2,1)S(1)}, u32[]{:S(2)}, u32[]{:S(2)}) collective-permute-start(bf16[2,40,360]{2,1,0:T(8,128)(2,1)S(1)} %get-tuple-element.30), channel_id=1, source_target_pairs={{0,1},{1,0},{4,5},{5,4},{8,9},{9,8},{12,13},{13,12},{2,3},{3,2},{6... | collective-permute-start | bytes 172808 | tf_op jit(solution)/shard_map/ppermute | solution.py:285
  149.1 16.4 %collective-permute-start.6 = (bf16[2,40,360]{2,1,0:T(8,128)(2,1)S(1)}, bf16[2,40,360]{2,1,0:T(8,128)(2,1)S(1)}, u32[]{:S(2)}, u32[]{:S(2)}) collective-permute-start(bf16[2,40,360]{2,1,0:T(8,128)(2,1)S(1)} %get-tuple-element.31), channel_id=1, source_target_pairs={{0,4},{1,5},{4,8},{5,9},{8,12},{9,13},{12,0},{13,1},{2,6},{3,7},{6... | collective-permute-start | bytes 172808 | tf_op jit(solution)/shard_map/ppermute | solution.py:285
  151.6 17.1 %collective-permute-start.7 = (bf16[2,40,360]{2,1,0:T(8,128)(2,1)S(1)}, bf16[2,40,360]{2,1,0:T(8,128)(2,1)S(1)}, u32[]{:S(2)}, u32[]{:S(2)}) collective-permute-start(bf16[2,40,360]{2,1,0:T(8,128)(2,1)S(1)} %get-tuple-element.32), channel_id=1, source_target_pairs={{0,5},{1,4},{4,9},{5,8},{8,13},{9,12},{12,1},{13,0},{2,7},{3,6},{6... | collective-permute-start | bytes 172808 | tf_op jit(solution)/shard_map/ppermute | solution.py:285
  153.6 15.1 %collective-permute-start.8 = (bf16[2,40,360]{2,1,0:T(8,128)(2,1)S(1)}, bf16[2,40,360]{2,1,0:T(8,128)(2,1)S(1)}, u32[]{:S(2)}, u32[]{:S(2)}) collective-permute-start(bf16[2,40,360]{2,1,0:T(8,128)(2,1)S(1)} %get-tuple-element.33), channel_id=1, source_target_pairs={{0,8},{1,9},{4,12},{5,13},{8,0},{9,1},{12,4},{13,5},{2,10},{3,11},... | collective-permute-start | bytes 172808 | tf_op jit(solution)/shard_map/ppermute | solution.py:285
  159.4 9.3 %collective-permute-start.9 = (bf16[2,40,360]{2,1,0:T(8,128)(2,1)S(1)}, bf16[2,40,360]{2,1,0:T(8,128)(2,1)S(1)}, u32[]{:S(2)}, u32[]{:S(2)}) collective-permute-start(bf16[2,40,360]{2,1,0:T(8,128)(2,1)S(1)} %get-tuple-element.34), channel_id=1, source_target_pairs={{0,9},{1,8},{4,13},{5,12},{8,1},{9,0},{12,5},{13,4},{2,11},{3,10},... | collective-permute-start | bytes 172808 | tf_op jit(solution)/shard_map/ppermute | solution.py:285
  161.3 7.4 %collective-permute-start.10 = (bf16[2,40,360]{2,1,0:T(8,128)(2,1)S(1)}, bf16[2,40,360]{2,1,0:T(8,128)(2,1)S(1)}, u32[]{:S(2)}, u32[]{:S(2)}) collective-permute-start(bf16[2,40,360]{2,1,0:T(8,128)(2,1)S(1)} %get-tuple-element.35), channel_id=1, source_target_pairs={{0,12},{1,13},{4,0},{5,1},{8,4},{9,5},{12,8},{13,9},{2,14},{3,15},... | collective-permute-start | bytes 172808 | tf_op jit(solution)/shard_map/ppermute | solution.py:285
  165.5 5.9 %collective-permute-start.11 = (bf16[2,40,360]{2,1,0:T(8,128)(2,1)S(1)}, bf16[2,40,360]{2,1,0:T(8,128)(2,1)S(1)}, u32[]{:S(2)}, u32[]{:S(2)}) collective-permute-start(bf16[2,40,360]{2,1,0:T(8,128)(2,1)S(1)} %get-tuple-element.36), channel_id=1, source_target_pairs={{0,13},{1,12},{4,1},{5,0},{8,5},{9,4},{12,9},{13,8},{2,15},{3,14},... | collective-permute-start | bytes 172808 | tf_op jit(solution)/shard_map/ppermute | solution.py:285
  171.4 19.5 %collective-permute-start.12 = (bf16[8,40,360]{2,1,0:T(8,128)(2,1)S(1)}, bf16[8,40,360]{2,1,0:T(8,128)(2,1)S(1)}, u32[]{:S(2)}, u32[]{:S(2)}) collective-permute-start(bf16[8,40,360]{2,1,0:T(8,128)(2,1)S(1)} %stack_other.1), channel_id=1, source_target_pairs={{0,2},{2,0},{1,3},{3,1},{4,6},{6,4},{5,7},{7,5},{8,10},{10,8},{9,1... | collective-permute-start | bytes 691208 | tf_op jit(solution)/shard_map/ppermute | solution.py:277
  215.3 0.7 copy-start.8
Sparse Core Ops, SparseCore 0:
  48.7 47.5 all-gather.1

commit v8 on v7

--- a/solution.py
+++ b/solution.py
@@ -21,6 +21,7 @@
 HSLOT = HALF * CAP
 STEP = 768
 HW = 384
+COVER_PAD = 50_000_000_000
 COVER_LOW = 10_000_000_000
 COVER = 50_000_000_000
 BLK = NY * PAD
@@ -167,8 +168,14 @@
         c.wait()
 
 
-def low_kernel(cot_ref, h_ref, out_hbm, scr, sems):
+def low_kernel(cot_ref, out_hbm, scr, sems):
     place = cot_ref[CW:].astype(F32)[:HALF]
+    for c in spread(slot_onehot(place, HALF).astype(BF), (cot_ref,), scr, out_hbm, sems):
+        c.wait()
+
+
+def high_kernel(cot_ref, pm_ref, h_ref, out_hbm, scr, sems):
+    place = pm_ref[CW:].astype(F32)[:HALF]
     copies = spread(slot_onehot(place, HALF).astype(BF), (cot_ref,), scr, out_hbm, sems)
     scr[:, CW:] = h_ref[...]
     send(copies, scr, out_hbm, CW, HW, sems)
@@ -176,14 +183,8 @@
         c.wait()
 
 
-def high_kernel(cot_ref, pm_ref, out_hbm, scr, sems):
-    place = pm_ref[CW:].astype(F32)[:HALF]
-    for c in spread(slot_onehot(place, HALF).astype(BF), (cot_ref,), scr, out_hbm, sems):
-        c.wait()
-
-
 def term_kernel(own_ref, low_ref, high_ref, _, out_hbm, scr, sems):
-    hid = [own_ref[:, WIDE:], low_ref[:, CW:]]
+    hid = [own_ref[:, WIDE:], high_ref[:, CW:]]
     gate = [h[:, FFW : FFW + 1].astype(F32) for h in hid]
     copies = []
     for z in range(NZ):
@@ -209,20 +210,15 @@
     out_ref[...] = v[:OWN]
 
 
-def pad_kernel(w_ref, out_ref):
+def pad_kernel(w_ref, _, out_ref):
     out_ref[...] = jnp.zeros((PAD, HW), BF)
     out_ref[:OWN, :FFW] = w_ref[...]
 
 
-def merge_kernel(bit):
-    def body(pos_ref, mine_ref, other_ref, *refs):
-        out_ref = refs[-1]
-        i = (pos_ref[1] >> bit) & 1
-        n = mine_ref.shape[0]
-        out_ref[pl.ds(pl.multiple_of(i * n, n), n)] = mine_ref[...]
-        out_ref[pl.ds(pl.multiple_of((1 - i) * n, n), n)] = other_ref[...]
-
-    return body
+def weight_kernel(pos_ref, *refs):
+    out_ref = refs[NY]
+    for j in range(NY):
+        out_ref[(pos_ref[1] + NY - j) % NY] = refs[j][...]
 
 
 def peer(pos_ref, r, sign):
@@ -233,7 +229,7 @@
 def back_kernel(pos_ref, own_ref, low_ref, high_ref, w_ref, *refs):
     outs, scr = refs[:HALF], refs[HALF]
     for i in range(2):
-        parts = (own_ref[:, :CW], own_ref[:, CW:WIDE]) if i == 0 else (low_ref[:, :CW], high_ref[...])
+        parts = (own_ref[:, :CW], own_ref[:, CW:WIDE]) if i == 0 else (low_ref[...], high_ref[:, :CW])
         acc = lax.dot_general(parts[0], w_ref[:CW, :FFW], NN, preferred_element_type=F32)
         scr[...] = acc + lax.dot_general(
             parts[1], w_ref[CW:, :FFW], NN, preferred_element_type=F32
@@ -297,6 +293,7 @@
     rt = routing.T
 
     low, high, pm = prep(pos, resp_lengths, advantage, gt, rt)
+    low_par = shift(low, "yh", 2, 1)
     own = call(
         own_kernel,
         "send_own",
@@ -312,21 +309,18 @@
         where=ANY,
     )(pos, *(pltpu.with_memory_space_constraint(v, pltpu.HBM) for v in (ht, gates, rt)), pm, low, high)[0]
 
-    weight = call(pad_kernel, "weight_pad", [VMEM], [((PAD, HW), BF)])(w_down[0].T)[0]
+
     ready = pltpu.with_memory_space_constraint(own, pltpu.HBM)
-    for bit in range(2):
-        other = lax.ppermute(weight, "yl", [(i, i ^ (1 << bit)) for i in range(NY)])
-        weight = call(
-            merge_kernel(bit),
-            "weight_pair",
-            [SMEM] + [VMEM] * 2 + [ANY],
-            [((2 * weight.shape[0], HW), BF)],
-        )(pos, weight, other, ready)[0]
-    pair = weight
-    weight = lax.all_gather(weight, "z", axis=0, tiled=True)
-
-    low_out, high_out, pm_out, _ = lax.optimization_barrier((low, high, pm, pair))
-    low_par = shift(low_out, "yh", 2, 1)
+    wt = call(pad_kernel, "weight_pad", [VMEM, ANY], [((PAD, HW), BF)], weight=COVER_PAD)(
+        w_down[0].T, ready
+    )[0]
+    parts = [wt] + [shift(wt, "yl", NY, j) for j in range(1, NY)]
+    w4 = call(weight_kernel, "weight_part", [SMEM] + [VMEM] * NY, [((NY, PAD, HW), BF)])(
+        pos, *parts
+    )[0].reshape(NY * PAD, HW)
+    weight = lax.all_gather(w4, "z", axis=0, tiled=True)
+
+    high_out, pm_out, _, _ = lax.optimization_barrier((high, pm, low_par, w4))
     high_par = shift(high_out, "yh", 2, 1)
     hid_par = call(other_kernel, "send_other", [SMEM] + [VMEM] * 4, [((HSLOT, HW), BF)])(
         pos, ht, gates, rt, pm_out
@@ -342,22 +336,22 @@
     par_low = call(
         low_kernel,
         "send_low",
-        [VMEM] * 2,
-        [((HSLOT, CW + HW), BF)],
-        spread_scratch(CW + HW),
+        [VMEM],
+        [((HSLOT, CW), BF)],
+        spread_scratch(CW),
         where=ANY,
         weight=COVER_LOW,
-    )(low_par, hid_par)[0]
+    )(low_par)[0]
     par_low = forward(par_low, own)
     par_high = call(
         high_kernel,
         "send_high",
-        [VMEM] * 2,
-        [((HSLOT, CW), BF)],
-        spread_scratch(CW),
+        [VMEM] * 3,
+        [((HSLOT, CW + HW), BF)],
+        spread_scratch(CW + HW),
         where=ANY,
         weight=COVER,
-    )(high_par, low_par)[0]
+    )(high_par, low_par, hid_par)[0]
     par_high = forward(par_high, par_low)
 
     terms = call(

time: 227 us -> 207 us (0.912)
  waiting for transfers between devices: 97.8 us -> 62 us
  starting transfers between devices: 63.2 us -> 76.8 us
    all_to_all x3, waiting for transfers between devices: 36.4 us -> 23.8 us  [exchange(): return lax.all_to_all(x, axes, split_axis=0, concat_axis=0, tiled=True)]
    ppermute x2 -> x0, waiting for transfers between devices: 12.6 us -> none  [local(): other = lax.ppermute(weight, 'yl', [(i, i ^ 1 << bit) for i in range(NY)])]
    ppermute x4 -> x7, starting transfers between devices: 16.1 us -> 27.9 us  [shift(): return lax.ppermute(x, axis, [(i, (i + by) % n) for i in range(n)])]
    ppermute x4 -> x7, waiting for transfers between devices: 46.1 us -> 35.6 us  [shift(): return lax.ppermute(x, axis, [(i, (i + by) % n) for i in range(n)])]
    all_to_all x3, starting transfers between devices: 20.3 us -> 27.4 us  [exchange(): return lax.all_to_all(x, axes, split_axis=0, concat_axis=0, tiled=True)]
    ppermute x2 -> x0, starting transfers between devices: 5.41 us -> none  [local(): other = lax.ppermute(weight, 'yl', [(i, i ^ 1 << bit) for i in range(NY)])]
    unnamed x19 -> x21, local copies, waits for them, and re-layouts: 5.57 us -> 6.57 us
    pallas_call x5 -> x4, Pallas kernels: 6.8 us -> 6.28 us  [the longest x1 2.6 us: local(): call(high_kernel, 'send_high', [VMEM] * 3, [((HSLOT, CW + HW), BF)], spre...]
  transfers between devices with their start and end apart: 17 -> 18, of which waited for: 8 -> 8; matrix products, arithmetic and copies ran while one was open for 0% -> 0% of each run, Pallas kernels for 6% -> 8%
where the time goes in v8:
time: 207 us; the launch traced here: 206 us
  starting transfers between devices  76.8 us (37%)
  waiting for transfers between devices  62 us (30%)
  Pallas kernels  24.4 us (12%)
  blocking collectives  21.5 us (10%)
  between operations  14.4 us (7%)
  local copies, waits for them, and re-layouts  6.65 us (3%)
    ppermute x7, waiting for transfers between devices, shift(): return lax.ppermute(x, axis, [(i, (i + by) % n) for i in range(n)])  35.6 us
    ppermute x7, starting transfers between devices, shift(): return lax.ppermute(x, axis, [(i, (i + by) % n) for i in range(n)])  27.9 us
    all_to_all x3, starting transfers between devices, exchange(): return lax.all_to_all(x, axes, split_axis=0, concat_axis=0, tiled=True)  27.4 us
    all_to_all x3, waiting for transfers between devices, exchange(): return lax.all_to_all(x, axes, split_axis=0, concat_axis=0, tiled=True)  23.8 us
    all_to_all x1, blocking collectives, exchange(): return lax.all_to_all(x, axes, split_axis=0, concat_axis=0, tiled=True)  21.5 us
    ppermute x7, starting transfers between devices, to_peer(): return lax.ppermute(x, ('x', 'c'), pairs)  21.4 us
    unnamed x21, local copies, waits for them, and re-layouts  6.57 us
    pallas_call x1, Pallas kernels, local(): call(term_kernel, 'grad_term', [VMEM] * 3 + [ANY], [((WIDE, FFW), BF)], [...  4.16 us
  transfers between devices with their start and end apart: 18, of which 8 were waited for; matrix products, arithmetic and copies ran while one was open for 0% of the time, Pallas kernels for 8%

profile of v8, /device:TPU:96, one launch (start us, length us, event | category | flops | bytes accessed | tf_op | source)
XLA Modules:
  0.0 205.7 jit_solution(13675461767417305678)
XLA Ops:
  7.2 0.1 stack.23.pos_ref
  7.3 2.7 %prep.1 = (bf16[1552,128]{1,0:T(8,128)(2,1)S(1)}, bf16[1536,128]{1,0:T(8,128)(2,1)}, f32[16,128]{1,0:T(8,128)S(1)}) custom-call(s32[5]{0:T(128)S(1)} %stack.23.pos_ref, s32[1,4]{1,0:T(1,128)} %len_hbm.1, f32[1,4]{1,0:T(1,128)} %adv_hbm.1, bf16[2880,128]{1,0:T(8,128)(2,1)} %bitcast.48, s32[4,128]{1,0:T(4,128)} %bitcast.35), custom_call_target="tpu_custom_call" | custom-call | tf_op jit(solution)/shard_map/prep/pallas_call | solution.py:111
  10.0 2.0 collective-permute-start
  12.0 3.3 %send_own.1._ = bf16[320,3456]{1,0:T(8,128)(2,1)} custom-call(s32[5]{0:T(128)S(1)} %stack.23.pos_ref, bf16[4,360,128]{2,1,0:T(8,128)(2,1)} %bitcast.31, bf16[4,128]{1,0:T(4,128)(2,1)} %bitcast.39, s32[4,128]{1,0:T(4,128)} %bitcast.36, f32[16,128]{1,0:T(8,128)S(1)} %get-tuple-element.25.pm_ref, bf16[1552,128]{1,0:T(8,128)(2,1)S(1)} %get-tuple-element.21.low_ref, ...), custom_call_target="tpu_custom_call" | custom-call | tf_op jit(solution)/shard_map/send_own/pallas_call | solution.py:297
  15.3 0.0 copy-start.9
  15.3 4.4 %all-to-all-start = ((bf16[8,40,3456]{2,1,0:T(8,128)(2,1)}), bf16[8,40,3456]{2,1,0:T(8,128)(2,1)S(1)}, u32[]{:S(2)}, u32[]{:S(2)}) async-start(bf16[8,40,3456]{2,1,0:T(8,128)(2,1)} %bitcast.45), calls=%async_computation | async-start | bytes 4423680 | tf_op jit(solution)/shard_map/all_to_all | solution.py:285
  19.8 0.0 all-gather.2.cloned.1.call-start
  19.8 0.0 copy-done.9
  19.8 0.0 copy-start.4
  19.8 0.0 copy-start.6
  19.9 0.0 copy-start.7
  19.9 5.6 %collective-permute-start.3 = (bf16[96,384]{1,0:T(8,128)(2,1)S(1)}, bf16[96,384]{1,0:T(8,128)(2,1)S(1)}, u32[]{:S(2)}, u32[]{:S(2)}) collective-permute-start(bf16[96,384]{1,0:T(8,128)(2,1)S(1)} %weight_pad.1.refs_0_), channel_id=1, source_target_pairs={{0,48},{16,0},{32,16},{48,32},{1,49},{17,1},{33,17},{49,33},{2,50}... | collective-permute-start | bytes 221192 | tf_op jit(solution)/shard_map/ppermute | solution.py:273
  25.5 1.9 collective-permute-start.2
  27.5 2.9 %collective-permute-start.1 = (bf16[96,384]{1,0:T(8,128)(2,1)S(1)}, bf16[96,384]{1,0:T(8,128)(2,1)S(1)}, u32[]{:S(2)}, u32[]{:S(2)}) collective-permute-start(bf16[96,384]{1,0:T(8,128)(2,1)S(1)} %weight_pad.1.refs_0_), channel_id=1, source_target_pairs={{0,16},{16,32},{32,48},{48,0},{1,17},{17,33},{33,49},{49,1},{2,18}... | collective-permute-start | bytes 221192 | tf_op jit(solution)/shard_map/ppermute | solution.py:273
  30.4 1.6 collective-permute-done.3.refs_3_
  32.0 7.3 %collective-permute-done.2.refs_2_ = bf16[96,384]{1,0:T(8,128)(2,1)S(1)} collective-permute-done((bf16[96,384]{1,0:T(8,128)(2,1)S(1)}, bf16[96,384]{1,0:T(8,128)(2,1)S(1)}, u32[]{:S(2)}, u32[]{:S(2)}) %collective-permute-start.2) | collective-permute-done | bytes 73760 | tf_op jit(solution)/shard_map/ppermute | solution.py:273
  39.4 0.0 collective-permute-done.1.refs_1_
  39.4 1.3 weight_part.1
  40.7 0.0 all-gather.2.cloned.1.call-update
  40.7 0.0 collective-permute-done.cot_ref.pm_ref
  40.7 0.0 copy-done.4
  40.7 0.0 copy-done.6
  40.7 0.0 copy-done.7
  40.7 0.9 send_other.1
  41.7 5.0 %collective-permute-start.5 = (bf16[320,384]{1,0:T(8,128)(2,1)S(1)}, bf16[320,384]{1,0:T(8,128)(2,1)}, u32[]{:S(2)}, u32[]{:S(2)}) collective-permute-start(bf16[320,384]{1,0:T(8,128)(2,1)S(1)} %send_other.1), channel_id=1, source_target_pairs={{0,2},{2,0},{1,3},{3,1},{4,6},{6,4},{5,7},{7,5},{8,10},{10,8},{9,1... | collective-permute-start | bytes 737288 | tf_op jit(solution)/shard_map/ppermute | solution.py:273
  46.7 4.7 %collective-permute-start.4 = (bf16[1536,128]{1,0:T(8,128)(2,1)}, bf16[1536,128]{1,0:T(8,128)(2,1)}, u32[]{:S(2)}, u32[]{:S(2)}) collective-permute-start(bf16[1536,128]{1,0:T(8,128)(2,1)} %get-tuple-element.24.high_ref), channel_id=1, source_target_pairs={{0,2},{2,0},{1,3},{3,1},{4,6},{6,4},{5,7},{7,5},{8,10},{10,8},{9,1... | collective-permute-start | bytes 1179656 | tf_op jit(solution)/shard_map/ppermute | solution.py:273
  51.5 2.4 %send_low.1 = bf16[320,1536]{1,0:T(8,128)(2,1)} custom-call(bf16[1552,128]{1,0:T(8,128)(2,1)} %collective-permute-done.cot_ref.pm_ref), custom_call_target="tpu_custom_call" | custom-call | flops 10000000000 | tf_op jit(solution)/shard_map/send_low/pallas_call | solution.py:336
  53.8 0.0 all-to-all-done
  53.8 4.3 %all-to-all-start.1 = ((bf16[8,40,1536]{2,1,0:T(8,128)(2,1)}), bf16[8,40,1536]{2,1,0:T(8,128)(2,1)S(1)}, u32[]{:S(2)}, u32[]{:S(2)}) async-start(bf16[8,40,1536]{2,1,0:T(8,128)(2,1)} %bitcast.47), calls=%async_computation.1 | async-start | bytes 1966080 | tf_op jit(solution)/shard_map/all_to_all | solution.py:285
  58.2 0.3 collective-permute-done.5.h_ref
  58.4 10.6 %collective-permute-done.4.cot_ref = bf16[1536,128]{1,0:T(8,128)(2,1)} collective-permute-done((bf16[1536,128]{1,0:T(8,128)(2,1)}, bf16[1536,128]{1,0:T(8,128)(2,1)}, u32[]{:S(2)}, u32[]{:S(2)}) %collective-permute-start.4) | collective-permute-done | bytes 393248 | tf_op jit(solution)/shard_map/ppermute | solution.py:273
  69.0 2.6 %send_high.1 = bf16[320,1920]{1,0:T(8,128)(2,1)} custom-call(bf16[1536,128]{1,0:T(8,128)(2,1)} %collective-permute-done.4.cot_ref, bf16[1552,128]{1,0:T(8,128)(2,1)} %collective-permute-done.cot_ref.pm_ref, bf16[320,384]{1,0:T(8,128)(2,1)} %collective-permute-done.5.h_ref), custom_call_target="tpu_custom_call" | custom-call | flops 49999998976 | tf_op jit(solution)/shard_map/send_high/pallas_call | solution.py:346
  71.6 1.8 all-to-all-done.1
  73.4 1.0 copy-done.1
  74.4 21.5 %all_to_all.20 = bf16[8,40,1920]{2,1,0:T(8,128)(2,1)S(1)} all-to-all(bf16[8,40,1920]{2,1,0:T(8,128)(2,1)} %bitcast.46), channel_id=1, replica_groups=mesh['z'=8,'yl'=4,'x'=4,'yh'=2,'c'=2] {'x','c'}, dimensions={0} | all-to-all | bytes 2457600 | tf_op jit(solution)/shard_map/all_to_all | solution.py:285
  95.9 1.2 copy-done.2
  97.1 4.2 %grad_term.1 = bf16[3072,360]{1,0:T(8,128)(2,1)} custom-call(bf16[320,3456]{1,0:T(8,128)(2,1)S(1)} %bitcast.25, bf16[320,1536]{1,0:T(8,128)(2,1)S(1)} %bitcast.29, bf16[320,1920]{1,0:T(8,128)(2,1)S(1)} %bitcast.27, bf16[3072,384]{1,0:T(8,128)(2,1)} %all-gather.2.cloned.1.call-done._.w_ref), custom_call_target="tpu_custom_call" | custom-call | tf_op jit(solution)/shard_map/grad_term/pallas_call | solution.py:357
  101.3 18.6 %all-to-all-start.3 = ((bf16[32,96,360]{2,1,0:T(8,128)(2,1)}), bf16[32,96,360]{2,1,0:T(8,128)(2,1)}, u32[]{:S(2)}, u32[]{:S(2)}) async-start(bf16[32,96,360]{2,1,0:T(8,128)(2,1)} %bitcast.44), calls=%async_computation.3 | async-start | bytes 4718592 | tf_op jit(solution)/shard_map/all_to_all | solution.py:285
  120.0 0.0 copy-start
  120.0 1.7 copy-done
  121.6 1.2 copy-done.3
  122.8 2.8 %back_product.1 = (bf16[2,40,360]{2,1,0:T(8,128)(2,1)S(1)}, bf16[2,40,360]{2,1,0:T(8,128)(2,1)S(1)}, bf16[2,40,360]{2,1,0:T(8,128)(2,1)S(1)}, bf16[2,40,360]{2,1...) custom-call(s32[5]{0:T(128)S(1)} %stack.23.pos_ref, ...), custom_call_target="tpu_custom_call" | custom-call | tf_op jit(solution)/shard_map/back_product/pallas_call | solution.py:368
  125.6 1.9 collective-permute-start.6
  127.5 2.5 %collective-permute-start.7 = (bf16[2,40,360]{2,1,0:T(8,128)(2,1)S(1)}, bf16[2,40,360]{2,1,0:T(8,128)(2,1)S(1)}, u32[]{:S(2)}, u32[]{:S(2)}) collective-permute-start(bf16[2,40,360]{2,1,0:T(8,128)(2,1)S(1)} %get-tuple-element.29), channel_id=1, source_target_pairs={{0,4},{1,5},{4,8},{5,9},{8,12},{9,13},{12,0},{13,1},{2,6},{3,7},{6... | collective-permute-start | bytes 172808 | tf_op jit(solution)/shard_map/ppermute | solution.py:281
  130.0 2.0 collective-permute-start.8
  132.0 5.8 %collective-permute-start.9 = (bf16[2,40,360]{2,1,0:T(8,128)(2,1)S(1)}, bf16[2,40,360]{2,1,0:T(8,128)(2,1)S(1)}, u32[]{:S(2)}, u32[]{:S(2)}) collective-permute-start(bf16[2,40,360]{2,1,0:T(8,128)(2,1)S(1)} %get-tuple-element.31), channel_id=1, source_target_pairs={{0,8},{1,9},{4,12},{5,13},{8,0},{9,1},{12,4},{13,5},{2,10},{3,11},... | collective-permute-start | bytes 172808 | tf_op jit(solution)/shard_map/ppermute | solution.py:281
  137.8 1.9 collective-permute-start.10
  139.7 0.0 collective-permute-done.6.refs_1_
  139.7 4.1 %collective-permute-start.11 = (bf16[2,40,360]{2,1,0:T(8,128)(2,1)S(1)}, bf16[2,40,360]{2,1,0:T(8,128)(2,1)S(1)}, u32[]{:S(2)}, u32[]{:S(2)}) collective-permute-start(bf16[2,40,360]{2,1,0:T(8,128)(2,1)S(1)} %get-tuple-element.33), channel_id=1, source_target_pairs={{0,12},{1,13},{4,0},{5,1},{8,4},{9,5},{12,8},{13,9},{2,14},{3,15},... | collective-permute-start | bytes 172808 | tf_op jit(solution)/shard_map/ppermute | solution.py:281
  143.9 0.0 collective-permute-done.7.refs_2_
  143.9 3.2 %collective-permute-start.12 = (bf16[2,40,360]{2,1,0:T(8,128)(2,1)S(1)}, bf16[2,40,360]{2,1,0:T(8,128)(2,1)S(1)}, u32[]{:S(2)}, u32[]{:S(2)}) collective-permute-start(bf16[2,40,360]{2,1,0:T(8,128)(2,1)S(1)} %get-tuple-element.34), channel_id=1, source_target_pairs={{0,13},{1,12},{4,1},{5,0},{8,5},{9,4},{12,9},{13,8},{2,15},{3,14},... | collective-permute-start | bytes 172808 | tf_op jit(solution)/shard_map/ppermute | solution.py:281
  147.1 0.0 collective-permute-done.8.refs_3_
  147.1 0.0 collective-permute-done.9.refs_4_
  147.1 0.0 collective-permute-done.10.refs_5_
  147.1 0.0 collective-permute-done.11.refs_6_
  147.1 2.6 %collective-permute-done.12.refs_7_ = bf16[2,40,360]{2,1,0:T(8,128)(2,1)S(1)} collective-permute-done((bf16[2,40,360]{2,1,0:T(8,128)(2,1)S(1)}, bf16[2,40,360]{2,1,0:T(8,128)(2,1)S(1)}, u32[]{:S(2)}, u32[]{:S(2)}) %collective-permute-start.12) | collective-permute-done | bytes 57632 | tf_op jit(solution)/shard_map/ppermute | solution.py:281
  149.8 5.7 %collective-permute-start.13 = (bf16[8,40,360]{2,1,0:T(8,128)(2,1)S(1)}, bf16[8,40,360]{2,1,0:T(8,128)(2,1)S(1)}, u32[]{:S(2)}, u32[]{:S(2)}) collective-permute-start(bf16[8,40,360]{2,1,0:T(8,128)(2,1)S(1)} %stack_other.1), channel_id=1, source_target_pairs={{0,2},{2,0},{1,3},{3,1},{4,6},{6,4},{5,7},{7,5},{8,10},{10,8},{9,1... | collective-permute-start | bytes 691208 | tf_op jit(solution)/shard_map/ppermute | solution.py:273
  155.5 15.8 %collective-permute-done.13.other_ref = bf16[8,40,360]{2,1,0:T(8,128)(2,1)S(1)} collective-permute-done((bf16[8,40,360]{2,1,0:T(8,128)(2,1)S(1)}, bf16[8,40,360]{2,1,0:T(8,128)(2,1)S(1)}, u32[]{:S(2)}, u32[]{:S(2)}) %collective-permute-start.13) | collective-permute-done | bytes 230432 | tf_op jit(solution)/shard_map/ppermute | solution.py:273
  171.3 0.0 copy-done.5
  171.3 2.2 %bring_home.1 = (f32[4,360,128]{2,1,0:T(8,128)}, f32[4,128]{1,0:T(4,128)}) custom-call(s32[5]{0:T(128)S(1)} %stack.23.pos_ref, bf16[4,360,128]{2,1,0:T(8,128)(2,1)S(1)} %bitcast.33, bf16[4,128]{1,0:T(4,128)(2,1)S(1)} %bitcast.41, f32[16,128]{1,0:T(8,128)S(1)} %get-tuple-element.25.pm_ref, s32[4,128]{1,0:T(4,128)S(1)} %bitcast.38, ...), custom_call_target="tpu_custom_call" | custom-call | tf_op jit(solution)/shard_map/bring_home/pallas_call | solution.py:379
  173.5 22.0 %all-to-all-done.3.x_ref = bf16[32,96,360]{2,1,0:T(8,128)(2,1)} async-done(((bf16[32,96,360]{2,1,0:T(8,128)(2,1)}), bf16[32,96,360]{2,1,0:T(8,128)(2,1)}, u32[]{:S(2)}, u32[]{:S(2)}) %all-to-all-start.3) | async-done | bytes 2211872 | tf_op jit(solution)/shard_map/all_to_all | solution.py:285
  195.4 0.7 copy-done.8
  196.1 2.0 sum_terms.1
  198.1 0.8 copy.10
  (8 shorter events, 0.0 us)
Async XLA Ops:
  10.0 30.7 %collective-permute-start = (bf16[1552,128]{1,0:T(8,128)(2,1)S(1)}, bf16[1552,128]{1,0:T(8,128)(2,1)}, u32[]{:S(2)}, u32[]{:S(2)}) collective-permute-start(bf16[1552,128]{1,0:T(8,128)(2,1)S(1)} %get-tuple-element.21.low_ref), channel_id=1, source_target_pairs={{0,2},{2,0},{1,3},{3,1},{4,6},{6,4},{5,7},{7,5},{8,10},{10,8},{9,1... | collective-permute-start | bytes 1191944 | tf_op jit(solution)/shard_map/ppermute | solution.py:273
  15.3 4.5 %copy-start.9 = (bf16[1,360,90]{1,2,0:T(8,128)(2,1)S(1)}, bf16[1,360,90]{1,2,0:T(8,128)(2,1)}, u32[]{:S(2)}) copy-start(bf16[1,360,90]{1,2,0:T(8,128)(2,1)} %param.13) | copy-start | bytes 194404
  15.3 38.5 %all-to-all-start = ((bf16[8,40,3456]{2,1,0:T(8,128)(2,1)}), bf16[8,40,3456]{2,1,0:T(8,128)(2,1)S(1)}, u32[]{:S(2)}, u32[]{:S(2)}) async-start(bf16[8,40,3456]{2,1,0:T(8,128)(2,1)} %bitcast.45), calls=%async_computation | async-start | bytes 4423680 | tf_op jit(solution)/shard_map/all_to_all | solution.py:285
  19.8 76.2 %all-gather.2.cloned.1.call-start = ((), (), s32[]{:S(2)}) async-start(), calls=%async_computation.4 | async-start | bytes 2654208 | tf_op jit(solution)/shard_map/all_gather | solution.py:321
  19.8 20.9 %copy-start.4 = (bf16[128,4,360]{0,2,1:T(8,128)(2,1)S(1)}, bf16[128,4,360]{0,2,1:T(8,128)(2,1)}, u32[]{:S(2)}) copy-start(bf16[128,4,360]{0,2,1:T(8,128)(2,1)} %param.8) | copy-start | bytes 1105924
  19.8 20.9 %copy-start.6 = (s32[128,4]{0,1:T(4,128)S(1)}, s32[128,4]{0,1:T(4,128)}, u32[]{:S(2)}) copy-start(s32[128,4]{0,1:T(4,128)} %param.10) | copy-start | bytes 6148
  19.9 20.9 %copy-start.7 = (bf16[128,4]{0,1:T(4,128)(2,1)S(1)}, bf16[128,4]{0,1:T(4,128)(2,1)}, u32[]{:S(2)}) copy-start(bf16[128,4]{0,1:T(4,128)(2,1)} %param.9) | copy-start | bytes 3076
  19.9 12.1 %collective-permute-start.3 = (bf16[96,384]{1,0:T(8,128)(2,1)S(1)}, bf16[96,384]{1,0:T(8,128)(2,1)S(1)}, u32[]{:S(2)}, u32[]{:S(2)}) collective-permute-start(bf16[96,384]{1,0:T(8,128)(2,1)S(1)} %weight_pad.1.refs_0_), channel_id=1, source_target_pairs={{0,48},{16,0},{32,16},{48,32},{1,49},{17,1},{33,17},{49,33},{2,50}... | collective-permute-start | bytes 221192 | tf_op jit(solution)/shard_map/ppermute | solution.py:273
  25.5 13.8 %collective-permute-start.2 = (bf16[96,384]{1,0:T(8,128)(2,1)S(1)}, bf16[96,384]{1,0:T(8,128)(2,1)S(1)}, u32[]{:S(2)}, u32[]{:S(2)}) collective-permute-start(bf16[96,384]{1,0:T(8,128)(2,1)S(1)} %weight_pad.1.refs_0_), channel_id=1, source_target_pairs={{0,32},{16,48},{32,0},{48,16},{1,33},{17,49},{33,1},{49,17},{2,34}... | collective-permute-start | bytes 221192 | tf_op jit(solution)/shard_map/ppermute | solution.py:273
  27.5 11.9 %collective-permute-start.1 = (bf16[96,384]{1,0:T(8,128)(2,1)S(1)}, bf16[96,384]{1,0:T(8,128)(2,1)S(1)}, u32[]{:S(2)}, u32[]{:S(2)}) collective-permute-start(bf16[96,384]{1,0:T(8,128)(2,1)S(1)} %weight_pad.1.refs_0_), channel_id=1, source_target_pairs={{0,16},{16,32},{32,48},{48,0},{1,17},{17,33},{33,49},{49,1},{2,18}... | collective-permute-start | bytes 221192 | tf_op jit(solution)/shard_map/ppermute | solution.py:273
  41.7 16.7 %collective-permute-start.5 = (bf16[320,384]{1,0:T(8,128)(2,1)S(1)}, bf16[320,384]{1,0:T(8,128)(2,1)}, u32[]{:S(2)}, u32[]{:S(2)}) collective-permute-start(bf16[320,384]{1,0:T(8,128)(2,1)S(1)} %send_other.1), channel_id=1, source_target_pairs={{0,2},{2,0},{1,3},{3,1},{4,6},{6,4},{5,7},{7,5},{8,10},{10,8},{9,1... | collective-permute-start | bytes 737288 | tf_op jit(solution)/shard_map/ppermute | solution.py:273
  46.7 22.3 %collective-permute-start.4 = (bf16[1536,128]{1,0:T(8,128)(2,1)}, bf16[1536,128]{1,0:T(8,128)(2,1)}, u32[]{:S(2)}, u32[]{:S(2)}) collective-permute-start(bf16[1536,128]{1,0:T(8,128)(2,1)} %get-tuple-element.24.high_ref), channel_id=1, source_target_pairs={{0,2},{2,0},{1,3},{3,1},{4,6},{6,4},{5,7},{7,5},{8,10},{10,8},{9,1... | collective-permute-start | bytes 1179656 | tf_op jit(solution)/shard_map/ppermute | solution.py:273
  53.8 19.6 %all-to-all-start.1 = ((bf16[8,40,1536]{2,1,0:T(8,128)(2,1)}), bf16[8,40,1536]{2,1,0:T(8,128)(2,1)S(1)}, u32[]{:S(2)}, u32[]{:S(2)}) async-start(bf16[8,40,1536]{2,1,0:T(8,128)(2,1)} %bitcast.47), calls=%async_computation.1 | async-start | bytes 1966080 | tf_op jit(solution)/shard_map/all_to_all | solution.py:285
  73.4 1.0 copy-start.1
  95.9 1.2 copy-start.2
  101.3 94.1 %all-to-all-start.3 = ((bf16[32,96,360]{2,1,0:T(8,128)(2,1)}), bf16[32,96,360]{2,1,0:T(8,128)(2,1)}, u32[]{:S(2)}, u32[]{:S(2)}) async-start(bf16[32,96,360]{2,1,0:T(8,128)(2,1)} %bitcast.44), calls=%async_computation.3 | async-start | bytes 4718592 | tf_op jit(solution)/shard_map/all_to_all | solution.py:285
  120.0 1.7 copy-start
  121.6 1.2 copy-start.3
  122.8 48.4 %copy-start.5 = (bf16[128,4,360]{0,2,1:T(8,128)(2,1)S(1)}, bf16[128,4,360]{0,2,1:T(8,128)(2,1)}, u32[]{:S(2)}) copy-start(bf16[128,4,360]{0,2,1:T(8,128)(2,1)} %param.8) | copy-start | bytes 1105924
  125.6 14.1 %collective-permute-start.6 = (bf16[2,40,360]{2,1,0:T(8,128)(2,1)S(1)}, bf16[2,40,360]{2,1,0:T(8,128)(2,1)S(1)}, u32[]{:S(2)}, u32[]{:S(2)}) collective-permute-start(bf16[2,40,360]{2,1,0:T(8,128)(2,1)S(1)} %get-tuple-element.28), channel_id=1, source_target_pairs={{0,1},{1,0},{4,5},{5,4},{8,9},{9,8},{12,13},{13,12},{2,3},{3,2},{6... | collective-permute-start | bytes 172808 | tf_op jit(solution)/shard_map/ppermute | solution.py:281
  127.5 16.4 %collective-permute-start.7 = (bf16[2,40,360]{2,1,0:T(8,128)(2,1)S(1)}, bf16[2,40,360]{2,1,0:T(8,128)(2,1)S(1)}, u32[]{:S(2)}, u32[]{:S(2)}) collective-permute-start(bf16[2,40,360]{2,1,0:T(8,128)(2,1)S(1)} %get-tuple-element.29), channel_id=1, source_target_pairs={{0,4},{1,5},{4,8},{5,9},{8,12},{9,13},{12,0},{13,1},{2,6},{3,7},{6... | collective-permute-start | bytes 172808 | tf_op jit(solution)/shard_map/ppermute | solution.py:281
  130.0 17.1 %collective-permute-start.8 = (bf16[2,40,360]{2,1,0:T(8,128)(2,1)S(1)}, bf16[2,40,360]{2,1,0:T(8,128)(2,1)S(1)}, u32[]{:S(2)}, u32[]{:S(2)}) collective-permute-start(bf16[2,40,360]{2,1,0:T(8,128)(2,1)S(1)} %get-tuple-element.30), channel_id=1, source_target_pairs={{0,5},{1,4},{4,9},{5,8},{8,13},{9,12},{12,1},{13,0},{2,7},{3,6},{6... | collective-permute-start | bytes 172808 | tf_op jit(solution)/shard_map/ppermute | solution.py:281
  132.0 15.1 %collective-permute-start.9 = (bf16[2,40,360]{2,1,0:T(8,128)(2,1)S(1)}, bf16[2,40,360]{2,1,0:T(8,128)(2,1)S(1)}, u32[]{:S(2)}, u32[]{:S(2)}) collective-permute-start(bf16[2,40,360]{2,1,0:T(8,128)(2,1)S(1)} %get-tuple-element.31), channel_id=1, source_target_pairs={{0,8},{1,9},{4,12},{5,13},{8,0},{9,1},{12,4},{13,5},{2,10},{3,11},... | collective-permute-start | bytes 172808 | tf_op jit(solution)/shard_map/ppermute | solution.py:281
  137.8 9.3 %collective-permute-start.10 = (bf16[2,40,360]{2,1,0:T(8,128)(2,1)S(1)}, bf16[2,40,360]{2,1,0:T(8,128)(2,1)S(1)}, u32[]{:S(2)}, u32[]{:S(2)}) collective-permute-start(bf16[2,40,360]{2,1,0:T(8,128)(2,1)S(1)} %get-tuple-element.32), channel_id=1, source_target_pairs={{0,9},{1,8},{4,13},{5,12},{8,1},{9,0},{12,5},{13,4},{2,11},{3,10},... | collective-permute-start | bytes 172808 | tf_op jit(solution)/shard_map/ppermute | solution.py:281
  139.7 7.4 %collective-permute-start.11 = (bf16[2,40,360]{2,1,0:T(8,128)(2,1)S(1)}, bf16[2,40,360]{2,1,0:T(8,128)(2,1)S(1)}, u32[]{:S(2)}, u32[]{:S(2)}) collective-permute-start(bf16[2,40,360]{2,1,0:T(8,128)(2,1)S(1)} %get-tuple-element.33), channel_id=1, source_target_pairs={{0,12},{1,13},{4,0},{5,1},{8,4},{9,5},{12,8},{13,9},{2,14},{3,15},... | collective-permute-start | bytes 172808 | tf_op jit(solution)/shard_map/ppermute | solution.py:281
  143.9 5.9 %collective-permute-start.12 = (bf16[2,40,360]{2,1,0:T(8,128)(2,1)S(1)}, bf16[2,40,360]{2,1,0:T(8,128)(2,1)S(1)}, u32[]{:S(2)}, u32[]{:S(2)}) collective-permute-start(bf16[2,40,360]{2,1,0:T(8,128)(2,1)S(1)} %get-tuple-element.34), channel_id=1, source_target_pairs={{0,13},{1,12},{4,1},{5,0},{8,5},{9,4},{12,9},{13,8},{2,15},{3,14},... | collective-permute-start | bytes 172808 | tf_op jit(solution)/shard_map/ppermute | solution.py:281
  149.8 21.4 %collective-permute-start.13 = (bf16[8,40,360]{2,1,0:T(8,128)(2,1)S(1)}, bf16[8,40,360]{2,1,0:T(8,128)(2,1)S(1)}, u32[]{:S(2)}, u32[]{:S(2)}) collective-permute-start(bf16[8,40,360]{2,1,0:T(8,128)(2,1)S(1)} %stack_other.1), channel_id=1, source_target_pairs={{0,2},{2,0},{1,3},{3,1},{4,6},{6,4},{5,7},{7,5},{8,10},{10,8},{9,1... | collective-permute-start | bytes 691208 | tf_op jit(solution)/shard_map/ppermute | solution.py:273
  195.4 0.7 copy-start.8
Sparse Core Ops, SparseCore 0:
  40.8 47.8 all-gather.1

commit v9 on v8

--- a/solution.py
+++ b/solution.py
@@ -183,11 +183,15 @@
         c.wait()
 
 
-def term_kernel(own_ref, low_ref, high_ref, _, out_hbm, scr, sems):
+def term_kernel(own_ref, low_hbm, high_ref, _, out_hbm, low_ref, scr, sems):
+    load = pltpu.make_async_copy(low_hbm, low_ref, sems.at[NZ])
+    load.start()
     hid = [own_ref[:, WIDE:], high_ref[:, CW:]]
     gate = [h[:, FFW : FFW + 1].astype(F32) for h in hid]
     copies = []
-    for z in range(NZ):
+    for z in [*range(NZ // 2, NZ), *range(NZ // 2)]:
+        if z == 0:
+            load.wait()
         acc = jnp.zeros((BLK, FFW), F32)
         at = z * BLK
         cots = [own_ref[:, at : at + BLK]]
@@ -203,7 +207,7 @@
         c.wait()
 
 
-def sum_kernel(x_ref, _, out_ref):
+def sum_kernel(x_ref, out_ref):
     v = x_ref[0].astype(F32)
     for d in range(1, NDP):
         v = v + x_ref[d].astype(F32)
@@ -273,6 +277,10 @@
     return lax.ppermute(x, axis, [(i, (i + by) % n) for i in range(n)])
 
 
+def held(x):
+    return pltpu.with_memory_space_constraint(x, pltpu.HBM)
+
+
 def to_peer(x, r):
     dx, dc = r // 2, r % 2
     if r == 0:
@@ -320,7 +328,7 @@
     )[0].reshape(NY * PAD, HW)
     weight = lax.all_gather(w4, "z", axis=0, tiled=True)
 
-    high_out, pm_out, _, _ = lax.optimization_barrier((high, pm, low_par, w4))
+    high_out, pm_out, _ = lax.optimization_barrier((high, pm, own))
     high_par = shift(high_out, "yh", 2, 1)
     hid_par = call(other_kernel, "send_other", [SMEM] + [VMEM] * 4, [((HSLOT, HW), BF)])(
         pos, ht, gates, rt, pm_out
@@ -357,12 +365,16 @@
     terms = call(
         term_kernel,
         "grad_term",
-        [VMEM] * 3 + [ANY],
+        [VMEM, ANY, VMEM, ANY],
         [((WIDE, FFW), BF)],
-        [pltpu.VMEM((WIDE, FFW), BF), pltpu.SemaphoreType.DMA((NZ,))],
+        [
+            pltpu.VMEM((HSLOT, CW), BF),
+            pltpu.VMEM((WIDE, FFW), BF),
+            pltpu.SemaphoreType.DMA((NZ + 1,)),
+        ],
         mib=20,
         where=ANY,
-    )(own, par_low, par_high, pltpu.with_memory_space_constraint(weight, pltpu.HBM))[0]
+    )(own, held(par_low), par_high, held(weight))[0]
     terms = exchange(terms.reshape(NDP, PAD, FFW), ("z", "yl"))
 
     backs = call(
@@ -382,7 +394,8 @@
         [SMEM] + [VMEM] * (5 + HALF),
         [((TOPK, FFW, ROWS), F32), ((TOPK, ROWS), F32)],
     )(pos, ht, gates, pm, rt, other, *backs)
-    gd = call(sum_kernel, "sum_terms", [VMEM, ANY], [((OWN, FFW), F32)])(terms, gg)[0]
+    terms, gg = lax.optimization_barrier((terms, gg))
+    gd = call(sum_kernel, "sum_terms", [VMEM], [((OWN, FFW), F32)])(terms)[0]
     return gd.T[None], jnp.transpose(gh, (2, 0, 1)), gg.T
 
 

time: 207 us -> 201 us (0.971)
  starting transfers between devices: 76.8 us -> 64.7 us
  waiting for transfers between devices: 62 us -> 69.9 us
    ppermute x7, waiting for transfers between devices: 35.6 us -> 19.1 us  [shift(): return lax.ppermute(x, axis, [(i, (i + by) % n) for i in range(n)])]
    all_gather x1, waiting for transfers between devices: 0.01 us -> 13.6 us  [local(): weight = lax.all_gather(w4, 'z', axis=0, tiled=True)]
    all_to_all x3, starting transfers between devices: 27.4 us -> 15.3 us  [exchange(): return lax.all_to_all(x, axes, split_axis=0, concat_axis=0, tiled=True)]
    all_to_all x3, waiting for transfers between devices: 23.8 us -> 34.5 us  [exchange(): return lax.all_to_all(x, axes, split_axis=0, concat_axis=0, tiled=True)]
  transfers between devices with their start and end apart: 18 -> 18, of which waited for: 8 -> 7; matrix products, arithmetic and copies ran while one was open for 0% -> 0% of each run, Pallas kernels for 8% -> 7%
where the time goes in v9:
time: 201 us; the launch traced here: 200 us
  waiting for transfers between devices  69.9 us (35%)
  starting transfers between devices  64.7 us (32%)
  Pallas kernels  23.4 us (12%)
  blocking collectives  21.5 us (11%)
  between operations  14.4 us (7%)
  local copies, waits for them, and re-layouts  5.77 us (3%)
    all_to_all x3, waiting for transfers between devices, exchange(): return lax.all_to_all(x, axes, split_axis=0, concat_axis=0, tiled=True)  34.5 us
    ppermute x7, starting transfers between devices, shift(): return lax.ppermute(x, axis, [(i, (i + by) % n) for i in range(n)])  27.9 us
    all_to_all x1, blocking collectives, exchange(): return lax.all_to_all(x, axes, split_axis=0, concat_axis=0, tiled=True)  21.5 us
    ppermute x7, starting transfers between devices, to_peer(): return lax.ppermute(x, ('x', 'c'), pairs)  21.4 us
    ppermute x7, waiting for transfers between devices, shift(): return lax.ppermute(x, axis, [(i, (i + by) % n) for i in range(n)])  19.1 us
    all_to_all x3, starting transfers between devices, exchange(): return lax.all_to_all(x, axes, split_axis=0, concat_axis=0, tiled=True)  15.3 us
    all_gather x1, waiting for transfers between devices, local(): weight = lax.all_gather(w4, 'z', axis=0, tiled=True)  13.6 us
    unnamed x21, local copies, waits for them, and re-layouts  5.69 us
  transfers between devices with their start and end apart: 18, of which 7 were waited for; matrix products, arithmetic and copies ran while one was open for 0% of the time, Pallas kernels for 7%

profile of v9, /device:TPU:96, one launch (start us, length us, event | category | flops | bytes accessed | tf_op | source)
XLA Modules:
  0.0 199.7 jit_solution(3331989936059915407)
XLA Ops:
  7.2 0.1 stack.23.pos_ref
  7.3 2.7 %prep.1 = (bf16[1552,128]{1,0:T(8,128)(2,1)S(1)}, bf16[1536,128]{1,0:T(8,128)(2,1)}, f32[16,128]{1,0:T(8,128)S(1)}) custom-call(s32[5]{0:T(128)S(1)} %stack.23.pos_ref, s32[1,4]{1,0:T(1,128)} %len_hbm.1, f32[1,4]{1,0:T(1,128)} %adv_hbm.1, bf16[2880,128]{1,0:T(8,128)(2,1)} %bitcast.47, s32[4,128]{1,0:T(4,128)} %bitcast.35), custom_call_target="tpu_custom_call" | custom-call | tf_op jit(solution)/shard_map/prep/pallas_call | solution.py:111
  10.0 2.0 %collective-permute-start = (bf16[1552,128]{1,0:T(8,128)(2,1)S(1)}, bf16[1552,128]{1,0:T(8,128)(2,1)S(1)}, u32[]{:S(2)}, u32[]{:S(2)}) collective-permute-start(bf16[1552,128]{1,0:T(8,128)(2,1)S(1)} %get-tuple-element.23.low_ref), channel_id=1, source_target_pairs={{0,2},{2,0},{1,3},{3,1},{4,6},{6,4},{5,7},{7,5},{8,10},{10,8},{9,1... | collective-permute-start | bytes 1191944 | tf_op jit(solution)/shard_map/ppermute | solution.py:277
  12.0 3.3 %send_own.1._ = bf16[320,3456]{1,0:T(8,128)(2,1)} custom-call(s32[5]{0:T(128)S(1)} %stack.23.pos_ref, bf16[4,360,128]{2,1,0:T(8,128)(2,1)} %bitcast.31, bf16[4,128]{1,0:T(4,128)(2,1)} %bitcast.39, s32[4,128]{1,0:T(4,128)} %bitcast.36, f32[16,128]{1,0:T(8,128)S(1)} %get-tuple-element.27.pm_ref, bf16[1552,128]{1,0:T(8,128)(2,1)S(1)} %get-tuple-element.23.low_ref, ...), custom_call_target="tpu_custom_call" | custom-call | tf_op jit(solution)/shard_map/send_own/pallas_call | solution.py:305
  15.3 0.0 copy-start.9
  15.3 4.4 %all-to-all-start = ((bf16[8,40,3456]{2,1,0:T(8,128)(2,1)}), bf16[8,40,3456]{2,1,0:T(8,128)(2,1)S(1)}, u32[]{:S(2)}, u32[]{:S(2)}) async-start(bf16[8,40,3456]{2,1,0:T(8,128)(2,1)} %bitcast.44), calls=%async_computation | async-start | bytes 4423680 | tf_op jit(solution)/shard_map/all_to_all | solution.py:293
  19.8 0.0 all-gather.2.cloned.1.call-start
  19.8 0.0 copy-done.9
  19.8 0.0 copy-start.3
  19.9 0.0 copy-start.5
  19.9 0.0 copy-start.6
  19.9 5.6 %collective-permute-start.5 = (bf16[96,384]{1,0:T(8,128)(2,1)S(1)}, bf16[96,384]{1,0:T(8,128)(2,1)S(1)}, u32[]{:S(2)}, u32[]{:S(2)}) collective-permute-start(bf16[96,384]{1,0:T(8,128)(2,1)S(1)} %weight_pad.1.refs_0_), channel_id=1, source_target_pairs={{0,48},{16,0},{32,16},{48,32},{1,49},{17,1},{33,17},{49,33},{2,50}... | collective-permute-start | bytes 221192 | tf_op jit(solution)/shard_map/ppermute | solution.py:277
  25.6 1.9 collective-permute-start.4
  27.5 2.9 %collective-permute-start.3 = (bf16[96,384]{1,0:T(8,128)(2,1)S(1)}, bf16[96,384]{1,0:T(8,128)(2,1)S(1)}, u32[]{:S(2)}, u32[]{:S(2)}) collective-permute-start(bf16[96,384]{1,0:T(8,128)(2,1)S(1)} %weight_pad.1.refs_0_), channel_id=1, source_target_pairs={{0,16},{16,32},{32,48},{48,0},{1,17},{17,33},{33,49},{49,1},{2,18}... | collective-permute-start | bytes 221192 | tf_op jit(solution)/shard_map/ppermute | solution.py:277
  30.4 0.0 copy-done.3
  30.4 1.0 send_other.1
  31.4 5.9 %collective-permute-start.2 = (bf16[320,384]{1,0:T(8,128)(2,1)S(1)}, bf16[320,384]{1,0:T(8,128)(2,1)}, u32[]{:S(2)}, u32[]{:S(2)}) collective-permute-start(bf16[320,384]{1,0:T(8,128)(2,1)S(1)} %send_other.1), channel_id=1, source_target_pairs={{0,2},{2,0},{1,3},{3,1},{4,6},{6,4},{5,7},{7,5},{8,10},{10,8},{9,1... | collective-permute-start | bytes 737288 | tf_op jit(solution)/shard_map/ppermute | solution.py:277
  37.3 0.0 collective-permute-done.5.refs_3_
  37.3 3.8 %collective-permute-start.1 = (bf16[1536,128]{1,0:T(8,128)(2,1)}, bf16[1536,128]{1,0:T(8,128)(2,1)}, u32[]{:S(2)}, u32[]{:S(2)}) collective-permute-start(bf16[1536,128]{1,0:T(8,128)(2,1)} %get-tuple-element.26.high_ref), channel_id=1, source_target_pairs={{0,2},{2,0},{1,3},{3,1},{4,6},{6,4},{5,7},{7,5},{8,10},{10,8},{9,1... | collective-permute-start | bytes 1179656 | tf_op jit(solution)/shard_map/ppermute | solution.py:277
  41.2 0.0 collective-permute-done.4.refs_2_
  41.2 0.0 collective-permute-done.3.refs_1_
  41.2 1.3 weight_part.1
  42.5 0.0 all-gather.2.cloned.1.call-update
  42.5 0.0 collective-permute-done.cot_ref.pm_ref
  42.5 0.0 copy-start.7
  42.5 1.4 send_low.1
  43.9 0.0 copy-done.7
  43.9 4.3 %all-to-all-done = bf16[8,40,3456]{2,1,0:T(8,128)(2,1)S(1)} async-done(((bf16[8,40,3456]{2,1,0:T(8,128)(2,1)}), bf16[8,40,3456]{2,1,0:T(8,128)(2,1)S(1)}, u32[]{:S(2)}, u32[]{:S(2)}) %all-to-all-start) | async-done | bytes 2211872 | tf_op jit(solution)/shard_map/all_to_all | solution.py:293
  48.2 3.6 %all-to-all-start.1 = ((bf16[8,40,1536]{2,1,0:T(8,128)(2,1)}), bf16[8,40,1536]{2,1,0:T(8,128)(2,1)S(1)}, u32[]{:S(2)}, u32[]{:S(2)}) async-start(bf16[8,40,1536]{2,1,0:T(8,128)(2,1)} %bitcast.46), calls=%async_computation.1 | async-start | bytes 1966080 | tf_op jit(solution)/shard_map/all_to_all | solution.py:293
  51.8 0.0 collective-permute-done.2.h_ref
  51.8 3.3 %collective-permute-done.1.cot_ref = bf16[1536,128]{1,0:T(8,128)(2,1)} collective-permute-done((bf16[1536,128]{1,0:T(8,128)(2,1)}, bf16[1536,128]{1,0:T(8,128)(2,1)}, u32[]{:S(2)}, u32[]{:S(2)}) %collective-permute-start.1) | collective-permute-done | bytes 393248 | tf_op jit(solution)/shard_map/ppermute | solution.py:277
  55.1 1.0 copy-done.8
  56.1 2.5 %send_high.1 = bf16[320,1920]{1,0:T(8,128)(2,1)} custom-call(bf16[1536,128]{1,0:T(8,128)(2,1)} %collective-permute-done.1.cot_ref, bf16[1552,128]{1,0:T(8,128)(2,1)S(1)} %copy-done.8, bf16[320,384]{1,0:T(8,128)(2,1)} %collective-permute-done.2.h_ref), custom_call_target="tpu_custom_call" | custom-call | flops 49999998976 | tf_op jit(solution)/shard_map/send_high/pallas_call | solution.py:354
  58.6 8.4 %all-to-all-done.1 = bf16[8,40,1536]{2,1,0:T(8,128)(2,1)S(1)} async-done(((bf16[8,40,1536]{2,1,0:T(8,128)(2,1)}), bf16[8,40,1536]{2,1,0:T(8,128)(2,1)S(1)}, u32[]{:S(2)}, u32[]{:S(2)}) %all-to-all-start.1) | async-done | bytes 983072 | tf_op jit(solution)/shard_map/all_to_all | solution.py:293
  67.0 1.0 copy-done.1
  68.0 21.5 %all_to_all.20 = bf16[8,40,1920]{2,1,0:T(8,128)(2,1)S(1)} all-to-all(bf16[8,40,1920]{2,1,0:T(8,128)(2,1)} %bitcast.45), channel_id=1, replica_groups=mesh['z'=8,'yl'=4,'x'=4,'yh'=2,'c'=2] {'x','c'}, dimensions={0} | all-to-all | bytes 2457600 | tf_op jit(solution)/shard_map/all_to_all | solution.py:293
  89.5 13.6 %all-gather.2.cloned.1.call-done._.w_ref = bf16[3072,384]{1,0:T(8,128)(2,1)} async-done(((bf16[384,384]{1,0:T(8,128)(2,1)}), bf16[3072,384]{1,0:T(8,128)(2,1)}) %all-gather.2.cloned.1.call-update) | async-done | bytes 2359312 | tf_op jit(solution)/shard_map/all_gather | solution.py:329
  103.1 4.2 %grad_term.1 = bf16[3072,360]{1,0:T(8,128)(2,1)} custom-call(bf16[320,3456]{1,0:T(8,128)(2,1)S(1)} %bitcast.25, bf16[320,1536]{1,0:T(8,128)(2,1)} %bitcast.29, bf16[320,1920]{1,0:T(8,128)(2,1)S(1)} %bitcast.27, bf16[3072,384]{1,0:T(8,128)(2,1)} %all-gather.2.cloned.1.call-done._.w_ref), custom_call_target="tpu_custom_call" | custom-call | tf_op jit(solution)/shard_map/grad_term/pallas_call | solution.py:365
  107.3 7.3 %all-to-all-start.3 = ((bf16[32,96,360]{2,1,0:T(8,128)(2,1)}), bf16[32,96,360]{2,1,0:T(8,128)(2,1)}, u32[]{:S(2)}, u32[]{:S(2)}) async-start(bf16[32,96,360]{2,1,0:T(8,128)(2,1)} %bitcast.43), calls=%async_computation.3 | async-start | bytes 4718592 | tf_op jit(solution)/shard_map/all_to_all | solution.py:293
  114.6 0.0 copy-start
  114.6 1.7 copy-done
  116.3 1.2 copy-done.2
  117.5 2.8 %back_product.1 = (bf16[2,40,360]{2,1,0:T(8,128)(2,1)S(1)}, bf16[2,40,360]{2,1,0:T(8,128)(2,1)S(1)}, bf16[2,40,360]{2,1,0:T(8,128)(2,1)S(1)}, bf16[2,40,360]{2,1...) custom-call(s32[5]{0:T(128)S(1)} %stack.23.pos_ref, ...), custom_call_target="tpu_custom_call" | custom-call | tf_op jit(solution)/shard_map/back_product/pallas_call | solution.py:380
  120.3 1.9 collective-permute-start.6
  122.2 2.5 %collective-permute-start.7 = (bf16[2,40,360]{2,1,0:T(8,128)(2,1)S(1)}, bf16[2,40,360]{2,1,0:T(8,128)(2,1)S(1)}, u32[]{:S(2)}, u32[]{:S(2)}) collective-permute-start(bf16[2,40,360]{2,1,0:T(8,128)(2,1)S(1)} %get-tuple-element.31), channel_id=1, source_target_pairs={{0,4},{1,5},{4,8},{5,9},{8,12},{9,13},{12,0},{13,1},{2,6},{3,7},{6... | collective-permute-start | bytes 172808 | tf_op jit(solution)/shard_map/ppermute | solution.py:289
  124.7 2.7 %collective-permute-start.8 = (bf16[2,40,360]{2,1,0:T(8,128)(2,1)S(1)}, bf16[2,40,360]{2,1,0:T(8,128)(2,1)S(1)}, u32[]{:S(2)}, u32[]{:S(2)}) collective-permute-start(bf16[2,40,360]{2,1,0:T(8,128)(2,1)S(1)} %get-tuple-element.32), channel_id=1, source_target_pairs={{0,5},{1,4},{4,9},{5,8},{8,13},{9,12},{12,1},{13,0},{2,7},{3,6},{6... | collective-permute-start | bytes 172808 | tf_op jit(solution)/shard_map/ppermute | solution.py:289
  127.3 5.1 %collective-permute-start.9 = (bf16[2,40,360]{2,1,0:T(8,128)(2,1)S(1)}, bf16[2,40,360]{2,1,0:T(8,128)(2,1)S(1)}, u32[]{:S(2)}, u32[]{:S(2)}) collective-permute-start(bf16[2,40,360]{2,1,0:T(8,128)(2,1)S(1)} %get-tuple-element.33), channel_id=1, source_target_pairs={{0,8},{1,9},{4,12},{5,13},{8,0},{9,1},{12,4},{13,5},{2,10},{3,11},... | collective-permute-start | bytes 172808 | tf_op jit(solution)/shard_map/ppermute | solution.py:289
  132.5 1.9 collective-permute-start.10
  134.4 0.0 collective-permute-done.6.refs_1_
  134.4 4.1 %collective-permute-start.11 = (bf16[2,40,360]{2,1,0:T(8,128)(2,1)S(1)}, bf16[2,40,360]{2,1,0:T(8,128)(2,1)S(1)}, u32[]{:S(2)}, u32[]{:S(2)}) collective-permute-start(bf16[2,40,360]{2,1,0:T(8,128)(2,1)S(1)} %get-tuple-element.35), channel_id=1, source_target_pairs={{0,12},{1,13},{4,0},{5,1},{8,4},{9,5},{12,8},{13,9},{2,14},{3,15},... | collective-permute-start | bytes 172808 | tf_op jit(solution)/shard_map/ppermute | solution.py:289
  138.6 0.0 collective-permute-done.7.refs_2_
  138.6 3.2 %collective-permute-start.12 = (bf16[2,40,360]{2,1,0:T(8,128)(2,1)S(1)}, bf16[2,40,360]{2,1,0:T(8,128)(2,1)S(1)}, u32[]{:S(2)}, u32[]{:S(2)}) collective-permute-start(bf16[2,40,360]{2,1,0:T(8,128)(2,1)S(1)} %get-tuple-element.36), channel_id=1, source_target_pairs={{0,13},{1,12},{4,1},{5,0},{8,5},{9,4},{12,9},{13,8},{2,15},{3,14},... | collective-permute-start | bytes 172808 | tf_op jit(solution)/shard_map/ppermute | solution.py:289
  141.8 0.0 collective-permute-done.8.refs_3_
  141.8 0.0 collective-permute-done.9.refs_4_
  141.8 0.0 collective-permute-done.10.refs_5_
  141.8 0.0 collective-permute-done.11.refs_6_
  141.8 2.6 %collective-permute-done.12.refs_7_ = bf16[2,40,360]{2,1,0:T(8,128)(2,1)S(1)} collective-permute-done((bf16[2,40,360]{2,1,0:T(8,128)(2,1)S(1)}, bf16[2,40,360]{2,1,0:T(8,128)(2,1)S(1)}, u32[]{:S(2)}, u32[]{:S(2)}) %collective-permute-start.12) | collective-permute-done | bytes 57632 | tf_op jit(solution)/shard_map/ppermute | solution.py:289
  144.5 5.7 %collective-permute-start.13 = (bf16[8,40,360]{2,1,0:T(8,128)(2,1)S(1)}, bf16[8,40,360]{2,1,0:T(8,128)(2,1)S(1)}, u32[]{:S(2)}, u32[]{:S(2)}) collective-permute-start(bf16[8,40,360]{2,1,0:T(8,128)(2,1)S(1)} %stack_other.1), channel_id=1, source_target_pairs={{0,2},{2,0},{1,3},{3,1},{4,6},{6,4},{5,7},{7,5},{8,10},{10,8},{9,1... | collective-permute-start | bytes 691208 | tf_op jit(solution)/shard_map/ppermute | solution.py:277
  150.2 15.8 %collective-permute-done.13.other_ref = bf16[8,40,360]{2,1,0:T(8,128)(2,1)S(1)} collective-permute-done((bf16[8,40,360]{2,1,0:T(8,128)(2,1)S(1)}, bf16[8,40,360]{2,1,0:T(8,128)(2,1)S(1)}, u32[]{:S(2)}, u32[]{:S(2)}) %collective-permute-start.13) | collective-permute-done | bytes 230432 | tf_op jit(solution)/shard_map/ppermute | solution.py:277
  166.0 0.0 copy-done.4
  166.0 2.2 %bring_home.1 = (f32[4,360,128]{2,1,0:T(8,128)}, f32[4,128]{1,0:T(4,128)}) custom-call(s32[5]{0:T(128)S(1)} %stack.23.pos_ref, bf16[4,360,128]{2,1,0:T(8,128)(2,1)S(1)} %bitcast.33, bf16[4,128]{1,0:T(4,128)(2,1)S(1)} %bitcast.41, f32[16,128]{1,0:T(8,128)S(1)} %get-tuple-element.27.pm_ref, s32[4,128]{1,0:T(4,128)S(1)} %bitcast.38, ...), custom_call_target="tpu_custom_call" | custom-call | tf_op jit(solution)/shard_map/bring_home/pallas_call | solution.py:391
  168.2 21.8 %all-to-all-done.3.x_ref = bf16[32,96,360]{2,1,0:T(8,128)(2,1)} async-done(((bf16[32,96,360]{2,1,0:T(8,128)(2,1)}), bf16[32,96,360]{2,1,0:T(8,128)(2,1)}, u32[]{:S(2)}, u32[]{:S(2)}) %all-to-all-start.3) | async-done | bytes 2211872 | tf_op jit(solution)/shard_map/all_to_all | solution.py:293
  190.0 2.0 sum_terms.1
  192.0 0.8 copy.10
  (8 shorter events, 0.0 us)
Async XLA Ops:
  10.0 32.5 %collective-permute-start = (bf16[1552,128]{1,0:T(8,128)(2,1)S(1)}, bf16[1552,128]{1,0:T(8,128)(2,1)S(1)}, u32[]{:S(2)}, u32[]{:S(2)}) collective-permute-start(bf16[1552,128]{1,0:T(8,128)(2,1)S(1)} %get-tuple-element.23.low_ref), channel_id=1, source_target_pairs={{0,2},{2,0},{1,3},{3,1},{4,6},{6,4},{5,7},{7,5},{8,10},{10,8},{9,1... | collective-permute-start | bytes 1191944 | tf_op jit(solution)/shard_map/ppermute | solution.py:277
  15.3 4.5 %copy-start.9 = (bf16[1,360,90]{1,2,0:T(8,128)(2,1)S(1)}, bf16[1,360,90]{1,2,0:T(8,128)(2,1)}, u32[]{:S(2)}) copy-start(bf16[1,360,90]{1,2,0:T(8,128)(2,1)} %param.13) | copy-start | bytes 194404
  15.3 32.9 %all-to-all-start = ((bf16[8,40,3456]{2,1,0:T(8,128)(2,1)}), bf16[8,40,3456]{2,1,0:T(8,128)(2,1)S(1)}, u32[]{:S(2)}, u32[]{:S(2)}) async-start(bf16[8,40,3456]{2,1,0:T(8,128)(2,1)} %bitcast.44), calls=%async_computation | async-start | bytes 4423680 | tf_op jit(solution)/shard_map/all_to_all | solution.py:293
  19.8 83.3 %all-gather.2.cloned.1.call-start = ((), (), s32[]{:S(2)}) async-start(), calls=%async_computation.4 | async-start | bytes 2654208 | tf_op jit(solution)/shard_map/all_gather | solution.py:329
  19.8 10.6 %copy-start.3 = (bf16[128,4,360]{0,2,1:T(8,128)(2,1)S(1)}, bf16[128,4,360]{0,2,1:T(8,128)(2,1)}, u32[]{:S(2)}) copy-start(bf16[128,4,360]{0,2,1:T(8,128)(2,1)} %param.8) | copy-start | bytes 1105924
  19.9 10.6 %copy-start.5 = (s32[128,4]{0,1:T(4,128)S(1)}, s32[128,4]{0,1:T(4,128)}, u32[]{:S(2)}) copy-start(s32[128,4]{0,1:T(4,128)} %param.10) | copy-start | bytes 6148
  19.9 10.6 %copy-start.6 = (bf16[128,4]{0,1:T(4,128)(2,1)S(1)}, bf16[128,4]{0,1:T(4,128)(2,1)}, u32[]{:S(2)}) copy-start(bf16[128,4]{0,1:T(4,128)(2,1)} %param.9) | copy-start | bytes 3076
  19.9 17.4 %collective-permute-start.5 = (bf16[96,384]{1,0:T(8,128)(2,1)S(1)}, bf16[96,384]{1,0:T(8,128)(2,1)S(1)}, u32[]{:S(2)}, u32[]{:S(2)}) collective-permute-start(bf16[96,384]{1,0:T(8,128)(2,1)S(1)} %weight_pad.1.refs_0_), channel_id=1, source_target_pairs={{0,48},{16,0},{32,16},{48,32},{1,49},{17,1},{33,17},{49,33},{2,50}... | collective-permute-start | bytes 221192 | tf_op jit(solution)/shard_map/ppermute | solution.py:277
  25.6 15.6 %collective-permute-start.4 = (bf16[96,384]{1,0:T(8,128)(2,1)S(1)}, bf16[96,384]{1,0:T(8,128)(2,1)S(1)}, u32[]{:S(2)}, u32[]{:S(2)}) collective-permute-start(bf16[96,384]{1,0:T(8,128)(2,1)S(1)} %weight_pad.1.refs_0_), channel_id=1, source_target_pairs={{0,32},{16,48},{32,0},{48,16},{1,33},{17,49},{33,1},{49,17},{2,34}... | collective-permute-start | bytes 221192 | tf_op jit(solution)/shard_map/ppermute | solution.py:277
  27.5 13.7 %collective-permute-start.3 = (bf16[96,384]{1,0:T(8,128)(2,1)S(1)}, bf16[96,384]{1,0:T(8,128)(2,1)S(1)}, u32[]{:S(2)}, u32[]{:S(2)}) collective-permute-start(bf16[96,384]{1,0:T(8,128)(2,1)S(1)} %weight_pad.1.refs_0_), channel_id=1, source_target_pairs={{0,16},{16,32},{32,48},{48,0},{1,17},{17,33},{33,49},{49,1},{2,18}... | collective-permute-start | bytes 221192 | tf_op jit(solution)/shard_map/ppermute | solution.py:277
  31.4 20.4 %collective-permute-start.2 = (bf16[320,384]{1,0:T(8,128)(2,1)S(1)}, bf16[320,384]{1,0:T(8,128)(2,1)}, u32[]{:S(2)}, u32[]{:S(2)}) collective-permute-start(bf16[320,384]{1,0:T(8,128)(2,1)S(1)} %send_other.1), channel_id=1, source_target_pairs={{0,2},{2,0},{1,3},{3,1},{4,6},{6,4},{5,7},{7,5},{8,10},{10,8},{9,1... | collective-permute-start | bytes 737288 | tf_op jit(solution)/shard_map/ppermute | solution.py:277
  37.3 17.7 %collective-permute-start.1 = (bf16[1536,128]{1,0:T(8,128)(2,1)}, bf16[1536,128]{1,0:T(8,128)(2,1)}, u32[]{:S(2)}, u32[]{:S(2)}) collective-permute-start(bf16[1536,128]{1,0:T(8,128)(2,1)} %get-tuple-element.26.high_ref), channel_id=1, source_target_pairs={{0,2},{2,0},{1,3},{3,1},{4,6},{6,4},{5,7},{7,5},{8,10},{10,8},{9,1... | collective-permute-start | bytes 1179656 | tf_op jit(solution)/shard_map/ppermute | solution.py:277
  42.5 1.4 copy-start.7
  48.2 18.7 %all-to-all-start.1 = ((bf16[8,40,1536]{2,1,0:T(8,128)(2,1)}), bf16[8,40,1536]{2,1,0:T(8,128)(2,1)S(1)}, u32[]{:S(2)}, u32[]{:S(2)}) async-start(bf16[8,40,1536]{2,1,0:T(8,128)(2,1)} %bitcast.46), calls=%async_computation.1 | async-start | bytes 1966080 | tf_op jit(solution)/shard_map/all_to_all | solution.py:293
  55.1 1.0 copy-start.8
  67.0 1.0 copy-start.1
  107.3 82.7 %all-to-all-start.3 = ((bf16[32,96,360]{2,1,0:T(8,128)(2,1)}), bf16[32,96,360]{2,1,0:T(8,128)(2,1)}, u32[]{:S(2)}, u32[]{:S(2)}) async-start(bf16[32,96,360]{2,1,0:T(8,128)(2,1)} %bitcast.43), calls=%async_computation.3 | async-start | bytes 4718592 | tf_op jit(solution)/shard_map/all_to_all | solution.py:293
  114.6 1.7 copy-start
  116.3 1.2 copy-start.2
  117.5 48.5 %copy-start.4 = (bf16[128,4,360]{0,2,1:T(8,128)(2,1)S(1)}, bf16[128,4,360]{0,2,1:T(8,128)(2,1)}, u32[]{:S(2)}) copy-start(bf16[128,4,360]{0,2,1:T(8,128)(2,1)} %param.8) | copy-start | bytes 1105924
  120.3 14.1 %collective-permute-start.6 = (bf16[2,40,360]{2,1,0:T(8,128)(2,1)S(1)}, bf16[2,40,360]{2,1,0:T(8,128)(2,1)S(1)}, u32[]{:S(2)}, u32[]{:S(2)}) collective-permute-start(bf16[2,40,360]{2,1,0:T(8,128)(2,1)S(1)} %get-tuple-element.30), channel_id=1, source_target_pairs={{0,1},{1,0},{4,5},{5,4},{8,9},{9,8},{12,13},{13,12},{2,3},{3,2},{6... | collective-permute-start | bytes 172808 | tf_op jit(solution)/shard_map/ppermute | solution.py:289
  122.2 16.4 %collective-permute-start.7 = (bf16[2,40,360]{2,1,0:T(8,128)(2,1)S(1)}, bf16[2,40,360]{2,1,0:T(8,128)(2,1)S(1)}, u32[]{:S(2)}, u32[]{:S(2)}) collective-permute-start(bf16[2,40,360]{2,1,0:T(8,128)(2,1)S(1)} %get-tuple-element.31), channel_id=1, source_target_pairs={{0,4},{1,5},{4,8},{5,9},{8,12},{9,13},{12,0},{13,1},{2,6},{3,7},{6... | collective-permute-start | bytes 172808 | tf_op jit(solution)/shard_map/ppermute | solution.py:289
  124.7 17.1 %collective-permute-start.8 = (bf16[2,40,360]{2,1,0:T(8,128)(2,1)S(1)}, bf16[2,40,360]{2,1,0:T(8,128)(2,1)S(1)}, u32[]{:S(2)}, u32[]{:S(2)}) collective-permute-start(bf16[2,40,360]{2,1,0:T(8,128)(2,1)S(1)} %get-tuple-element.32), channel_id=1, source_target_pairs={{0,5},{1,4},{4,9},{5,8},{8,13},{9,12},{12,1},{13,0},{2,7},{3,6},{6... | collective-permute-start | bytes 172808 | tf_op jit(solution)/shard_map/ppermute | solution.py:289
  127.3 14.4 %collective-permute-start.9 = (bf16[2,40,360]{2,1,0:T(8,128)(2,1)S(1)}, bf16[2,40,360]{2,1,0:T(8,128)(2,1)S(1)}, u32[]{:S(2)}, u32[]{:S(2)}) collective-permute-start(bf16[2,40,360]{2,1,0:T(8,128)(2,1)S(1)} %get-tuple-element.33), channel_id=1, source_target_pairs={{0,8},{1,9},{4,12},{5,13},{8,0},{9,1},{12,4},{13,5},{2,10},{3,11},... | collective-permute-start | bytes 172808 | tf_op jit(solution)/shard_map/ppermute | solution.py:289
  132.5 9.3 %collective-permute-start.10 = (bf16[2,40,360]{2,1,0:T(8,128)(2,1)S(1)}, bf16[2,40,360]{2,1,0:T(8,128)(2,1)S(1)}, u32[]{:S(2)}, u32[]{:S(2)}) collective-permute-start(bf16[2,40,360]{2,1,0:T(8,128)(2,1)S(1)} %get-tuple-element.34), channel_id=1, source_target_pairs={{0,9},{1,8},{4,13},{5,12},{8,1},{9,0},{12,5},{13,4},{2,11},{3,10},... | collective-permute-start | bytes 172808 | tf_op jit(solution)/shard_map/ppermute | solution.py:289
  134.4 7.4 %collective-permute-start.11 = (bf16[2,40,360]{2,1,0:T(8,128)(2,1)S(1)}, bf16[2,40,360]{2,1,0:T(8,128)(2,1)S(1)}, u32[]{:S(2)}, u32[]{:S(2)}) collective-permute-start(bf16[2,40,360]{2,1,0:T(8,128)(2,1)S(1)} %get-tuple-element.35), channel_id=1, source_target_pairs={{0,12},{1,13},{4,0},{5,1},{8,4},{9,5},{12,8},{13,9},{2,14},{3,15},... | collective-permute-start | bytes 172808 | tf_op jit(solution)/shard_map/ppermute | solution.py:289
  138.6 5.9 %collective-permute-start.12 = (bf16[2,40,360]{2,1,0:T(8,128)(2,1)S(1)}, bf16[2,40,360]{2,1,0:T(8,128)(2,1)S(1)}, u32[]{:S(2)}, u32[]{:S(2)}) collective-permute-start(bf16[2,40,360]{2,1,0:T(8,128)(2,1)S(1)} %get-tuple-element.36), channel_id=1, source_target_pairs={{0,13},{1,12},{4,1},{5,0},{8,5},{9,4},{12,9},{13,8},{2,15},{3,14},... | collective-permute-start | bytes 172808 | tf_op jit(solution)/shard_map/ppermute | solution.py:289
  144.5 21.5 %collective-permute-start.13 = (bf16[8,40,360]{2,1,0:T(8,128)(2,1)S(1)}, bf16[8,40,360]{2,1,0:T(8,128)(2,1)S(1)}, u32[]{:S(2)}, u32[]{:S(2)}) collective-permute-start(bf16[8,40,360]{2,1,0:T(8,128)(2,1)S(1)} %stack_other.1), channel_id=1, source_target_pairs={{0,2},{2,0},{1,3},{3,1},{4,6},{6,4},{5,7},{7,5},{8,10},{10,8},{9,1... | collective-permute-start | bytes 691208 | tf_op jit(solution)/shard_map/ppermute | solution.py:277
Sparse Core Ops, SparseCore 0:
  42.6 60.4 all-gather.1

commit v10 on v9

--- a/solution.py
+++ b/solution.py
@@ -183,7 +183,7 @@
         c.wait()
 
 
-def term_kernel(own_ref, low_hbm, high_ref, _, out_hbm, low_ref, scr, sems):
+def term_kernel(own_ref, low_hbm, high_ref, out_hbm, low_ref, scr, sems):
     load = pltpu.make_async_copy(low_hbm, low_ref, sems.at[NZ])
     load.start()
     hid = [own_ref[:, WIDE:], high_ref[:, CW:]]
@@ -365,7 +365,7 @@
     terms = call(
         term_kernel,
         "grad_term",
-        [VMEM, ANY, VMEM, ANY],
+        [VMEM, ANY, VMEM],
         [((WIDE, FFW), BF)],
         [
             pltpu.VMEM((HSLOT, CW), BF),
@@ -374,7 +374,8 @@
         ],
         mib=20,
         where=ANY,
-    )(own, held(par_low), par_high, held(weight))[0]
+    )(own, held(par_low), par_high)[0]
+    terms, weight = lax.optimization_barrier((terms, weight))
     terms = exchange(terms.reshape(NDP, PAD, FFW), ("z", "yl"))
 
     backs = call(

time: 201 us -> 201 us (level)
  waiting for transfers between devices: 69.9 us -> 65.6 us
  starting transfers between devices: 64.7 us -> 68.9 us
    all_to_all x3, starting transfers between devices: 15.3 us -> 19.5 us  [exchange(): return lax.all_to_all(x, axes, split_axis=0, concat_axis=0, tiled=True)]
    all_gather x1, waiting for transfers between devices: 13.6 us -> 9.37 us  [local(): weight = lax.all_gather(w4, 'z', axis=0, tiled=True)]
  transfers between devices with their start and end apart: 18 -> 18, of which waited for: 7 -> 7; matrix products, arithmetic and copies ran while one was open for 0% -> 0% of each run, Pallas kernels for 7% -> 9%
where the time goes in v10:
time: 201 us; the launch traced here: 200 us
  starting transfers between devices  68.9 us (34%)
  waiting for transfers between devices  65.6 us (33%)
  Pallas kernels  23.4 us (12%)
  blocking collectives  21.5 us (11%)
  between operations  14.4 us (7%)
  local copies, waits for them, and re-layouts  5.77 us (3%)
    all_to_all x3, waiting for transfers between devices, exchange(): return lax.all_to_all(x, axes, split_axis=0, concat_axis=0, tiled=True)  34.3 us
    ppermute x7, starting transfers between devices, shift(): return lax.ppermute(x, axis, [(i, (i + by) % n) for i in range(n)])  27.9 us
    all_to_all x1, blocking collectives, exchange(): return lax.all_to_all(x, axes, split_axis=0, concat_axis=0, tiled=True)  21.5 us
    ppermute x7, starting transfers between devices, to_peer(): return lax.ppermute(x, ('x', 'c'), pairs)  21.4 us
    all_to_all x3, starting transfers between devices, exchange(): return lax.all_to_all(x, axes, split_axis=0, concat_axis=0, tiled=True)  19.5 us
    ppermute x7, waiting for transfers between devices, shift(): return lax.ppermute(x, axis, [(i, (i + by) % n) for i in range(n)])  19.2 us
    all_gather x1, waiting for transfers between devices, local(): weight = lax.all_gather(w4, 'z', axis=0, tiled=True)  9.37 us
    unnamed x21, local copies, waits for them, and re-layouts  5.69 us
  transfers between devices with their start and end apart: 18, of which 7 were waited for; matrix products, arithmetic and copies ran while one was open for 0% of the time, Pallas kernels for 9%

profile of v10, /device:TPU:96, one launch (start us, length us, event | category | flops | bytes accessed | tf_op | source)
XLA Modules:
  0.0 199.7 jit_solution(2239465947760739437)
XLA Ops:
  7.2 0.1 stack.23.pos_ref
  7.3 2.7 %prep.1 = (bf16[1552,128]{1,0:T(8,128)(2,1)S(1)}, bf16[1536,128]{1,0:T(8,128)(2,1)}, f32[16,128]{1,0:T(8,128)S(1)}) custom-call(s32[5]{0:T(128)S(1)} %stack.23.pos_ref, s32[1,4]{1,0:T(1,128)} %len_hbm.1, f32[1,4]{1,0:T(1,128)} %adv_hbm.1, bf16[2880,128]{1,0:T(8,128)(2,1)} %bitcast.47, s32[4,128]{1,0:T(4,128)} %bitcast.35), custom_call_target="tpu_custom_call" | custom-call | tf_op jit(solution)/shard_map/prep/pallas_call | solution.py:111
  10.0 2.0 %collective-permute-start = (bf16[1552,128]{1,0:T(8,128)(2,1)S(1)}, bf16[1552,128]{1,0:T(8,128)(2,1)S(1)}, u32[]{:S(2)}, u32[]{:S(2)}) collective-permute-start(bf16[1552,128]{1,0:T(8,128)(2,1)S(1)} %get-tuple-element.25.low_ref), channel_id=1, source_target_pairs={{0,2},{2,0},{1,3},{3,1},{4,6},{6,4},{5,7},{7,5},{8,10},{10,8},{9,1... | collective-permute-start | bytes 1191944 | tf_op jit(solution)/shard_map/ppermute | solution.py:277
  12.0 3.3 %send_own.1._ = bf16[320,3456]{1,0:T(8,128)(2,1)} custom-call(s32[5]{0:T(128)S(1)} %stack.23.pos_ref, bf16[4,360,128]{2,1,0:T(8,128)(2,1)} %bitcast.31, bf16[4,128]{1,0:T(4,128)(2,1)} %bitcast.39, s32[4,128]{1,0:T(4,128)} %bitcast.36, f32[16,128]{1,0:T(8,128)S(1)} %get-tuple-element.29.pm_ref, bf16[1552,128]{1,0:T(8,128)(2,1)S(1)} %get-tuple-element.25.low_ref, ...), custom_call_target="tpu_custom_call" | custom-call | tf_op jit(solution)/shard_map/send_own/pallas_call | solution.py:305
  15.3 0.0 copy-start.9
  15.3 4.4 %all-to-all-start = ((bf16[8,40,3456]{2,1,0:T(8,128)(2,1)}), bf16[8,40,3456]{2,1,0:T(8,128)(2,1)S(1)}, u32[]{:S(2)}, u32[]{:S(2)}) async-start(bf16[8,40,3456]{2,1,0:T(8,128)(2,1)} %bitcast.44), calls=%async_computation | async-start | bytes 4423680 | tf_op jit(solution)/shard_map/all_to_all | solution.py:293
  19.8 0.0 all-gather.2.cloned.1.call-start
  19.8 0.0 copy-done.9
  19.8 0.0 copy-start.2
  19.9 0.0 copy-start.5
  19.9 0.0 copy-start.6
  19.9 5.6 %collective-permute-start.5 = (bf16[96,384]{1,0:T(8,128)(2,1)S(1)}, bf16[96,384]{1,0:T(8,128)(2,1)S(1)}, u32[]{:S(2)}, u32[]{:S(2)}) collective-permute-start(bf16[96,384]{1,0:T(8,128)(2,1)S(1)} %weight_pad.1.refs_0_), channel_id=1, source_target_pairs={{0,48},{16,0},{32,16},{48,32},{1,49},{17,1},{33,17},{49,33},{2,50}... | collective-permute-start | bytes 221192 | tf_op jit(solution)/shard_map/ppermute | solution.py:277
  25.6 1.9 collective-permute-start.4
  27.5 2.9 %collective-permute-start.3 = (bf16[96,384]{1,0:T(8,128)(2,1)S(1)}, bf16[96,384]{1,0:T(8,128)(2,1)S(1)}, u32[]{:S(2)}, u32[]{:S(2)}) collective-permute-start(bf16[96,384]{1,0:T(8,128)(2,1)S(1)} %weight_pad.1.refs_0_), channel_id=1, source_target_pairs={{0,16},{16,32},{32,48},{48,0},{1,17},{17,33},{33,49},{49,1},{2,18}... | collective-permute-start | bytes 221192 | tf_op jit(solution)/shard_map/ppermute | solution.py:277
  30.4 0.0 copy-done.2
  30.4 0.0 copy-done.5
  30.4 1.0 send_other.1
  31.4 5.9 %collective-permute-start.2 = (bf16[320,384]{1,0:T(8,128)(2,1)S(1)}, bf16[320,384]{1,0:T(8,128)(2,1)}, u32[]{:S(2)}, u32[]{:S(2)}) collective-permute-start(bf16[320,384]{1,0:T(8,128)(2,1)S(1)} %send_other.1), channel_id=1, source_target_pairs={{0,2},{2,0},{1,3},{3,1},{4,6},{6,4},{5,7},{7,5},{8,10},{10,8},{9,1... | collective-permute-start | bytes 737288 | tf_op jit(solution)/shard_map/ppermute | solution.py:277
  37.3 0.0 collective-permute-done.5.refs_3_
  37.3 3.8 %collective-permute-start.1 = (bf16[1536,128]{1,0:T(8,128)(2,1)}, bf16[1536,128]{1,0:T(8,128)(2,1)}, u32[]{:S(2)}, u32[]{:S(2)}) collective-permute-start(bf16[1536,128]{1,0:T(8,128)(2,1)} %get-tuple-element.28.high_ref), channel_id=1, source_target_pairs={{0,2},{2,0},{1,3},{3,1},{4,6},{6,4},{5,7},{7,5},{8,10},{10,8},{9,1... | collective-permute-start | bytes 1179656 | tf_op jit(solution)/shard_map/ppermute | solution.py:277
  41.2 0.0 collective-permute-done.4.refs_2_
  41.2 0.0 collective-permute-done.3.refs_1_
  41.2 1.3 weight_part.1
  42.5 0.0 all-gather.2.cloned.1.call-update
  42.5 0.0 collective-permute-done.cot_ref.pm_ref
  42.5 0.0 copy-start.7
  42.5 1.4 send_low.1
  43.9 0.0 copy-done.7
  43.9 4.3 %all-to-all-done = bf16[8,40,3456]{2,1,0:T(8,128)(2,1)S(1)} async-done(((bf16[8,40,3456]{2,1,0:T(8,128)(2,1)}), bf16[8,40,3456]{2,1,0:T(8,128)(2,1)S(1)}, u32[]{:S(2)}, u32[]{:S(2)}) %all-to-all-start) | async-done | bytes 2211872 | tf_op jit(solution)/shard_map/all_to_all | solution.py:293
  48.2 3.6 %all-to-all-start.1 = ((bf16[8,40,1536]{2,1,0:T(8,128)(2,1)}), bf16[8,40,1536]{2,1,0:T(8,128)(2,1)S(1)}, u32[]{:S(2)}, u32[]{:S(2)}) async-start(bf16[8,40,1536]{2,1,0:T(8,128)(2,1)} %bitcast.46), calls=%async_computation.1 | async-start | bytes 1966080 | tf_op jit(solution)/shard_map/all_to_all | solution.py:293
  51.8 0.0 collective-permute-done.2.h_ref
  51.8 3.3 %collective-permute-done.1.cot_ref = bf16[1536,128]{1,0:T(8,128)(2,1)} collective-permute-done((bf16[1536,128]{1,0:T(8,128)(2,1)}, bf16[1536,128]{1,0:T(8,128)(2,1)}, u32[]{:S(2)}, u32[]{:S(2)}) %collective-permute-start.1) | collective-permute-done | bytes 393248 | tf_op jit(solution)/shard_map/ppermute | solution.py:277
  55.1 1.0 copy-done.8
  56.1 2.5 %send_high.1 = bf16[320,1920]{1,0:T(8,128)(2,1)} custom-call(bf16[1536,128]{1,0:T(8,128)(2,1)} %collective-permute-done.1.cot_ref, bf16[1552,128]{1,0:T(8,128)(2,1)S(1)} %copy-done.8, bf16[320,384]{1,0:T(8,128)(2,1)} %collective-permute-done.2.h_ref), custom_call_target="tpu_custom_call" | custom-call | flops 49999998976 | tf_op jit(solution)/shard_map/send_high/pallas_call | solution.py:354
  58.6 8.4 %all-to-all-done.1 = bf16[8,40,1536]{2,1,0:T(8,128)(2,1)S(1)} async-done(((bf16[8,40,1536]{2,1,0:T(8,128)(2,1)}), bf16[8,40,1536]{2,1,0:T(8,128)(2,1)S(1)}, u32[]{:S(2)}, u32[]{:S(2)}) %all-to-all-start.1) | async-done | bytes 983072 | tf_op jit(solution)/shard_map/all_to_all | solution.py:293
  67.0 1.0 copy-done
  68.0 21.5 %all_to_all.20 = bf16[8,40,1920]{2,1,0:T(8,128)(2,1)S(1)} all-to-all(bf16[8,40,1920]{2,1,0:T(8,128)(2,1)} %bitcast.45), channel_id=1, replica_groups=mesh['z'=8,'yl'=4,'x'=4,'yh'=2,'c'=2] {'x','c'}, dimensions={0} | all-to-all | bytes 2457600 | tf_op jit(solution)/shard_map/all_to_all | solution.py:293
  89.5 4.2 %grad_term.1 = bf16[3072,360]{1,0:T(8,128)(2,1)} custom-call(bf16[320,3456]{1,0:T(8,128)(2,1)S(1)} %bitcast.25, bf16[320,1536]{1,0:T(8,128)(2,1)} %bitcast.29, bf16[320,1920]{1,0:T(8,128)(2,1)S(1)} %bitcast.27), custom_call_target="tpu_custom_call" | custom-call | tf_op jit(solution)/shard_map/grad_term/pallas_call | solution.py:365
  93.7 9.4 %all-gather.2.cloned.1.call-done.w_ref = bf16[3072,384]{1,0:T(8,128)(2,1)} async-done(((bf16[384,384]{1,0:T(8,128)(2,1)}), bf16[3072,384]{1,0:T(8,128)(2,1)}) %all-gather.2.cloned.1.call-update) | async-done | bytes 2359312 | tf_op jit(solution)/shard_map/all_gather | solution.py:329
  103.1 11.5 %all-to-all-start.3 = ((bf16[32,96,360]{2,1,0:T(8,128)(2,1)}), bf16[32,96,360]{2,1,0:T(8,128)(2,1)}, u32[]{:S(2)}, u32[]{:S(2)}) async-start(bf16[32,96,360]{2,1,0:T(8,128)(2,1)} %bitcast.43), calls=%async_computation.3 | async-start | bytes 4718592 | tf_op jit(solution)/shard_map/all_to_all | solution.py:293
  114.6 0.0 copy-start.1
  114.7 1.2 copy-done.1
  115.9 1.7 copy-done.4
  117.5 2.8 %back_product.1 = (bf16[2,40,360]{2,1,0:T(8,128)(2,1)S(1)}, bf16[2,40,360]{2,1,0:T(8,128)(2,1)S(1)}, bf16[2,40,360]{2,1,0:T(8,128)(2,1)S(1)}, bf16[2,40,360]{2,1...) custom-call(s32[5]{0:T(128)S(1)} %stack.23.pos_ref, ...), custom_call_target="tpu_custom_call" | custom-call | tf_op jit(solution)/shard_map/back_product/pallas_call | solution.py:381
  120.3 1.9 collective-permute-start.6
  122.2 2.5 %collective-permute-start.7 = (bf16[2,40,360]{2,1,0:T(8,128)(2,1)S(1)}, bf16[2,40,360]{2,1,0:T(8,128)(2,1)S(1)}, u32[]{:S(2)}, u32[]{:S(2)}) collective-permute-start(bf16[2,40,360]{2,1,0:T(8,128)(2,1)S(1)} %get-tuple-element.35), channel_id=1, source_target_pairs={{0,4},{1,5},{4,8},{5,9},{8,12},{9,13},{12,0},{13,1},{2,6},{3,7},{6... | collective-permute-start | bytes 172808 | tf_op jit(solution)/shard_map/ppermute | solution.py:289
  124.7 2.0 %collective-permute-start.8 = (bf16[2,40,360]{2,1,0:T(8,128)(2,1)S(1)}, bf16[2,40,360]{2,1,0:T(8,128)(2,1)S(1)}, u32[]{:S(2)}, u32[]{:S(2)}) collective-permute-start(bf16[2,40,360]{2,1,0:T(8,128)(2,1)S(1)} %get-tuple-element.36), channel_id=1, source_target_pairs={{0,5},{1,4},{4,9},{5,8},{8,13},{9,12},{12,1},{13,0},{2,7},{3,6},{6... | collective-permute-start | bytes 172808 | tf_op jit(solution)/shard_map/ppermute | solution.py:289
  126.7 5.7 %collective-permute-start.9 = (bf16[2,40,360]{2,1,0:T(8,128)(2,1)S(1)}, bf16[2,40,360]{2,1,0:T(8,128)(2,1)S(1)}, u32[]{:S(2)}, u32[]{:S(2)}) collective-permute-start(bf16[2,40,360]{2,1,0:T(8,128)(2,1)S(1)} %get-tuple-element.37), channel_id=1, source_target_pairs={{0,8},{1,9},{4,12},{5,13},{8,0},{9,1},{12,4},{13,5},{2,10},{3,11},... | collective-permute-start | bytes 172808 | tf_op jit(solution)/shard_map/ppermute | solution.py:289
  132.5 1.9 collective-permute-start.10
  134.4 0.0 collective-permute-done.6.refs_1_
  134.4 4.2 %collective-permute-start.11 = (bf16[2,40,360]{2,1,0:T(8,128)(2,1)S(1)}, bf16[2,40,360]{2,1,0:T(8,128)(2,1)S(1)}, u32[]{:S(2)}, u32[]{:S(2)}) collective-permute-start(bf16[2,40,360]{2,1,0:T(8,128)(2,1)S(1)} %get-tuple-element.39), channel_id=1, source_target_pairs={{0,12},{1,13},{4,0},{5,1},{8,4},{9,5},{12,8},{13,9},{2,14},{3,15},... | collective-permute-start | bytes 172808 | tf_op jit(solution)/shard_map/ppermute | solution.py:289
  138.6 0.0 collective-permute-done.7.refs_2_
  138.6 3.2 %collective-permute-start.12 = (bf16[2,40,360]{2,1,0:T(8,128)(2,1)S(1)}, bf16[2,40,360]{2,1,0:T(8,128)(2,1)S(1)}, u32[]{:S(2)}, u32[]{:S(2)}) collective-permute-start(bf16[2,40,360]{2,1,0:T(8,128)(2,1)S(1)} %get-tuple-element.40), channel_id=1, source_target_pairs={{0,13},{1,12},{4,1},{5,0},{8,5},{9,4},{12,9},{13,8},{2,15},{3,14},... | collective-permute-start | bytes 172808 | tf_op jit(solution)/shard_map/ppermute | solution.py:289
  141.8 0.0 collective-permute-done.8.refs_3_
  141.8 0.0 collective-permute-done.9.refs_4_
  141.8 0.0 collective-permute-done.10.refs_5_
  141.8 0.0 collective-permute-done.11.refs_6_
  141.8 2.6 %collective-permute-done.12.refs_7_ = bf16[2,40,360]{2,1,0:T(8,128)(2,1)S(1)} collective-permute-done((bf16[2,40,360]{2,1,0:T(8,128)(2,1)S(1)}, bf16[2,40,360]{2,1,0:T(8,128)(2,1)S(1)}, u32[]{:S(2)}, u32[]{:S(2)}) %collective-permute-start.12) | collective-permute-done | bytes 57632 | tf_op jit(solution)/shard_map/ppermute | solution.py:289
  144.5 5.7 %collective-permute-start.13 = (bf16[8,40,360]{2,1,0:T(8,128)(2,1)S(1)}, bf16[8,40,360]{2,1,0:T(8,128)(2,1)S(1)}, u32[]{:S(2)}, u32[]{:S(2)}) collective-permute-start(bf16[8,40,360]{2,1,0:T(8,128)(2,1)S(1)} %stack_other.1), channel_id=1, source_target_pairs={{0,2},{2,0},{1,3},{3,1},{4,6},{6,4},{5,7},{7,5},{8,10},{10,8},{9,1... | collective-permute-start | bytes 691208 | tf_op jit(solution)/shard_map/ppermute | solution.py:277
  150.2 15.9 %collective-permute-done.13.other_ref = bf16[8,40,360]{2,1,0:T(8,128)(2,1)S(1)} collective-permute-done((bf16[8,40,360]{2,1,0:T(8,128)(2,1)S(1)}, bf16[8,40,360]{2,1,0:T(8,128)(2,1)S(1)}, u32[]{:S(2)}, u32[]{:S(2)}) %collective-permute-start.13) | collective-permute-done | bytes 230432 | tf_op jit(solution)/shard_map/ppermute | solution.py:277
  166.2 2.2 %bring_home.1 = (f32[4,360,128]{2,1,0:T(8,128)}, f32[4,128]{1,0:T(4,128)}) custom-call(s32[5]{0:T(128)S(1)} %stack.23.pos_ref, bf16[4,360,128]{2,1,0:T(8,128)(2,1)S(1)} %bitcast.33, bf16[4,128]{1,0:T(4,128)(2,1)S(1)} %bitcast.41, f32[16,128]{1,0:T(8,128)S(1)} %get-tuple-element.29.pm_ref, s32[4,128]{1,0:T(4,128)S(1)} %bitcast.38, ...), custom_call_target="tpu_custom_call" | custom-call | tf_op jit(solution)/shard_map/bring_home/pallas_call | solution.py:392
  168.4 21.7 %all-to-all-done.3.x_ref = bf16[32,96,360]{2,1,0:T(8,128)(2,1)} async-done(((bf16[32,96,360]{2,1,0:T(8,128)(2,1)}), bf16[32,96,360]{2,1,0:T(8,128)(2,1)}, u32[]{:S(2)}, u32[]{:S(2)}) %all-to-all-start.3) | async-done | bytes 2211872 | tf_op jit(solution)/shard_map/all_to_all | solution.py:293
  190.1 2.0 sum_terms.1
  192.0 0.8 copy.10
  (8 shorter events, 0.0 us)
Async XLA Ops:
  10.0 32.5 %collective-permute-start = (bf16[1552,128]{1,0:T(8,128)(2,1)S(1)}, bf16[1552,128]{1,0:T(8,128)(2,1)S(1)}, u32[]{:S(2)}, u32[]{:S(2)}) collective-permute-start(bf16[1552,128]{1,0:T(8,128)(2,1)S(1)} %get-tuple-element.25.low_ref), channel_id=1, source_target_pairs={{0,2},{2,0},{1,3},{3,1},{4,6},{6,4},{5,7},{7,5},{8,10},{10,8},{9,1... | collective-permute-start | bytes 1191944 | tf_op jit(solution)/shard_map/ppermute | solution.py:277
  15.3 4.5 %copy-start.9 = (bf16[1,360,90]{1,2,0:T(8,128)(2,1)S(1)}, bf16[1,360,90]{1,2,0:T(8,128)(2,1)}, u32[]{:S(2)}) copy-start(bf16[1,360,90]{1,2,0:T(8,128)(2,1)} %param.13) | copy-start | bytes 194404
  15.3 32.9 %all-to-all-start = ((bf16[8,40,3456]{2,1,0:T(8,128)(2,1)}), bf16[8,40,3456]{2,1,0:T(8,128)(2,1)S(1)}, u32[]{:S(2)}, u32[]{:S(2)}) async-start(bf16[8,40,3456]{2,1,0:T(8,128)(2,1)} %bitcast.44), calls=%async_computation | async-start | bytes 4423680 | tf_op jit(solution)/shard_map/all_to_all | solution.py:293
  19.8 83.3 %all-gather.2.cloned.1.call-start = ((), (), s32[]{:S(2)}) async-start(), calls=%async_computation.4 | async-start | bytes 2654208 | tf_op jit(solution)/shard_map/all_gather | solution.py:329
  19.8 10.6 %copy-start.2 = (bf16[128,4,360]{0,2,1:T(8,128)(2,1)S(1)}, bf16[128,4,360]{0,2,1:T(8,128)(2,1)}, u32[]{:S(2)}) copy-start(bf16[128,4,360]{0,2,1:T(8,128)(2,1)} %param.8) | copy-start | bytes 1105924
  19.9 10.6 %copy-start.5 = (s32[128,4]{0,1:T(4,128)S(1)}, s32[128,4]{0,1:T(4,128)}, u32[]{:S(2)}) copy-start(s32[128,4]{0,1:T(4,128)} %param.10) | copy-start | bytes 6148
  19.9 10.6 %copy-start.6 = (bf16[128,4]{0,1:T(4,128)(2,1)S(1)}, bf16[128,4]{0,1:T(4,128)(2,1)}, u32[]{:S(2)}) copy-start(bf16[128,4]{0,1:T(4,128)(2,1)} %param.9) | copy-start | bytes 3076
  19.9 17.4 %collective-permute-start.5 = (bf16[96,384]{1,0:T(8,128)(2,1)S(1)}, bf16[96,384]{1,0:T(8,128)(2,1)S(1)}, u32[]{:S(2)}, u32[]{:S(2)}) collective-permute-start(bf16[96,384]{1,0:T(8,128)(2,1)S(1)} %weight_pad.1.refs_0_), channel_id=1, source_target_pairs={{0,48},{16,0},{32,16},{48,32},{1,49},{17,1},{33,17},{49,33},{2,50}... | collective-permute-start | bytes 221192 | tf_op jit(solution)/shard_map/ppermute | solution.py:277
  25.6 15.6 %collective-permute-start.4 = (bf16[96,384]{1,0:T(8,128)(2,1)S(1)}, bf16[96,384]{1,0:T(8,128)(2,1)S(1)}, u32[]{:S(2)}, u32[]{:S(2)}) collective-permute-start(bf16[96,384]{1,0:T(8,128)(2,1)S(1)} %weight_pad.1.refs_0_), channel_id=1, source_target_pairs={{0,32},{16,48},{32,0},{48,16},{1,33},{17,49},{33,1},{49,17},{2,34}... | collective-permute-start | bytes 221192 | tf_op jit(solution)/shard_map/ppermute | solution.py:277
  27.5 13.7 %collective-permute-start.3 = (bf16[96,384]{1,0:T(8,128)(2,1)S(1)}, bf16[96,384]{1,0:T(8,128)(2,1)S(1)}, u32[]{:S(2)}, u32[]{:S(2)}) collective-permute-start(bf16[96,384]{1,0:T(8,128)(2,1)S(1)} %weight_pad.1.refs_0_), channel_id=1, source_target_pairs={{0,16},{16,32},{32,48},{48,0},{1,17},{17,33},{33,49},{49,1},{2,18}... | collective-permute-start | bytes 221192 | tf_op jit(solution)/shard_map/ppermute | solution.py:277
  31.4 20.4 %collective-permute-start.2 = (bf16[320,384]{1,0:T(8,128)(2,1)S(1)}, bf16[320,384]{1,0:T(8,128)(2,1)}, u32[]{:S(2)}, u32[]{:S(2)}) collective-permute-start(bf16[320,384]{1,0:T(8,128)(2,1)S(1)} %send_other.1), channel_id=1, source_target_pairs={{0,2},{2,0},{1,3},{3,1},{4,6},{6,4},{5,7},{7,5},{8,10},{10,8},{9,1... | collective-permute-start | bytes 737288 | tf_op jit(solution)/shard_map/ppermute | solution.py:277
  37.3 17.7 %collective-permute-start.1 = (bf16[1536,128]{1,0:T(8,128)(2,1)}, bf16[1536,128]{1,0:T(8,128)(2,1)}, u32[]{:S(2)}, u32[]{:S(2)}) collective-permute-start(bf16[1536,128]{1,0:T(8,128)(2,1)} %get-tuple-element.28.high_ref), channel_id=1, source_target_pairs={{0,2},{2,0},{1,3},{3,1},{4,6},{6,4},{5,7},{7,5},{8,10},{10,8},{9,1... | collective-permute-start | bytes 1179656 | tf_op jit(solution)/shard_map/ppermute | solution.py:277
  42.5 1.4 copy-start.7
  48.2 18.7 %all-to-all-start.1 = ((bf16[8,40,1536]{2,1,0:T(8,128)(2,1)}), bf16[8,40,1536]{2,1,0:T(8,128)(2,1)S(1)}, u32[]{:S(2)}, u32[]{:S(2)}) async-start(bf16[8,40,1536]{2,1,0:T(8,128)(2,1)} %bitcast.46), calls=%async_computation.1 | async-start | bytes 1966080 | tf_op jit(solution)/shard_map/all_to_all | solution.py:293
  55.1 1.0 copy-start.8
  67.0 1.0 copy-start
  103.1 87.0 %all-to-all-start.3 = ((bf16[32,96,360]{2,1,0:T(8,128)(2,1)}), bf16[32,96,360]{2,1,0:T(8,128)(2,1)}, u32[]{:S(2)}, u32[]{:S(2)}) async-start(bf16[32,96,360]{2,1,0:T(8,128)(2,1)} %bitcast.43), calls=%async_computation.3 | async-start | bytes 4718592 | tf_op jit(solution)/shard_map/all_to_all | solution.py:293
  114.6 1.2 copy-start.1
  115.8 1.7 copy-start.4
  117.5 48.6 %copy-start.3 = (bf16[128,4,360]{0,2,1:T(8,128)(2,1)S(1)}, bf16[128,4,360]{0,2,1:T(8,128)(2,1)}, u32[]{:S(2)}) copy-start(bf16[128,4,360]{0,2,1:T(8,128)(2,1)} %param.8) | copy-start | bytes 1105924
  120.3 14.1 %collective-permute-start.6 = (bf16[2,40,360]{2,1,0:T(8,128)(2,1)S(1)}, bf16[2,40,360]{2,1,0:T(8,128)(2,1)S(1)}, u32[]{:S(2)}, u32[]{:S(2)}) collective-permute-start(bf16[2,40,360]{2,1,0:T(8,128)(2,1)S(1)} %get-tuple-element.34), channel_id=1, source_target_pairs={{0,1},{1,0},{4,5},{5,4},{8,9},{9,8},{12,13},{13,12},{2,3},{3,2},{6... | collective-permute-start | bytes 172808 | tf_op jit(solution)/shard_map/ppermute | solution.py:289
  122.2 16.4 %collective-permute-start.7 = (bf16[2,40,360]{2,1,0:T(8,128)(2,1)S(1)}, bf16[2,40,360]{2,1,0:T(8,128)(2,1)S(1)}, u32[]{:S(2)}, u32[]{:S(2)}) collective-permute-start(bf16[2,40,360]{2,1,0:T(8,128)(2,1)S(1)} %get-tuple-element.35), channel_id=1, source_target_pairs={{0,4},{1,5},{4,8},{5,9},{8,12},{9,13},{12,0},{13,1},{2,6},{3,7},{6... | collective-permute-start | bytes 172808 | tf_op jit(solution)/shard_map/ppermute | solution.py:289
  124.7 17.1 %collective-permute-start.8 = (bf16[2,40,360]{2,1,0:T(8,128)(2,1)S(1)}, bf16[2,40,360]{2,1,0:T(8,128)(2,1)S(1)}, u32[]{:S(2)}, u32[]{:S(2)}) collective-permute-start(bf16[2,40,360]{2,1,0:T(8,128)(2,1)S(1)} %get-tuple-element.36), channel_id=1, source_target_pairs={{0,5},{1,4},{4,9},{5,8},{8,13},{9,12},{12,1},{13,0},{2,7},{3,6},{6... | collective-permute-start | bytes 172808 | tf_op jit(solution)/shard_map/ppermute | solution.py:289
  126.7 15.1 %collective-permute-start.9 = (bf16[2,40,360]{2,1,0:T(8,128)(2,1)S(1)}, bf16[2,40,360]{2,1,0:T(8,128)(2,1)S(1)}, u32[]{:S(2)}, u32[]{:S(2)}) collective-permute-start(bf16[2,40,360]{2,1,0:T(8,128)(2,1)S(1)} %get-tuple-element.37), channel_id=1, source_target_pairs={{0,8},{1,9},{4,12},{5,13},{8,0},{9,1},{12,4},{13,5},{2,10},{3,11},... | collective-permute-start | bytes 172808 | tf_op jit(solution)/shard_map/ppermute | solution.py:289
  132.5 9.3 %collective-permute-start.10 = (bf16[2,40,360]{2,1,0:T(8,128)(2,1)S(1)}, bf16[2,40,360]{2,1,0:T(8,128)(2,1)S(1)}, u32[]{:S(2)}, u32[]{:S(2)}) collective-permute-start(bf16[2,40,360]{2,1,0:T(8,128)(2,1)S(1)} %get-tuple-element.38), channel_id=1, source_target_pairs={{0,9},{1,8},{4,13},{5,12},{8,1},{9,0},{12,5},{13,4},{2,11},{3,10},... | collective-permute-start | bytes 172808 | tf_op jit(solution)/shard_map/ppermute | solution.py:289
  134.4 7.4 %collective-permute-start.11 = (bf16[2,40,360]{2,1,0:T(8,128)(2,1)S(1)}, bf16[2,40,360]{2,1,0:T(8,128)(2,1)S(1)}, u32[]{:S(2)}, u32[]{:S(2)}) collective-permute-start(bf16[2,40,360]{2,1,0:T(8,128)(2,1)S(1)} %get-tuple-element.39), channel_id=1, source_target_pairs={{0,12},{1,13},{4,0},{5,1},{8,4},{9,5},{12,8},{13,9},{2,14},{3,15},... | collective-permute-start | bytes 172808 | tf_op jit(solution)/shard_map/ppermute | solution.py:289
  138.6 5.9 %collective-permute-start.12 = (bf16[2,40,360]{2,1,0:T(8,128)(2,1)S(1)}, bf16[2,40,360]{2,1,0:T(8,128)(2,1)S(1)}, u32[]{:S(2)}, u32[]{:S(2)}) collective-permute-start(bf16[2,40,360]{2,1,0:T(8,128)(2,1)S(1)} %get-tuple-element.40), channel_id=1, source_target_pairs={{0,13},{1,12},{4,1},{5,0},{8,5},{9,4},{12,9},{13,8},{2,15},{3,14},... | collective-permute-start | bytes 172808 | tf_op jit(solution)/shard_map/ppermute | solution.py:289
  144.5 21.6 %collective-permute-start.13 = (bf16[8,40,360]{2,1,0:T(8,128)(2,1)S(1)}, bf16[8,40,360]{2,1,0:T(8,128)(2,1)S(1)}, u32[]{:S(2)}, u32[]{:S(2)}) collective-permute-start(bf16[8,40,360]{2,1,0:T(8,128)(2,1)S(1)} %stack_other.1), channel_id=1, source_target_pairs={{0,2},{2,0},{1,3},{3,1},{4,6},{6,4},{5,7},{7,5},{8,10},{10,8},{9,1... | collective-permute-start | bytes 691208 | tf_op jit(solution)/shard_map/ppermute | solution.py:277
Sparse Core Ops, SparseCore 0:
  42.6 60.4 all-gather.1

commit v11 on v10

--- a/solution.py
+++ b/solution.py
@@ -17,6 +17,8 @@
 OWN = D // NDP
 PAD = 96
 WIDE = NDP * PAD
+SLABS = ((0, 128), (128, 256), (256, FFW))
+SENT = 272
 HALF = NEXP // 2
 HSLOT = HALF * CAP
 STEP = 768
@@ -183,9 +185,10 @@
         c.wait()
 
 
-def term_kernel(own_ref, low_hbm, high_ref, out_hbm, low_ref, scr, sems):
+def term_kernel(own_ref, low_hbm, high_ref, out_hbm, low_ref, pack, scr, sems):
     load = pltpu.make_async_copy(low_hbm, low_ref, sems.at[NZ])
     load.start()
+    pack[...] = jnp.zeros((NY, SENT, 128), F32)
     hid = [own_ref[:, WIDE:], high_ref[:, CW:]]
     gate = [h[:, FFW : FFW + 1].astype(F32) for h in hid]
     copies = []
@@ -199,19 +202,26 @@
         for cot, h, g in zip(cots, hid, gate):
             gated = (cot.astype(F32) * g).astype(BF)
             acc = acc + lax.dot_general(gated, h[:, :FFW], TN, preferred_element_type=F32)
-        rows = pl.ds(at, BLK)
-        scr[rows] = acc.astype(BF)
+        for y in range(NY):
+            v = acc[y * PAD : y * PAD + OWN]
+            for n, (a, b) in enumerate(SLABS):
+                pack[y, n * OWN : (n + 1) * OWN, : b - a] = v[:, a:b]
+            at = (z * NY + y) * SENT
+            scr[at : at + SENT] = pack[y].astype(BF)
+        rows = pl.ds(z * NY * SENT, NY * SENT)
         copies.append(pltpu.make_async_copy(scr.at[rows], out_hbm.at[rows], sems.at[z]))
         copies[-1].start()
     for c in copies:
         c.wait()
 
 
-def sum_kernel(x_ref, out_ref):
+def sum_kernel(x_ref, out_ref, scr):
     v = x_ref[0].astype(F32)
     for d in range(1, NDP):
         v = v + x_ref[d].astype(F32)
-    out_ref[...] = v[:OWN]
+    scr[...] = v
+    for n, (a, b) in enumerate(SLABS):
+        out_ref[:, a:b] = scr[n * OWN : (n + 1) * OWN, : b - a]
 
 
 def pad_kernel(w_ref, _, out_ref):
@@ -366,17 +376,18 @@
         term_kernel,
         "grad_term",
         [VMEM, ANY, VMEM],
-        [((WIDE, FFW), BF)],
+        [((NDP * SENT, 128), BF)],
         [
             pltpu.VMEM((HSLOT, CW), BF),
-            pltpu.VMEM((WIDE, FFW), BF),
+            pltpu.VMEM((NY, SENT, 128), F32),
+            pltpu.VMEM((NDP * SENT, 128), BF),
             pltpu.SemaphoreType.DMA((NZ + 1,)),
         ],
         mib=20,
         where=ANY,
     )(own, held(par_low), par_high)[0]
     terms, weight = lax.optimization_barrier((terms, weight))
-    terms = exchange(terms.reshape(NDP, PAD, FFW), ("z", "yl"))
+    terms = exchange(terms.reshape(NDP, SENT, 128), ("z", "yl"))
 
     backs = call(
         back_kernel,
@@ -396,7 +407,7 @@
         [((TOPK, FFW, ROWS), F32), ((TOPK, ROWS), F32)],
     )(pos, ht, gates, pm, rt, other, *backs)
     terms, gg = lax.optimization_barrier((terms, gg))
-    gd = call(sum_kernel, "sum_terms", [VMEM], [((OWN, FFW), F32)])(terms)[0]
+    gd = call(sum_kernel, "sum_terms", [VMEM], [((OWN, FFW), F32)], [pltpu.VMEM((SENT, 128), F32)])(terms)[0]
     return gd.T[None], jnp.transpose(gh, (2, 0, 1)), gg.T
 
 

time: 201 us -> 195 us (0.970)
  waiting for transfers between devices: 65.6 us -> 59.4 us
    all_to_all x3, waiting for transfers between devices: 34.3 us -> 30.9 us  [exchange(): return lax.all_to_all(x, axes, split_axis=0, concat_axis=0, tiled=True)]
    ppermute x7, waiting for transfers between devices: 19.2 us -> 16.7 us  [shift(): return lax.ppermute(x, axis, [(i, (i + by) % n) for i in range(n)])]
  transfers between devices with their start and end apart: 18 -> 18, of which waited for: 7 -> 7; matrix products, arithmetic and copies ran while one was open for 0% -> 0% of each run, Pallas kernels for 9% -> 10%
where the time goes in v11:
time: 195 us; the launch traced here: 194 us
  starting transfers between devices  69.3 us (36%)
  waiting for transfers between devices  59.4 us (30%)
  Pallas kernels  23.8 us (12%)
  blocking collectives  21.5 us (11%)
  between operations  14.4 us (7%)
  local copies, waits for them, and re-layouts  5.73 us (3%)
    all_to_all x3, waiting for transfers between devices, exchange(): return lax.all_to_all(x, axes, split_axis=0, concat_axis=0, tiled=True)  30.9 us
    ppermute x7, starting transfers between devices, shift(): return lax.ppermute(x, axis, [(i, (i + by) % n) for i in range(n)])  27.9 us
    all_to_all x1, blocking collectives, exchange(): return lax.all_to_all(x, axes, split_axis=0, concat_axis=0, tiled=True)  21.5 us
    ppermute x7, starting transfers between devices, to_peer(): return lax.ppermute(x, ('x', 'c'), pairs)  21.4 us
    all_to_all x3, starting transfers between devices, exchange(): return lax.all_to_all(x, axes, split_axis=0, concat_axis=0, tiled=True)  19.9 us
    ppermute x7, waiting for transfers between devices, shift(): return lax.ppermute(x, axis, [(i, (i + by) % n) for i in range(n)])  16.7 us
    all_gather x1, waiting for transfers between devices, local(): weight = lax.all_gather(w4, 'z', axis=0, tiled=True)  9.04 us
    unnamed x21, local copies, waits for them, and re-layouts  5.64 us
  transfers between devices with their start and end apart: 18, of which 7 were waited for; matrix products, arithmetic and copies ran while one was open for 0% of the time, Pallas kernels for 10%

profile of v11, /device:TPU:96, one launch (start us, length us, event | category | flops | bytes accessed | tf_op | source)
XLA Modules:
  0.0 194.1 jit_solution(1377559359226228831)
XLA Ops:
  7.2 0.1 stack.23.pos_ref
  7.3 2.7 %prep.1 = (bf16[1552,128]{1,0:T(8,128)(2,1)S(1)}, bf16[1536,128]{1,0:T(8,128)(2,1)}, f32[16,128]{1,0:T(8,128)S(1)}) custom-call(s32[5]{0:T(128)S(1)} %stack.23.pos_ref, s32[1,4]{1,0:T(1,128)} %len_hbm.1, f32[1,4]{1,0:T(1,128)} %adv_hbm.1, bf16[2880,128]{1,0:T(8,128)(2,1)} %bitcast.47, s32[4,128]{1,0:T(4,128)} %bitcast.35), custom_call_target="tpu_custom_call" | custom-call | tf_op jit(solution)/shard_map/prep/pallas_call | solution.py:113
  10.0 2.0 %collective-permute-start = (bf16[1552,128]{1,0:T(8,128)(2,1)S(1)}, bf16[1552,128]{1,0:T(8,128)(2,1)S(1)}, u32[]{:S(2)}, u32[]{:S(2)}) collective-permute-start(bf16[1552,128]{1,0:T(8,128)(2,1)S(1)} %get-tuple-element.25.low_ref), channel_id=1, source_target_pairs={{0,2},{2,0},{1,3},{3,1},{4,6},{6,4},{5,7},{7,5},{8,10},{10,8},{9,1... | collective-permute-start | bytes 1191944 | tf_op jit(solution)/shard_map/ppermute | solution.py:287
  12.0 3.3 %send_own.1._ = bf16[320,3456]{1,0:T(8,128)(2,1)} custom-call(s32[5]{0:T(128)S(1)} %stack.23.pos_ref, bf16[4,360,128]{2,1,0:T(8,128)(2,1)} %bitcast.31, bf16[4,128]{1,0:T(4,128)(2,1)} %bitcast.39, s32[4,128]{1,0:T(4,128)} %bitcast.36, f32[16,128]{1,0:T(8,128)S(1)} %get-tuple-element.29.pm_ref, bf16[1552,128]{1,0:T(8,128)(2,1)S(1)} %get-tuple-element.25.low_ref, ...), custom_call_target="tpu_custom_call" | custom-call | tf_op jit(solution)/shard_map/send_own/pallas_call | solution.py:315
  15.3 0.0 copy-start.9
  15.3 4.4 %all-to-all-start = ((bf16[8,40,3456]{2,1,0:T(8,128)(2,1)}), bf16[8,40,3456]{2,1,0:T(8,128)(2,1)S(1)}, u32[]{:S(2)}, u32[]{:S(2)}) async-start(bf16[8,40,3456]{2,1,0:T(8,128)(2,1)} %bitcast.44), calls=%async_computation | async-start | bytes 4423680 | tf_op jit(solution)/shard_map/all_to_all | solution.py:303
  19.8 0.0 all-gather.2.cloned.1.call-start
  19.8 0.0 copy-done.9
  19.8 0.0 copy-start.2
  19.9 0.0 copy-start.5
  19.9 0.0 copy-start.6
  19.9 5.6 %collective-permute-start.5 = (bf16[96,384]{1,0:T(8,128)(2,1)S(1)}, bf16[96,384]{1,0:T(8,128)(2,1)S(1)}, u32[]{:S(2)}, u32[]{:S(2)}) collective-permute-start(bf16[96,384]{1,0:T(8,128)(2,1)S(1)} %weight_pad.1.refs_0_), channel_id=1, source_target_pairs={{0,48},{16,0},{32,16},{48,32},{1,49},{17,1},{33,17},{49,33},{2,50}... | collective-permute-start | bytes 221192 | tf_op jit(solution)/shard_map/ppermute | solution.py:287
  25.6 1.9 collective-permute-start.4
  27.5 2.9 %collective-permute-start.3 = (bf16[96,384]{1,0:T(8,128)(2,1)S(1)}, bf16[96,384]{1,0:T(8,128)(2,1)S(1)}, u32[]{:S(2)}, u32[]{:S(2)}) collective-permute-start(bf16[96,384]{1,0:T(8,128)(2,1)S(1)} %weight_pad.1.refs_0_), channel_id=1, source_target_pairs={{0,16},{16,32},{32,48},{48,0},{1,17},{17,33},{33,49},{49,1},{2,18}... | collective-permute-start | bytes 221192 | tf_op jit(solution)/shard_map/ppermute | solution.py:287
  30.4 0.0 copy-done.2
  30.4 0.0 copy-done.5
  30.4 0.0 copy-done.6
  30.4 1.0 send_other.1
  31.4 5.9 %collective-permute-start.2 = (bf16[320,384]{1,0:T(8,128)(2,1)S(1)}, bf16[320,384]{1,0:T(8,128)(2,1)}, u32[]{:S(2)}, u32[]{:S(2)}) collective-permute-start(bf16[320,384]{1,0:T(8,128)(2,1)S(1)} %send_other.1), channel_id=1, source_target_pairs={{0,2},{2,0},{1,3},{3,1},{4,6},{6,4},{5,7},{7,5},{8,10},{10,8},{9,1... | collective-permute-start | bytes 737288 | tf_op jit(solution)/shard_map/ppermute | solution.py:287
  37.3 0.0 collective-permute-done.5.refs_3_
  37.3 3.8 %collective-permute-start.1 = (bf16[1536,128]{1,0:T(8,128)(2,1)}, bf16[1536,128]{1,0:T(8,128)(2,1)}, u32[]{:S(2)}, u32[]{:S(2)}) collective-permute-start(bf16[1536,128]{1,0:T(8,128)(2,1)} %get-tuple-element.28.high_ref), channel_id=1, source_target_pairs={{0,2},{2,0},{1,3},{3,1},{4,6},{6,4},{5,7},{7,5},{8,10},{10,8},{9,1... | collective-permute-start | bytes 1179656 | tf_op jit(solution)/shard_map/ppermute | solution.py:287
  41.2 0.0 collective-permute-done.4.refs_2_
  41.2 0.0 collective-permute-done.3.refs_1_
  41.2 1.3 weight_part.1
  42.5 0.0 all-gather.2.cloned.1.call-update
  42.5 0.0 collective-permute-done.cot_ref.pm_ref
  42.5 0.0 copy-start.7
  42.5 1.4 send_low.1
  43.9 0.0 copy-done.7
  43.9 4.3 %all-to-all-done = bf16[8,40,3456]{2,1,0:T(8,128)(2,1)S(1)} async-done(((bf16[8,40,3456]{2,1,0:T(8,128)(2,1)}), bf16[8,40,3456]{2,1,0:T(8,128)(2,1)S(1)}, u32[]{:S(2)}, u32[]{:S(2)}) %all-to-all-start) | async-done | bytes 2211872 | tf_op jit(solution)/shard_map/all_to_all | solution.py:303
  48.2 3.6 %all-to-all-start.1 = ((bf16[8,40,1536]{2,1,0:T(8,128)(2,1)}), bf16[8,40,1536]{2,1,0:T(8,128)(2,1)S(1)}, u32[]{:S(2)}, u32[]{:S(2)}) async-start(bf16[8,40,1536]{2,1,0:T(8,128)(2,1)} %bitcast.46), calls=%async_computation.1 | async-start | bytes 1966080 | tf_op jit(solution)/shard_map/all_to_all | solution.py:303
  51.8 0.0 collective-permute-done.2.h_ref
  51.8 3.3 %collective-permute-done.1.cot_ref = bf16[1536,128]{1,0:T(8,128)(2,1)} collective-permute-done((bf16[1536,128]{1,0:T(8,128)(2,1)}, bf16[1536,128]{1,0:T(8,128)(2,1)}, u32[]{:S(2)}, u32[]{:S(2)}) %collective-permute-start.1) | collective-permute-done | bytes 393248 | tf_op jit(solution)/shard_map/ppermute | solution.py:287
  55.1 1.0 copy-done.8
  56.1 2.5 %send_high.1 = bf16[320,1920]{1,0:T(8,128)(2,1)} custom-call(bf16[1536,128]{1,0:T(8,128)(2,1)} %collective-permute-done.1.cot_ref, bf16[1552,128]{1,0:T(8,128)(2,1)S(1)} %copy-done.8, bf16[320,384]{1,0:T(8,128)(2,1)} %collective-permute-done.2.h_ref), custom_call_target="tpu_custom_call" | custom-call | flops 49999998976 | tf_op jit(solution)/shard_map/send_high/pallas_call | solution.py:364
  58.6 8.4 %all-to-all-done.1 = bf16[8,40,1536]{2,1,0:T(8,128)(2,1)S(1)} async-done(((bf16[8,40,1536]{2,1,0:T(8,128)(2,1)}), bf16[8,40,1536]{2,1,0:T(8,128)(2,1)S(1)}, u32[]{:S(2)}, u32[]{:S(2)}) %all-to-all-start.1) | async-done | bytes 983072 | tf_op jit(solution)/shard_map/all_to_all | solution.py:303
  67.0 0.9 copy-done
  67.9 21.5 %all_to_all.20 = bf16[8,40,1920]{2,1,0:T(8,128)(2,1)S(1)} all-to-all(bf16[8,40,1920]{2,1,0:T(8,128)(2,1)} %bitcast.45), channel_id=1, replica_groups=mesh['z'=8,'yl'=4,'x'=4,'yh'=2,'c'=2] {'x','c'}, dimensions={0} | all-to-all | bytes 2457600 | tf_op jit(solution)/shard_map/all_to_all | solution.py:303
  89.4 4.6 %grad_term.1 = bf16[8704,128]{1,0:T(8,128)(2,1)} custom-call(bf16[320,3456]{1,0:T(8,128)(2,1)S(1)} %bitcast.25, bf16[320,1536]{1,0:T(8,128)(2,1)} %bitcast.29, bf16[320,1920]{1,0:T(8,128)(2,1)S(1)} %bitcast.27), custom_call_target="tpu_custom_call" | custom-call | tf_op jit(solution)/shard_map/grad_term/pallas_call | solution.py:375
  94.1 9.0 %all-gather.2.cloned.1.call-done.w_ref = bf16[3072,384]{1,0:T(8,128)(2,1)} async-done(((bf16[384,384]{1,0:T(8,128)(2,1)}), bf16[3072,384]{1,0:T(8,128)(2,1)}) %all-gather.2.cloned.1.call-update) | async-done | bytes 2359312 | tf_op jit(solution)/shard_map/all_gather | solution.py:339
  103.1 11.9 %all-to-all-start.3 = ((bf16[32,272,128]{2,1,0:T(8,128)(2,1)}), bf16[32,272,128]{2,1,0:T(8,128)(2,1)}, u32[]{:S(2)}, u32[]{:S(2)}) async-start(bf16[32,272,128]{2,1,0:T(8,128)(2,1)} %bitcast.43), calls=%async_computation.3 | async-start | bytes 4456448 | tf_op jit(solution)/shard_map/all_to_all | solution.py:303
  115.0 1.2 copy-done.1
  116.2 1.7 copy-done.4
  117.8 2.8 %back_product.1 = (bf16[2,40,360]{2,1,0:T(8,128)(2,1)S(1)}, bf16[2,40,360]{2,1,0:T(8,128)(2,1)S(1)}, bf16[2,40,360]{2,1,0:T(8,128)(2,1)S(1)}, bf16[2,40,360]{2,1...) custom-call(s32[5]{0:T(128)S(1)} %stack.23.pos_ref, ...), custom_call_target="tpu_custom_call" | custom-call | tf_op jit(solution)/shard_map/back_product/pallas_call | solution.py:392
  120.6 1.9 collective-permute-start.6
  122.5 2.5 %collective-permute-start.7 = (bf16[2,40,360]{2,1,0:T(8,128)(2,1)S(1)}, bf16[2,40,360]{2,1,0:T(8,128)(2,1)S(1)}, u32[]{:S(2)}, u32[]{:S(2)}) collective-permute-start(bf16[2,40,360]{2,1,0:T(8,128)(2,1)S(1)} %get-tuple-element.35), channel_id=1, source_target_pairs={{0,4},{1,5},{4,8},{5,9},{8,12},{9,13},{12,0},{13,1},{2,6},{3,7},{6... | collective-permute-start | bytes 172808 | tf_op jit(solution)/shard_map/ppermute | solution.py:299
  125.0 2.0 %collective-permute-start.8 = (bf16[2,40,360]{2,1,0:T(8,128)(2,1)S(1)}, bf16[2,40,360]{2,1,0:T(8,128)(2,1)S(1)}, u32[]{:S(2)}, u32[]{:S(2)}) collective-permute-start(bf16[2,40,360]{2,1,0:T(8,128)(2,1)S(1)} %get-tuple-element.36), channel_id=1, source_target_pairs={{0,5},{1,4},{4,9},{5,8},{8,13},{9,12},{12,1},{13,0},{2,7},{3,6},{6... | collective-permute-start | bytes 172808 | tf_op jit(solution)/shard_map/ppermute | solution.py:299
  127.1 5.7 %collective-permute-start.9 = (bf16[2,40,360]{2,1,0:T(8,128)(2,1)S(1)}, bf16[2,40,360]{2,1,0:T(8,128)(2,1)S(1)}, u32[]{:S(2)}, u32[]{:S(2)}) collective-permute-start(bf16[2,40,360]{2,1,0:T(8,128)(2,1)S(1)} %get-tuple-element.37), channel_id=1, source_target_pairs={{0,8},{1,9},{4,12},{5,13},{8,0},{9,1},{12,4},{13,5},{2,10},{3,11},... | collective-permute-start | bytes 172808 | tf_op jit(solution)/shard_map/ppermute | solution.py:299
  132.8 1.9 collective-permute-start.10
  134.7 0.0 collective-permute-done.6.refs_1_
  134.8 4.1 %collective-permute-start.11 = (bf16[2,40,360]{2,1,0:T(8,128)(2,1)S(1)}, bf16[2,40,360]{2,1,0:T(8,128)(2,1)S(1)}, u32[]{:S(2)}, u32[]{:S(2)}) collective-permute-start(bf16[2,40,360]{2,1,0:T(8,128)(2,1)S(1)} %get-tuple-element.39), channel_id=1, source_target_pairs={{0,12},{1,13},{4,0},{5,1},{8,4},{9,5},{12,8},{13,9},{2,14},{3,15},... | collective-permute-start | bytes 172808 | tf_op jit(solution)/shard_map/ppermute | solution.py:299
  138.9 0.0 collective-permute-done.7.refs_2_
  138.9 3.2 %collective-permute-start.12 = (bf16[2,40,360]{2,1,0:T(8,128)(2,1)S(1)}, bf16[2,40,360]{2,1,0:T(8,128)(2,1)S(1)}, u32[]{:S(2)}, u32[]{:S(2)}) collective-permute-start(bf16[2,40,360]{2,1,0:T(8,128)(2,1)S(1)} %get-tuple-element.40), channel_id=1, source_target_pairs={{0,13},{1,12},{4,1},{5,0},{8,5},{9,4},{12,9},{13,8},{2,15},{3,14},... | collective-permute-start | bytes 172808 | tf_op jit(solution)/shard_map/ppermute | solution.py:299
  142.1 0.0 collective-permute-done.8.refs_3_
  142.1 0.0 collective-permute-done.9.refs_4_
  142.1 0.0 collective-permute-done.10.refs_5_
  142.2 0.0 collective-permute-done.11.refs_6_
  142.2 2.6 %collective-permute-done.12.refs_7_ = bf16[2,40,360]{2,1,0:T(8,128)(2,1)S(1)} collective-permute-done((bf16[2,40,360]{2,1,0:T(8,128)(2,1)S(1)}, bf16[2,40,360]{2,1,0:T(8,128)(2,1)S(1)}, u32[]{:S(2)}, u32[]{:S(2)}) %collective-permute-start.12) | collective-permute-done | bytes 57632 | tf_op jit(solution)/shard_map/ppermute | solution.py:299
  144.8 5.7 %collective-permute-start.13 = (bf16[8,40,360]{2,1,0:T(8,128)(2,1)S(1)}, bf16[8,40,360]{2,1,0:T(8,128)(2,1)S(1)}, u32[]{:S(2)}, u32[]{:S(2)}) collective-permute-start(bf16[8,40,360]{2,1,0:T(8,128)(2,1)S(1)} %stack_other.1), channel_id=1, source_target_pairs={{0,2},{2,0},{1,3},{3,1},{4,6},{6,4},{5,7},{7,5},{8,10},{10,8},{9,1... | collective-permute-start | bytes 691208 | tf_op jit(solution)/shard_map/ppermute | solution.py:287
  150.5 13.4 %collective-permute-done.13.other_ref = bf16[8,40,360]{2,1,0:T(8,128)(2,1)S(1)} collective-permute-done((bf16[8,40,360]{2,1,0:T(8,128)(2,1)S(1)}, bf16[8,40,360]{2,1,0:T(8,128)(2,1)S(1)}, u32[]{:S(2)}, u32[]{:S(2)}) %collective-permute-start.13) | collective-permute-done | bytes 230432 | tf_op jit(solution)/shard_map/ppermute | solution.py:287
  163.9 2.2 %bring_home.1 = (f32[4,360,128]{2,1,0:T(8,128)}, f32[4,128]{1,0:T(4,128)}) custom-call(s32[5]{0:T(128)S(1)} %stack.23.pos_ref, bf16[4,360,128]{2,1,0:T(8,128)(2,1)S(1)} %bitcast.33, bf16[4,128]{1,0:T(4,128)(2,1)S(1)} %bitcast.41, f32[16,128]{1,0:T(8,128)S(1)} %get-tuple-element.29.pm_ref, s32[4,128]{1,0:T(4,128)S(1)} %bitcast.38, ...), custom_call_target="tpu_custom_call" | custom-call | tf_op jit(solution)/shard_map/bring_home/pallas_call | solution.py:403
  166.2 18.3 %all-to-all-done.3.x_ref = bf16[32,272,128]{2,1,0:T(8,128)(2,1)} async-done(((bf16[32,272,128]{2,1,0:T(8,128)(2,1)}), bf16[32,272,128]{2,1,0:T(8,128)(2,1)}, u32[]{:S(2)}, u32[]{:S(2)}) %all-to-all-start.3) | async-done | bytes 2228256 | tf_op jit(solution)/shard_map/all_to_all | solution.py:303
  184.4 2.0 %sum_terms.1 = f32[90,360]{1,0:T(8,128)S(1)} custom-call(bf16[32,272,128]{2,1,0:T(8,128)(2,1)} %all-to-all-done.3.x_ref), custom_call_target="tpu_custom_call" | custom-call | tf_op jit(solution)/shard_map/sum_terms/pallas_call | solution.py:410
  186.4 0.8 copy.10
  (8 shorter events, 0.0 us)
Async XLA Ops:
  10.0 32.5 %collective-permute-start = (bf16[1552,128]{1,0:T(8,128)(2,1)S(1)}, bf16[1552,128]{1,0:T(8,128)(2,1)S(1)}, u32[]{:S(2)}, u32[]{:S(2)}) collective-permute-start(bf16[1552,128]{1,0:T(8,128)(2,1)S(1)} %get-tuple-element.25.low_ref), channel_id=1, source_target_pairs={{0,2},{2,0},{1,3},{3,1},{4,6},{6,4},{5,7},{7,5},{8,10},{10,8},{9,1... | collective-permute-start | bytes 1191944 | tf_op jit(solution)/shard_map/ppermute | solution.py:287
  15.3 4.5 %copy-start.9 = (bf16[1,360,90]{1,2,0:T(8,128)(2,1)S(1)}, bf16[1,360,90]{1,2,0:T(8,128)(2,1)}, u32[]{:S(2)}) copy-start(bf16[1,360,90]{1,2,0:T(8,128)(2,1)} %param.13) | copy-start | bytes 194404
  15.3 32.9 %all-to-all-start = ((bf16[8,40,3456]{2,1,0:T(8,128)(2,1)}), bf16[8,40,3456]{2,1,0:T(8,128)(2,1)S(1)}, u32[]{:S(2)}, u32[]{:S(2)}) async-start(bf16[8,40,3456]{2,1,0:T(8,128)(2,1)} %bitcast.44), calls=%async_computation | async-start | bytes 4423680 | tf_op jit(solution)/shard_map/all_to_all | solution.py:303
  19.8 83.3 %all-gather.2.cloned.1.call-start = ((), (), s32[]{:S(2)}) async-start(), calls=%async_computation.4 | async-start | bytes 2654208 | tf_op jit(solution)/shard_map/all_gather | solution.py:339
  19.8 10.6 %copy-start.2 = (bf16[128,4,360]{0,2,1:T(8,128)(2,1)S(1)}, bf16[128,4,360]{0,2,1:T(8,128)(2,1)}, u32[]{:S(2)}) copy-start(bf16[128,4,360]{0,2,1:T(8,128)(2,1)} %param.8) | copy-start | bytes 1105924
  19.9 10.6 %copy-start.5 = (s32[128,4]{0,1:T(4,128)S(1)}, s32[128,4]{0,1:T(4,128)}, u32[]{:S(2)}) copy-start(s32[128,4]{0,1:T(4,128)} %param.10) | copy-start | bytes 6148
  19.9 10.6 %copy-start.6 = (bf16[128,4]{0,1:T(4,128)(2,1)S(1)}, bf16[128,4]{0,1:T(4,128)(2,1)}, u32[]{:S(2)}) copy-start(bf16[128,4]{0,1:T(4,128)(2,1)} %param.9) | copy-start | bytes 3076
  19.9 17.4 %collective-permute-start.5 = (bf16[96,384]{1,0:T(8,128)(2,1)S(1)}, bf16[96,384]{1,0:T(8,128)(2,1)S(1)}, u32[]{:S(2)}, u32[]{:S(2)}) collective-permute-start(bf16[96,384]{1,0:T(8,128)(2,1)S(1)} %weight_pad.1.refs_0_), channel_id=1, source_target_pairs={{0,48},{16,0},{32,16},{48,32},{1,49},{17,1},{33,17},{49,33},{2,50}... | collective-permute-start | bytes 221192 | tf_op jit(solution)/shard_map/ppermute | solution.py:287
  25.6 15.6 %collective-permute-start.4 = (bf16[96,384]{1,0:T(8,128)(2,1)S(1)}, bf16[96,384]{1,0:T(8,128)(2,1)S(1)}, u32[]{:S(2)}, u32[]{:S(2)}) collective-permute-start(bf16[96,384]{1,0:T(8,128)(2,1)S(1)} %weight_pad.1.refs_0_), channel_id=1, source_target_pairs={{0,32},{16,48},{32,0},{48,16},{1,33},{17,49},{33,1},{49,17},{2,34}... | collective-permute-start | bytes 221192 | tf_op jit(solution)/shard_map/ppermute | solution.py:287
  27.5 13.7 %collective-permute-start.3 = (bf16[96,384]{1,0:T(8,128)(2,1)S(1)}, bf16[96,384]{1,0:T(8,128)(2,1)S(1)}, u32[]{:S(2)}, u32[]{:S(2)}) collective-permute-start(bf16[96,384]{1,0:T(8,128)(2,1)S(1)} %weight_pad.1.refs_0_), channel_id=1, source_target_pairs={{0,16},{16,32},{32,48},{48,0},{1,17},{17,33},{33,49},{49,1},{2,18}... | collective-permute-start | bytes 221192 | tf_op jit(solution)/shard_map/ppermute | solution.py:287
  31.4 20.4 %collective-permute-start.2 = (bf16[320,384]{1,0:T(8,128)(2,1)S(1)}, bf16[320,384]{1,0:T(8,128)(2,1)}, u32[]{:S(2)}, u32[]{:S(2)}) collective-permute-start(bf16[320,384]{1,0:T(8,128)(2,1)S(1)} %send_other.1), channel_id=1, source_target_pairs={{0,2},{2,0},{1,3},{3,1},{4,6},{6,4},{5,7},{7,5},{8,10},{10,8},{9,1... | collective-permute-start | bytes 737288 | tf_op jit(solution)/shard_map/ppermute | solution.py:287
  37.3 17.7 %collective-permute-start.1 = (bf16[1536,128]{1,0:T(8,128)(2,1)}, bf16[1536,128]{1,0:T(8,128)(2,1)}, u32[]{:S(2)}, u32[]{:S(2)}) collective-permute-start(bf16[1536,128]{1,0:T(8,128)(2,1)} %get-tuple-element.28.high_ref), channel_id=1, source_target_pairs={{0,2},{2,0},{1,3},{3,1},{4,6},{6,4},{5,7},{7,5},{8,10},{10,8},{9,1... | collective-permute-start | bytes 1179656 | tf_op jit(solution)/shard_map/ppermute | solution.py:287
  42.5 1.4 copy-start.7
  48.2 18.7 %all-to-all-start.1 = ((bf16[8,40,1536]{2,1,0:T(8,128)(2,1)}), bf16[8,40,1536]{2,1,0:T(8,128)(2,1)S(1)}, u32[]{:S(2)}, u32[]{:S(2)}) async-start(bf16[8,40,1536]{2,1,0:T(8,128)(2,1)} %bitcast.46), calls=%async_computation.1 | async-start | bytes 1966080 | tf_op jit(solution)/shard_map/all_to_all | solution.py:303
  55.1 1.0 copy-start.8
  67.0 1.0 copy-start
  103.1 81.3 %all-to-all-start.3 = ((bf16[32,272,128]{2,1,0:T(8,128)(2,1)}), bf16[32,272,128]{2,1,0:T(8,128)(2,1)}, u32[]{:S(2)}, u32[]{:S(2)}) async-start(bf16[32,272,128]{2,1,0:T(8,128)(2,1)} %bitcast.43), calls=%async_computation.3 | async-start | bytes 4456448 | tf_op jit(solution)/shard_map/all_to_all | solution.py:303
  115.0 1.2 copy-start.1
  116.2 1.7 copy-start.4
  117.8 46.1 %copy-start.3 = (bf16[128,4,360]{0,2,1:T(8,128)(2,1)S(1)}, bf16[128,4,360]{0,2,1:T(8,128)(2,1)}, u32[]{:S(2)}) copy-start(bf16[128,4,360]{0,2,1:T(8,128)(2,1)} %param.8) | copy-start | bytes 1105924
  120.6 14.1 %collective-permute-start.6 = (bf16[2,40,360]{2,1,0:T(8,128)(2,1)S(1)}, bf16[2,40,360]{2,1,0:T(8,128)(2,1)S(1)}, u32[]{:S(2)}, u32[]{:S(2)}) collective-permute-start(bf16[2,40,360]{2,1,0:T(8,128)(2,1)S(1)} %get-tuple-element.34), channel_id=1, source_target_pairs={{0,1},{1,0},{4,5},{5,4},{8,9},{9,8},{12,13},{13,12},{2,3},{3,2},{6... | collective-permute-start | bytes 172808 | tf_op jit(solution)/shard_map/ppermute | solution.py:299
  122.5 16.4 %collective-permute-start.7 = (bf16[2,40,360]{2,1,0:T(8,128)(2,1)S(1)}, bf16[2,40,360]{2,1,0:T(8,128)(2,1)S(1)}, u32[]{:S(2)}, u32[]{:S(2)}) collective-permute-start(bf16[2,40,360]{2,1,0:T(8,128)(2,1)S(1)} %get-tuple-element.35), channel_id=1, source_target_pairs={{0,4},{1,5},{4,8},{5,9},{8,12},{9,13},{12,0},{13,1},{2,6},{3,7},{6... | collective-permute-start | bytes 172808 | tf_op jit(solution)/shard_map/ppermute | solution.py:299
  125.0 17.1 %collective-permute-start.8 = (bf16[2,40,360]{2,1,0:T(8,128)(2,1)S(1)}, bf16[2,40,360]{2,1,0:T(8,128)(2,1)S(1)}, u32[]{:S(2)}, u32[]{:S(2)}) collective-permute-start(bf16[2,40,360]{2,1,0:T(8,128)(2,1)S(1)} %get-tuple-element.36), channel_id=1, source_target_pairs={{0,5},{1,4},{4,9},{5,8},{8,13},{9,12},{12,1},{13,0},{2,7},{3,6},{6... | collective-permute-start | bytes 172808 | tf_op jit(solution)/shard_map/ppermute | solution.py:299
  127.1 15.1 %collective-permute-start.9 = (bf16[2,40,360]{2,1,0:T(8,128)(2,1)S(1)}, bf16[2,40,360]{2,1,0:T(8,128)(2,1)S(1)}, u32[]{:S(2)}, u32[]{:S(2)}) collective-permute-start(bf16[2,40,360]{2,1,0:T(8,128)(2,1)S(1)} %get-tuple-element.37), channel_id=1, source_target_pairs={{0,8},{1,9},{4,12},{5,13},{8,0},{9,1},{12,4},{13,5},{2,10},{3,11},... | collective-permute-start | bytes 172808 | tf_op jit(solution)/shard_map/ppermute | solution.py:299
  132.8 9.3 %collective-permute-start.10 = (bf16[2,40,360]{2,1,0:T(8,128)(2,1)S(1)}, bf16[2,40,360]{2,1,0:T(8,128)(2,1)S(1)}, u32[]{:S(2)}, u32[]{:S(2)}) collective-permute-start(bf16[2,40,360]{2,1,0:T(8,128)(2,1)S(1)} %get-tuple-element.38), channel_id=1, source_target_pairs={{0,9},{1,8},{4,13},{5,12},{8,1},{9,0},{12,5},{13,4},{2,11},{3,10},... | collective-permute-start | bytes 172808 | tf_op jit(solution)/shard_map/ppermute | solution.py:299
  134.8 7.4 %collective-permute-start.11 = (bf16[2,40,360]{2,1,0:T(8,128)(2,1)S(1)}, bf16[2,40,360]{2,1,0:T(8,128)(2,1)S(1)}, u32[]{:S(2)}, u32[]{:S(2)}) collective-permute-start(bf16[2,40,360]{2,1,0:T(8,128)(2,1)S(1)} %get-tuple-element.39), channel_id=1, source_target_pairs={{0,12},{1,13},{4,0},{5,1},{8,4},{9,5},{12,8},{13,9},{2,14},{3,15},... | collective-permute-start | bytes 172808 | tf_op jit(solution)/shard_map/ppermute | solution.py:299
  138.9 5.9 %collective-permute-start.12 = (bf16[2,40,360]{2,1,0:T(8,128)(2,1)S(1)}, bf16[2,40,360]{2,1,0:T(8,128)(2,1)S(1)}, u32[]{:S(2)}, u32[]{:S(2)}) collective-permute-start(bf16[2,40,360]{2,1,0:T(8,128)(2,1)S(1)} %get-tuple-element.40), channel_id=1, source_target_pairs={{0,13},{1,12},{4,1},{5,0},{8,5},{9,4},{12,9},{13,8},{2,15},{3,14},... | collective-permute-start | bytes 172808 | tf_op jit(solution)/shard_map/ppermute | solution.py:299
  144.8 19.1 %collective-permute-start.13 = (bf16[8,40,360]{2,1,0:T(8,128)(2,1)S(1)}, bf16[8,40,360]{2,1,0:T(8,128)(2,1)S(1)}, u32[]{:S(2)}, u32[]{:S(2)}) collective-permute-start(bf16[8,40,360]{2,1,0:T(8,128)(2,1)S(1)} %stack_other.1), channel_id=1, source_target_pairs={{0,2},{2,0},{1,3},{3,1},{4,6},{6,4},{5,7},{7,5},{8,10},{10,8},{9,1... | collective-permute-start | bytes 691208 | tf_op jit(solution)/shard_map/ppermute | solution.py:287
Sparse Core Ops, SparseCore 0:
  42.6 60.4 all-gather.1

commit v12 on v11

--- a/solution.py
+++ b/solution.py
@@ -221,7 +221,7 @@
         v = v + x_ref[d].astype(F32)
     scr[...] = v
     for n, (a, b) in enumerate(SLABS):
-        out_ref[:, a:b] = scr[n * OWN : (n + 1) * OWN, : b - a]
+        out_ref[:, 0, a:b] = scr[n * OWN : (n + 1) * OWN, : b - a]
 
 
 def pad_kernel(w_ref, _, out_ref):
@@ -407,8 +407,8 @@
         [((TOPK, FFW, ROWS), F32), ((TOPK, ROWS), F32)],
     )(pos, ht, gates, pm, rt, other, *backs)
     terms, gg = lax.optimization_barrier((terms, gg))
-    gd = call(sum_kernel, "sum_terms", [VMEM], [((OWN, FFW), F32)], [pltpu.VMEM((SENT, 128), F32)])(terms)[0]
-    return gd.T[None], jnp.transpose(gh, (2, 0, 1)), gg.T
+    gd = call(sum_kernel, "sum_terms", [VMEM], [((OWN, 1, FFW), F32)], [pltpu.VMEM((SENT, 128), F32)])(terms)[0]
+    return jnp.transpose(gd, (1, 2, 0)), jnp.transpose(gh, (2, 0, 1)), gg.T
 
 
 def solution(mesh):

time: 195 us -> 195 us (level)
    unnamed x21 -> x20, local copies, waits for them, and re-layouts: 5.64 us -> 4.84 us
where the time goes in v12:
time: 195 us; the launch traced here: 194 us
  starting transfers between devices  69.3 us (36%)
  waiting for transfers between devices  59.4 us (30%)
  Pallas kernels  24.5 us (13%)
  blocking collectives  21.5 us (11%)
  between operations  14.4 us (7%)
  local copies, waits for them, and re-layouts  4.93 us (3%)
    all_to_all x3, waiting for transfers between devices, exchange(): return lax.all_to_all(x, axes, split_axis=0, concat_axis=0, tiled=True)  30.9 us
    ppermute x7, starting transfers between devices, shift(): return lax.ppermute(x, axis, [(i, (i + by) % n) for i in range(n)])  27.9 us
    all_to_all x1, blocking collectives, exchange(): return lax.all_to_all(x, axes, split_axis=0, concat_axis=0, tiled=True)  21.5 us
    ppermute x7, starting transfers between devices, to_peer(): return lax.ppermute(x, ('x', 'c'), pairs)  21.4 us
    all_to_all x3, starting transfers between devices, exchange(): return lax.all_to_all(x, axes, split_axis=0, concat_axis=0, tiled=True)  19.9 us
    ppermute x7, waiting for transfers between devices, shift(): return lax.ppermute(x, axis, [(i, (i + by) % n) for i in range(n)])  16.7 us
    all_gather x1, waiting for transfers between devices, local(): weight = lax.all_gather(w4, 'z', axis=0, tiled=True)  9.04 us
    unnamed x20, local copies, waits for them, and re-layouts  4.84 us
  transfers between devices with their start and end apart: 18, of which 7 were waited for; matrix products, arithmetic and copies ran while one was open for 0% of the time, Pallas kernels for 10%

profile of v12, /device:TPU:96, one launch (start us, length us, event | category | flops | bytes accessed | tf_op | source)
XLA Modules:
  0.0 194.0 jit_solution(8180888160619808149)
XLA Ops:
  7.2 0.1 stack.23.pos_ref
  7.3 2.7 %prep.1 = (bf16[1552,128]{1,0:T(8,128)(2,1)S(1)}, bf16[1536,128]{1,0:T(8,128)(2,1)}, f32[16,128]{1,0:T(8,128)S(1)}) custom-call(s32[5]{0:T(128)S(1)} %stack.23.pos_ref, s32[1,4]{1,0:T(1,128)} %len_hbm.1, f32[1,4]{1,0:T(1,128)} %adv_hbm.1, bf16[2880,128]{1,0:T(8,128)(2,1)} %bitcast.44, s32[4,128]{1,0:T(4,128)} %bitcast.32), custom_call_target="tpu_custom_call" | custom-call | tf_op jit(solution)/shard_map/prep/pallas_call | solution.py:113
  10.0 2.0 %collective-permute-start = (bf16[1552,128]{1,0:T(8,128)(2,1)S(1)}, bf16[1552,128]{1,0:T(8,128)(2,1)S(1)}, u32[]{:S(2)}, u32[]{:S(2)}) collective-permute-start(bf16[1552,128]{1,0:T(8,128)(2,1)S(1)} %get-tuple-element.25.low_ref), channel_id=1, source_target_pairs={{0,2},{2,0},{1,3},{3,1},{4,6},{6,4},{5,7},{7,5},{8,10},{10,8},{9,1... | collective-permute-start | bytes 1191944 | tf_op jit(solution)/shard_map/ppermute | solution.py:287
  12.0 3.3 %send_own.1._ = bf16[320,3456]{1,0:T(8,128)(2,1)} custom-call(s32[5]{0:T(128)S(1)} %stack.23.pos_ref, bf16[4,360,128]{2,1,0:T(8,128)(2,1)} %bitcast.29, bf16[4,128]{1,0:T(4,128)(2,1)} %bitcast.36, s32[4,128]{1,0:T(4,128)} %bitcast.33, f32[16,128]{1,0:T(8,128)S(1)} %get-tuple-element.29.pm_ref, bf16[1552,128]{1,0:T(8,128)(2,1)S(1)} %get-tuple-element.25.low_ref, ...), custom_call_target="tpu_custom_call" | custom-call | tf_op jit(solution)/shard_map/send_own/pallas_call | solution.py:315
  15.3 0.0 copy-start.9
  15.3 4.4 %all-to-all-start = ((bf16[8,40,3456]{2,1,0:T(8,128)(2,1)}), bf16[8,40,3456]{2,1,0:T(8,128)(2,1)S(1)}, u32[]{:S(2)}, u32[]{:S(2)}) async-start(bf16[8,40,3456]{2,1,0:T(8,128)(2,1)} %bitcast.41), calls=%async_computation | async-start | bytes 4423680 | tf_op jit(solution)/shard_map/all_to_all | solution.py:303
  19.8 0.0 all-gather.2.cloned.1.call-start
  19.8 0.0 copy-done.9
  19.8 0.0 copy-start.2
  19.9 0.0 copy-start.5
  19.9 0.0 copy-start.6
  19.9 5.6 %collective-permute-start.5 = (bf16[96,384]{1,0:T(8,128)(2,1)S(1)}, bf16[96,384]{1,0:T(8,128)(2,1)S(1)}, u32[]{:S(2)}, u32[]{:S(2)}) collective-permute-start(bf16[96,384]{1,0:T(8,128)(2,1)S(1)} %weight_pad.1.refs_0_), channel_id=1, source_target_pairs={{0,48},{16,0},{32,16},{48,32},{1,49},{17,1},{33,17},{49,33},{2,50}... | collective-permute-start | bytes 221192 | tf_op jit(solution)/shard_map/ppermute | solution.py:287
  25.6 1.9 collective-permute-start.4
  27.5 2.9 %collective-permute-start.3 = (bf16[96,384]{1,0:T(8,128)(2,1)S(1)}, bf16[96,384]{1,0:T(8,128)(2,1)S(1)}, u32[]{:S(2)}, u32[]{:S(2)}) collective-permute-start(bf16[96,384]{1,0:T(8,128)(2,1)S(1)} %weight_pad.1.refs_0_), channel_id=1, source_target_pairs={{0,16},{16,32},{32,48},{48,0},{1,17},{17,33},{33,49},{49,1},{2,18}... | collective-permute-start | bytes 221192 | tf_op jit(solution)/shard_map/ppermute | solution.py:287
  30.4 0.0 copy-done.2
  30.4 0.0 copy-done.5
  30.4 0.0 copy-done.6
  30.4 1.0 send_other.1
  31.4 5.9 %collective-permute-start.2 = (bf16[320,384]{1,0:T(8,128)(2,1)S(1)}, bf16[320,384]{1,0:T(8,128)(2,1)}, u32[]{:S(2)}, u32[]{:S(2)}) collective-permute-start(bf16[320,384]{1,0:T(8,128)(2,1)S(1)} %send_other.1), channel_id=1, source_target_pairs={{0,2},{2,0},{1,3},{3,1},{4,6},{6,4},{5,7},{7,5},{8,10},{10,8},{9,1... | collective-permute-start | bytes 737288 | tf_op jit(solution)/shard_map/ppermute | solution.py:287
  37.3 0.0 collective-permute-done.5.refs_3_
  37.3 3.8 %collective-permute-start.1 = (bf16[1536,128]{1,0:T(8,128)(2,1)}, bf16[1536,128]{1,0:T(8,128)(2,1)}, u32[]{:S(2)}, u32[]{:S(2)}) collective-permute-start(bf16[1536,128]{1,0:T(8,128)(2,1)} %get-tuple-element.28.high_ref), channel_id=1, source_target_pairs={{0,2},{2,0},{1,3},{3,1},{4,6},{6,4},{5,7},{7,5},{8,10},{10,8},{9,1... | collective-permute-start | bytes 1179656 | tf_op jit(solution)/shard_map/ppermute | solution.py:287
  41.2 0.0 collective-permute-done.4.refs_2_
  41.2 0.0 collective-permute-done.3.refs_1_
  41.2 1.3 weight_part.1
  42.5 0.0 all-gather.2.cloned.1.call-update
  42.5 0.0 collective-permute-done.cot_ref.pm_ref
  42.5 0.0 copy-start.7
  42.5 1.4 send_low.1
  43.9 0.0 copy-done.7
  43.9 4.3 %all-to-all-done = bf16[8,40,3456]{2,1,0:T(8,128)(2,1)S(1)} async-done(((bf16[8,40,3456]{2,1,0:T(8,128)(2,1)}), bf16[8,40,3456]{2,1,0:T(8,128)(2,1)S(1)}, u32[]{:S(2)}, u32[]{:S(2)}) %all-to-all-start) | async-done | bytes 2211872 | tf_op jit(solution)/shard_map/all_to_all | solution.py:303
  48.2 3.6 %all-to-all-start.1 = ((bf16[8,40,1536]{2,1,0:T(8,128)(2,1)}), bf16[8,40,1536]{2,1,0:T(8,128)(2,1)S(1)}, u32[]{:S(2)}, u32[]{:S(2)}) async-start(bf16[8,40,1536]{2,1,0:T(8,128)(2,1)} %bitcast.43), calls=%async_computation.1 | async-start | bytes 1966080 | tf_op jit(solution)/shard_map/all_to_all | solution.py:303
  51.8 0.0 collective-permute-done.2.h_ref
  51.8 3.3 %collective-permute-done.1.cot_ref = bf16[1536,128]{1,0:T(8,128)(2,1)} collective-permute-done((bf16[1536,128]{1,0:T(8,128)(2,1)}, bf16[1536,128]{1,0:T(8,128)(2,1)}, u32[]{:S(2)}, u32[]{:S(2)}) %collective-permute-start.1) | collective-permute-done | bytes 393248 | tf_op jit(solution)/shard_map/ppermute | solution.py:287
  55.1 1.0 copy-done.8
  56.1 2.5 %send_high.1 = bf16[320,1920]{1,0:T(8,128)(2,1)} custom-call(bf16[1536,128]{1,0:T(8,128)(2,1)} %collective-permute-done.1.cot_ref, bf16[1552,128]{1,0:T(8,128)(2,1)S(1)} %copy-done.8, bf16[320,384]{1,0:T(8,128)(2,1)} %collective-permute-done.2.h_ref), custom_call_target="tpu_custom_call" | custom-call | flops 49999998976 | tf_op jit(solution)/shard_map/send_high/pallas_call | solution.py:364
  58.6 8.4 %all-to-all-done.1 = bf16[8,40,1536]{2,1,0:T(8,128)(2,1)S(1)} async-done(((bf16[8,40,1536]{2,1,0:T(8,128)(2,1)}), bf16[8,40,1536]{2,1,0:T(8,128)(2,1)S(1)}, u32[]{:S(2)}, u32[]{:S(2)}) %all-to-all-start.1) | async-done | bytes 983072 | tf_op jit(solution)/shard_map/all_to_all | solution.py:303
  67.0 0.9 copy-done
  67.9 21.5 %all_to_all.20 = bf16[8,40,1920]{2,1,0:T(8,128)(2,1)S(1)} all-to-all(bf16[8,40,1920]{2,1,0:T(8,128)(2,1)} %bitcast.42), channel_id=1, replica_groups=mesh['z'=8,'yl'=4,'x'=4,'yh'=2,'c'=2] {'x','c'}, dimensions={0} | all-to-all | bytes 2457600 | tf_op jit(solution)/shard_map/all_to_all | solution.py:303
  89.4 4.6 %grad_term.1 = bf16[8704,128]{1,0:T(8,128)(2,1)} custom-call(bf16[320,3456]{1,0:T(8,128)(2,1)S(1)} %bitcast.23, bf16[320,1536]{1,0:T(8,128)(2,1)} %bitcast.27, bf16[320,1920]{1,0:T(8,128)(2,1)S(1)} %bitcast.25), custom_call_target="tpu_custom_call" | custom-call | tf_op jit(solution)/shard_map/grad_term/pallas_call | solution.py:375
  94.1 9.0 %all-gather.2.cloned.1.call-done.w_ref = bf16[3072,384]{1,0:T(8,128)(2,1)} async-done(((bf16[384,384]{1,0:T(8,128)(2,1)}), bf16[3072,384]{1,0:T(8,128)(2,1)}) %all-gather.2.cloned.1.call-update) | async-done | bytes 2359312 | tf_op jit(solution)/shard_map/all_gather | solution.py:339
  103.1 11.9 %all-to-all-start.3 = ((bf16[32,272,128]{2,1,0:T(8,128)(2,1)}), bf16[32,272,128]{2,1,0:T(8,128)(2,1)}, u32[]{:S(2)}, u32[]{:S(2)}) async-start(bf16[32,272,128]{2,1,0:T(8,128)(2,1)} %bitcast.40), calls=%async_computation.3 | async-start | bytes 4456448 | tf_op jit(solution)/shard_map/all_to_all | solution.py:303
  115.0 0.0 copy-start.1
  115.0 1.2 copy-done.1
  116.2 1.7 copy-done.4
  117.8 2.8 %back_product.1 = (bf16[2,40,360]{2,1,0:T(8,128)(2,1)S(1)}, bf16[2,40,360]{2,1,0:T(8,128)(2,1)S(1)}, bf16[2,40,360]{2,1,0:T(8,128)(2,1)S(1)}, bf16[2,40,360]{2,1...) custom-call(s32[5]{0:T(128)S(1)} %stack.23.pos_ref, ...), custom_call_target="tpu_custom_call" | custom-call | tf_op jit(solution)/shard_map/back_product/pallas_call | solution.py:392
  120.6 1.9 collective-permute-start.6
  122.5 2.5 %collective-permute-start.7 = (bf16[2,40,360]{2,1,0:T(8,128)(2,1)S(1)}, bf16[2,40,360]{2,1,0:T(8,128)(2,1)S(1)}, u32[]{:S(2)}, u32[]{:S(2)}) collective-permute-start(bf16[2,40,360]{2,1,0:T(8,128)(2,1)S(1)} %get-tuple-element.35), channel_id=1, source_target_pairs={{0,4},{1,5},{4,8},{5,9},{8,12},{9,13},{12,0},{13,1},{2,6},{3,7},{6... | collective-permute-start | bytes 172808 | tf_op jit(solution)/shard_map/ppermute | solution.py:299
  125.0 2.0 %collective-permute-start.8 = (bf16[2,40,360]{2,1,0:T(8,128)(2,1)S(1)}, bf16[2,40,360]{2,1,0:T(8,128)(2,1)S(1)}, u32[]{:S(2)}, u32[]{:S(2)}) collective-permute-start(bf16[2,40,360]{2,1,0:T(8,128)(2,1)S(1)} %get-tuple-element.36), channel_id=1, source_target_pairs={{0,5},{1,4},{4,9},{5,8},{8,13},{9,12},{12,1},{13,0},{2,7},{3,6},{6... | collective-permute-start | bytes 172808 | tf_op jit(solution)/shard_map/ppermute | solution.py:299
  127.1 5.7 %collective-permute-start.9 = (bf16[2,40,360]{2,1,0:T(8,128)(2,1)S(1)}, bf16[2,40,360]{2,1,0:T(8,128)(2,1)S(1)}, u32[]{:S(2)}, u32[]{:S(2)}) collective-permute-start(bf16[2,40,360]{2,1,0:T(8,128)(2,1)S(1)} %get-tuple-element.37), channel_id=1, source_target_pairs={{0,8},{1,9},{4,12},{5,13},{8,0},{9,1},{12,4},{13,5},{2,10},{3,11},... | collective-permute-start | bytes 172808 | tf_op jit(solution)/shard_map/ppermute | solution.py:299
  132.8 1.9 collective-permute-start.10
  134.7 0.0 collective-permute-done.6.refs_1_
  134.8 4.1 %collective-permute-start.11 = (bf16[2,40,360]{2,1,0:T(8,128)(2,1)S(1)}, bf16[2,40,360]{2,1,0:T(8,128)(2,1)S(1)}, u32[]{:S(2)}, u32[]{:S(2)}) collective-permute-start(bf16[2,40,360]{2,1,0:T(8,128)(2,1)S(1)} %get-tuple-element.39), channel_id=1, source_target_pairs={{0,12},{1,13},{4,0},{5,1},{8,4},{9,5},{12,8},{13,9},{2,14},{3,15},... | collective-permute-start | bytes 172808 | tf_op jit(solution)/shard_map/ppermute | solution.py:299
  138.9 0.0 collective-permute-done.7.refs_2_
  138.9 3.2 %collective-permute-start.12 = (bf16[2,40,360]{2,1,0:T(8,128)(2,1)S(1)}, bf16[2,40,360]{2,1,0:T(8,128)(2,1)S(1)}, u32[]{:S(2)}, u32[]{:S(2)}) collective-permute-start(bf16[2,40,360]{2,1,0:T(8,128)(2,1)S(1)} %get-tuple-element.40), channel_id=1, source_target_pairs={{0,13},{1,12},{4,1},{5,0},{8,5},{9,4},{12,9},{13,8},{2,15},{3,14},... | collective-permute-start | bytes 172808 | tf_op jit(solution)/shard_map/ppermute | solution.py:299
  142.1 0.0 collective-permute-done.8.refs_3_
  142.1 0.0 collective-permute-done.9.refs_4_
  142.1 0.0 collective-permute-done.10.refs_5_
  142.2 0.0 collective-permute-done.11.refs_6_
  142.2 2.6 %collective-permute-done.12.refs_7_ = bf16[2,40,360]{2,1,0:T(8,128)(2,1)S(1)} collective-permute-done((bf16[2,40,360]{2,1,0:T(8,128)(2,1)S(1)}, bf16[2,40,360]{2,1,0:T(8,128)(2,1)S(1)}, u32[]{:S(2)}, u32[]{:S(2)}) %collective-permute-start.12) | collective-permute-done | bytes 57632 | tf_op jit(solution)/shard_map/ppermute | solution.py:299
  144.8 5.7 %collective-permute-start.13 = (bf16[8,40,360]{2,1,0:T(8,128)(2,1)S(1)}, bf16[8,40,360]{2,1,0:T(8,128)(2,1)S(1)}, u32[]{:S(2)}, u32[]{:S(2)}) collective-permute-start(bf16[8,40,360]{2,1,0:T(8,128)(2,1)S(1)} %stack_other.1), channel_id=1, source_target_pairs={{0,2},{2,0},{1,3},{3,1},{4,6},{6,4},{5,7},{7,5},{8,10},{10,8},{9,1... | collective-permute-start | bytes 691208 | tf_op jit(solution)/shard_map/ppermute | solution.py:287
  150.5 13.4 %collective-permute-done.13.other_ref = bf16[8,40,360]{2,1,0:T(8,128)(2,1)S(1)} collective-permute-done((bf16[8,40,360]{2,1,0:T(8,128)(2,1)S(1)}, bf16[8,40,360]{2,1,0:T(8,128)(2,1)S(1)}, u32[]{:S(2)}, u32[]{:S(2)}) %collective-permute-start.13) | collective-permute-done | bytes 230432 | tf_op jit(solution)/shard_map/ppermute | solution.py:287
  163.9 2.2 %bring_home.1 = (f32[4,360,128]{2,1,0:T(8,128)}, f32[4,128]{1,0:T(4,128)}) custom-call(s32[5]{0:T(128)S(1)} %stack.23.pos_ref, bf16[4,360,128]{2,1,0:T(8,128)(2,1)S(1)} %bitcast.31, bf16[4,128]{1,0:T(4,128)(2,1)S(1)} %bitcast.38, f32[16,128]{1,0:T(8,128)S(1)} %get-tuple-element.29.pm_ref, s32[4,128]{1,0:T(4,128)S(1)} %bitcast.35, ...), custom_call_target="tpu_custom_call" | custom-call | tf_op jit(solution)/shard_map/bring_home/pallas_call | solution.py:403
  166.2 18.3 %all-to-all-done.3.x_ref = bf16[32,272,128]{2,1,0:T(8,128)(2,1)} async-done(((bf16[32,272,128]{2,1,0:T(8,128)(2,1)}), bf16[32,272,128]{2,1,0:T(8,128)(2,1)}, u32[]{:S(2)}, u32[]{:S(2)}) %all-to-all-start.3) | async-done | bytes 2228256 | tf_op jit(solution)/shard_map/all_to_all | solution.py:303
  184.4 2.7 %sum_terms.1 = f32[90,1,360]{2,1,0:T(1,128)} custom-call(bf16[32,272,128]{2,1,0:T(8,128)(2,1)} %all-to-all-done.3.x_ref), custom_call_target="tpu_custom_call" | custom-call | tf_op jit(solution)/shard_map/sum_terms/pallas_call | solution.py:410
  (7 shorter events, 0.0 us)
Async XLA Ops:
  10.0 32.5 %collective-permute-start = (bf16[1552,128]{1,0:T(8,128)(2,1)S(1)}, bf16[1552,128]{1,0:T(8,128)(2,1)S(1)}, u32[]{:S(2)}, u32[]{:S(2)}) collective-permute-start(bf16[1552,128]{1,0:T(8,128)(2,1)S(1)} %get-tuple-element.25.low_ref), channel_id=1, source_target_pairs={{0,2},{2,0},{1,3},{3,1},{4,6},{6,4},{5,7},{7,5},{8,10},{10,8},{9,1... | collective-permute-start | bytes 1191944 | tf_op jit(solution)/shard_map/ppermute | solution.py:287
  15.3 4.5 %copy-start.9 = (bf16[1,360,90]{1,2,0:T(8,128)(2,1)S(1)}, bf16[1,360,90]{1,2,0:T(8,128)(2,1)}, u32[]{:S(2)}) copy-start(bf16[1,360,90]{1,2,0:T(8,128)(2,1)} %param.13) | copy-start | bytes 194404
  15.3 32.9 %all-to-all-start = ((bf16[8,40,3456]{2,1,0:T(8,128)(2,1)}), bf16[8,40,3456]{2,1,0:T(8,128)(2,1)S(1)}, u32[]{:S(2)}, u32[]{:S(2)}) async-start(bf16[8,40,3456]{2,1,0:T(8,128)(2,1)} %bitcast.41), calls=%async_computation | async-start | bytes 4423680 | tf_op jit(solution)/shard_map/all_to_all | solution.py:303
  19.8 83.3 %all-gather.2.cloned.1.call-start = ((), (), s32[]{:S(2)}) async-start(), calls=%async_computation.4 | async-start | bytes 2654208 | tf_op jit(solution)/shard_map/all_gather | solution.py:339
  19.8 10.6 %copy-start.2 = (bf16[128,4,360]{0,2,1:T(8,128)(2,1)S(1)}, bf16[128,4,360]{0,2,1:T(8,128)(2,1)}, u32[]{:S(2)}) copy-start(bf16[128,4,360]{0,2,1:T(8,128)(2,1)} %param.8) | copy-start | bytes 1105924
  19.9 10.6 %copy-start.5 = (s32[128,4]{0,1:T(4,128)S(1)}, s32[128,4]{0,1:T(4,128)}, u32[]{:S(2)}) copy-start(s32[128,4]{0,1:T(4,128)} %param.10) | copy-start | bytes 6148
  19.9 10.6 %copy-start.6 = (bf16[128,4]{0,1:T(4,128)(2,1)S(1)}, bf16[128,4]{0,1:T(4,128)(2,1)}, u32[]{:S(2)}) copy-start(bf16[128,4]{0,1:T(4,128)(2,1)} %param.9) | copy-start | bytes 3076
  19.9 17.4 %collective-permute-start.5 = (bf16[96,384]{1,0:T(8,128)(2,1)S(1)}, bf16[96,384]{1,0:T(8,128)(2,1)S(1)}, u32[]{:S(2)}, u32[]{:S(2)}) collective-permute-start(bf16[96,384]{1,0:T(8,128)(2,1)S(1)} %weight_pad.1.refs_0_), channel_id=1, source_target_pairs={{0,48},{16,0},{32,16},{48,32},{1,49},{17,1},{33,17},{49,33},{2,50}... | collective-permute-start | bytes 221192 | tf_op jit(solution)/shard_map/ppermute | solution.py:287
  25.6 15.6 %collective-permute-start.4 = (bf16[96,384]{1,0:T(8,128)(2,1)S(1)}, bf16[96,384]{1,0:T(8,128)(2,1)S(1)}, u32[]{:S(2)}, u32[]{:S(2)}) collective-permute-start(bf16[96,384]{1,0:T(8,128)(2,1)S(1)} %weight_pad.1.refs_0_), channel_id=1, source_target_pairs={{0,32},{16,48},{32,0},{48,16},{1,33},{17,49},{33,1},{49,17},{2,34}... | collective-permute-start | bytes 221192 | tf_op jit(solution)/shard_map/ppermute | solution.py:287
  27.5 13.7 %collective-permute-start.3 = (bf16[96,384]{1,0:T(8,128)(2,1)S(1)}, bf16[96,384]{1,0:T(8,128)(2,1)S(1)}, u32[]{:S(2)}, u32[]{:S(2)}) collective-permute-start(bf16[96,384]{1,0:T(8,128)(2,1)S(1)} %weight_pad.1.refs_0_), channel_id=1, source_target_pairs={{0,16},{16,32},{32,48},{48,0},{1,17},{17,33},{33,49},{49,1},{2,18}... | collective-permute-start | bytes 221192 | tf_op jit(solution)/shard_map/ppermute | solution.py:287
  31.4 20.4 %collective-permute-start.2 = (bf16[320,384]{1,0:T(8,128)(2,1)S(1)}, bf16[320,384]{1,0:T(8,128)(2,1)}, u32[]{:S(2)}, u32[]{:S(2)}) collective-permute-start(bf16[320,384]{1,0:T(8,128)(2,1)S(1)} %send_other.1), channel_id=1, source_target_pairs={{0,2},{2,0},{1,3},{3,1},{4,6},{6,4},{5,7},{7,5},{8,10},{10,8},{9,1... | collective-permute-start | bytes 737288 | tf_op jit(solution)/shard_map/ppermute | solution.py:287
  37.3 17.7 %collective-permute-start.1 = (bf16[1536,128]{1,0:T(8,128)(2,1)}, bf16[1536,128]{1,0:T(8,128)(2,1)}, u32[]{:S(2)}, u32[]{:S(2)}) collective-permute-start(bf16[1536,128]{1,0:T(8,128)(2,1)} %get-tuple-element.28.high_ref), channel_id=1, source_target_pairs={{0,2},{2,0},{1,3},{3,1},{4,6},{6,4},{5,7},{7,5},{8,10},{10,8},{9,1... | collective-permute-start | bytes 1179656 | tf_op jit(solution)/shard_map/ppermute | solution.py:287
  42.5 1.4 copy-start.7
  48.2 18.7 %all-to-all-start.1 = ((bf16[8,40,1536]{2,1,0:T(8,128)(2,1)}), bf16[8,40,1536]{2,1,0:T(8,128)(2,1)S(1)}, u32[]{:S(2)}, u32[]{:S(2)}) async-start(bf16[8,40,1536]{2,1,0:T(8,128)(2,1)} %bitcast.43), calls=%async_computation.1 | async-start | bytes 1966080 | tf_op jit(solution)/shard_map/all_to_all | solution.py:303
  55.1 1.0 copy-start.8
  67.0 1.0 copy-start
  103.1 81.3 %all-to-all-start.3 = ((bf16[32,272,128]{2,1,0:T(8,128)(2,1)}), bf16[32,272,128]{2,1,0:T(8,128)(2,1)}, u32[]{:S(2)}, u32[]{:S(2)}) async-start(bf16[32,272,128]{2,1,0:T(8,128)(2,1)} %bitcast.40), calls=%async_computation.3 | async-start | bytes 4456448 | tf_op jit(solution)/shard_map/all_to_all | solution.py:303
  115.0 1.2 copy-start.1
  116.2 1.7 copy-start.4
  117.8 46.1 %copy-start.3 = (bf16[128,4,360]{0,2,1:T(8,128)(2,1)S(1)}, bf16[128,4,360]{0,2,1:T(8,128)(2,1)}, u32[]{:S(2)}) copy-start(bf16[128,4,360]{0,2,1:T(8,128)(2,1)} %param.8) | copy-start | bytes 1105924
  120.6 14.1 %collective-permute-start.6 = (bf16[2,40,360]{2,1,0:T(8,128)(2,1)S(1)}, bf16[2,40,360]{2,1,0:T(8,128)(2,1)S(1)}, u32[]{:S(2)}, u32[]{:S(2)}) collective-permute-start(bf16[2,40,360]{2,1,0:T(8,128)(2,1)S(1)} %get-tuple-element.34), channel_id=1, source_target_pairs={{0,1},{1,0},{4,5},{5,4},{8,9},{9,8},{12,13},{13,12},{2,3},{3,2},{6... | collective-permute-start | bytes 172808 | tf_op jit(solution)/shard_map/ppermute | solution.py:299
  122.5 16.4 %collective-permute-start.7 = (bf16[2,40,360]{2,1,0:T(8,128)(2,1)S(1)}, bf16[2,40,360]{2,1,0:T(8,128)(2,1)S(1)}, u32[]{:S(2)}, u32[]{:S(2)}) collective-permute-start(bf16[2,40,360]{2,1,0:T(8,128)(2,1)S(1)} %get-tuple-element.35), channel_id=1, source_target_pairs={{0,4},{1,5},{4,8},{5,9},{8,12},{9,13},{12,0},{13,1},{2,6},{3,7},{6... | collective-permute-start | bytes 172808 | tf_op jit(solution)/shard_map/ppermute | solution.py:299
  125.0 17.1 %collective-permute-start.8 = (bf16[2,40,360]{2,1,0:T(8,128)(2,1)S(1)}, bf16[2,40,360]{2,1,0:T(8,128)(2,1)S(1)}, u32[]{:S(2)}, u32[]{:S(2)}) collective-permute-start(bf16[2,40,360]{2,1,0:T(8,128)(2,1)S(1)} %get-tuple-element.36), channel_id=1, source_target_pairs={{0,5},{1,4},{4,9},{5,8},{8,13},{9,12},{12,1},{13,0},{2,7},{3,6},{6... | collective-permute-start | bytes 172808 | tf_op jit(solution)/shard_map/ppermute | solution.py:299
  127.1 15.1 %collective-permute-start.9 = (bf16[2,40,360]{2,1,0:T(8,128)(2,1)S(1)}, bf16[2,40,360]{2,1,0:T(8,128)(2,1)S(1)}, u32[]{:S(2)}, u32[]{:S(2)}) collective-permute-start(bf16[2,40,360]{2,1,0:T(8,128)(2,1)S(1)} %get-tuple-element.37), channel_id=1, source_target_pairs={{0,8},{1,9},{4,12},{5,13},{8,0},{9,1},{12,4},{13,5},{2,10},{3,11},... | collective-permute-start | bytes 172808 | tf_op jit(solution)/shard_map/ppermute | solution.py:299
  132.8 9.3 %collective-permute-start.10 = (bf16[2,40,360]{2,1,0:T(8,128)(2,1)S(1)}, bf16[2,40,360]{2,1,0:T(8,128)(2,1)S(1)}, u32[]{:S(2)}, u32[]{:S(2)}) collective-permute-start(bf16[2,40,360]{2,1,0:T(8,128)(2,1)S(1)} %get-tuple-element.38), channel_id=1, source_target_pairs={{0,9},{1,8},{4,13},{5,12},{8,1},{9,0},{12,5},{13,4},{2,11},{3,10},... | collective-permute-start | bytes 172808 | tf_op jit(solution)/shard_map/ppermute | solution.py:299
  134.8 7.4 %collective-permute-start.11 = (bf16[2,40,360]{2,1,0:T(8,128)(2,1)S(1)}, bf16[2,40,360]{2,1,0:T(8,128)(2,1)S(1)}, u32[]{:S(2)}, u32[]{:S(2)}) collective-permute-start(bf16[2,40,360]{2,1,0:T(8,128)(2,1)S(1)} %get-tuple-element.39), channel_id=1, source_target_pairs={{0,12},{1,13},{4,0},{5,1},{8,4},{9,5},{12,8},{13,9},{2,14},{3,15},... | collective-permute-start | bytes 172808 | tf_op jit(solution)/shard_map/ppermute | solution.py:299
  138.9 5.9 %collective-permute-start.12 = (bf16[2,40,360]{2,1,0:T(8,128)(2,1)S(1)}, bf16[2,40,360]{2,1,0:T(8,128)(2,1)S(1)}, u32[]{:S(2)}, u32[]{:S(2)}) collective-permute-start(bf16[2,40,360]{2,1,0:T(8,128)(2,1)S(1)} %get-tuple-element.40), channel_id=1, source_target_pairs={{0,13},{1,12},{4,1},{5,0},{8,5},{9,4},{12,9},{13,8},{2,15},{3,14},... | collective-permute-start | bytes 172808 | tf_op jit(solution)/shard_map/ppermute | solution.py:299
  144.8 19.1 %collective-permute-start.13 = (bf16[8,40,360]{2,1,0:T(8,128)(2,1)S(1)}, bf16[8,40,360]{2,1,0:T(8,128)(2,1)S(1)}, u32[]{:S(2)}, u32[]{:S(2)}) collective-permute-start(bf16[8,40,360]{2,1,0:T(8,128)(2,1)S(1)} %stack_other.1), channel_id=1, source_target_pairs={{0,2},{2,0},{1,3},{3,1},{4,6},{6,4},{5,7},{7,5},{8,10},{10,8},{9,1... | collective-permute-start | bytes 691208 | tf_op jit(solution)/shard_map/ppermute | solution.py:287
Sparse Core Ops, SparseCore 0:
  42.6 60.4 all-gather.1
